TPU v7x, 32 devices: a whole 2x2x4 slice. The times are simulated.
32 devices in a mesh: dp: 4 (over z), expert: 8 (over y, x, core).
Axes of the slice: x: 2, y: 2, z: 4, core: 2. Of those that a mesh axis runs over, the one named last changes fastest.
Arguments:
- tokens: bfloat16 [4096, 2048], P(('dp', 'expert')), may hold values from -6 to 6
- lengths: int32 [32], P(('dp', 'expert')), may hold values from 1 to 128, 2944 in all
- routes: int32 [4096, 4], P(('dp', 'expert')), may hold values from 0 to 7, all different within a row; in each aligned block of 128 rows (0 to 127, 128 to 255, ...) at most 80 rows name the same one
- gate_values: float32 [4096, 4], P(('dp', 'expert')), may hold values from 0.15 to 0.45
- cotangent: bfloat16 [4096, 2048], P(('dp', 'expert')), may hold values from -6 to 6
- norm1_gain: bfloat16 [2048], P(('dp', 'expert')), may hold values from 0.5 to 1.5
- qkv_weight: bfloat16 [2048, 6144], P(('dp', 'expert')), may hold values from -0.125 to 0.125
- qkv_bias: bfloat16 [6144], P(('dp', 'expert')), may hold values from -2 to 2
- out_weight: bfloat16 [2048, 2048], P(('dp', 'expert')), may hold values from -0.5 to 0.5
- norm2_gain: bfloat16 [2048], P(('dp', 'expert')), may hold values from 0.5 to 1.5
- shared_in: bfloat16 [2048, 2, 5632], P(None, None, ('dp', 'expert')), may hold values from -0.125 to 0.125
- shared_out: bfloat16 [5632, 2048], P(('dp', 'expert')), may hold values from -0.15625 to 0.15625
- shared_gate: bfloat16 [2048], P(('dp', 'expert')), may hold values from -0.125 to 0.125
- expert_in: bfloat16 [8, 2048, 2816], P('expert'), may hold values from -0.125 to 0.125
- expert_out: bfloat16 [8, 1408, 2048], P('expert'), may hold values from -0.21875 to 0.21875
Outputs:
- output: bfloat16 [4096, 2048], P(('dp', 'expert'))
- tokens_grad: float32 [4096, 2048], P(('dp', 'expert'))
- norm1_grad: float32 [2048], P(('dp', 'expert'))
- qkv_weight_grad: float32 [2048, 6144], P(('dp', 'expert'))
- qkv_bias_grad: float32 [6144], P(('dp', 'expert'))
- out_weight_grad: float32 [2048, 2048], P(('dp', 'expert'))
- norm2_grad: float32 [2048], P(('dp', 'expert'))
- shared_in_grad: float32 [2048, 2, 5632], P(None, None, ('dp', 'expert'))
- shared_out_grad: float32 [5632, 2048], P(('dp', 'expert'))
- shared_gate_grad: float32 [2048], P(('dp', 'expert'))
- expert_in_grad: float32 [8, 2048, 2816], P('expert', 'dp')
- expert_out_grad: float32 [8, 1408, 2048], P('expert', 'dp')
- gate_values_grad: float32 [4096, 4], P(('dp', 'expert'))
Inputs may be any that keep to these rules, and one draw needn't show every extreme that they name: `routes`: each row names 4 different experts; among the 128 rows of one device no expert is named more than 80 times, a bound that some block reaches. The lengths sum to 2944; the largest is 128.
All inputs are finite; a program needn't handle non-finite values. No bound on the sum of `lengths` on one device may be relied on, other than what follows from the above.
Results may differ from a plain program's by a relative error of at most 0.015.
Values may be sent and summed in bfloat16 or wider, within the bound.
No kernel may reach another device: no remote copies, remote signals or barrier semaphores. Data moves between devices by JAX's collectives and lax.ppermute only.
A program may use at most 320 MiB of HBM per device.

v0:
```python
import math

import jax
import jax.numpy as jnp
from jax import lax
from jax.sharding import PartitionSpec as P

HEAD = 128


NORM_EPS = 1e-06
THETA = 1000000.0


def carried_in(shard, axis, combine, identity):
    count, mine = (lax.axis_size(axis), lax.axis_index(axis))
    everything = lax.all_gather(shard, axis)
    start = jnp.broadcast_to(jnp.asarray(identity, shard.dtype), shard.shape)

    def step(k, before):
        reached = k < mine
        new = combine(before, everything[k])
        return jnp.where(reached, new, before)

    return lax.fori_loop(0, count, step, start)


def rms_scale(inputs, gain_vec):
    return (
        inputs * lax.rsqrt(jnp.mean(inputs * inputs, axis=-1, keepdims=True) + NORM_EPS) * gain_vec
    )


def rotary_tables(row_count, head_width):
    half_width = head_width // 2
    freqs = THETA ** (-(jnp.arange(half_width, dtype=jnp.float32) * 2.0) / head_width)
    angles = jnp.arange(row_count, dtype=jnp.float32)[:, None] * freqs[None, :]
    return (jnp.cos(angles), jnp.sin(angles))


def rotate(inputs, cos_table, sin_table):
    half_width = inputs.shape[-1] // 2
    first = inputs[..., :half_width]
    second = inputs[..., half_width:]
    cos_part = cos_table[:, None, :]
    sin_part = sin_table[:, None, :]
    return jnp.concatenate(
        [first * cos_part - second * sin_part, second * cos_part + first * sin_part], axis=-1
    )


def swiglu(joined):
    half_width = joined.shape[-1] // 2
    return jax.nn.silu(joined[..., :half_width]) * joined[..., half_width:]


def shards(
    tokens,
    lengths,
    routes,
    gate_values,
    cotangent,
    norm1_gain,
    qkv_weight,
    qkv_bias,
    out_weight,
    norm2_gain,
    shared_in,
    shared_out,
    shared_gate,
    expert_in,
    expert_out,
):
    row_count, model_width = tokens.shape
    head_count = model_width // HEAD
    top_count = routes.shape[1]
    local_experts = expert_in.shape[0]
    owners = lax.axis_size("expert")
    expert_count = owners * local_experts
    devices = lax.axis_size("dp") * owners
    valid_total = 23 * row_count * devices // 32
    capacity = 5 * valid_total * top_count // (4 * expert_count * lax.axis_size("dp"))
    slot_most = 5 * row_count * top_count // (4 * expert_count)
    slot_total = expert_count * slot_most

    def dense_params():
        return (
            lax.all_gather(norm1_gain, ("dp", "expert"), axis=0, tiled=True),
            lax.all_gather(qkv_weight, ("dp", "expert"), axis=0, tiled=True),
            lax.all_gather(qkv_bias, ("dp", "expert"), axis=0, tiled=True),
            lax.all_gather(out_weight, ("dp", "expert"), axis=0, tiled=True),
            lax.all_gather(norm2_gain, ("dp", "expert"), axis=0, tiled=True),
            lax.all_gather(shared_gate, ("dp", "expert"), axis=0, tiled=True),
        )

    norm1_full, qkv_full, bias_full, out_full, norm2_full, shared_gate_full = dense_params()
    token_rows = tokens.astype(jnp.float32)
    positions = jnp.arange(row_count, dtype=jnp.int32)
    valid_tok = positions < lengths[0]
    valid_float = valid_tok.astype(jnp.float32)[:, None]
    normed1 = rms_scale(token_rows, norm1_full.astype(jnp.float32))
    normed1_low = normed1.astype(jnp.bfloat16)
    qkv_lin = jnp.dot(normed1_low, qkv_full, preferred_element_type=jnp.float32) + bias_full.astype(
        jnp.float32
    )
    cos_table, sin_table = rotary_tables(row_count, HEAD)

    def rotate_pair(pair_lin):
        query_part = pair_lin[:, :model_width].reshape(row_count, head_count, HEAD)
        key_part = pair_lin[:, model_width:].reshape(row_count, head_count, HEAD)
        return (rotate(query_part, cos_table, sin_table), rotate(key_part, cos_table, sin_table))

    query_rot, key_rot = rotate_pair(qkv_lin[:, : 2 * model_width])
    query_heads = query_rot.astype(jnp.bfloat16)
    key_heads = key_rot.astype(jnp.bfloat16)
    value_heads = (
        qkv_lin[:, 2 * model_width :].reshape(row_count, head_count, HEAD).astype(jnp.bfloat16)
    )
    score_scale = 1.0 / math.sqrt(HEAD)
    causal = positions[:, None] >= positions[None, :]
    scores = (
        jnp.einsum("qhd,khd->hqk", query_heads, key_heads, preferred_element_type=jnp.float32)
        * score_scale
    )
    scores = jnp.where(causal[None, :, :], scores, -1e30)
    score_peak = jnp.max(scores, axis=-1, keepdims=True)
    unscaled = jnp.exp(scores - score_peak)
    denominator = jnp.sum(unscaled, axis=-1, keepdims=True)
    log_total = score_peak + jnp.log(denominator)
    attn_probs = unscaled / denominator
    mixed_rows = jnp.einsum(
        "hqk,khd->qhd",
        attn_probs.astype(jnp.bfloat16),
        value_heads,
        preferred_element_type=jnp.float32,
    )
    mixed_low = mixed_rows.reshape(row_count, model_width).astype(jnp.bfloat16)
    branch = jnp.dot(mixed_low, out_full, preferred_element_type=jnp.float32)
    hidden = token_rows + branch
    normed2 = rms_scale(hidden, norm2_full.astype(jnp.float32))
    normed2_low = normed2.astype(jnp.bfloat16)

    def group_rows(rows):
        return lax.all_gather(rows, "expert", axis=0, tiled=True)

    def group_sums(terms):
        return lax.psum_scatter(terms, "expert", scatter_dimension=0, tiled=True)

    unit_in, unit_out = (
        lax.all_gather(shared_in, "dp", axis=2, tiled=True),
        lax.all_gather(shared_out, "dp", axis=0, tiled=True),
    )
    unit_count = unit_in.shape[2]
    unit_in_flat = unit_in.reshape(model_width, 2 * unit_count)
    group_normed = group_rows(normed2_low)
    shared_pre = jnp.dot(group_normed, unit_in_flat, preferred_element_type=jnp.float32)
    shared_act = swiglu(shared_pre).astype(jnp.bfloat16)
    shared_val = group_sums(jnp.dot(shared_act, unit_out, preferred_element_type=jnp.float32))
    shared_logit = jnp.dot(normed2_low, shared_gate_full, preferred_element_type=jnp.float32)
    shared_weight = jax.nn.sigmoid(shared_logit)
    pair_live = jnp.broadcast_to(valid_tok[:, None], routes.shape).reshape(-1)
    pair_expert = routes.reshape(-1)
    onehot = (
        (pair_expert[:, None] == jnp.arange(expert_count, dtype=jnp.int32)[None, :])
        & pair_live[:, None]
    ).astype(jnp.int32)
    local_counts = jnp.sum(onehot, axis=0)
    earlier = jnp.cumsum(onehot, axis=0) - onehot
    local_rank = jnp.sum(earlier * onehot, axis=1)
    offsets = carried_in(local_counts, "expert", jnp.add, jnp.zeros_like(local_counts))
    slot_rank = jnp.sum(offsets[None, :] * onehot, axis=1) + local_rank
    pair_kept = pair_live & (slot_rank < capacity)
    slot_index = jnp.where(pair_kept, pair_expert * slot_most + local_rank, slot_total)
    pair_token = jnp.arange(row_count * top_count, dtype=jnp.int32) // top_count
    slot_token = jnp.zeros((slot_total,), jnp.int32).at[slot_index].set(pair_token, mode="drop")
    slot_live = jnp.zeros((slot_total,), jnp.float32).at[slot_index].set(1.0, mode="drop")
    send_rows = jnp.take(normed2_low, slot_token, axis=0) * slot_live[:, None].astype(jnp.bfloat16)
    send_rows = send_rows.reshape(owners, local_experts, slot_most, model_width)
    arrived = lax.all_to_all(send_rows, "expert", split_axis=0, concat_axis=0, tiled=True)
    expert_pre = jnp.einsum(
        "semd,edf->semf", arrived, expert_in, preferred_element_type=jnp.float32
    )
    expert_act = swiglu(expert_pre).astype(jnp.bfloat16)
    produced = jnp.einsum(
        "semf,efd->semd", expert_act, expert_out, preferred_element_type=jnp.float32
    ).astype(jnp.bfloat16)
    returned = lax.all_to_all(produced, "expert", split_axis=0, concat_axis=0, tiled=True).reshape(
        slot_total, model_width
    )
    pair_slot = jnp.minimum(slot_index, slot_total - 1)
    picked = (
        jnp.take(returned, pair_slot, axis=0)
        .reshape(row_count, top_count, model_width)
        .astype(jnp.float32)
    )
    kept_float = pair_kept.reshape(row_count, top_count).astype(jnp.float32)
    pair_weight = gate_values * kept_float
    routed = jnp.sum(picked * pair_weight[:, :, None], axis=1)
    output = (valid_float * (hidden + shared_weight[:, None] * shared_val + routed)).astype(
        jnp.bfloat16
    )
    grad_out = cotangent.astype(jnp.float32) * valid_float
    gate_values_grad = jnp.einsum("td,tkd->tk", grad_out, picked) * kept_float
    shared_val_grad = (grad_out * shared_weight[:, None]).astype(jnp.bfloat16)
    logit_grad = jnp.sum(grad_out * shared_val, axis=1) * shared_weight * (1.0 - shared_weight)
    shared_gate_grad_full = jnp.einsum("t,td->d", logit_grad, normed2_low.astype(jnp.float32))
    val_grad_rows = group_rows(shared_val_grad)
    unit_out_grad = jnp.dot(shared_act.T, val_grad_rows, preferred_element_type=jnp.float32)
    shared_act_grad = jnp.dot(val_grad_rows, unit_out.T, preferred_element_type=jnp.float32)
    swiglu_value, swiglu_back = jax.vjp(swiglu, shared_pre)
    shared_pre_grad = swiglu_back(shared_act_grad)[0].astype(jnp.bfloat16)
    unit_in_grad = jnp.dot(
        group_normed.T, shared_pre_grad, preferred_element_type=jnp.float32
    ).reshape(model_width, 2, unit_count)
    normed2_grad = group_sums(
        jnp.dot(shared_pre_grad, unit_in_flat.T, preferred_element_type=jnp.float32)
    )
    shared_in_grad, shared_out_grad = (
        lax.psum_scatter(
            unit_in_grad.astype(jnp.bfloat16), "dp", scatter_dimension=2, tiled=True
        ).astype(jnp.float32),
        lax.psum_scatter(
            unit_out_grad.astype(jnp.bfloat16), "dp", scatter_dimension=0, tiled=True
        ).astype(jnp.float32),
    )
    normed2_grad = (
        normed2_grad + logit_grad[:, None] * shared_gate_full.astype(jnp.float32)[None, :]
    )
    slot_gate = (
        jnp.zeros((slot_total,), jnp.float32)
        .at[slot_index]
        .set(gate_values.reshape(-1), mode="drop")
    )
    back_send = (jnp.take(grad_out, slot_token, axis=0) * slot_gate[:, None]).astype(jnp.bfloat16)
    back_send = back_send.reshape(owners, local_experts, slot_most, model_width)
    back_arrived = lax.all_to_all(back_send, "expert", split_axis=0, concat_axis=0, tiled=True)
    expert_act_grad = jnp.einsum(
        "semd,efd->semf", back_arrived, expert_out, preferred_element_type=jnp.float32
    )
    expert_out_grad_full = jnp.einsum(
        "semf,semd->efd", expert_act, back_arrived, preferred_element_type=jnp.float32
    )
    expert_value, expert_swiglu_back = jax.vjp(swiglu, expert_pre)
    expert_pre_grad = expert_swiglu_back(expert_act_grad)[0].astype(jnp.bfloat16)
    expert_in_grad_full = jnp.einsum(
        "semd,semf->edf", arrived, expert_pre_grad, preferred_element_type=jnp.float32
    )
    rows_grad = jnp.einsum(
        "semf,edf->semd", expert_pre_grad, expert_in, preferred_element_type=jnp.float32
    ).astype(jnp.bfloat16)
    rows_back = lax.all_to_all(
        rows_grad, "expert", split_axis=0, concat_axis=0, tiled=True
    ).reshape(slot_total, model_width)
    expert_sums = (
        lax.psum_scatter(
            expert_in_grad_full.astype(jnp.bfloat16), "dp", scatter_dimension=1, tiled=True
        ).astype(jnp.float32),
        lax.psum_scatter(
            expert_out_grad_full.astype(jnp.bfloat16), "dp", scatter_dimension=1, tiled=True
        ).astype(jnp.float32),
    )
    routed_grad = (
        jnp.take(rows_back, pair_slot, axis=0)
        .reshape(row_count, top_count, model_width)
        .astype(jnp.float32)
    )
    normed2_grad = normed2_grad + jnp.sum(routed_grad * kept_float[:, :, None], axis=1)
    norm2_value, norm2_back = jax.vjp(rms_scale, hidden, norm2_full.astype(jnp.float32))
    hidden_grad_norm, norm2_grad_full = norm2_back(normed2_grad)
    hidden_grad = grad_out + hidden_grad_norm
    norm1_full, qkv_full, bias_full, out_full, norm2_again, gate_again = dense_params()
    branch_grad = hidden_grad.astype(jnp.bfloat16)
    out_weight_grad_full = jnp.dot(mixed_low.T, branch_grad, preferred_element_type=jnp.float32)
    mixed_grad = jnp.dot(branch_grad, out_full.T, preferred_element_type=jnp.float32).astype(
        jnp.bfloat16
    )
    mixed_grad = mixed_grad.reshape(row_count, head_count, HEAD)
    scores_again = (
        jnp.einsum("qhd,khd->hqk", query_heads, key_heads, preferred_element_type=jnp.float32)
        * score_scale
    )
    scores_again = jnp.where(causal[None, :, :], scores_again, -1e30)
    probs_again = jnp.exp(scores_again - log_total)
    value_grad = jnp.einsum(
        "hqk,qhd->khd",
        probs_again.astype(jnp.bfloat16),
        mixed_grad,
        preferred_element_type=jnp.float32,
    )
    probs_grad = jnp.einsum(
        "qhd,khd->hqk", mixed_grad, value_heads, preferred_element_type=jnp.float32
    )
    score_grad = probs_again * (
        probs_grad - jnp.sum(probs_grad * probs_again, axis=-1, keepdims=True)
    )
    score_grad = score_grad.astype(jnp.bfloat16)
    query_grad = (
        jnp.einsum("hqk,khd->qhd", score_grad, key_heads, preferred_element_type=jnp.float32)
        * score_scale
    )
    key_grad = (
        jnp.einsum("hqk,qhd->khd", score_grad, query_heads, preferred_element_type=jnp.float32)
        * score_scale
    )
    rotate_value, rotate_back = jax.vjp(rotate_pair, qkv_lin[:, : 2 * model_width])
    pair_grad = rotate_back((query_grad, key_grad))[0]
    qkv_grad = jnp.concatenate(
        [pair_grad, value_grad.reshape(row_count, model_width)], axis=1
    ).astype(jnp.bfloat16)
    qkv_bias_grad_full = jnp.sum(qkv_grad.astype(jnp.float32), axis=0)
    qkv_weight_grad_full = jnp.dot(normed1_low.T, qkv_grad, preferred_element_type=jnp.float32)
    normed1_grad = jnp.dot(qkv_grad, qkv_full.T, preferred_element_type=jnp.float32)
    norm1_value, norm1_back = jax.vjp(rms_scale, token_rows, norm1_full.astype(jnp.float32))
    token_grad_norm, norm1_grad_full = norm1_back(normed1_grad)
    tokens_grad = hidden_grad + token_grad_norm
    attn_sums = (
        lax.psum_scatter(norm1_grad_full, ("dp", "expert"), scatter_dimension=0, tiled=True),
        lax.psum_scatter(qkv_weight_grad_full, ("dp", "expert"), scatter_dimension=0, tiled=True),
        lax.psum_scatter(qkv_bias_grad_full, ("dp", "expert"), scatter_dimension=0, tiled=True),
        lax.psum_scatter(out_weight_grad_full, ("dp", "expert"), scatter_dimension=0, tiled=True),
        lax.psum_scatter(norm2_grad_full, ("dp", "expert"), scatter_dimension=0, tiled=True),
        lax.psum_scatter(shared_gate_grad_full, ("dp", "expert"), scatter_dimension=0, tiled=True),
    )
    return (
        output,
        tokens_grad,
        attn_sums[0],
        attn_sums[1],
        attn_sums[2],
        attn_sums[3],
        attn_sums[4],
        shared_in_grad,
        shared_out_grad,
        attn_sums[5],
        expert_sums[0],
        expert_sums[1],
        gate_values_grad,
    )


def solution(mesh):
    in_specs = (
        P(("dp", "expert"), None),
        P(("dp", "expert")),
        P(("dp", "expert"), None),
        P(("dp", "expert"), None),
        P(("dp", "expert"), None),
        P(("dp", "expert")),
        P(("dp", "expert"), None),
        P(("dp", "expert")),
        P(("dp", "expert"), None),
        P(("dp", "expert")),
        P(None, None, ("dp", "expert")),
        P(("dp", "expert"), None),
        P(("dp", "expert")),
        P("expert", None, None),
        P("expert", None, None),
    )
    out_specs = (
        P(("dp", "expert"), None),
        P(("dp", "expert"), None),
        P(("dp", "expert")),
        P(("dp", "expert"), None),
        P(("dp", "expert")),
        P(("dp", "expert"), None),
        P(("dp", "expert")),
        P(None, None, ("dp", "expert")),
        P(("dp", "expert"), None),
        P(("dp", "expert")),
        P("expert", "dp", None),
        P("expert", "dp", None),
        P(("dp", "expert"), None),
    )
    return jax.shard_map(shards, mesh=mesh, in_specs=in_specs, out_specs=out_specs, check_vma=False)
```

profile of v0, /device:TPU:0, one launch (start us, length us, event | category | flops | bytes accessed | tf_op | source)
XLA Modules:
  0.0 1788.6 jit_solution(120973237257444419)
XLA Ops:
  12.9 43.6 %all-reduce.20 = (bf16[6144]{0:T(1024)(128)(2,1)S(1)}, bf16[2048]{0:T(1024)(128)(2,1)S(1)}, bf16[2048]{0:T(1024)(128)(2,1)S(1)}, bf16[2048]{0:T(1024)(128)(2,1)S(1)}) all-reduce(bf16[6144]{0:T(1024)(128)(2,1)S(1)} %dynamic-update-slice.1, bf16[2048]{0:T(1024)(128)(2,1)S(1)} %dynamic-update-slice, ...), channel_id=1, replica_groups=mesh['dp'=4,'expert'=8] {'dp','expert'}, use_global_device_ids=true, to_apply=%add.11 | all-reduce | flops 12288 | bytes 49152
  58.7 111.3 %all-gather.8.cloned.1.call-done = bf16[2048,6144]{1,0:T(8,128)(2,1)} async-done(((bf16[64,6144]{1,0:T(8,128)(2,1)}), bf16[2048,6144]{1,0:T(8,128)(2,1)}) %all-gather.8.cloned.1.call-update) | async-done | bytes 25165840 | tf_op jit(solution)/shard_map/all_gather | solution.py:89
  170.0 10.1 convolution_add_fusion
  186.4 62.1 %all-gather.10.cloned.1.call-done = bf16[2048,2048]{1,0:T(8,128)(2,1)} async-done(((bf16[64,2048]{1,0:T(8,128)(2,1)}), bf16[2048,2048]{1,0:T(8,128)(2,1)}) %all-gather.10.cloned.1.call-update) | async-done | bytes 8388624 | tf_op jit(solution)/shard_map/all_gather | solution.py:91
  248.6 4.7 multiply_reduce_fusion.6
  259.4 96.0 %all-gather.14.cloned.1.call-done = bf16[2048,2,704]{0,2,1:T(8,128)(2,1)} async-done(((bf16[2048,2,176]{0,2,1:T(8,128)(2,1)}), bf16[2048,2,704]{0,2,1:T(8,128)(2,1)}) %all-gather.14.cloned.1.call-update) | async-done | bytes 5767184 | tf_op jit(solution)/shard_map/all_gather | solution.py:150
  355.5 36.8 %all-gather.12.cloned.1.call-done = bf16[1024,2048]{1,0:T(8,128)(2,1)} async-done(((bf16[128,2048]{1,0:T(8,128)(2,1)}), bf16[1024,2048]{1,0:T(8,128)(2,1)}) %all-gather.12.cloned.1.call-update) | async-done | bytes 4194320 | tf_op jit(solution)/shard_map/all_gather | solution.py:144
  392.3 11.8 fusion.119
  404.0 48.9 %all-gather.16.cloned.1.call-done = bf16[704,2048]{1,0:T(8,128)(2,1)} async-done(((bf16[176,2048]{1,0:T(8,128)(2,1)}), bf16[704,2048]{1,0:T(8,128)(2,1)}) %all-gather.16.cloned.1.call-update) | async-done | bytes 2883600 | tf_op jit(solution)/shard_map/all_gather | solution.py:151
  452.9 37.7 %all-gather.18.cloned.1.call-done = bf16[1024,2048]{1,0:T(8,128)(2,1)} async-done(((bf16[128,2048]{1,0:T(8,128)(2,1)}), bf16[1024,2048]{1,0:T(8,128)(2,1)}) %all-gather.18.cloned.1.call-update) | async-done | bytes 4194320 | tf_op jit(solution)/shard_map/all_gather | solution.py:144
  490.6 11.6 fusion.71
  503.4 5.6 fusion.120
  509.1 1.8 copy-done.59
  510.9 12.4 fusion.75
  524.9 7.2 convolution_convert_fusion.1
  532.2 13.6 convolution_convert_fusion
  548.9 7.3 all-reduce.14
  558.1 2.4 scatter_custom_fusion
  560.7 2.4 scatter_custom_fusion.1
  563.3 3.4 gather_fusion
  566.7 1.8 select_multiply_fusion
  568.5 4.7 all-to-all-start
  573.5 2.4 scatter_custom_fusion.2
  576.0 7.2 reduce-scatter.9.cloned.1.call-done
  584.7 4.6 gather_fusion.1
  589.3 4.6 multiply_convert_fusion
  593.9 14.2 all-to-all-done
  608.1 3.6 all-to-all-start.2
  611.8 13.8 fusion.10
  625.6 40.4 %all-to-all-done.2 = bf16[8,1,80,2048]{3,2,1,0:T(8,128)(2,1)S(1)} async-done(((bf16[8,1,80,2048]{3,2,1,0:T(8,128)(2,1)}), bf16[8,1,80,2048]{3,2,1,0:T(8,128)(2,1)S(1)}, u32[]{:S(2)}, u32[]{:S(2)}) %all-to-all-start.2) | async-done | bytes 2621472 | tf_op jit(solution)/shard_map/all_to_all | solution.py:236
  666.0 11.2 bitcast_multiply_fusion.1
  678.4 6.6 fusion.5
  685.5 15.6 fusion.4
  701.1 13.8 fusion.26
  714.8 3.6 all-to-all-start.3
  718.4 9.0 fusion.29
  727.5 23.2 %all-to-all-done.3 = bf16[8,1,80,2048]{3,2,1,0:T(8,128)(2,1)S(1)} async-done(((bf16[8,1,80,2048]{3,2,1,0:T(8,128)(2,1)}), bf16[8,1,80,2048]{3,2,1,0:T(8,128)(2,1)S(1)}, u32[]{:S(2)}, u32[]{:S(2)}) %all-to-all-start.3) | async-done | bytes 2621472 | tf_op jit(solution)/shard_map/all_to_all | solution.py:251
  750.6 4.4 all-to-all-start.1
  756.3 3.3 gather_fusion.3
  759.6 27.7 %all-to-all-done.1 = bf16[8,1,80,2048]{3,2,1,0:T(8,128)(2,1)} async-done(((bf16[8,1,80,2048]{3,2,1,0:T(8,128)(2,1)}), bf16[8,1,80,2048]{3,2,1,0:T(8,128)(2,1)}, u32[]{:S(2)}, u32[]{:S(2)}) %all-to-all-start.1) | async-done | bytes 2621472 | tf_op jit(solution)/shard_map/all_to_all | solution.py:187
  787.3 7.4 gather_fusion.2
  794.8 4.7 select_convert_fusion
  799.5 5.4 reshape.423
  804.9 2.3 reshape.414
  807.3 5.4 multiply_reduce_fusion
  812.8 1.9 multiply_reduce_fusion.2
  814.8 2.8 fusion.52
  817.8 3.5 multiply_reduce_fusion.1
  822.7 8.1 fusion.72
  831.5 6.4 convolution_convert_fusion.2
  838.2 1.8 multiply_reduce_fusion.3
  841.6 2.0 multiply_add_fusion.3
  845.3 1.9 pad_add_fusion
  851.9 20.8 %fusion.69 = f32[2048,6144]{1,0:T(8,128)} fusion(bf16[128,2048]{0,1:T(8,128)(2,1)S(1)} %bitcast.205, bf16[128,4096]{0,1:T(8,128)(2,1)S(1)} %add_convert_fusion.2, bf16[128,2048]{1,0:T(8,128)(2,1)S(1)} %copy-done.7, f32[2048]{0:T(1024)S(1)} %copy-done.33, f32[128]{0:T(128)S(1)} %copy-done.41), kind=kOutput, calls=%fused_computation.132 | convolution fusion | flops 3225419776 | bytes 52437504 | tf_op jit(solution)/shard_map/dot_general | solution.py:311
  872.8 2.4 convert_element_type.225
  875.2 3.3 convert_element_type.223
  881.0 13.6 fusion.47
  894.6 47.3 %all-reduce.19 = (f32[2048]{0:T(1024)S(1)}, f32[6144]{0:T(1024)S(1)}, f32[2048]{0:T(1024)S(1)}, f32[2048]{0:T(1024)S(1)}) all-reduce(f32[2048]{0:T(1024)S(1)} %get-tuple-element.137, f32[6144]{0:T(1024)S(1)} %convert_reduce_fusion, f32[2048]{0:T(1024)S(1)} %get-tuple-element.135, ...), channel_id=5, replica_groups=mesh['dp'=4,'expert'=8] {'dp','expert'}, use_global_device_ids=true, to_apply=%region_23.25.clone | all-reduce | flops 12288 | bytes 98304
  945.6 11.6 reduce-scatter.23.cloned.1.call-done
  957.2 3.3 convert_element_type.231
  960.5 194.4 %reduce-scatter.21.cloned.1.call-done = bf16[1,512,2816]{2,1,0:T(8,128)(2,1)} async-done(((bf16[1,2048,2816]{2,1,0:T(8,128)(2,1)}), bf16[1,512,2816]{2,1,0:T(8,128)(2,1)}) %reduce-scatter.21.cloned.1.call-update) | async-done | bytes 2883600 | tf_op jit(solution)/shard_map/reduce_scatter | solution.py:255
  1154.8 4.8 convert_element_type.228
  1159.6 182.0 %reduce-scatter.15.cloned.1.call-done = f32[64,2048]{1,0:T(8,128)} async-done(((f32[2048,2048]{1,0:T(8,128)}), f32[64,2048]{1,0:T(8,128)}) %reduce-scatter.15.cloned.1.call-update) | async-done | bytes 524304 | tf_op jit(solution)/shard_map/reduce_scatter | solution.py:320
  1341.6 440.1 %reduce-scatter.13.cloned.1.call-done = f32[64,6144]{1,0:T(8,128)} async-done(((f32[2048,6144]{1,0:T(8,128)}), f32[64,6144]{1,0:T(8,128)}) %reduce-scatter.13.cloned.1.call-update) | async-done | bytes 1572880 | tf_op jit(solution)/shard_map/reduce_scatter | solution.py:318
  (256 shorter events, 48.5 us)
Async XLA Ops:
  7.2 162.8 %copy-start.6 = (bf16[128,2048]{1,0:T(8,128)(2,1)S(1)}, bf16[128,2048]{1,0:T(8,128)(2,1)}, u32[]{:S(2)}) copy-start(bf16[128,2048]{1,0:T(8,128)(2,1)} %param.19) | copy-start | bytes 1572868
  7.2 162.8 %all-gather.8.cloned.1.call-start = ((), (), s32[]{:S(2)}) async-start(), calls=%async_computation.12 | async-start | bytes 25952256 | tf_op jit(solution)/shard_map/all_gather | solution.py:89
  7.9 240.6 %all-gather.10.cloned.1.call-start = ((), (), s32[]{:S(2)}) async-start(), calls=%async_computation.13 | async-start | bytes 8650752 | tf_op jit(solution)/shard_map/all_gather | solution.py:91
  8.7 346.8 %all-gather.14.cloned.1.call-start = ((), (), s32[]{:S(2)}) async-start(), calls=%async_computation.15 | async-start | bytes 7208960 | tf_op jit(solution)/shard_map/all_gather | solution.py:150
  9.4 382.9 %all-gather.12.cloned.1.call-start = ((), (), s32[]{:S(2)}) async-start(), calls=%async_computation.14 | async-start | bytes 4718592 | tf_op jit(solution)/shard_map/all_gather | solution.py:144
  56.5 200.1 %copy-start.42 = (bf16[2048]{0:T(1024)(128)(2,1)}, bf16[2048]{0:T(1024)(128)(2,1)S(1)}, u32[]{:S(2)}) copy-start(bf16[2048]{0:T(1024)(128)(2,1)S(1)} %get-tuple-element.156) | copy-start | bytes 12292
  56.5 123.6 %copy-start.32 = (f32[2048]{0:T(1024)}, f32[2048]{0:T(1024)S(1)}, u32[]{:S(2)}) copy-start(f32[2048]{0:T(1024)S(1)} %convert_element_type.182) | copy-start | bytes 24580
  56.5 197.4 %copy-start.34 = (f32[2048]{0:T(1024)}, f32[2048]{0:T(1024)S(1)}, u32[]{:S(2)}) copy-start(f32[2048]{0:T(1024)S(1)} %convert_element_type.190) | copy-start | bytes 24580
  58.4 121.7 %copy-start.40 = (f32[128]{0:T(128)}, f32[128]{0:T(128)S(1)}, u32[]{:S(2)}) copy-start(f32[128]{0:T(128)S(1)} %fusion.96) | copy-start | bytes 1540
  58.7 122.8 %copy-start.27 = (f32[128,64]{1,0:T(8,128)}, f32[128,64]{1,0:T(8,128)S(1)}, u32[]{:S(2)}) copy-start(f32[128,64]{1,0:T(8,128)S(1)} %get-tuple-element.193) | copy-start | bytes 98308
  58.7 122.8 %copy-start.29 = (f32[128,64]{1,0:T(8,128)}, f32[128,64]{1,0:T(8,128)S(1)}, u32[]{:S(2)}) copy-start(f32[128,64]{1,0:T(8,128)S(1)} %get-tuple-element.194) | copy-start | bytes 98308
  180.1 4.5 copy-start.8
  182.8 1.6 copy-start.17
  182.8 1.6 copy-start.19
  182.9 1.6 copy-start.21
  186.4 66.9 %copy-start.24 = (bf16[16,128,128]{2,1,0:T(8,128)(2,1)}, bf16[16,128,128]{2,1,0:T(8,128)(2,1)S(1)}, u32[]{:S(2)}) copy-start(bf16[16,128,128]{2,1,0:T(8,128)(2,1)S(1)} %convolution_convert_fusion.4) | copy-start | bytes 1572868
  253.3 4.7 copy-start.10
  253.9 2.7 copy-start.47
  255.3 197.6 %all-gather.16.cloned.1.call-start = ((), (), s32[]{:S(2)}) async-start(), calls=%async_computation.16 | async-start | bytes 3604480 | tf_op jit(solution)/shard_map/all_gather | solution.py:151
  255.9 234.8 %all-gather.18.cloned.1.call-start = ((), (), s32[]{:S(2)}) async-start(), calls=%async_computation.18 | async-start | bytes 4718592 | tf_op jit(solution)/shard_map/all_gather | solution.py:144
  258.0 146.0 %copy-start.45 = (f32[128]{0:T(128)}, f32[128]{0:T(128)S(1)}, u32[]{:S(2)}) copy-start(f32[128]{0:T(128)S(1)} %fusion.45) | copy-start | bytes 1540
  259.2 324.0 %reduce-scatter.9.cloned.1.call-start = ((), (), s32[]{:S(2)}) async-start(), calls=%async_computation.17 | async-start | bytes 9437184 | tf_op jit(solution)/shard_map/reduce_scatter | solution.py:147
  452.9 50.5 %copy-start.54 = (bf16[704,2048]{1,0:T(8,128)(2,1)S(1)}, bf16[704,2048]{1,0:T(8,128)(2,1)}, u32[]{:S(2)}) copy-start(bf16[704,2048]{1,0:T(8,128)(2,1)} %all-gather.16.cloned.1.call-done) | copy-start | bytes 8650756
  509.0 1.9 copy-start.59
  509.0 303.7 %reduce-scatter.11.cloned.1.call-start = ((), (), s32[]{:S(2)}) async-start(), calls=%async_computation.19 | async-start | bytes 9437184 | tf_op jit(solution)/shard_map/reduce_scatter | solution.py:147
  523.3 1.7 copy-start.57
  523.3 349.5 %reduce-scatter.19.cloned.1.call-start = ((), (), s32[]{:S(2)}) async-start(), calls=%async_computation.23 | async-start | bytes 3604480 | tf_op jit(solution)/shard_map/reduce_scatter | solution.py:222
  532.1 343.1 %reduce-scatter.17.cloned.1.call-start = ((), (), s32[]{:S(2)}) async-start(), calls=%async_computation.22 | async-start | bytes 7208960 | tf_op jit(solution)/shard_map/reduce_scatter | solution.py:219
  545.8 17.4 copy-start
  568.5 4.7 copy-start.49
  568.5 14.6 copy-start.11
  568.5 39.6 %all-to-all-start = ((bf16[8,1,80,2048]{3,2,1,0:T(8,128)(2,1)}), bf16[8,1,80,2048]{3,2,1,0:T(8,128)(2,1)}, u32[]{:S(2)}, u32[]{:S(2)}) async-start(bf16[8,1,80,2048]{3,2,1,0:T(8,128)(2,1)} %select_multiply_fusion), calls=%async_computation.1 | async-start | bytes 5242880 | tf_op jit(solution)/shard_map/all_to_all | solution.py:179
  608.1 57.9 %all-to-all-start.2 = ((bf16[8,1,80,2048]{3,2,1,0:T(8,128)(2,1)}), bf16[8,1,80,2048]{3,2,1,0:T(8,128)(2,1)S(1)}, u32[]{:S(2)}, u32[]{:S(2)}) async-start(bf16[8,1,80,2048]{3,2,1,0:T(8,128)(2,1)} %multiply_convert_fusion), calls=%async_computation.4 | async-start | bytes 5242880 | tf_op jit(solution)/shard_map/all_to_all | solution.py:236
  611.8 345.5 %reduce-scatter.23.cloned.1.call-start = ((), (), s32[]{:S(2)}) async-start(), calls=%async_computation.25 | async-start | bytes 7208960 | tf_op jit(solution)/shard_map/reduce_scatter | solution.py:258
  677.2 1.3 copy-start.58
  685.0 469.8 %reduce-scatter.21.cloned.1.call-start = ((), (), s32[]{:S(2)}) async-start(), calls=%async_computation.24 | async-start | bytes 14417920 | tf_op jit(solution)/shard_map/reduce_scatter | solution.py:255
  714.8 35.8 %all-to-all-start.3 = ((bf16[8,1,80,2048]{3,2,1,0:T(8,128)(2,1)}), bf16[8,1,80,2048]{3,2,1,0:T(8,128)(2,1)S(1)}, u32[]{:S(2)}, u32[]{:S(2)}) async-start(bf16[8,1,80,2048]{3,2,1,0:T(8,128)(2,1)} %fusion.26), calls=%async_computation.5 | async-start | bytes 5242880 | tf_op jit(solution)/shard_map/all_to_all | solution.py:251
  727.5 27.6 %copy-start.43 = (bf16[2048]{0:T(1024)(128)(2,1)S(1)}, bf16[2048]{0:T(1024)(128)(2,1)}, u32[]{:S(2)}) copy-start(bf16[2048]{0:T(1024)(128)(2,1)} %copy-done.42) | copy-start | bytes 12292
  727.5 28.9 %copy-start.46 = (f32[128]{0:T(128)S(1)}, f32[128]{0:T(128)}, u32[]{:S(2)}) copy-start(f32[128]{0:T(128)} %copy-done.45) | copy-start | bytes 1540
  750.6 36.7 %all-to-all-start.1 = ((bf16[8,1,80,2048]{3,2,1,0:T(8,128)(2,1)}), bf16[8,1,80,2048]{3,2,1,0:T(8,128)(2,1)}, u32[]{:S(2)}, u32[]{:S(2)}) async-start(bf16[8,1,80,2048]{3,2,1,0:T(8,128)(2,1)} %fusion.29), calls=%async_computation.2 | async-start | bytes 5242880 | tf_op jit(solution)/shard_map/all_to_all | solution.py:187
  755.1 586.5 %reduce-scatter.15.cloned.1.call-start = ((), (), s32[]{:S(2)}) async-start(), calls=%async_computation.21 | async-start | bytes 17301504 | tf_op jit(solution)/shard_map/reduce_scatter | solution.py:320
  787.3 7.4 copy-start.13
  799.5 5.4 copy-start.14
  807.2 5.5 copy-start.5
  807.2 5.5 copy-start.35
  807.3 5.5 copy-start.48
  812.7 2.0 copy-start.51
  812.7 2.0 copy-start.31
  812.8 2.0 copy-start.12
  817.7 3.6 copy-start.26
  821.3 1.4 copy-start.25
  830.8 950.9 %reduce-scatter.13.cloned.1.call-start = ((), (), s32[]{:S(2)}) async-start(), calls=%async_computation.20 | async-start | bytes 51904512 | tf_op jit(solution)/shard_map/reduce_scatter | solution.py:318
  831.5 6.7 copy-start.3
  838.1 2.1 copy-start.23
  838.1 2.1 copy-start.20
  838.1 2.1 copy-start.22
  840.2 1.4 copy-start.28
  840.2 1.4 copy-start.30
  848.5 3.4 copy-start.7
  848.5 3.4 copy-start.33
  848.5 3.4 copy-start.41
  851.8 20.9 %copy-start.9 = (bf16[128,4096]{0,1:T(8,128)(2,1)}, bf16[128,4096]{0,1:T(8,128)(2,1)S(1)}, u32[]{:S(2)}) copy-start(bf16[128,4096]{0,1:T(8,128)(2,1)S(1)} %add_convert_fusion.2) | copy-start | bytes 3145732
  872.7 5.7 copy-start.1
  881.0 63.3 %copy-start.53 = (f32[128]{0:T(128)S(1)}, f32[128]{0:T(128)}, u32[]{:S(2)}) copy-start(f32[128]{0:T(128)} %copy-done.52) | copy-start | bytes 1540
  (14 other events, 12.0 us)
Sparse Core Ops, SparseCore 0:
  10.9 159.0 all-gather.7
  172.9 75.6 all-gather.9
  250.1 105.2 all-gather.13
  357.2 35.0 all-gather.11
  393.7 59.1 all-gather.15
  455.2 35.3 all-gather.17
  509.1 73.9 reduce-scatter.8
  587.0 100.0 reduce-scatter.10
  690.0 56.1 reduce-scatter.18
  748.9 102.1 reduce-scatter.16
  853.4 103.7 reduce-scatter.22
  959.4 195.3 reduce-scatter.20
  1157.7 183.8 reduce-scatter.14
  1348.4 433.2 reduce-scatter.12
where the time goes:
time: 1800 us; the launch traced here: 1790 us
  waiting for transfers between devices  1340 us (74%)
  matrix products  206 us (11%)
  blocking collectives  98.2 us (5%)
  local copies, waits for them, and re-layouts  57.7 us (3%)
  other arithmetic  55.7 us (3%)
  starting transfers between devices  18.2 us (1%)
    reduce_scatter x1, waiting for transfers between devices, shards(): lax.psum_scatter(qkv_weight_grad_full, ('dp', 'expert'), scatter_dimensio...  440 us
    reduce_scatter x1, waiting for transfers between devices, shards(): lax.psum_scatter(expert_in_grad_full.astype(jnp.bfloat16), 'dp', scatter_...  194 us
    reduce_scatter x1, waiting for transfers between devices, shards(): lax.psum_scatter(out_weight_grad_full, ('dp', 'expert'), scatter_dimensio...  182 us
    all_gather x1, waiting for transfers between devices, dense_params(): lax.all_gather(qkv_weight, ('dp', 'expert'), axis=0, tiled=True)  111 us
    unnamed x3, blocking collectives  98.2 us
    all_gather x1, waiting for transfers between devices, shards(): lax.all_gather(shared_in, 'dp', axis=2, tiled=True)  96 us
    all_gather x2, waiting for transfers between devices, group_rows(): return lax.all_gather(rows, 'expert', axis=0, tiled=True)  74.5 us
    all_gather x1, waiting for transfers between devices, dense_params(): lax.all_gather(out_weight, ('dp', 'expert'), axis=0, tiled=True)  62.1 us
  transfers between devices with their start and end apart: 18, of which 15 were waited for; matrix products, arithmetic and copies ran while one was open for 16% of the time, Pallas kernels for 0%

commit v1 on v0

v1 whole, which is shorter than its diff:
```python
import math

import jax
import jax.numpy as jnp
from jax import lax
from jax.sharding import PartitionSpec as P

HEAD = 128
NORM_EPS = 1e-06
THETA = 1000000.0
F32 = jnp.float32
BF16 = jnp.bfloat16


def dot(a, b, dims):
    return lax.dot_general(a, b, (dims, ((), ())), preferred_element_type=F32)


def mm(a, b):
    return dot(a, b, ((1,), (0,)))


def mm_nt(a, b):
    return dot(a, b, ((1,), (1,)))


def mm_tn(a, b):
    return dot(a, b, ((0,), (0,)))


def plane_masks(size, me):
    if size == 8:
        even = jnp.array([0, 2, 4, 6, 1, 5, 3, 7], jnp.int32)
        odd = jnp.array([0, 4, 2, 6, 1, 3, 5, 7], jnp.int32)
        return jnp.where(me % 2 == 0, even, odd)
    return jnp.arange(size, dtype=jnp.int32)


def first_hop(i):
    return i ^ 2 if i % 2 == 0 else i ^ 4


def second_hop(i):
    return i ^ 4 if i % 2 == 0 else i ^ 2


def send(block, size, target):
    return lax.ppermute(block, "expert", [(i, target(i)) for i in range(size)])


def core_swap(i):
    return i ^ 1


def plane_gather(block, size):
    if size == 8:
        one = send(block, size, first_hop)
        two = send(block, size, second_hop)
        three = send(one, size, second_hop)
        near = [block, one, two, three]
        return near + [send(part, size, core_swap) for part in near]
    return [block] + [send(block, size, lambda i, m=m: i ^ m) for m in range(1, size)]


def plane_sum(parts, size):
    if size == 8:
        low = parts.astype(BF16)
        got = send(low[4:], size, core_swap)
        near = parts[:4] + got.astype(F32)
        got = send(near[2:].astype(BF16), size, second_hop)
        near = near[:2] + got.astype(F32)
        got = send(near[1].astype(BF16), size, first_hop)
        return near[0] + got.astype(F32)
    low = parts.astype(BF16)
    total = parts[0]
    for m in range(1, size):
        total = total + send(low[m], size, lambda i, m=m: i ^ m).astype(F32)
    return total


def norm_scale(rows):
    return lax.rsqrt(jnp.mean(rows * rows, axis=-1, keepdims=True) + NORM_EPS)


def norm_back(rows, scale, gain, grad):
    unit = rows * scale
    weighted = grad * gain
    inner = jnp.mean(weighted * unit, axis=-1, keepdims=True)
    return scale * (weighted - unit * inner), jnp.sum(grad * unit, axis=0)


def swiglu_parts(gate, up):
    sig = jax.nn.sigmoid(gate)
    return sig, gate * sig * up


def swiglu_back(gate, up, grad):
    sig = jax.nn.sigmoid(gate)
    silu = gate * sig
    return grad * up * (sig + silu * (1.0 - sig)), grad * silu


def rotary_tables(row_count, head_width):
    half_width = head_width // 2
    freqs = THETA ** (-(jnp.arange(half_width, dtype=F32) * 2.0) / head_width)
    angles = jnp.arange(row_count, dtype=F32)[:, None] * freqs[None, :]
    return (jnp.cos(angles), jnp.sin(angles))


def rotate(inputs, cos_table, sin_table):
    half = inputs.shape[-1] // 2
    first, second = inputs[..., :half], inputs[..., half:]
    cos_part, sin_part = cos_table[None, :, None, :], sin_table[None, :, None, :]
    return jnp.concatenate(
        [first * cos_part - second * sin_part, second * cos_part + first * sin_part], axis=-1
    )


def shards(
    tokens,
    lengths,
    routes,
    gate_values,
    cotangent,
    norm1_gain,
    qkv_weight,
    qkv_bias,
    out_weight,
    norm2_gain,
    shared_in,
    shared_out,
    shared_gate,
    expert_in,
    expert_out,
):
    rows, width = tokens.shape
    top = routes.shape[1]
    group = lax.axis_size("expert")
    planes = lax.axis_size("dp")
    devices = group * planes
    both = ("dp", "expert")
    me = lax.axis_index("expert")
    plane = lax.axis_index("dp")
    heads = width // HEAD
    own_heads = heads // group
    shard = qkv_weight.shape[0]
    split = HEAD // shard
    lanes = group // split
    experts = group * expert_in.shape[0]
    valid_total = 23 * rows * devices // 32
    capacity = 5 * valid_total * top // (4 * experts * planes)
    slots = -(-capacity // 16) * 16
    order = me ^ plane_masks(group, me)
    group_rows = group * rows

    vectors = jnp.concatenate([norm1_gain, norm2_gain, shared_gate, qkv_bias]).astype(F32)
    vector_rows = -(-vectors.shape[0] // 128)
    vectors = jnp.pad(vectors, (0, vector_rows * 128 - vectors.shape[0])).reshape(vector_rows, 128)
    info = jnp.concatenate(
        [
            vectors,
            routes.T.astype(F32),
            gate_values.T,
            jnp.broadcast_to(lengths.astype(F32)[:, None], (1, rows)),
        ],
        axis=0,
    )
    told = lax.all_to_all(
        jnp.broadcast_to(info[None], (devices,) + info.shape), both, 0, 0, tiled=True
    )
    flat = told[:, :vector_rows].reshape(devices, vector_rows * 128)
    norm1_full = flat[:, :shard].reshape(width)
    norm2_full = flat[:, shard : 2 * shard].reshape(width)
    gate_full = flat[:, 2 * shard : 3 * shard].reshape(width)
    bias_full = flat[:, 3 * shard : 3 * shard + qkv_bias.shape[0]].reshape(
        3, split, own_heads, lanes, HEAD
    )
    rest = told[:, vector_rows:].reshape(planes, group, 2 * top + 1, rows)
    mine = lax.dynamic_index_in_dim(rest, plane, 0, keepdims=False)
    column = lax.dynamic_index_in_dim(rest, me, 1, keepdims=False)
    slot = jnp.arange(rows, dtype=F32)
    group_routes = mine[:, :top].astype(jnp.int32)
    group_gates = mine[:, top : 2 * top]
    group_valid = slot[None, :] < mine[:, 2 * top]
    column_valid = (slot[None, :] < column[:, 2 * top]).astype(F32).reshape(planes * rows, 1)
    valid_float = (slot < lengths.astype(F32)[0]).astype(F32)[:, None]

    lane, part = me // split, me % split
    by_head = qkv_weight.reshape(shard, 3, split, own_heads, lanes, HEAD)
    by_head = by_head.transpose(4, 2, 0, 1, 3, 5).reshape(group, shard, 3 * own_heads * HEAD)
    by_head = lax.all_to_all(by_head, "expert", 0, 0, tiled=True)
    qkv_own = lax.all_gather(by_head, "dp", axis=0, tiled=True).reshape(width, 3 * own_heads * HEAD)
    bias_own = lax.dynamic_index_in_dim(bias_full, part, 1, keepdims=False)
    bias_own = lax.dynamic_index_in_dim(bias_own, lane, 2, keepdims=False).reshape(-1)
    out_parts = lax.all_gather(out_weight[None], "dp", axis=0, tiled=True)
    pairs = [[k * split + p for p in range(split)] for k in range(lanes)]
    out_own = lax.all_to_all(
        out_parts.reshape(split, own_heads, shard, width),
        "expert",
        0,
        0,
        axis_index_groups=pairs,
        tiled=True,
    )
    out_own = out_own.transpose(1, 0, 2, 3).reshape(own_heads * HEAD, width)

    group_tokens = jnp.concatenate(plane_gather(tokens, group), axis=0).astype(F32)
    normed1 = (group_tokens * norm_scale(group_tokens) * norm1_full).astype(BF16)
    qkv_lin = mm(normed1, qkv_own) + bias_own
    own_width = own_heads * HEAD
    cos_table, sin_table = rotary_tables(rows, HEAD)
    head_shape = (group, rows, own_heads, HEAD)
    query = rotate(qkv_lin[:, :own_width].reshape(head_shape), cos_table, sin_table).astype(BF16)
    key = rotate(qkv_lin[:, own_width : 2 * own_width].reshape(head_shape), cos_table, sin_table)
    key = key.astype(BF16)
    value = qkv_lin[:, 2 * own_width :].reshape(head_shape).astype(BF16)
    score_scale = 1.0 / math.sqrt(HEAD)
    positions = jnp.arange(rows, dtype=jnp.int32)
    causal = (positions[:, None] >= positions[None, :])[None, None]

    def probs_of(query, key):
        scores = jnp.einsum("sqhd,skhd->shqk", query, key, preferred_element_type=F32)
        scores = jnp.where(causal, scores * score_scale, -1e30)
        peak = jnp.max(scores, axis=-1, keepdims=True)
        raised = jnp.exp(scores - peak)
        return raised / jnp.sum(raised, axis=-1, keepdims=True)

    probs = probs_of(query, key)
    mixed = jnp.einsum("shqk,skhd->sqhd", probs.astype(BF16), value, preferred_element_type=F32)
    mixed = mixed.reshape(group_rows, own_width).astype(BF16)
    branch = plane_sum(mm(mixed, out_own).reshape(group, rows, width), group)
    hidden = tokens.astype(F32) + branch
    scale2 = norm_scale(hidden)
    normed2 = (hidden * scale2 * norm2_full).astype(BF16)
    group_normed = jnp.concatenate(plane_gather(normed2, group), axis=0)
    column_normed = lax.all_gather(normed2, "dp", axis=0, tiled=True)
    group_cot = jnp.concatenate(plane_gather(cotangent, group), axis=0)
    column_cot = lax.all_gather(cotangent, "dp", axis=0, tiled=True)

    named = group_routes == me
    taken = jnp.any(named, axis=1) & group_valid
    gate_here = jnp.sum(jnp.where(named, group_gates, 0.0), axis=1)
    taken_low = taken.astype(BF16)
    before = (positions[:, None] < positions[None, :]).astype(BF16)
    inside = mm(taken_low, before)
    counts = jnp.sum(taken.astype(F32), axis=1)
    places = jnp.arange(group, dtype=jnp.int32)
    offsets = jnp.sum(jnp.where(places[None, :] < places[:, None], counts[None, :], 0.0), axis=1)
    rank = (inside + offsets[:, None]).astype(jnp.int32)
    rank = jnp.where(taken & (rank < capacity), rank, -1)
    rank = jnp.take(rank, order, axis=0).reshape(1, group_rows)
    gate_rel = jnp.take(gate_here, order, axis=0).reshape(1, group_rows)
    chosen = rank == jnp.arange(slots, dtype=jnp.int32)[:, None]
    pick = chosen.astype(BF16)
    row_gate = jnp.sum(jnp.where(chosen, gate_rel, 0.0), axis=1, keepdims=True)
    weight_in, weight_out = expert_in[0], expert_out[0]
    hidden_units = weight_out.shape[0]
    expert_rows = mm(pick, group_normed).astype(BF16)
    cot_rows = mm(pick, group_cot)
    val_grad = (cot_rows * row_gate).astype(BF16)
    expert_pre = mm(expert_rows, weight_in)
    e_gate, e_up = expert_pre[:, :hidden_units], expert_pre[:, hidden_units:]
    expert_act = swiglu_parts(e_gate, e_up)[1].astype(BF16)
    act_grad = mm_nt(val_grad, weight_out)
    out_grad = mm_tn(expert_act, val_grad).astype(BF16)
    expert_out_grad = lax.psum_scatter(out_grad, "dp", scatter_dimension=0, tiled=True)
    pre_grad = jnp.concatenate(swiglu_back(e_gate, e_up, act_grad), axis=1).astype(BF16)
    in_grad = mm_tn(expert_rows, pre_grad).astype(BF16)
    expert_in_grad = lax.psum_scatter(in_grad, "dp", scatter_dimension=0, tiled=True)
    row_grad = mm_nt(pre_grad, weight_in).astype(BF16)
    expert_val = mm(expert_act, weight_out)
    pair_dot = jnp.sum(cot_rows * expert_val, axis=1, keepdims=True)
    routed_part = mm_tn(pick, (expert_val * row_gate).astype(BF16))
    normed_part = mm_tn(pick, row_grad)
    routed_sum = plane_sum(routed_part.reshape(group, rows, width), group)
    routed_grad = plane_sum(normed_part.reshape(group, rows, width), group)
    pair_dots = jnp.sum(jnp.where(chosen, pair_dot, 0.0), axis=0).reshape(group, rows)
    inverse = jnp.argmax(order[None, :] == places[:, None], axis=1)
    pair_dots = jnp.take(pair_dots, inverse, axis=0)
    pair_back = lax.all_to_all(pair_dots, "expert", 0, 0, tiled=True)
    gate_values_grad = jnp.sum(
        jnp.where(routes.T[None] == places[:, None, None], pair_back[:, None, :], 0.0), axis=0
    ).T

    units = shared_out.shape[0]
    unit_in = jnp.concatenate(plane_gather(shared_in.transpose(1, 2, 0), group), axis=1)
    unit_out = jnp.concatenate(plane_gather(shared_out, group), axis=0)
    plane_units = group * units
    shared_weight = jax.nn.sigmoid(
        jnp.sum(column_normed.astype(F32) * gate_full, axis=1, keepdims=True)
    )
    unit_flat = unit_in.reshape(2 * plane_units, width)
    shared_pre = mm_nt(column_normed, unit_flat)
    s_gate, s_up = shared_pre[:, :plane_units], shared_pre[:, plane_units:]
    shared_act = swiglu_parts(s_gate, s_up)[1].astype(BF16)
    shared_val = mm(shared_act, unit_out)
    column_grad = column_cot.astype(F32) * column_valid
    shared_val_grad = (column_grad * shared_weight).astype(BF16)
    logit_grad = jnp.sum(column_grad * shared_val, axis=1, keepdims=True)
    logit_grad = logit_grad * shared_weight * (1.0 - shared_weight)
    gate_grad = jnp.sum(logit_grad * column_normed.astype(F32), axis=0)
    shared_act_grad = mm_nt(shared_val_grad, unit_out)
    shared_pre_grad = jnp.concatenate(swiglu_back(s_gate, s_up, shared_act_grad), axis=1)
    shared_pre_grad = shared_pre_grad.astype(BF16)
    normed_term = mm(shared_pre_grad, unit_flat) + logit_grad * gate_full
    shared_grad = lax.psum_scatter(
        normed_term.astype(BF16), "dp", scatter_dimension=0, tiled=True
    ).astype(F32)
    shared_sum = lax.psum_scatter(
        (shared_weight * shared_val).astype(BF16), "dp", scatter_dimension=0, tiled=True
    ).astype(F32)
    unit_out_grad = mm_tn(shared_act, shared_val_grad)
    unit_in_grad = mm_tn(shared_pre_grad, column_normed)
    shared_out_grad = plane_sum(unit_out_grad.reshape(group, units, width), group)
    unit_in_grad = unit_in_grad.reshape(2, group, units, width).transpose(1, 0, 2, 3)
    shared_in_grad = plane_sum(unit_in_grad, group).transpose(2, 0, 1)

    output = (valid_float * (hidden + shared_sum + routed_sum)).astype(BF16)
    normed2_grad = shared_grad + routed_grad
    norm_term, norm2_part = norm_back(hidden, scale2, norm2_full, normed2_grad)
    hidden_grad = cotangent.astype(F32) * valid_float + norm_term
    branch_grad = jnp.concatenate(plane_gather(hidden_grad.astype(BF16), group), axis=0)

    out_own_grad = mm_tn(mixed, branch_grad).astype(BF16)
    out_own_grad = out_own_grad.reshape(own_heads, split, shard, width).transpose(1, 0, 2, 3)
    out_own_grad = lax.all_to_all(
        out_own_grad, "expert", 0, 0, axis_index_groups=pairs, tiled=True
    ).reshape(planes * shard, width)
    out_weight_grad = lax.psum_scatter(out_own_grad, "dp", scatter_dimension=0, tiled=True)
    mixed_grad = mm_nt(branch_grad, out_own).astype(BF16).reshape(head_shape)
    value_grad = jnp.einsum(
        "shqk,sqhd->skhd", probs.astype(BF16), mixed_grad, preferred_element_type=F32
    )
    probs_grad = jnp.einsum("sqhd,skhd->shqk", mixed_grad, value, preferred_element_type=F32)
    score_grad = probs * (probs_grad - jnp.sum(probs_grad * probs, axis=-1, keepdims=True))
    score_grad = score_grad.astype(BF16)
    query_grad = jnp.einsum("shqk,skhd->sqhd", score_grad, key, preferred_element_type=F32)
    key_grad = jnp.einsum("shqk,sqhd->skhd", score_grad, query, preferred_element_type=F32)
    query_grad = rotate(query_grad * score_scale, cos_table, -sin_table)
    key_grad = rotate(key_grad * score_scale, cos_table, -sin_table)
    flat_shape = (group_rows, own_width)
    qkv_grad = jnp.concatenate(
        [
            query_grad.reshape(flat_shape),
            key_grad.reshape(flat_shape),
            value_grad.reshape(flat_shape),
        ],
        axis=1,
    ).astype(BF16)
    bias_part = jnp.sum(qkv_grad.astype(F32), axis=0)
    normed1_grad = plane_sum(mm_nt(qkv_grad, qkv_own).reshape(group, rows, width), group)
    qkv_own_grad = mm_tn(normed1, qkv_grad).astype(BF16)
    qkv_own_grad = lax.psum_scatter(qkv_own_grad, "dp", scatter_dimension=0, tiled=True)
    qkv_own_grad = lax.all_to_all(
        qkv_own_grad.reshape(group, shard, 3 * own_width), "expert", 0, 0, tiled=True
    )
    qkv_weight_grad = (
        qkv_own_grad.reshape(lanes, split, shard, 3, own_heads, HEAD)
        .transpose(2, 3, 1, 4, 0, 5)
        .reshape(shard, 3 * width)
        .astype(F32)
    )
    own_tokens = tokens.astype(F32)
    token_term, norm1_part = norm_back(own_tokens, norm_scale(own_tokens), norm1_full, normed1_grad)
    tokens_grad = hidden_grad + token_term

    here = (jnp.arange(split)[:, None] == part) & (jnp.arange(lanes)[None, :] == lane)
    bias_all = jnp.where(
        here[None, :, None, :, None], bias_part.reshape(3, 1, own_heads, 1, HEAD), 0.0
    ).reshape(devices, qkv_bias.shape[0])
    sums = jnp.concatenate(
        [
            norm1_part.reshape(devices, shard),
            norm2_part.reshape(devices, shard),
            gate_grad.reshape(devices, shard),
            bias_all,
        ],
        axis=1,
    )
    sums = jnp.pad(sums, ((0, 0), (0, vector_rows * 128 - sums.shape[1])))
    sums = lax.all_to_all(sums.reshape(devices, vector_rows, 128), both, 0, 0, tiled=True)
    sums = jnp.sum(sums, axis=0).reshape(-1)

    return (
        output,
        tokens_grad,
        sums[:shard],
        qkv_weight_grad,
        sums[3 * shard : 3 * shard + qkv_bias.shape[0]],
        out_weight_grad.astype(F32),
        sums[shard : 2 * shard],
        shared_in_grad,
        shared_out_grad,
        sums[2 * shard : 3 * shard],
        expert_in_grad.astype(F32)[None],
        expert_out_grad.astype(F32)[None],
        gate_values_grad,
    )


def solution(mesh):
    both = ("dp", "expert")
    in_specs = (
        P(both, None),
        P(both),
        P(both, None),
        P(both, None),
        P(both, None),
        P(both),
        P(both, None),
        P(both),
        P(both, None),
        P(both),
        P(None, None, both),
        P(both, None),
        P(both),
        P("expert", None, None),
        P("expert", None, None),
    )
    out_specs = (
        P(both, None),
        P(both, None),
        P(both),
        P(both, None),
        P(both),
        P(both, None),
        P(both),
        P(None, None, both),
        P(both, None),
        P(both),
        P("expert", "dp", None),
        P("expert", "dp", None),
        P(both, None),
    )
    return jax.shard_map(shards, mesh=mesh, in_specs=in_specs, out_specs=out_specs, check_vma=False)
```

time: 1800 us -> 883 us (0.49)
  waiting for transfers between devices: 1340 us -> 418 us
  local copies, waits for them, and re-layouts: 57.7 us -> 131 us
  blocking collectives: 98.2 us -> 28.9 us
  matrix products: 206 us -> 144 us
  starting transfers between devices: 18.2 us -> 56.9 us
  other arithmetic: 55.7 us -> 81.6 us
    reduce_scatter x8 -> x6, waiting for transfers between devices: 835 us -> 149 us  [the longest x1 140 us: shards(): lax.psum_scatter(in_grad, 'dp', scatter_dimension=0, tiled=True)]
    all_gather x6 -> x4, waiting for transfers between devices: 393 us -> 33 us  [the longest x1 33 us: shards(): lax.all_gather(by_head, 'dp', axis=0, tiled=True)]
    ppermute x0 -> x60, waiting for transfers between devices: none -> 178 us  [send(): return lax.ppermute(block, 'expert', [(i, target(i)) for i in range(size)])]
    unnamed x3 -> x0, blocking collectives: 98.2 us -> none
    dot_general x27 -> x28, matrix products: 206 us -> 142 us  [the longest x23 133 us: dot(): return lax.dot_general(a, b, (dims, ((), ())), preferred_element_type=F32)]
    all_to_all x4, waiting for transfers between devices: 106 us -> 57.4 us  [the longest x1 35.2 us: shards(): pair_back = lax.all_to_all(pair_dots, 'expert', 0, 0, tiled=True)]
    unnamed x142 -> x232, local copies, waits for them, and re-layouts: 18.6 us -> 59.2 us
    ppermute x0 -> x60, starting transfers between devices: none -> 39.3 us  [send(): return lax.ppermute(block, 'expert', [(i, target(i)) for i in range(size)])]
  transfers between devices with their start and end apart: 18 -> 74, of which waited for: 15 -> 30; matrix products, arithmetic and copies ran while one was open for 16% -> 29% of each run, Pallas kernels for 0% -> 0%
where the time goes in v1:
time: 883 us; the launch traced here: 877 us
  waiting for transfers between devices  418 us (47%)
  matrix products  144 us (16%)
  local copies, waits for them, and re-layouts  131 us (15%)
  other arithmetic  81.6 us (9%)
  starting transfers between devices  56.9 us (6%)
  blocking collectives  28.9 us (3%)
  between operations  16.9 us (2%)
    ppermute x60, waiting for transfers between devices, send(): return lax.ppermute(block, 'expert', [(i, target(i)) for i in range(size)])  178 us
    reduce_scatter x1, waiting for transfers between devices, shards(): lax.psum_scatter(in_grad, 'dp', scatter_dimension=0, tiled=True)  140 us
    dot_general x23, matrix products, dot(): return lax.dot_general(a, b, (dims, ((), ())), preferred_element_type=F32)  133 us
    unnamed x232, local copies, waits for them, and re-layouts  59.2 us
    ppermute x60, starting transfers between devices, send(): return lax.ppermute(block, 'expert', [(i, target(i)) for i in range(size)])  39.3 us
    all_to_all x1, waiting for transfers between devices, shards(): pair_back = lax.all_to_all(pair_dots, 'expert', 0, 0, tiled=True)  35.2 us
    all_gather x1, waiting for transfers between devices, shards(): lax.all_gather(by_head, 'dp', axis=0, tiled=True)  33 us
    add x6, other arithmetic, plane_sum(): near = parts[:4] + got.astype(F32)  24.3 us
  transfers between devices with their start and end apart: 74, of which 30 were waited for; matrix products, arithmetic and copies ran while one was open for 29% of the time, Pallas kernels for 0%

profile of v1, /device:TPU:0, one launch (start us, length us, event | category | flops | bytes accessed | tf_op | source)
XLA Modules:
  0.0 877.3 jit_solution(5071454144281727424)
XLA Ops:
  11.3 17.6 %all_to_all.39 = bf16[8,64,768]{2,1,0:T(8,128)(2,1)} all-to-all(bf16[8,64,768]{2,1,0:T(8,128)(2,1)S(1)} %reshape.391), channel_id=1, replica_groups=mesh['dp'=4,'expert'=8] {'expert'}, dimensions={0} | all-to-all | bytes 1572864 | tf_op jit(solution)/shard_map/all_to_all | solution.py:191
  31.8 5.9 all-to-all-start
  40.1 8.2 all-to-all-done
  52.6 5.0 collective-permute-done.2
  61.8 3.1 fusion.5
  65.0 5.9 all_to_all.40
  71.9 33.0 %all-gather.6.cloned.1.call-done = bf16[32,64,768]{2,1,0:T(8,128)(2,1)} async-done(((bf16[8,64,768]{2,1,0:T(8,128)(2,1)}), bf16[32,64,768]{2,1,0:T(8,128)(2,1)}) %all-gather.6.cloned.1.call-update) | async-done | bytes 3145744 | tf_op jit(solution)/shard_map/all_gather | solution.py:192
  104.9 6.4 convolution_add_fusion
  121.5 3.1 fusion.34
  129.0 3.7 collective-permute-done.7
  135.2 13.3 %collective-permute-done.8 = bf16[2,128,2048]{2,1,0:T(8,128)(2,1)S(1)} collective-permute-done((bf16[2,128,2048]{2,1,0:T(8,128)(2,1)S(1)}, bf16[2,128,2048]{2,1,0:T(8,128)(2,1)S(1)}, u32[]{:S(2)}, u32[]{:S(2)}) %collective-permute-start.8) | collective-permute-done | bytes 1048608 | tf_op jit(solution)/shard_map/ppermute | solution.py:48
  151.3 8.0 collective-permute-done.9
  184.0 9.8 %collective-permute-done.17 = bf16[176,2048]{1,0:T(8,128)(2,1)} collective-permute-done((bf16[176,2048]{1,0:T(8,128)(2,1)}, bf16[176,2048]{1,0:T(8,128)(2,1)}, u32[]{:S(2)}, u32[]{:S(2)}) %collective-permute-start.17) | collective-permute-done | bytes 720928 | tf_op jit(solution)/shard_map/ppermute | solution.py:48
  199.4 7.0 collective-permute-done.36
  212.8 11.9 %collective-permute-done.10 = bf16[2,176,2048]{2,1,0:T(8,128)(2,1)S(1)} collective-permute-done((bf16[2,176,2048]{2,1,0:T(8,128)(2,1)S(1)}, bf16[2,176,2048]{2,1,0:T(8,128)(2,1)S(1)}, u32[]{:S(2)}, u32[]{:S(2)}) %collective-permute-start.10) | collective-permute-done | bytes 1441824 | tf_op jit(solution)/shard_map/ppermute | solution.py:48
  230.4 5.0 collective-permute-done.19
  241.5 9.3 %collective-permute-done.12 = bf16[2,176,2048]{2,1,0:T(8,128)(2,1)S(1)} collective-permute-done((bf16[2,176,2048]{2,1,0:T(8,128)(2,1)S(1)}, bf16[2,176,2048]{2,1,0:T(8,128)(2,1)S(1)}, u32[]{:S(2)}, u32[]{:S(2)}) %collective-permute-start.12) | collective-permute-done | bytes 1441824 | tf_op jit(solution)/shard_map/ppermute | solution.py:48
  260.1 7.3 collective-permute-done.24
  269.4 7.2 collective-permute-done.26
  280.8 5.6 fusion.3
  287.3 3.6 fusion.10
  290.9 4.2 multiply_reduce_fusion.1
  298.2 12.6 %fusion.106 = f32[512,2816]{1,0:T(8,128)} fusion(bf16[512,2048]{1,0:T(8,128)(2,1)} %all-gather.8.cloned.1.call-done, bf16[2816,2048]{1,0:T(8,128)(2,1)} %bitcast.262), kind=kOutput, calls=%fused_computation.306 | convolution fusion | flops 5905580032 | bytes 19398656 | tf_op jit(solution)/shard_map/dot_general | solution.py:16
  310.8 9.3 %multiply_convert_fusion.5 = (bf16[512,1408]{1,0:T(8,128)(2,1)S(1)}, bf16[512,1408]{1,0:T(8,128)(2,1)S(1)}, bf16[512,1408]{1,0:T(8,128)(2,1)S(1)}) fusion(f32[512,2816]{1,0:T(8,128)} %fusion.106, bf16[1408,2048]{1,0:T(8,128)(2,1)} %constant_dynamic-update-slice_fusion.16, bf16[512,2048]{1,0:T(8,128)(2,1)} %all-gather.10.cloned.1.call-done, ...), kind=kOutput, calls=%fused_computation.59 | convolution fusion | flops 2967076864 | bytes 17960960 | tf_op jit(solution)/shard_map/dot_general | solution.py:16
  320.2 9.5 %multiply_reduce_fusion = (f32[512]{0:T(512)S(1)}, bf16[512,2048]{1,0:T(8,128)(2,1)}) fusion(bf16[512,2048]{1,0:T(8,128)(2,1)S(1)} %copy-done.77, f32[512]{0:T(512)S(1)} %fusion.80, f32[512]{0:T(512)S(1)} %add_divide_fusion.2, bf16[512,1408]{1,0:T(8,128)(2,1)S(1)} %get-tuple-element.39, bf16[1408,2048]{1,0:T(8,128)(2,1)} %constant_dynamic-update-slice_fusion.16), kind=kOutput, calls=%fused_computation.37 | convolution fusion | flops 2959080960 | bytes 11409408 | tf_op jit(solution)/shard_map/dot_general | solution.py:16
  329.7 10.2 %add_convert_fusion = bf16[512,2048]{1,0:T(8,128)(2,1)} fusion(bf16[2816,2048]{1,0:T(8,128)(2,1)} %bitcast.263, f32[512]{0:T(512)S(1)} %subtract_multiply_fusion, f32[2048]{0:T(1024)S(1)} %mul.583, bf16[512,1408]{1,0:T(8,128)(2,1)S(1)} %get-tuple-element.36, bf16[512,1408]{1,0:T(8,128)(2,1)S(1)} %get-tuple-element.35), kind=kOutput, calls=%fused_computation.36 | convolution fusion | flops 5914492928 | bytes 16525312 | tf_op jit(solution)/shard_map/dot_general | solution.py:16
  339.9 9.4 %multiply_convert_fusion.8 = (bf16[464,1408]{1,0:T(8,128)(2,1)S(1)}, bf16[464,1408]{1,0:T(8,128)(2,1)S(1)}) fusion(f32[464,2816]{1,0:T(8,128)} %copy-done.13, bf16[1,1408,2048]{2,1,0:T(8,128)(2,1)} %param.33, f32[464,2048]{1,0:T(8,128)} %get-tuple-element.74, f32[464]{0:T(512)S(1)} %get-tuple-element.21), kind=kOutput, calls=%fused_computation.65 | convolution fusion | flops 2685706240 | bytes 17409856 | tf_op jit(solution)/shard_map/dot_general | solution.py:16
  349.3 9.4 %fusion.14 = bf16[464,2048]{1,0:T(8,128)(2,1)S(1)} fusion(bf16[1,2048,2816]{2,1,0:T(8,128)(2,1)} %param.32, bf16[464,1408]{1,0:T(8,128)(2,1)S(1)} %get-tuple-element.38, bf16[464,1408]{1,0:T(8,128)(2,1)S(1)} %get-tuple-element.37), kind=kOutput, calls=%fused_computation.49 | convolution fusion | flops 5358108672 | bytes 16048128 | tf_op jit(solution)/shard_map/dot_general | solution.py:16
  372.1 3.5 convert_add_fusion.2
  379.0 11.6 %collective-permute-done.42 = bf16[2,128,2048]{2,1,0:T(8,128)(2,1)S(1)} collective-permute-done((bf16[2,128,2048]{2,1,0:T(8,128)(2,1)S(1)}, bf16[2,128,2048]{2,1,0:T(8,128)(2,1)S(1)}, u32[]{:S(2)}, u32[]{:S(2)}) %collective-permute-start.42) | collective-permute-done | bytes 1048608 | tf_op jit(solution)/shard_map/ppermute | solution.py:48
  392.5 14.9 %collective-permute-done.32 = bf16[2,128,2048]{2,1,0:T(8,128)(2,1)S(1)} collective-permute-done((bf16[2,128,2048]{2,1,0:T(8,128)(2,1)S(1)}, bf16[2,128,2048]{2,1,0:T(8,128)(2,1)S(1)}, u32[]{:S(2)}, u32[]{:S(2)}) %collective-permute-start.32) | collective-permute-done | bytes 1048608 | tf_op jit(solution)/shard_map/ppermute | solution.py:48
  410.8 7.8 collective-permute-done.33
  418.5 9.0 %reduce-scatter.7.cloned.1.call-done = bf16[128,2048]{1,0:T(8,128)(2,1)} async-done(((bf16[512,2048]{1,0:T(8,128)(2,1)}), bf16[128,2048]{1,0:T(8,128)(2,1)}) %reduce-scatter.7.cloned.1.call-update) | async-done | bytes 524304 | tf_op jit(solution)/shard_map/reduce_scatter | solution.py:309
  427.6 3.3 multiply_reduce_fusion.2
  436.5 11.8 %collective-permute-done.44 = bf16[128,2048]{1,0:T(8,128)(2,1)S(1)} collective-permute-done((bf16[128,2048]{1,0:T(8,128)(2,1)S(1)}, bf16[128,2048]{1,0:T(8,128)(2,1)S(1)}, u32[]{:S(2)}, u32[]{:S(2)}) %collective-permute-start.44) | collective-permute-done | bytes 524320 | tf_op jit(solution)/shard_map/ppermute | solution.py:48
  449.5 8.0 collective-permute-done.46
  469.3 5.4 all_to_all.41
  486.1 5.5 convolution_convert_fusion.2
  491.7 7.8 convolution_convert_fusion.1
  501.4 10.4 %convolution_convert_fusion = bf16[2048,2816]{1,0:T(8,128)(2,1)} fusion(bf16[464,2048]{1,0:T(8,128)(2,1)S(1)} %copy-done.83, bf16[464,1408]{1,0:T(8,128)(2,1)} %copy-done.88, bf16[464,1408]{1,0:T(8,128)(2,1)S(1)} %copy-done.87), kind=kOutput, calls=%fused_computation.11 | convolution fusion | flops 5362925568 | bytes 16048128 | tf_op jit(solution)/shard_map/dot_general | solution.py:16
  513.4 4.8 fusion.95
  518.1 4.3 copy-done
  524.6 8.7 fusion.23
  533.3 8.6 copy.205
  541.9 7.8 slice.516
  552.3 3.2 convert_add_fusion
  559.5 17.8 %collective-permute-done.58 = bf16[2,176,2048]{2,1,0:T(8,128)(2,1)} collective-permute-done((bf16[2,176,2048]{2,1,0:T(8,128)(2,1)S(1)}, bf16[2,176,2048]{2,1,0:T(8,128)(2,1)}, u32[]{:S(2)}, u32[]{:S(2)}) %collective-permute-start.58) | collective-permute-done | bytes 1441824 | tf_op jit(solution)/shard_map/ppermute | solution.py:48
  579.9 4.9 fusion.107
  584.8 3.2 copy-done.6
  589.7 13.1 %slice_add_fusion = f32[4,2,176,2048]{3,2,1,0:T(8,128)} fusion(f32[8,2,176,2048]{3,2,1,0:T(8,128)} %bitcast.230, bf16[4,2,176,2048]{3,2,1,0:T(8,128)(2,1)} %collective-permute-done.54), kind=kLoop, calls=%fused_computation.6 | loop fusion | flops 5767168 | bytes 28835840 | tf_op jit(solution)/shard_map/add | solution.py:69
  602.9 4.7 slice.518
  611.3 3.6 all-to-all-start.6
  614.9 35.2 %all-to-all-done.6 = f32[8,1,128]{2,1,0:T(1,128)S(1)} async-done(((f32[8,1,128]{2,1,0:T(1,128)}), f32[8,1,128]{2,1,0:T(1,128)S(1)}, u32[]{:S(2)}, u32[]{:S(2)}) %all-to-all-start.6) | async-done | bytes 4128 | tf_op jit(solution)/shard_map/all_to_all | solution.py:280
  665.4 5.0 slice_add_fusion.1
  670.5 6.7 collective-permute-done.52
  682.2 5.8 collective-permute-done.53
  689.3 3.6 all-to-all-start.3
  695.4 9.1 %all-to-all-done.3 = f32[32,3,128]{2,1,0:T(4,128)S(1)} async-done(((f32[32,3,128]{2,1,0:T(4,128)}), f32[32,3,128]{2,1,0:T(4,128)S(1)}, u32[]{:S(2)}, u32[]{:S(2)}) %all-to-all-start.3) | async-done | bytes 49184 | tf_op jit(solution)/shard_map/all_to_all | solution.py:381
  705.8 3.5 all-to-all-start.4
  709.4 3.3 bitcast_convert_fusion.1
  712.7 4.3 fusion.18
  717.0 4.9 all-to-all-done.4
  725.5 139.9 %reduce-scatter.15.cloned.1.call-done = bf16[512,2816]{1,0:T(8,128)(2,1)} async-done(((bf16[2048,2816]{1,0:T(8,128)(2,1)}), bf16[512,2816]{1,0:T(8,128)(2,1)}) %reduce-scatter.15.cloned.1.call-update) | async-done | bytes 2883600 | tf_op jit(solution)/shard_map/reduce_scatter | solution.py:269
  865.4 4.8 bitcast_convert_fusion
  (508 shorter events, 206.0 us)
Async XLA Ops:
  7.3 57.7 %all-gather.12.cloned.1.call-start = ((), (), s32[]{:S(2)}) async-start(), calls=%async_computation.22 | async-start | bytes 1310720 | tf_op jit(solution)/shard_map/all_gather | solution.py:195
  8.0 96.9 %all-gather.6.cloned.1.call-start = ((), (), s32[]{:S(2)}) async-start(), calls=%async_computation.13 | async-start | bytes 3932160 | tf_op jit(solution)/shard_map/all_gather | solution.py:192
  29.0 19.3 %collective-permute-start = (bf16[128,2048]{1,0:T(8,128)(2,1)S(1)}, bf16[128,2048]{1,0:T(8,128)(2,1)S(1)}, u32[]{:S(2)}, u32[]{:S(2)}) collective-permute-start(bf16[128,2048]{1,0:T(8,128)(2,1)S(1)} %copy-done.9), channel_id=1, source_target_pairs={{0,2},{1,5},{2,0},{3,7},{4,6},{5,1},{6,4},{7,3},{8,10},{9,13},{10,... | collective-permute-start | bytes 1572872 | tf_op jit(solution)/shard_map/ppermute | solution.py:48
  29.6 21.5 %collective-permute-start.1 = (bf16[128,2048]{1,0:T(8,128)(2,1)S(1)}, bf16[128,2048]{1,0:T(8,128)(2,1)S(1)}, u32[]{:S(2)}, u32[]{:S(2)}) collective-permute-start(bf16[128,2048]{1,0:T(8,128)(2,1)S(1)} %copy-done.9), channel_id=1, source_target_pairs={{0,4},{1,3},{2,6},{3,1},{4,0},{5,7},{6,2},{7,5},{8,12},{9,11},{10,... | collective-permute-start | bytes 1572872 | tf_op jit(solution)/shard_map/ppermute | solution.py:48
  30.2 28.2 %collective-permute-start.3 = (bf16[128,2048]{1,0:T(8,128)(2,1)S(1)}, bf16[128,2048]{1,0:T(8,128)(2,1)S(1)}, u32[]{:S(2)}, u32[]{:S(2)}) collective-permute-start(bf16[128,2048]{1,0:T(8,128)(2,1)S(1)} %copy-done.9), channel_id=1, source_target_pairs={{0,1},{1,0},{2,3},{3,2},{4,5},{5,4},{6,7},{7,6},{8,9},{9,8},{10,11... | collective-permute-start | bytes 1572872 | tf_op jit(solution)/shard_map/ppermute | solution.py:48
  31.8 16.5 %all-to-all-start = ((f32[32,12,128]{2,1,0:T(8,128)}), f32[32,12,128]{2,1,0:T(8,128)S(1)}, u32[]{:S(2)}, u32[]{:S(2)}) async-start(f32[32,12,128]{2,1,0:T(8,128)} %broadcast_in_dim.182), calls=%async_computation | async-start | bytes 524288 | tf_op jit(solution)/shard_map/all_to_all | solution.py:168
  37.7 258.4 %all-gather.8.cloned.1.call-start = ((), (), s32[]{:S(2)}) async-start(), calls=%async_computation.14 | async-start | bytes 2621440 | tf_op jit(solution)/shard_map/all_gather | solution.py:236
  48.4 9.2 %collective-permute-start.2 = (bf16[128,2048]{1,0:T(8,128)(2,1)S(1)}, bf16[128,2048]{1,0:T(8,128)(2,1)S(1)}, u32[]{:S(2)}, u32[]{:S(2)}) collective-permute-start(bf16[128,2048]{1,0:T(8,128)(2,1)S(1)} %collective-permute-done), channel_id=1, source_target_pairs={{0,4},{1,3},{2,6},{3,1},{4,0},{5,7},{6,2},{7,5},{8,12},{9,11},{10,... | collective-permute-start | bytes 1572872 | tf_op jit(solution)/shard_map/ppermute | solution.py:48
  50.3 9.0 %collective-permute-start.4 = (bf16[128,2048]{1,0:T(8,128)(2,1)S(1)}, bf16[128,2048]{1,0:T(8,128)(2,1)S(1)}, u32[]{:S(2)}, u32[]{:S(2)}) collective-permute-start(bf16[128,2048]{1,0:T(8,128)(2,1)S(1)} %collective-permute-done), channel_id=1, source_target_pairs={{0,1},{1,0},{2,3},{3,2},{4,5},{5,4},{6,7},{7,6},{8,9},{9,8},{10,11... | collective-permute-start | bytes 1572872 | tf_op jit(solution)/shard_map/ppermute | solution.py:48
  51.2 9.0 %collective-permute-start.5 = (bf16[128,2048]{1,0:T(8,128)(2,1)S(1)}, bf16[128,2048]{1,0:T(8,128)(2,1)S(1)}, u32[]{:S(2)}, u32[]{:S(2)}) collective-permute-start(bf16[128,2048]{1,0:T(8,128)(2,1)S(1)} %collective-permute-done.1), channel_id=1, source_target_pairs={{0,1},{1,0},{2,3},{3,2},{4,5},{5,4},{6,7},{7,6},{8,9},{9,8},{10,11... | collective-permute-start | bytes 1572872 | tf_op jit(solution)/shard_map/ppermute | solution.py:48
  133.7 14.9 %collective-permute-start.8 = (bf16[2,128,2048]{2,1,0:T(8,128)(2,1)S(1)}, bf16[2,128,2048]{2,1,0:T(8,128)(2,1)S(1)}, u32[]{:S(2)}, u32[]{:S(2)}) collective-permute-start(bf16[2,128,2048]{2,1,0:T(8,128)(2,1)S(1)} %slice.527), channel_id=1, source_target_pairs={{0,4},{1,3},{2,6},{3,1},{4,0},{5,7},{6,2},{7,5},{8,12},{9,11},{10,... | collective-permute-start | bytes 3145736 | tf_op jit(solution)/shard_map/ppermute | solution.py:48
  149.8 9.5 %collective-permute-start.9 = (bf16[128,2048]{1,0:T(8,128)(2,1)}, bf16[128,2048]{1,0:T(8,128)(2,1)}, u32[]{:S(2)}, u32[]{:S(2)}) collective-permute-start(bf16[128,2048]{1,0:T(8,128)(2,1)} %fusion.58), channel_id=1, source_target_pairs={{0,2},{1,5},{2,0},{3,7},{4,6},{5,1},{6,4},{7,3},{8,10},{9,13},{10,... | collective-permute-start | bytes 1572872 | tf_op jit(solution)/shard_map/ppermute | solution.py:48
  163.3 147.5 %all-gather.10.cloned.1.call-start = ((), (), s32[]{:S(2)}) async-start(), calls=%async_computation.16 | async-start | bytes 2621440 | tf_op jit(solution)/shard_map/all_gather | solution.py:238
  163.4 15.0 %collective-permute-start.34 = (bf16[128,2048]{1,0:T(8,128)(2,1)S(1)}, bf16[128,2048]{1,0:T(8,128)(2,1)}, u32[]{:S(2)}, u32[]{:S(2)}) collective-permute-start(bf16[128,2048]{1,0:T(8,128)(2,1)S(1)} %copy-done.14), channel_id=1, source_target_pairs={{0,2},{1,5},{2,0},{3,7},{4,6},{5,1},{6,4},{7,3},{8,10},{9,13},{10,... | collective-permute-start | bytes 1572872 | tf_op jit(solution)/shard_map/ppermute | solution.py:48
  164.9 16.8 %collective-permute-start.35 = (bf16[128,2048]{1,0:T(8,128)(2,1)S(1)}, bf16[128,2048]{1,0:T(8,128)(2,1)S(1)}, u32[]{:S(2)}, u32[]{:S(2)}) collective-permute-start(bf16[128,2048]{1,0:T(8,128)(2,1)S(1)} %copy-done.14), channel_id=1, source_target_pairs={{0,4},{1,3},{2,6},{3,1},{4,0},{5,7},{6,2},{7,5},{8,12},{9,11},{10,... | collective-permute-start | bytes 1572872 | tf_op jit(solution)/shard_map/ppermute | solution.py:48
  166.3 40.9 %collective-permute-start.37 = (bf16[128,2048]{1,0:T(8,128)(2,1)S(1)}, bf16[128,2048]{1,0:T(8,128)(2,1)}, u32[]{:S(2)}, u32[]{:S(2)}) collective-permute-start(bf16[128,2048]{1,0:T(8,128)(2,1)S(1)} %copy-done.14), channel_id=1, source_target_pairs={{0,1},{1,0},{2,3},{3,2},{4,5},{5,4},{6,7},{7,6},{8,9},{9,8},{10,11... | collective-permute-start | bytes 1572872 | tf_op jit(solution)/shard_map/ppermute | solution.py:48
  166.4 27.5 %collective-permute-start.17 = (bf16[176,2048]{1,0:T(8,128)(2,1)}, bf16[176,2048]{1,0:T(8,128)(2,1)}, u32[]{:S(2)}, u32[]{:S(2)}) collective-permute-start(bf16[176,2048]{1,0:T(8,128)(2,1)} %param.30), channel_id=1, source_target_pairs={{0,2},{1,5},{2,0},{3,7},{4,6},{5,1},{6,4},{7,3},{8,10},{9,13},{10,... | collective-permute-start | bytes 2162696 | tf_op jit(solution)/shard_map/ppermute | solution.py:48
  166.9 30.4 %collective-permute-start.18 = (bf16[176,2048]{1,0:T(8,128)(2,1)}, bf16[176,2048]{1,0:T(8,128)(2,1)}, u32[]{:S(2)}, u32[]{:S(2)}) collective-permute-start(bf16[176,2048]{1,0:T(8,128)(2,1)} %param.30), channel_id=1, source_target_pairs={{0,4},{1,3},{2,6},{3,1},{4,0},{5,7},{6,2},{7,5},{8,12},{9,11},{10,... | collective-permute-start | bytes 2162696 | tf_op jit(solution)/shard_map/ppermute | solution.py:48
  167.5 251.0 %reduce-scatter.9.cloned.1.call-start = ((), (), s32[]{:S(2)}) async-start(), calls=%async_computation.17 | async-start | bytes 2621440 | tf_op jit(solution)/shard_map/reduce_scatter | solution.py:306
  178.4 46.2 %collective-permute-start.10 = (bf16[2,176,2048]{2,1,0:T(8,128)(2,1)S(1)}, bf16[2,176,2048]{2,1,0:T(8,128)(2,1)S(1)}, u32[]{:S(2)}, u32[]{:S(2)}) collective-permute-start(bf16[2,176,2048]{2,1,0:T(8,128)(2,1)S(1)} %bitcast.250), channel_id=1, source_target_pairs={{0,2},{1,5},{2,0},{3,7},{4,6},{5,1},{6,4},{7,3},{8,10},{9,13},{10,... | collective-permute-start | bytes 4325384 | tf_op jit(solution)/shard_map/ppermute | solution.py:48
  181.7 24.7 %collective-permute-start.36 = (bf16[128,2048]{1,0:T(8,128)(2,1)}, bf16[128,2048]{1,0:T(8,128)(2,1)S(1)}, u32[]{:S(2)}, u32[]{:S(2)}) collective-permute-start(bf16[128,2048]{1,0:T(8,128)(2,1)} %collective-permute-done.34), channel_id=1, source_target_pairs={{0,4},{1,3},{2,6},{3,1},{4,0},{5,7},{6,2},{7,5},{8,12},{9,11},{10,... | collective-permute-start | bytes 1572872 | tf_op jit(solution)/shard_map/ppermute | solution.py:48
  193.8 33.8 %collective-permute-start.11 = (bf16[2,176,2048]{2,1,0:T(8,128)(2,1)S(1)}, bf16[2,176,2048]{2,1,0:T(8,128)(2,1)S(1)}, u32[]{:S(2)}, u32[]{:S(2)}) collective-permute-start(bf16[2,176,2048]{2,1,0:T(8,128)(2,1)S(1)} %bitcast.251), channel_id=1, source_target_pairs={{0,4},{1,3},{2,6},{3,1},{4,0},{5,7},{6,2},{7,5},{8,12},{9,11},{10,... | collective-permute-start | bytes 4325384 | tf_op jit(solution)/shard_map/ppermute | solution.py:48
  197.4 12.3 %collective-permute-start.38 = (bf16[128,2048]{1,0:T(8,128)(2,1)}, bf16[128,2048]{1,0:T(8,128)(2,1)S(1)}, u32[]{:S(2)}, u32[]{:S(2)}) collective-permute-start(bf16[128,2048]{1,0:T(8,128)(2,1)} %collective-permute-done.34), channel_id=1, source_target_pairs={{0,1},{1,0},{2,3},{3,2},{4,5},{5,4},{6,7},{7,6},{8,9},{9,8},{10,11... | collective-permute-start | bytes 1572872 | tf_op jit(solution)/shard_map/ppermute | solution.py:48
  207.3 30.4 %collective-permute-start.20 = (bf16[176,2048]{1,0:T(8,128)(2,1)}, bf16[176,2048]{1,0:T(8,128)(2,1)S(1)}, u32[]{:S(2)}, u32[]{:S(2)}) collective-permute-start(bf16[176,2048]{1,0:T(8,128)(2,1)} %param.30), channel_id=1, source_target_pairs={{0,1},{1,0},{2,3},{3,2},{4,5},{5,4},{6,7},{7,6},{8,9},{9,8},{10,11... | collective-permute-start | bytes 2162696 | tf_op jit(solution)/shard_map/ppermute | solution.py:48
  209.7 25.7 %collective-permute-start.19 = (bf16[176,2048]{1,0:T(8,128)(2,1)}, bf16[176,2048]{1,0:T(8,128)(2,1)S(1)}, u32[]{:S(2)}, u32[]{:S(2)}) collective-permute-start(bf16[176,2048]{1,0:T(8,128)(2,1)} %collective-permute-done.17), channel_id=1, source_target_pairs={{0,4},{1,3},{2,6},{3,1},{4,0},{5,7},{6,2},{7,5},{8,12},{9,11},{10,... | collective-permute-start | bytes 2162696 | tf_op jit(solution)/shard_map/ppermute | solution.py:48
  212.0 26.7 %collective-permute-start.21 = (bf16[176,2048]{1,0:T(8,128)(2,1)}, bf16[176,2048]{1,0:T(8,128)(2,1)S(1)}, u32[]{:S(2)}, u32[]{:S(2)}) collective-permute-start(bf16[176,2048]{1,0:T(8,128)(2,1)} %collective-permute-done.17), channel_id=1, source_target_pairs={{0,1},{1,0},{2,3},{3,2},{4,5},{5,4},{6,7},{7,6},{8,9},{9,8},{10,11... | collective-permute-start | bytes 2162696 | tf_op jit(solution)/shard_map/ppermute | solution.py:48
  224.6 26.2 %collective-permute-start.12 = (bf16[2,176,2048]{2,1,0:T(8,128)(2,1)S(1)}, bf16[2,176,2048]{2,1,0:T(8,128)(2,1)S(1)}, u32[]{:S(2)}, u32[]{:S(2)}) collective-permute-start(bf16[2,176,2048]{2,1,0:T(8,128)(2,1)S(1)} %collective-permute-done.10), channel_id=1, source_target_pairs={{0,4},{1,3},{2,6},{3,1},{4,0},{5,7},{6,2},{7,5},{8,12},{9,11},{10,... | collective-permute-start | bytes 4325384 | tf_op jit(solution)/shard_map/ppermute | solution.py:48
  227.7 11.5 %collective-permute-start.22 = (bf16[176,2048]{1,0:T(8,128)(2,1)}, bf16[176,2048]{1,0:T(8,128)(2,1)S(1)}, u32[]{:S(2)}, u32[]{:S(2)}) collective-permute-start(bf16[176,2048]{1,0:T(8,128)(2,1)} %collective-permute-done.18), channel_id=1, source_target_pairs={{0,1},{1,0},{2,3},{3,2},{4,5},{5,4},{6,7},{7,6},{8,9},{9,8},{10,11... | collective-permute-start | bytes 2162696 | tf_op jit(solution)/shard_map/ppermute | solution.py:48
  237.7 18.2 %collective-permute-start.13 = (bf16[2,176,2048]{2,1,0:T(8,128)(2,1)S(1)}, bf16[2,176,2048]{2,1,0:T(8,128)(2,1)S(1)}, u32[]{:S(2)}, u32[]{:S(2)}) collective-permute-start(bf16[2,176,2048]{2,1,0:T(8,128)(2,1)S(1)} %bitcast.252), channel_id=1, source_target_pairs={{0,1},{1,0},{2,3},{3,2},{4,5},{5,4},{6,7},{7,6},{8,9},{9,8},{10,11... | collective-permute-start | bytes 4325384 | tf_op jit(solution)/shard_map/ppermute | solution.py:48
  238.6 18.5 %collective-permute-start.14 = (bf16[2,176,2048]{2,1,0:T(8,128)(2,1)S(1)}, bf16[2,176,2048]{2,1,0:T(8,128)(2,1)S(1)}, u32[]{:S(2)}, u32[]{:S(2)}) collective-permute-start(bf16[2,176,2048]{2,1,0:T(8,128)(2,1)S(1)} %collective-permute-done.10), channel_id=1, source_target_pairs={{0,1},{1,0},{2,3},{3,2},{4,5},{5,4},{6,7},{7,6},{8,9},{9,8},{10,11... | collective-permute-start | bytes 4325384 | tf_op jit(solution)/shard_map/ppermute | solution.py:48
  239.1 13.1 %collective-permute-start.23 = (bf16[176,2048]{1,0:T(8,128)(2,1)S(1)}, bf16[176,2048]{1,0:T(8,128)(2,1)S(1)}, u32[]{:S(2)}, u32[]{:S(2)}) collective-permute-start(bf16[176,2048]{1,0:T(8,128)(2,1)S(1)} %collective-permute-done.19), channel_id=1, source_target_pairs={{0,1},{1,0},{2,3},{3,2},{4,5},{5,4},{6,7},{7,6},{8,9},{9,8},{10,11... | collective-permute-start | bytes 2162696 | tf_op jit(solution)/shard_map/ppermute | solution.py:48
  240.2 18.7 %collective-permute-start.15 = (bf16[2,176,2048]{2,1,0:T(8,128)(2,1)S(1)}, bf16[2,176,2048]{2,1,0:T(8,128)(2,1)S(1)}, u32[]{:S(2)}, u32[]{:S(2)}) collective-permute-start(bf16[2,176,2048]{2,1,0:T(8,128)(2,1)S(1)} %collective-permute-done.11), channel_id=1, source_target_pairs={{0,1},{1,0},{2,3},{3,2},{4,5},{5,4},{6,7},{7,6},{8,9},{9,8},{10,11... | collective-permute-start | bytes 4325384 | tf_op jit(solution)/shard_map/ppermute | solution.py:48
  250.8 16.6 %collective-permute-start.16 = (bf16[2,176,2048]{2,1,0:T(8,128)(2,1)S(1)}, bf16[2,176,2048]{2,1,0:T(8,128)(2,1)S(1)}, u32[]{:S(2)}, u32[]{:S(2)}) collective-permute-start(bf16[2,176,2048]{2,1,0:T(8,128)(2,1)S(1)} %collective-permute-done.12), channel_id=1, source_target_pairs={{0,1},{1,0},{2,3},{3,2},{4,5},{5,4},{6,7},{7,6},{8,9},{9,8},{10,11... | collective-permute-start | bytes 4325384 | tf_op jit(solution)/shard_map/ppermute | solution.py:48
  254.4 13.0 %collective-permute-start.24 = (bf16[128,2048]{1,0:T(8,128)(2,1)S(1)}, bf16[128,2048]{1,0:T(8,128)(2,1)S(1)}, u32[]{:S(2)}, u32[]{:S(2)}) collective-permute-start(bf16[128,2048]{1,0:T(8,128)(2,1)S(1)} %copy-done.33), channel_id=1, source_target_pairs={{0,2},{1,5},{2,0},{3,7},{4,6},{5,1},{6,4},{7,3},{8,10},{9,13},{10,... | collective-permute-start | bytes 1572872 | tf_op jit(solution)/shard_map/ppermute | solution.py:48
  258.3 10.9 %collective-permute-start.25 = (bf16[128,2048]{1,0:T(8,128)(2,1)S(1)}, bf16[128,2048]{1,0:T(8,128)(2,1)S(1)}, u32[]{:S(2)}, u32[]{:S(2)}) collective-permute-start(bf16[128,2048]{1,0:T(8,128)(2,1)S(1)} %copy-done.33), channel_id=1, source_target_pairs={{0,4},{1,3},{2,6},{3,1},{4,0},{5,7},{6,2},{7,5},{8,12},{9,11},{10,... | collective-permute-start | bytes 1572872 | tf_op jit(solution)/shard_map/ppermute | solution.py:48
  267.4 9.2 %collective-permute-start.26 = (bf16[128,2048]{1,0:T(8,128)(2,1)S(1)}, bf16[128,2048]{1,0:T(8,128)(2,1)S(1)}, u32[]{:S(2)}, u32[]{:S(2)}) collective-permute-start(bf16[128,2048]{1,0:T(8,128)(2,1)S(1)} %collective-permute-done.24), channel_id=1, source_target_pairs={{0,4},{1,3},{2,6},{3,1},{4,0},{5,7},{6,2},{7,5},{8,12},{9,11},{10,... | collective-permute-start | bytes 1572872 | tf_op jit(solution)/shard_map/ppermute | solution.py:48
  339.9 87.7 %reduce-scatter.7.cloned.1.call-start = ((), (), s32[]{:S(2)}) async-start(), calls=%async_computation.15 | async-start | bytes 2621440 | tf_op jit(solution)/shard_map/reduce_scatter | solution.py:309
  362.8 9.2 %collective-permute-start.41 = (bf16[4,128,2048]{2,1,0:T(8,128)(2,1)}, bf16[4,128,2048]{2,1,0:T(8,128)(2,1)}, u32[]{:S(2)}, u32[]{:S(2)}) collective-permute-start(bf16[4,128,2048]{2,1,0:T(8,128)(2,1)} %bitcast.31), channel_id=1, source_target_pairs={{0,1},{1,0},{2,3},{3,2},{4,5},{5,4},{6,7},{7,6},{8,9},{9,8},{10,11... | collective-permute-start | bytes 6291464 | tf_op jit(solution)/shard_map/ppermute | solution.py:48
  371.7 291.9 %reduce-scatter.13.cloned.1.call-start = ((), (), s32[]{:S(2)}) async-start(), calls=%async_computation.19 | async-start | bytes 1310720 | tf_op jit(solution)/shard_map/reduce_scatter | solution.py:329
  375.7 14.9 %collective-permute-start.42 = (bf16[2,128,2048]{2,1,0:T(8,128)(2,1)S(1)}, bf16[2,128,2048]{2,1,0:T(8,128)(2,1)S(1)}, u32[]{:S(2)}, u32[]{:S(2)}) collective-permute-start(bf16[2,128,2048]{2,1,0:T(8,128)(2,1)S(1)} %slice.525), channel_id=1, source_target_pairs={{0,4},{1,3},{2,6},{3,1},{4,0},{5,7},{6,2},{7,5},{8,12},{9,11},{10,... | collective-permute-start | bytes 3145736 | tf_op jit(solution)/shard_map/ppermute | solution.py:48
  379.0 28.5 %collective-permute-start.32 = (bf16[2,128,2048]{2,1,0:T(8,128)(2,1)S(1)}, bf16[2,128,2048]{2,1,0:T(8,128)(2,1)S(1)}, u32[]{:S(2)}, u32[]{:S(2)}) collective-permute-start(bf16[2,128,2048]{2,1,0:T(8,128)(2,1)S(1)} %slice.526), channel_id=1, source_target_pairs={{0,4},{1,3},{2,6},{3,1},{4,0},{5,7},{6,2},{7,5},{8,12},{9,11},{10,... | collective-permute-start | bytes 3145736 | tf_op jit(solution)/shard_map/ppermute | solution.py:48
  391.0 19.8 %collective-permute-start.43 = (bf16[128,2048]{1,0:T(8,128)(2,1)S(1)}, bf16[128,2048]{1,0:T(8,128)(2,1)}, u32[]{:S(2)}, u32[]{:S(2)}) collective-permute-start(bf16[128,2048]{1,0:T(8,128)(2,1)S(1)} %fusion.60), channel_id=1, source_target_pairs={{0,2},{1,5},{2,0},{3,7},{4,6},{5,1},{6,4},{7,3},{8,10},{9,13},{10,... | collective-permute-start | bytes 1572872 | tf_op jit(solution)/shard_map/ppermute | solution.py:48
  409.2 9.4 %collective-permute-start.33 = (bf16[128,2048]{1,0:T(8,128)(2,1)S(1)}, bf16[128,2048]{1,0:T(8,128)(2,1)}, u32[]{:S(2)}, u32[]{:S(2)}) collective-permute-start(bf16[128,2048]{1,0:T(8,128)(2,1)S(1)} %fusion.59), channel_id=1, source_target_pairs={{0,2},{1,5},{2,0},{3,7},{4,6},{5,1},{6,4},{7,3},{8,10},{9,13},{10,... | collective-permute-start | bytes 1572872 | tf_op jit(solution)/shard_map/ppermute | solution.py:48
  433.5 14.8 %collective-permute-start.44 = (bf16[128,2048]{1,0:T(8,128)(2,1)S(1)}, bf16[128,2048]{1,0:T(8,128)(2,1)S(1)}, u32[]{:S(2)}, u32[]{:S(2)}) collective-permute-start(bf16[128,2048]{1,0:T(8,128)(2,1)S(1)} %get-tuple-element.23), channel_id=1, source_target_pairs={{0,2},{1,5},{2,0},{3,7},{4,6},{5,1},{6,4},{7,3},{8,10},{9,13},{10,... | collective-permute-start | bytes 1572872 | tf_op jit(solution)/shard_map/ppermute | solution.py:48
  435.0 14.3 %collective-permute-start.45 = (bf16[128,2048]{1,0:T(8,128)(2,1)S(1)}, bf16[128,2048]{1,0:T(8,128)(2,1)S(1)}, u32[]{:S(2)}, u32[]{:S(2)}) collective-permute-start(bf16[128,2048]{1,0:T(8,128)(2,1)S(1)} %get-tuple-element.23), channel_id=1, source_target_pairs={{0,4},{1,3},{2,6},{3,1},{4,0},{5,7},{6,2},{7,5},{8,12},{9,11},{10,... | collective-permute-start | bytes 1572872 | tf_op jit(solution)/shard_map/ppermute | solution.py:48
  448.3 9.2 %collective-permute-start.46 = (bf16[128,2048]{1,0:T(8,128)(2,1)S(1)}, bf16[128,2048]{1,0:T(8,128)(2,1)S(1)}, u32[]{:S(2)}, u32[]{:S(2)}) collective-permute-start(bf16[128,2048]{1,0:T(8,128)(2,1)S(1)} %collective-permute-done.44), channel_id=1, source_target_pairs={{0,4},{1,3},{2,6},{3,1},{4,0},{5,7},{6,2},{7,5},{8,12},{9,11},{10,... | collective-permute-start | bytes 1572872 | tf_op jit(solution)/shard_map/ppermute | solution.py:48
  448.8 8.8 %collective-permute-start.47 = (bf16[128,2048]{1,0:T(8,128)(2,1)S(1)}, bf16[128,2048]{1,0:T(8,128)(2,1)S(1)}, u32[]{:S(2)}, u32[]{:S(2)}) collective-permute-start(bf16[128,2048]{1,0:T(8,128)(2,1)S(1)} %get-tuple-element.23), channel_id=1, source_target_pairs={{0,1},{1,0},{2,3},{3,2},{4,5},{5,4},{6,7},{7,6},{8,9},{9,8},{10,11... | collective-permute-start | bytes 1572872 | tf_op jit(solution)/shard_map/ppermute | solution.py:48
  448.8 8.8 %collective-permute-start.48 = (bf16[128,2048]{1,0:T(8,128)(2,1)S(1)}, bf16[128,2048]{1,0:T(8,128)(2,1)S(1)}, u32[]{:S(2)}, u32[]{:S(2)}) collective-permute-start(bf16[128,2048]{1,0:T(8,128)(2,1)S(1)} %collective-permute-done.44), channel_id=1, source_target_pairs={{0,1},{1,0},{2,3},{3,2},{4,5},{5,4},{6,7},{7,6},{8,9},{9,8},{10,11... | collective-permute-start | bytes 1572872 | tf_op jit(solution)/shard_map/ppermute | solution.py:48
  449.4 8.3 collective-permute-start.49
  474.7 231.2 %reduce-scatter.11.cloned.1.call-start = ((), (), s32[]{:S(2)}) async-start(), calls=%async_computation.18 | async-start | bytes 3932160 | tf_op jit(solution)/shard_map/reduce_scatter | solution.py:353
  491.6 217.8 %reduce-scatter.17.cloned.1.call-start = ((), (), s32[]{:S(2)}) async-start(), calls=%async_computation.21 | async-start | bytes 7208960 | tf_op jit(solution)/shard_map/reduce_scatter | solution.py:266
  499.5 365.9 %reduce-scatter.15.cloned.1.call-start = ((), (), s32[]{:S(2)}) async-start(), calls=%async_computation.20 | async-start | bytes 14417920 | tf_op jit(solution)/shard_map/reduce_scatter | solution.py:269
  524.4 25.6 %collective-permute-start.57 = (bf16[4,176,2048]{2,1,0:T(8,128)(2,1)}, bf16[4,176,2048]{2,1,0:T(8,128)(2,1)}, u32[]{:S(2)}, u32[]{:S(2)}) collective-permute-start(bf16[4,176,2048]{2,1,0:T(8,128)(2,1)} %bitcast.53), channel_id=1, source_target_pairs={{0,1},{1,0},{2,3},{3,2},{4,5},{5,4},{6,7},{7,6},{8,9},{9,8},{10,11... | collective-permute-start | bytes 8650760 | tf_op jit(solution)/shard_map/ppermute | solution.py:48
  549.6 40.1 %collective-permute-start.54 = (bf16[4,2,176,2048]{3,2,1,0:T(8,128)(2,1)}, bf16[4,2,176,2048]{3,2,1,0:T(8,128)(2,1)}, u32[]{:S(2)}, u32[]{:S(2)}) collective-permute-start(bf16[4,2,176,2048]{3,2,1,0:T(8,128)(2,1)} %slice.516), channel_id=1, source_target_pairs={{0,1},{1,0},{2,3},{3,2},{4,5},{5,4},{6,7},{7,6},{8,9},{9,8},{10,11... | collective-permute-start | bytes 17301512 | tf_op jit(solution)/shard_map/ppermute | solution.py:48
  558.2 19.2 %collective-permute-start.58 = (bf16[2,176,2048]{2,1,0:T(8,128)(2,1)S(1)}, bf16[2,176,2048]{2,1,0:T(8,128)(2,1)}, u32[]{:S(2)}, u32[]{:S(2)}) collective-permute-start(bf16[2,176,2048]{2,1,0:T(8,128)(2,1)S(1)} %slice.523), channel_id=1, source_target_pairs={{0,4},{1,3},{2,6},{3,1},{4,0},{5,7},{6,2},{7,5},{8,12},{9,11},{10,... | collective-permute-start | bytes 4325384 | tf_op jit(solution)/shard_map/ppermute | solution.py:48
  589.7 65.6 %collective-permute-start.51 = (bf16[4,128,2048]{2,1,0:T(8,128)(2,1)}, bf16[4,128,2048]{2,1,0:T(8,128)(2,1)}, u32[]{:S(2)}, u32[]{:S(2)}) collective-permute-start(bf16[4,128,2048]{2,1,0:T(8,128)(2,1)} %bitcast.38), channel_id=1, source_target_pairs={{0,1},{1,0},{2,3},{3,2},{4,5},{5,4},{6,7},{7,6},{8,9},{9,8},{10,11... | collective-permute-start | bytes 6291464 | tf_op jit(solution)/shard_map/ppermute | solution.py:48
  607.5 57.9 %collective-permute-start.55 = (bf16[2,2,176,2048]{3,2,1,0:T(8,128)(2,1)}, bf16[2,2,176,2048]{3,2,1,0:T(8,128)(2,1)}, u32[]{:S(2)}, u32[]{:S(2)}) collective-permute-start(bf16[2,2,176,2048]{3,2,1,0:T(8,128)(2,1)} %slice.518), channel_id=1, source_target_pairs={{0,4},{1,3},{2,6},{3,1},{4,0},{5,7},{6,2},{7,5},{8,12},{9,11},{10,... | collective-permute-start | bytes 8650760 | tf_op jit(solution)/shard_map/ppermute | solution.py:48
  609.2 43.8 %collective-permute-start.59 = (bf16[176,2048]{1,0:T(8,128)(2,1)}, bf16[176,2048]{1,0:T(8,128)(2,1)}, u32[]{:S(2)}, u32[]{:S(2)}) collective-permute-start(bf16[176,2048]{1,0:T(8,128)(2,1)} %fusion.57), channel_id=1, source_target_pairs={{0,2},{1,5},{2,0},{3,7},{4,6},{5,1},{6,4},{7,3},{8,10},{9,13},{10,... | collective-permute-start | bytes 2162696 | tf_op jit(solution)/shard_map/ppermute | solution.py:48
  611.3 38.8 %all-to-all-start.6 = ((f32[8,1,128]{2,1,0:T(1,128)}), f32[8,1,128]{2,1,0:T(1,128)S(1)}, u32[]{:S(2)}, u32[]{:S(2)}) async-start(f32[8,1,128]{2,1,0:T(1,128)} %bitcast.60), calls=%async_computation.12 | async-start | bytes 8192 | tf_op jit(solution)/shard_map/all_to_all | solution.py:280
  662.3 15.0 %collective-permute-start.52 = (bf16[2,128,2048]{2,1,0:T(8,128)(2,1)S(1)}, bf16[2,128,2048]{2,1,0:T(8,128)(2,1)}, u32[]{:S(2)}, u32[]{:S(2)}) collective-permute-start(bf16[2,128,2048]{2,1,0:T(8,128)(2,1)S(1)} %slice.524), channel_id=1, source_target_pairs={{0,4},{1,3},{2,6},{3,1},{4,0},{5,7},{6,2},{7,5},{8,12},{9,11},{10,... | collective-permute-start | bytes 3145736 | tf_op jit(solution)/shard_map/ppermute | solution.py:48
  678.8 9.2 %collective-permute-start.53 = (bf16[128,2048]{1,0:T(8,128)(2,1)S(1)}, bf16[128,2048]{1,0:T(8,128)(2,1)S(1)}, u32[]{:S(2)}, u32[]{:S(2)}) collective-permute-start(bf16[128,2048]{1,0:T(8,128)(2,1)S(1)} %fusion.61), channel_id=1, source_target_pairs={{0,2},{1,5},{2,0},{3,7},{4,6},{5,1},{6,4},{7,3},{8,10},{9,13},{10,... | collective-permute-start | bytes 1572872 | tf_op jit(solution)/shard_map/ppermute | solution.py:48
  681.7 31.0 %collective-permute-start.56 = (bf16[2,176,2048]{2,1,0:T(8,128)(2,1)}, bf16[2,176,2048]{2,1,0:T(8,128)(2,1)}, u32[]{:S(2)}, u32[]{:S(2)}) collective-permute-start(bf16[2,176,2048]{2,1,0:T(8,128)(2,1)} %fusion.28), channel_id=1, source_target_pairs={{0,2},{1,5},{2,0},{3,7},{4,6},{5,1},{6,4},{7,3},{8,10},{9,13},{10,... | collective-permute-start | bytes 4325384 | tf_op jit(solution)/shard_map/ppermute | solution.py:48
  689.3 15.3 %all-to-all-start.3 = ((f32[32,3,128]{2,1,0:T(4,128)}), f32[32,3,128]{2,1,0:T(4,128)S(1)}, u32[]{:S(2)}, u32[]{:S(2)}) async-start(f32[32,3,128]{2,1,0:T(4,128)} %reshape.407), calls=%async_computation.5 | async-start | bytes 131072 | tf_op jit(solution)/shard_map/all_to_all | solution.py:381
  705.8 16.1 %all-to-all-start.4 = ((bf16[8,64,768]{2,1,0:T(8,128)(2,1)}), bf16[8,64,768]{2,1,0:T(8,128)(2,1)S(1)}, u32[]{:S(2)}, u32[]{:S(2)}) async-start(bf16[8,64,768]{2,1,0:T(8,128)(2,1)} %bitcast.255), calls=%async_computation.7 | async-start | bytes 1572864 | tf_op jit(solution)/shard_map/all_to_all | solution.py:354
  (107 other events, 1175.2 us)
Sparse Core Ops, SparseCore 0:
  9.7 30.6 all-gather.11
  41.9 62.9 all-gather.5
  163.4 44.5 all-gather.7
  209.5 44.6 all-gather.9
  340.0 41.4 reduce-scatter.8
  384.3 43.1 reduce-scatter.6
  474.8 25.6 reduce-scatter.12
  502.9 58.8 reduce-scatter.10
  564.2 102.2 reduce-scatter.16
  668.9 196.4 reduce-scatter.14

commit v2 on v1

--- a/solution.py
+++ b/solution.py
@@ -2,6 +2,7 @@
 
 import jax
 import jax.numpy as jnp
+import numpy as np
 from jax import lax
 from jax.sharding import PartitionSpec as P
 
@@ -9,6 +10,7 @@
 NORM_EPS = 1e-06
 THETA = 1000000.0
 F32 = jnp.float32
+barrier = lax.optimization_barrier
 BF16 = jnp.bfloat16
 
 
@@ -28,12 +30,12 @@
     return dot(a, b, ((0,), (0,)))
 
 
-def plane_masks(size, me):
+def plane_order(size, me):
     if size == 8:
-        even = jnp.array([0, 2, 4, 6, 1, 5, 3, 7], jnp.int32)
-        odd = jnp.array([0, 4, 2, 6, 1, 3, 5, 7], jnp.int32)
-        return jnp.where(me % 2 == 0, even, odd)
-    return jnp.arange(size, dtype=jnp.int32)
+        even, odd = [0, 2, 4, 6, 1, 5, 3, 7], [0, 4, 2, 6, 1, 3, 5, 7]
+        first = me % 2 == 0
+        return [me ^ (a if a == b else jnp.where(first, a, b)) for a, b in zip(even, odd)]
+    return [me ^ m for m in range(size)]
 
 
 def first_hop(i):
@@ -52,14 +54,39 @@
     return i ^ 1
 
 
+def gather_first(block, size):
+    if size == 8:
+        return [block, send(block, size, first_hop), send(block, size, second_hop)]
+    return [block] + [send(block, size, lambda i, m=m: i ^ m) for m in range(1, size)]
+
+
+def gather_second(parts, size):
+    return parts + [send(parts[1], size, second_hop)] if size == 8 else parts
+
+
+def gather_third(parts, size):
+    return parts + [send(part, size, core_swap) for part in parts] if size == 8 else parts
+
+
 def plane_gather(block, size):
-    if size == 8:
-        one = send(block, size, first_hop)
-        two = send(block, size, second_hop)
-        three = send(one, size, second_hop)
-        near = [block, one, two, three]
-        return near + [send(part, size, core_swap) for part in near]
-    return [block] + [send(block, size, lambda i, m=m: i ^ m) for m in range(1, size)]
+    return gather_third(gather_second(gather_first(block, size), size), size)
+
+
+def plane_place(parts, order, whole, place):
+    for j, part in enumerate(parts):
+        whole = place(whole, part, order[j])
+    return whole
+
+
+def plane_rows(block, size, order):
+    rows = block.shape[0]
+    whole = jnp.zeros((size * rows,) + block.shape[1:], block.dtype)
+    return plane_place(
+        plane_gather(block, size),
+        order,
+        whole,
+        lambda whole, part, source: lax.dynamic_update_slice_in_dim(whole, part, source * rows, 0),
+    )
 
 
 def plane_sum(parts, size):
@@ -102,9 +129,10 @@
 
 def rotary_tables(row_count, head_width):
     half_width = head_width // 2
-    freqs = THETA ** (-(jnp.arange(half_width, dtype=F32) * 2.0) / head_width)
-    angles = jnp.arange(row_count, dtype=F32)[:, None] * freqs[None, :]
-    return (jnp.cos(angles), jnp.sin(angles))
+    powers = -(np.arange(half_width, dtype=np.float32) * np.float32(2.0)) / np.float32(head_width)
+    freqs = np.power(np.float32(THETA), powers).astype(np.float32)
+    angles = np.arange(row_count, dtype=np.float32)[:, None] * freqs[None, :]
+    return (jnp.asarray(np.cos(angles)), jnp.asarray(np.sin(angles)))
 
 
 def rotate(inputs, cos_table, sin_table):
@@ -150,7 +178,8 @@
     valid_total = 23 * rows * devices // 32
     capacity = 5 * valid_total * top // (4 * experts * planes)
     slots = -(-capacity // 16) * 16
-    order = me ^ plane_masks(group, me)
+    order = plane_order(group, me)
+    order_list = jnp.stack(order)
     group_rows = group * rows
 
     vectors = jnp.concatenate([norm1_gain, norm2_gain, shared_gate, qkv_bias]).astype(F32)
@@ -165,6 +194,15 @@
         ],
         axis=0,
     )
+    lane, part = me // split, me % split
+    out_parts = lax.all_gather(out_weight[None], "dp", axis=0, tiled=True)
+    by_head = qkv_weight.reshape(shard, 3, split, own_heads, lanes, HEAD)
+    by_head = by_head.transpose(4, 2, 0, 1, 3, 5).reshape(group, shard, 3 * own_heads * HEAD)
+    by_head = lax.all_to_all(by_head, "expert", 0, 0, tiled=True)
+    by_head, token_source, cot_source = barrier((by_head, tokens, cotangent))
+    out_parts, info = barrier((out_parts, info))
+    qkv_own = lax.all_gather(by_head, "dp", axis=0, tiled=True).reshape(width, 3 * own_heads * HEAD)
+
     told = lax.all_to_all(
         jnp.broadcast_to(info[None], (devices,) + info.shape), both, 0, 0, tiled=True
     )
@@ -185,30 +223,27 @@
     column_valid = (slot[None, :] < column[:, 2 * top]).astype(F32).reshape(planes * rows, 1)
     valid_float = (slot < lengths.astype(F32)[0]).astype(F32)[:, None]
 
-    lane, part = me // split, me % split
-    by_head = qkv_weight.reshape(shard, 3, split, own_heads, lanes, HEAD)
-    by_head = by_head.transpose(4, 2, 0, 1, 3, 5).reshape(group, shard, 3 * own_heads * HEAD)
-    by_head = lax.all_to_all(by_head, "expert", 0, 0, tiled=True)
-    qkv_own = lax.all_gather(by_head, "dp", axis=0, tiled=True).reshape(width, 3 * own_heads * HEAD)
     bias_own = lax.dynamic_index_in_dim(bias_full, part, 1, keepdims=False)
     bias_own = lax.dynamic_index_in_dim(bias_own, lane, 2, keepdims=False).reshape(-1)
-    out_parts = lax.all_gather(out_weight[None], "dp", axis=0, tiled=True)
     pairs = [[k * split + p for p in range(split)] for k in range(lanes)]
-    out_own = lax.all_to_all(
-        out_parts.reshape(split, own_heads, shard, width),
-        "expert",
-        0,
-        0,
-        axis_index_groups=pairs,
-        tiled=True,
-    )
-    out_own = out_own.transpose(1, 0, 2, 3).reshape(own_heads * HEAD, width)
-
-    group_tokens = jnp.concatenate(plane_gather(tokens, group), axis=0).astype(F32)
+    out_whole = plane_place(
+        plane_gather(out_parts.reshape(split, own_heads, shard, width), group),
+        order,
+        jnp.zeros((lanes, split, own_heads, split, shard, width), BF16),
+        lambda whole, block, source: lax.dynamic_update_slice(
+            whole, block[None, :, :, None], (source // split, 0, 0, source % split, 0, 0)
+        ),
+    ).reshape(width, width)
+    group_tokens = plane_rows(token_source, group, order).astype(F32)
+    group_cot = plane_rows(cot_source, group, order)
+    qkv_own, column_source = barrier((qkv_own, cotangent))
+    column_cot = lax.all_gather(column_source, "dp", axis=0, tiled=True)
+
     normed1 = (group_tokens * norm_scale(group_tokens) * norm1_full).astype(BF16)
     qkv_lin = mm(normed1, qkv_own) + bias_own
     own_width = own_heads * HEAD
     cos_table, sin_table = rotary_tables(rows, HEAD)
+    places = jnp.arange(group, dtype=jnp.int32)
     head_shape = (group, rows, own_heads, HEAD)
     query = rotate(qkv_lin[:, :own_width].reshape(head_shape), cos_table, sin_table).astype(BF16)
     key = rotate(qkv_lin[:, own_width : 2 * own_width].reshape(head_shape), cos_table, sin_table)
@@ -228,14 +263,27 @@
     probs = probs_of(query, key)
     mixed = jnp.einsum("shqk,skhd->sqhd", probs.astype(BF16), value, preferred_element_type=F32)
     mixed = mixed.reshape(group_rows, own_width).astype(BF16)
-    branch = plane_sum(mm(mixed, out_own).reshape(group, rows, width), group)
-    hidden = tokens.astype(F32) + branch
-    scale2 = norm_scale(hidden)
-    normed2 = (hidden * scale2 * norm2_full).astype(BF16)
-    group_normed = jnp.concatenate(plane_gather(normed2, group), axis=0)
+    mixed, out_whole, group_cot = barrier((mixed, out_whole, group_cot))
+    mixed_parts = gather_first(mixed, group)
+    mixed_parts, column_cot = barrier((mixed_parts, column_cot))
+    mixed_parts = gather_third(gather_second(mixed_parts, group), group)
+    mixed_whole = plane_place(
+        mixed_parts,
+        order,
+        jnp.zeros((group_rows, width), BF16),
+        lambda whole, block, source: lax.dynamic_update_slice(whole, block, (0, source * own_width)),
+    )
+    mixed_whole, unit_in, unit_out = barrier(
+        (mixed_whole, shared_in.transpose(1, 2, 0), shared_out)
+    )
+    unit_in, unit_out = gather_first(unit_in, group), gather_first(unit_out, group)
+    group_hidden = group_tokens + mm(mixed_whole, out_whole)
+    group_scale2 = norm_scale(group_hidden)
+    group_normed = (group_hidden * group_scale2 * norm2_full).astype(BF16)
+    hidden = lax.dynamic_slice_in_dim(group_hidden, me * rows, rows, 0)
+    scale2 = lax.dynamic_slice_in_dim(group_scale2, me * rows, rows, 0)
+    normed2 = lax.dynamic_slice_in_dim(group_normed, me * rows, rows, 0)
     column_normed = lax.all_gather(normed2, "dp", axis=0, tiled=True)
-    group_cot = jnp.concatenate(plane_gather(cotangent, group), axis=0)
-    column_cot = lax.all_gather(cotangent, "dp", axis=0, tiled=True)
 
     named = group_routes == me
     taken = jnp.any(named, axis=1) & group_valid
@@ -248,43 +296,47 @@
     offsets = jnp.sum(jnp.where(places[None, :] < places[:, None], counts[None, :], 0.0), axis=1)
     rank = (inside + offsets[:, None]).astype(jnp.int32)
     rank = jnp.where(taken & (rank < capacity), rank, -1)
-    rank = jnp.take(rank, order, axis=0).reshape(1, group_rows)
-    gate_rel = jnp.take(gate_here, order, axis=0).reshape(1, group_rows)
-    chosen = rank == jnp.arange(slots, dtype=jnp.int32)[:, None]
+    slot_ids = jnp.arange(slots, dtype=jnp.int32)[:, None]
+    chosen = rank.reshape(1, group_rows) == slot_ids
     pick = chosen.astype(BF16)
-    row_gate = jnp.sum(jnp.where(chosen, gate_rel, 0.0), axis=1, keepdims=True)
+    put = (jnp.take(rank, order_list, axis=0).reshape(1, group_rows) == slot_ids).astype(BF16)
+    row_gate = jnp.sum(
+        jnp.where(chosen, gate_here.reshape(1, group_rows), 0.0), axis=1, keepdims=True
+    )
     weight_in, weight_out = expert_in[0], expert_out[0]
     hidden_units = weight_out.shape[0]
     expert_rows = mm(pick, group_normed).astype(BF16)
     cot_rows = mm(pick, group_cot)
     val_grad = (cot_rows * row_gate).astype(BF16)
     expert_pre = mm(expert_rows, weight_in)
+    expert_pre, unit_in, unit_out = barrier((expert_pre, unit_in, unit_out))
+    unit_in, unit_out = gather_second(unit_in, group), gather_second(unit_out, group)
     e_gate, e_up = expert_pre[:, :hidden_units], expert_pre[:, hidden_units:]
     expert_act = swiglu_parts(e_gate, e_up)[1].astype(BF16)
     act_grad = mm_nt(val_grad, weight_out)
     out_grad = mm_tn(expert_act, val_grad).astype(BF16)
-    expert_out_grad = lax.psum_scatter(out_grad, "dp", scatter_dimension=0, tiled=True)
     pre_grad = jnp.concatenate(swiglu_back(e_gate, e_up, act_grad), axis=1).astype(BF16)
     in_grad = mm_tn(expert_rows, pre_grad).astype(BF16)
-    expert_in_grad = lax.psum_scatter(in_grad, "dp", scatter_dimension=0, tiled=True)
     row_grad = mm_nt(pre_grad, weight_in).astype(BF16)
     expert_val = mm(expert_act, weight_out)
     pair_dot = jnp.sum(cot_rows * expert_val, axis=1, keepdims=True)
-    routed_part = mm_tn(pick, (expert_val * row_gate).astype(BF16))
-    normed_part = mm_tn(pick, row_grad)
+    routed_part = mm_tn(put, (expert_val * row_gate).astype(BF16))
+    normed_part = mm_tn(put, row_grad)
     routed_sum = plane_sum(routed_part.reshape(group, rows, width), group)
     routed_grad = plane_sum(normed_part.reshape(group, rows, width), group)
     pair_dots = jnp.sum(jnp.where(chosen, pair_dot, 0.0), axis=0).reshape(group, rows)
-    inverse = jnp.argmax(order[None, :] == places[:, None], axis=1)
-    pair_dots = jnp.take(pair_dots, inverse, axis=0)
     pair_back = lax.all_to_all(pair_dots, "expert", 0, 0, tiled=True)
     gate_values_grad = jnp.sum(
         jnp.where(routes.T[None] == places[:, None, None], pair_back[:, None, :], 0.0), axis=0
     ).T
 
     units = shared_out.shape[0]
-    unit_in = jnp.concatenate(plane_gather(shared_in.transpose(1, 2, 0), group), axis=1)
-    unit_out = jnp.concatenate(plane_gather(shared_out, group), axis=0)
+    column_normed, out_grad, in_grad, unit_in, unit_out = barrier(
+        (column_normed, out_grad, in_grad, unit_in, unit_out)
+    )
+    unit_in = jnp.concatenate(gather_third(unit_in, group), axis=1)
+    unit_out = jnp.concatenate(gather_third(unit_out, group), axis=0)
+    expert_out_grad = lax.psum_scatter(out_grad, "dp", scatter_dimension=0, tiled=True)
     plane_units = group * units
     shared_weight = jax.nn.sigmoid(
         jnp.sum(column_normed.astype(F32) * gate_full, axis=1, keepdims=True)
@@ -303,30 +355,28 @@
     shared_pre_grad = jnp.concatenate(swiglu_back(s_gate, s_up, shared_act_grad), axis=1)
     shared_pre_grad = shared_pre_grad.astype(BF16)
     normed_term = mm(shared_pre_grad, unit_flat) + logit_grad * gate_full
-    shared_grad = lax.psum_scatter(
-        normed_term.astype(BF16), "dp", scatter_dimension=0, tiled=True
-    ).astype(F32)
-    shared_sum = lax.psum_scatter(
-        (shared_weight * shared_val).astype(BF16), "dp", scatter_dimension=0, tiled=True
-    ).astype(F32)
+    normed_term, expert_out_grad = barrier((normed_term.astype(BF16), expert_out_grad))
+    shared_grad = lax.psum_scatter(normed_term, "dp", scatter_dimension=0, tiled=True)
+    shared_grad, in_grad = barrier((shared_grad, in_grad))
+    shared_grad = shared_grad.astype(F32)
+    expert_in_grad = lax.psum_scatter(in_grad, "dp", scatter_dimension=0, tiled=True)
     unit_out_grad = mm_tn(shared_act, shared_val_grad)
     unit_in_grad = mm_tn(shared_pre_grad, column_normed)
     shared_out_grad = plane_sum(unit_out_grad.reshape(group, units, width), group)
     unit_in_grad = unit_in_grad.reshape(2, group, units, width).transpose(1, 0, 2, 3)
     shared_in_grad = plane_sum(unit_in_grad, group).transpose(2, 0, 1)
 
-    output = (valid_float * (hidden + shared_sum + routed_sum)).astype(BF16)
     normed2_grad = shared_grad + routed_grad
     norm_term, norm2_part = norm_back(hidden, scale2, norm2_full, normed2_grad)
     hidden_grad = cotangent.astype(F32) * valid_float + norm_term
-    branch_grad = jnp.concatenate(plane_gather(hidden_grad.astype(BF16), group), axis=0)
+    branch_grad = plane_rows(hidden_grad.astype(BF16), group, order)
 
     out_own_grad = mm_tn(mixed, branch_grad).astype(BF16)
     out_own_grad = out_own_grad.reshape(own_heads, split, shard, width).transpose(1, 0, 2, 3)
     out_own_grad = lax.all_to_all(
         out_own_grad, "expert", 0, 0, axis_index_groups=pairs, tiled=True
     ).reshape(planes * shard, width)
-    out_weight_grad = lax.psum_scatter(out_own_grad, "dp", scatter_dimension=0, tiled=True)
+    out_own = lax.dynamic_slice_in_dim(out_whole, me * own_width, own_width, 0)
     mixed_grad = mm_nt(branch_grad, out_own).astype(BF16).reshape(head_shape)
     value_grad = jnp.einsum(
         "shqk,sqhd->skhd", probs.astype(BF16), mixed_grad, preferred_element_type=F32
@@ -348,9 +398,19 @@
         axis=1,
     ).astype(BF16)
     bias_part = jnp.sum(qkv_grad.astype(F32), axis=0)
-    normed1_grad = plane_sum(mm_nt(qkv_grad, qkv_own).reshape(group, rows, width), group)
+    sent_grad = jnp.take(qkv_grad.reshape(group, rows, 3 * own_width), order_list, axis=0)
+    normed1_grad = mm_nt(sent_grad.reshape(group_rows, 3 * own_width), qkv_own)
+    normed1_grad = plane_sum(normed1_grad.reshape(group, rows, width), group)
     qkv_own_grad = mm_tn(normed1, qkv_grad).astype(BF16)
+    shared_part = (shared_weight * shared_val).astype(BF16)
+    shared_part, expert_in_grad = barrier((shared_part, expert_in_grad))
+    shared_sum = lax.psum_scatter(shared_part, "dp", scatter_dimension=0, tiled=True)
+    qkv_own_grad, shared_sum = barrier((qkv_own_grad, shared_sum))
+    shared_sum = shared_sum.astype(F32)
     qkv_own_grad = lax.psum_scatter(qkv_own_grad, "dp", scatter_dimension=0, tiled=True)
+    out_own_grad, qkv_own_grad = barrier((out_own_grad, qkv_own_grad))
+    out_weight_grad = lax.psum_scatter(out_own_grad, "dp", scatter_dimension=0, tiled=True)
+    output = (valid_float * (hidden + shared_sum + routed_sum)).astype(BF16)
     qkv_own_grad = lax.all_to_all(
         qkv_own_grad.reshape(group, shard, 3 * own_width), "expert", 0, 0, tiled=True
     )

time: 883 us -> 787 us (0.89)
  waiting for transfers between devices: 418 us -> 256 us
  local copies, waits for them, and re-layouts: 131 us -> 182 us
  blocking collectives: 28.9 us -> 0 us
  matrix products: 144 us -> 164 us
  starting transfers between devices: 56.9 us -> 73.1 us
    reduce_scatter x1, waiting for transfers between devices: 140 us -> 11.1 us  [shards(): lax.psum_scatter(in_grad, 'dp', scatter_dimension=0, tiled=True)]
    ppermute x60 -> x64, waiting for transfers between devices: 178 us -> 118 us  [send(): return lax.ppermute(block, 'expert', [(i, target(i)) for i in range(size)])]
    reduce_scatter x1, waiting for transfers between devices: 0.02 us -> 43.3 us  [shards(): lax.psum_scatter(out_grad, 'dp', scatter_dimension=0, tiled=True)]
    dynamic_update_slice x0 -> x39, local copies, waits for them, and re-layouts: none -> 42.6 us  [the longest x23 24.2 us: plane_rows(): lax.dynamic_update_slice_in_dim(whole, part, source * rows, 0)]
    reduce_scatter x2, waiting for transfers between devices: 8.99 us -> 47.1 us  [the longest x1 47.1 us: shards(): lax.psum_scatter(normed_term, 'dp', scatter_dimension=0, tiled=True)]
    all_to_all x1, waiting for transfers between devices: 35.2 us -> 0.01 us  [shards(): pair_back = lax.all_to_all(pair_dots, 'expert', 0, 0, tiled=True)]
    all_gather x1, waiting for transfers between devices: 33 us -> 0.01 us  [shards(): lax.all_gather(by_head, 'dp', axis=0, tiled=True)]
    all_to_all x3 -> x0, blocking collectives: 28.9 us -> none  [the longest x1 17.6 us: shards(): by_head = lax.all_to_all(by_head, 'expert', 0, 0, tiled=True)]
  transfers between devices with their start and end apart: 74 -> 80, of which waited for: 30 -> 26; matrix products, arithmetic and copies ran while one was open for 29% -> 51% of each run, Pallas kernels for 0% -> 0%
where the time goes in v2:
time: 787 us; the launch traced here: 778 us
  waiting for transfers between devices  256 us (33%)
  local copies, waits for them, and re-layouts  182 us (23%)
  matrix products  164 us (21%)
  other arithmetic  84.7 us (11%)
  starting transfers between devices  73.1 us (9%)
  between operations  17.1 us (2%)
    dot_general x23, matrix products, dot(): return lax.dot_general(a, b, (dims, ((), ())), preferred_element_type=F32)  152 us
    ppermute x64, waiting for transfers between devices, send(): return lax.ppermute(block, 'expert', [(i, target(i)) for i in range(size)])  118 us
    reduce_scatter x1, waiting for transfers between devices, shards(): lax.psum_scatter(normed_term, 'dp', scatter_dimension=0, tiled=True)  47.1 us
    ppermute x64, starting transfers between devices, send(): return lax.ppermute(block, 'expert', [(i, target(i)) for i in range(size)])  45.6 us
    reduce_scatter x1, waiting for transfers between devices, shards(): lax.psum_scatter(out_grad, 'dp', scatter_dimension=0, tiled=True)  43.3 us
    unnamed x215, local copies, waits for them, and re-layouts  41.1 us
    add x5, other arithmetic, plane_sum(): near = parts[:4] + got.astype(F32)  26.4 us
    dynamic_update_slice x23, local copies, waits for them, and re-layouts, plane_rows(): lax.dynamic_update_slice_in_dim(whole, part, source * rows, 0)  24.2 us
  transfers between devices with their start and end apart: 80, of which 26 were waited for; matrix products, arithmetic and copies ran while one was open for 51% of the time, Pallas kernels for 0%

profile of v2, /device:TPU:0, one launch (start us, length us, event | category | flops | bytes accessed | tf_op | source)
XLA Modules:
  0.0 777.8 jit_solution(13175708563407806456)
XLA Ops:
  12.2 5.2 all-to-all-start
  18.3 11.7 %all-to-all-done = bf16[8,64,768]{2,1,0:T(8,128)(2,1)S(1)} async-done(((bf16[8,64,768]{2,1,0:T(8,128)(2,1)}), bf16[8,64,768]{2,1,0:T(8,128)(2,1)S(1)}, u32[]{:S(2)}, u32[]{:S(2)}) %all-to-all-start) | async-done | bytes 786464 | tf_op jit(solution)/shard_map/all_to_all | solution.py:201
  41.4 3.4 collective-permute-done
  45.7 10.2 %collective-permute-done.14 = bf16[128,2048]{1,0:T(8,128)(2,1)} collective-permute-done((bf16[128,2048]{1,0:T(8,128)(2,1)S(1)}, bf16[128,2048]{1,0:T(8,128)(2,1)}, u32[]{:S(2)}, u32[]{:S(2)}) %collective-permute-start.14) | collective-permute-done | bytes 524320 | tf_op jit(solution)/shard_map/ppermute | solution.py:50
  63.3 4.7 all-to-all-start.1
  68.0 4.4 broadcast_in_dim.207
  93.8 3.1 fusion.5
  96.9 6.8 collective-permute-done.7
  110.4 9.0 %collective-permute-done.9 = bf16[2,2,64,2048]{3,2,1,0:T(8,128)(2,1)} collective-permute-done((bf16[2,2,64,2048]{3,2,1,0:T(8,128)(2,1)S(1)}, bf16[2,2,64,2048]{3,2,1,0:T(8,128)(2,1)}, u32[]{:S(2)}, u32[]{:S(2)}) %collective-permute-start.9) | collective-permute-done | bytes 1048608 | tf_op jit(solution)/shard_map/ppermute | solution.py:50
  128.8 6.5 convolution_add_fusion
  150.7 10.4 %collective-permute-done.21 = bf16[1024,256]{1,0:T(8,128)(2,1)} collective-permute-done((bf16[1024,256]{1,0:T(8,128)(2,1)S(1)}, bf16[1024,256]{1,0:T(8,128)(2,1)}, u32[]{:S(2)}, u32[]{:S(2)}) %collective-permute-start.21) | collective-permute-done | bytes 524320 | tf_op jit(solution)/shard_map/ppermute | solution.py:50
  162.3 11.1 %all-gather.8.cloned.1.call-done = bf16[512,2048]{1,0:T(8,128)(2,1)} async-done(((bf16[128,2048]{1,0:T(8,128)(2,1)}), bf16[512,2048]{1,0:T(8,128)(2,1)}) %all-gather.8.cloned.1.call-update) | async-done | bytes 2097168 | tf_op jit(solution)/shard_map/all_gather | solution.py:240
  178.0 4.9 collective-permute-done.23
  190.7 12.5 %multiply_reduce_fusion = (f32[1024]{0:T(1024)S(1)}, f32[1024,2048]{1,0:T(8,128)S(1)}) fusion(bf16[1024,2048]{1,0:T(8,128)(2,1)S(1)} %constant_dynamic-update-slice_fusion.24, bf16[2048,2048]{1,0:T(8,128)(2,1)} %bitcast.23, bf16[1024,2048]{1,0:T(8,128)(2,1)} %constant_dynamic-update-slice_fusion.41), kind=kOutput, calls=%fused_computation.18 | convolution fusion | flops 8598322176 | bytes 25169920 | tf_op jit(solution)/shard_map/dot_general | solution.py:18
  206.4 3.4 convolution_convert_fusion.3
  210.7 9.9 %fusion.3 = f32[464,2816]{1,0:T(8,128)S(1)} fusion(bf16[464,2048]{1,0:T(8,128)(2,1)} %convolution_convert_fusion.3, bf16[1,2048,2816]{2,1,0:T(8,128)(2,1)} %param.30), kind=kOutput, calls=%fused_computation.11 | convolution fusion | flops 5351931904 | bytes 18661376 | tf_op jit(solution)/shard_map/dot_general | solution.py:18
  220.7 15.3 %collective-permute-done.30 = bf16[176,2048]{1,0:T(8,128)(2,1)} collective-permute-done((bf16[176,2048]{1,0:T(8,128)(2,1)S(1)}, bf16[176,2048]{1,0:T(8,128)(2,1)}, u32[]{:S(2)}, u32[]{:S(2)}) %collective-permute-start.30) | collective-permute-done | bytes 720928 | tf_op jit(solution)/shard_map/ppermute | solution.py:50
  239.0 5.2 fusion.8
  244.3 7.6 multiply_reduce_fusion.2
  253.0 6.0 multiply_convert_fusion.9
  260.5 9.1 %convolution_convert_fusion = bf16[2048,2816]{1,0:T(8,128)(2,1)} fusion(bf16[464,2048]{1,0:T(8,128)(2,1)S(1)} %copy-done.85, bf16[464,1408]{1,0:T(8,128)(2,1)S(1)} %get-tuple-element.119, bf16[464,1408]{1,0:T(8,128)(2,1)S(1)} %get-tuple-element.118), kind=kOutput, calls=%fused_computation.13 | convolution fusion | flops 5362925568 | bytes 16048128 | tf_op jit(solution)/shard_map/dot_general | solution.py:18
  269.6 8.2 %convolution_convert_fusion.1 = bf16[1408,2048]{1,0:T(8,128)(2,1)} fusion(bf16[464,1408]{1,0:T(8,128)(2,1)} %copy-done.36, f32[464,2048]{1,0:T(8,128)} %get-tuple-element.152, f32[464]{0:T(512)S(1)} %get-tuple-element.108), kind=kOutput, calls=%fused_computation.19 | convolution fusion | flops 2680750080 | bytes 10876736 | tf_op jit(solution)/shard_map/dot_general | solution.py:18
  289.2 3.3 collective-permute-done.37
  295.2 4.3 copy-done.45
  299.5 11.5 %fusion.97 = f32[512,2816]{1,0:T(8,128)} fusion(bf16[512,2048]{1,0:T(8,128)(2,1)S(1)} %copy-done.7, bf16[2816,2048]{1,0:T(8,128)(2,1)} %bitcast.307), kind=kOutput, calls=%fused_computation.297 | convolution fusion | flops 5905580032 | bytes 19398656 | tf_op jit(solution)/shard_map/dot_general | solution.py:18
  311.0 8.3 %multiply_convert_fusion.7 = (bf16[512,1408]{1,0:T(8,128)(2,1)S(1)}, bf16[512,1408]{1,0:T(8,128)(2,1)S(1)}, bf16[512,1408]{1,0:T(8,128)(2,1)S(1)}) fusion(f32[512,2816]{1,0:T(8,128)} %fusion.97, bf16[1408,2048]{1,0:T(8,128)(2,1)} %copy-done.48, bf16[512,2048]{1,0:T(8,128)(2,1)S(1)} %copy-done.79, f32[512]{0:T(512)S(1)} %add_divide_fusion.2, f32[512]{0:T(512)S(1)} %fusion.72), kind=kOutput, calls=%fused_computation.60 | convolution fusion | flops 2967076864 | bytes 17960960 | tf_op jit(solution)/shard_map/dot_general | solution.py:18
  319.3 9.3 %multiply_convert_fusion.1 = (bf16[512,2048]{1,0:T(8,128)(2,1)}, f32[512]{0:T(512)S(1)}) fusion(f32[512]{0:T(512)S(1)} %add_divide_fusion.2, f32[512]{0:T(512)S(1)} %fusion.72, bf16[512,2048]{1,0:T(8,128)(2,1)S(1)} %copy-done.79, bf16[512,1408]{1,0:T(8,128)(2,1)S(1)} %get-tuple-element.120, bf16[1408,2048]{1,0:T(8,128)(2,1)} %copy-done.48), kind=kOutput, calls=%fused_computation.37 | convolution fusion | flops 2959080960 | bytes 11409408 | tf_op jit(solution)/shard_map/dot_general | solution.py:18
  328.6 7.5 add_convert_fusion
  336.1 43.3 %reduce-scatter.7.cloned.1.call-done = bf16[352,2048]{1,0:T(8,128)(2,1)} async-done(((bf16[1408,2048]{1,0:T(8,128)(2,1)}), bf16[352,2048]{1,0:T(8,128)(2,1)}) %reduce-scatter.7.cloned.1.call-update) | async-done | bytes 1441808 | tf_op jit(solution)/shard_map/reduce_scatter | solution.py:339
  379.5 47.1 %reduce-scatter.9.cloned.1.call-done = bf16[128,2048]{1,0:T(8,128)(2,1)} async-done(((bf16[512,2048]{1,0:T(8,128)(2,1)}), bf16[128,2048]{1,0:T(8,128)(2,1)}) %reduce-scatter.9.cloned.1.call-update) | async-done | bytes 524304 | tf_op jit(solution)/shard_map/reduce_scatter | solution.py:359
  427.4 9.1 %fusion.14 = bf16[464,2048]{1,0:T(8,128)(2,1)S(1)} fusion(bf16[1,2048,2816]{2,1,0:T(8,128)(2,1)} %param.30, bf16[464,1408]{1,0:T(8,128)(2,1)} %copy-done.90, bf16[464,1408]{1,0:T(8,128)(2,1)S(1)} %copy-done.89), kind=kOutput, calls=%fused_computation.49 | convolution fusion | flops 5358108672 | bytes 16048128 | tf_op jit(solution)/shard_map/dot_general | solution.py:18
  448.7 3.3 copy-done.13
  454.1 3.7 all-to-all-start.5
  465.6 3.5 fusion.87
  469.1 4.3 copy-done
  475.4 8.7 %fusion.23 = f32[2816,2048]{1,0:T(8,128)S(1)} fusion(bf16[512,2048]{1,0:T(8,128)(2,1)} %all-gather.10.cloned.1.call-done, bf16[512,1408]{1,0:T(8,128)(2,1)} %copy-done.87, bf16[512,1408]{1,0:T(8,128)(2,1)} %copy-done.86), kind=kOutput, calls=%fused_computation.84 | convolution fusion | flops 5911347200 | bytes 28049408 | tf_op jit(solution)/shard_map/dot_general | solution.py:18
  484.1 8.7 %copy.207 = f32[2,8,176,2048]{3,2,0,1:T(8,128)} copy(f32[2,8,176,2048]{3,2,1,0:T(8,128)S(1)} %bitcast.269) | data formatting | bytes 46137344 | tf_op jit(solution)/shard_map/reshape | solution.py:366
  492.7 7.7 slice.461
  501.7 4.7 slice.312
  507.0 4.0 convert_add_fusion.3
  517.2 14.5 %collective-permute-done.53 = bf16[2,128,2048]{2,1,0:T(8,128)(2,1)S(1)} collective-permute-done((bf16[2,128,2048]{2,1,0:T(8,128)(2,1)S(1)}, bf16[2,128,2048]{2,1,0:T(8,128)(2,1)S(1)}, u32[]{:S(2)}, u32[]{:S(2)}) %collective-permute-start.53) | collective-permute-done | bytes 1048608 | tf_op jit(solution)/shard_map/ppermute | solution.py:50
  532.0 3.9 convert_add_fusion.1
  546.5 3.0 constant_dynamic-update-slice_fusion.23
  550.5 19.7 %collective-permute-done.62 = bf16[2,176,2048]{2,1,0:T(8,128)(2,1)} collective-permute-done((bf16[2,176,2048]{2,1,0:T(8,128)(2,1)}, bf16[2,176,2048]{2,1,0:T(8,128)(2,1)}, u32[]{:S(2)}, u32[]{:S(2)}) %collective-permute-start.62) | collective-permute-done | bytes 1441824 | tf_op jit(solution)/shard_map/ppermute | solution.py:50
  574.2 13.3 %slice_add_fusion = f32[4,2,176,2048]{3,2,1,0:T(8,128)} fusion(f32[8,2,176,2048]{3,2,1,0:T(8,128)} %bitcast.267, bf16[4,2,176,2048]{3,2,1,0:T(8,128)(2,1)} %collective-permute-done.58), kind=kLoop, calls=%fused_computation.8 | loop fusion | flops 5767168 | bytes 28835840 | tf_op jit(solution)/shard_map/add | solution.py:96
  587.4 4.8 slice.463
  601.6 3.3 convolution_convert_fusion.7
  608.8 3.4 multiply_reduce_fusion.4
  612.2 11.1 %reduce-scatter.11.cloned.1.call-done = bf16[512,2816]{1,0:T(8,128)(2,1)} async-done(((bf16[2048,2816]{1,0:T(8,128)(2,1)}), bf16[512,2816]{1,0:T(8,128)(2,1)}) %reduce-scatter.11.cloned.1.call-update) | async-done | bytes 2883600 | tf_op jit(solution)/shard_map/reduce_scatter | solution.py:362
  636.8 3.6 convolution_convert_fusion.5
  643.0 3.4 gather_fusion.1
  657.6 5.8 fusion.98
  663.4 3.3 copy-done.2
  669.8 7.8 %convolution_convert_fusion.2 = bf16[2048,768]{1,0:T(8,128)(2,1)} fusion(bf16[1024,768]{0,1:T(8,128)(2,1)S(1)} %bitcast_dynamic-update-slice_fusion.7, bf16[1024,2048]{1,0:T(8,128)(2,1)} %constant_dynamic-update-slice_fusion.41, f32[2048]{0:T(1024)S(1)} %copy-done.50, f32[1024]{0:T(1024)S(1)} %copy-done.66), kind=kOutput, calls=%fused_computation.46 | convolution fusion | flops 3231186944 | bytes 8925184 | tf_op jit(solution)/shard_map/dot_general | solution.py:18
  679.4 4.8 slice_add_fusion.1
  685.0 4.2 collective-permute-done.63
  699.8 10.5 %collective-permute-done.60 = bf16[2,176,2048]{2,1,0:T(8,128)(2,1)S(1)} collective-permute-done((bf16[2,176,2048]{2,1,0:T(8,128)(2,1)S(1)}, bf16[2,176,2048]{2,1,0:T(8,128)(2,1)S(1)}, u32[]{:S(2)}, u32[]{:S(2)}) %collective-permute-start.60) | collective-permute-done | bytes 1441824 | tf_op jit(solution)/shard_map/ppermute | solution.py:50
  720.2 3.7 convolution_convert_fusion.4
  724.9 4.5 all-to-all-start.3
  731.7 4.9 all-to-all-start.2
  745.3 3.6 all-to-all-start.4
  748.8 4.9 bitcast_convert_fusion
  756.3 5.1 all-to-all-done.4
  765.0 3.7 reduce-scatter.17.cloned.1.call-done
  (538 shorter events, 249.3 us)
Async XLA Ops:
  7.3 55.3 %all-gather.12.cloned.1.call-start = ((), (), s32[]{:S(2)}) async-start(), calls=%async_computation.21 | async-start | bytes 1310720 | tf_op jit(solution)/shard_map/all_gather | solution.py:198
  12.2 17.8 %all-to-all-start = ((bf16[8,64,768]{2,1,0:T(8,128)(2,1)}), bf16[8,64,768]{2,1,0:T(8,128)(2,1)S(1)}, u32[]{:S(2)}, u32[]{:S(2)}) async-start(bf16[8,64,768]{2,1,0:T(8,128)(2,1)} %reshape.686), calls=%async_computation | async-start | bytes 1572864 | tf_op jit(solution)/shard_map/all_to_all | solution.py:201
  17.4 108.8 %all-gather.6.cloned.1.call-start = ((), (), s32[]{:S(2)}) async-start(), calls=%async_computation.12 | async-start | bytes 3932160 | tf_op jit(solution)/shard_map/all_gather | solution.py:204
  30.0 14.8 %collective-permute-start = (bf16[128,2048]{1,0:T(8,128)(2,1)S(1)}, bf16[128,2048]{1,0:T(8,128)(2,1)S(1)}, u32[]{:S(2)}, u32[]{:S(2)}) collective-permute-start(bf16[128,2048]{1,0:T(8,128)(2,1)S(1)} %copy-done.9), channel_id=1, source_target_pairs={{0,2},{1,5},{2,0},{3,7},{4,6},{5,1},{6,4},{7,3},{8,10},{9,13},{10,... | collective-permute-start | bytes 1572872 | tf_op jit(solution)/shard_map/ppermute | solution.py:50
  31.1 27.5 %collective-permute-start.1 = (bf16[128,2048]{1,0:T(8,128)(2,1)S(1)}, bf16[128,2048]{1,0:T(8,128)(2,1)S(1)}, u32[]{:S(2)}, u32[]{:S(2)}) collective-permute-start(bf16[128,2048]{1,0:T(8,128)(2,1)S(1)} %copy-done.9), channel_id=1, source_target_pairs={{0,4},{1,3},{2,6},{3,1},{4,0},{5,7},{6,2},{7,5},{8,12},{9,11},{10,... | collective-permute-start | bytes 1572872 | tf_op jit(solution)/shard_map/ppermute | solution.py:50
  31.7 46.1 %collective-permute-start.3 = (bf16[128,2048]{1,0:T(8,128)(2,1)S(1)}, bf16[128,2048]{1,0:T(8,128)(2,1)}, u32[]{:S(2)}, u32[]{:S(2)}) collective-permute-start(bf16[128,2048]{1,0:T(8,128)(2,1)S(1)} %copy-done.9), channel_id=1, source_target_pairs={{0,1},{1,0},{2,3},{3,2},{4,5},{5,4},{6,7},{7,6},{8,9},{9,8},{10,11... | collective-permute-start | bytes 1572872 | tf_op jit(solution)/shard_map/ppermute | solution.py:50
  31.7 24.2 %collective-permute-start.14 = (bf16[128,2048]{1,0:T(8,128)(2,1)S(1)}, bf16[128,2048]{1,0:T(8,128)(2,1)}, u32[]{:S(2)}, u32[]{:S(2)}) collective-permute-start(bf16[128,2048]{1,0:T(8,128)(2,1)S(1)} %copy-done.16), channel_id=1, source_target_pairs={{0,2},{1,5},{2,0},{3,7},{4,6},{5,1},{6,4},{7,3},{8,10},{9,13},{10,... | collective-permute-start | bytes 1572872 | tf_op jit(solution)/shard_map/ppermute | solution.py:50
  33.2 26.3 %collective-permute-start.15 = (bf16[128,2048]{1,0:T(8,128)(2,1)S(1)}, bf16[128,2048]{1,0:T(8,128)(2,1)}, u32[]{:S(2)}, u32[]{:S(2)}) collective-permute-start(bf16[128,2048]{1,0:T(8,128)(2,1)S(1)} %copy-done.16), channel_id=1, source_target_pairs={{0,4},{1,3},{2,6},{3,1},{4,0},{5,7},{6,2},{7,5},{8,12},{9,11},{10,... | collective-permute-start | bytes 1572872 | tf_op jit(solution)/shard_map/ppermute | solution.py:50
  44.8 35.1 %collective-permute-start.17 = (bf16[128,2048]{1,0:T(8,128)(2,1)S(1)}, bf16[128,2048]{1,0:T(8,128)(2,1)}, u32[]{:S(2)}, u32[]{:S(2)}) collective-permute-start(bf16[128,2048]{1,0:T(8,128)(2,1)S(1)} %copy-done.16), channel_id=1, source_target_pairs={{0,1},{1,0},{2,3},{3,2},{4,5},{5,4},{6,7},{7,6},{8,9},{9,8},{10,11... | collective-permute-start | bytes 1572872 | tf_op jit(solution)/shard_map/ppermute | solution.py:50
  55.9 17.6 %collective-permute-start.2 = (bf16[128,2048]{1,0:T(8,128)(2,1)S(1)}, bf16[128,2048]{1,0:T(8,128)(2,1)}, u32[]{:S(2)}, u32[]{:S(2)}) collective-permute-start(bf16[128,2048]{1,0:T(8,128)(2,1)S(1)} %collective-permute-done), channel_id=1, source_target_pairs={{0,4},{1,3},{2,6},{3,1},{4,0},{5,7},{6,2},{7,5},{8,12},{9,11},{10,... | collective-permute-start | bytes 1572872 | tf_op jit(solution)/shard_map/ppermute | solution.py:50
  58.5 24.9 %collective-permute-start.4 = (bf16[128,2048]{1,0:T(8,128)(2,1)S(1)}, bf16[128,2048]{1,0:T(8,128)(2,1)}, u32[]{:S(2)}, u32[]{:S(2)}) collective-permute-start(bf16[128,2048]{1,0:T(8,128)(2,1)S(1)} %collective-permute-done), channel_id=1, source_target_pairs={{0,1},{1,0},{2,3},{3,2},{4,5},{5,4},{6,7},{7,6},{8,9},{9,8},{10,11... | collective-permute-start | bytes 1572872 | tf_op jit(solution)/shard_map/ppermute | solution.py:50
  59.5 16.2 %collective-permute-start.16 = (bf16[128,2048]{1,0:T(8,128)(2,1)}, bf16[128,2048]{1,0:T(8,128)(2,1)}, u32[]{:S(2)}, u32[]{:S(2)}) collective-permute-start(bf16[128,2048]{1,0:T(8,128)(2,1)} %collective-permute-done.14), channel_id=1, source_target_pairs={{0,4},{1,3},{2,6},{3,1},{4,0},{5,7},{6,2},{7,5},{8,12},{9,11},{10,... | collective-permute-start | bytes 1572872 | tf_op jit(solution)/shard_map/ppermute | solution.py:50
  63.3 26.6 %all-to-all-start.1 = ((f32[32,12,128]{2,1,0:T(8,128)}), f32[32,12,128]{2,1,0:T(8,128)S(1)}, u32[]{:S(2)}, u32[]{:S(2)}) async-start(f32[32,12,128]{2,1,0:T(8,128)} %broadcast_in_dim.204), calls=%async_computation.1 | async-start | bytes 524288 | tf_op jit(solution)/shard_map/all_to_all | solution.py:206
  68.0 105.5 %all-gather.8.cloned.1.call-start = ((), (), s32[]{:S(2)}) async-start(), calls=%async_computation.13 | async-start | bytes 2621440 | tf_op jit(solution)/shard_map/all_gather | solution.py:240
  73.5 14.1 %collective-permute-start.5 = (bf16[128,2048]{1,0:T(8,128)(2,1)S(1)}, bf16[128,2048]{1,0:T(8,128)(2,1)S(1)}, u32[]{:S(2)}, u32[]{:S(2)}) collective-permute-start(bf16[128,2048]{1,0:T(8,128)(2,1)S(1)} %copy-done.41), channel_id=1, source_target_pairs={{0,1},{1,0},{2,3},{3,2},{4,5},{5,4},{6,7},{7,6},{8,9},{9,8},{10,11... | collective-permute-start | bytes 1572872 | tf_op jit(solution)/shard_map/ppermute | solution.py:50
  75.6 11.2 %collective-permute-start.18 = (bf16[128,2048]{1,0:T(8,128)(2,1)}, bf16[128,2048]{1,0:T(8,128)(2,1)S(1)}, u32[]{:S(2)}, u32[]{:S(2)}) collective-permute-start(bf16[128,2048]{1,0:T(8,128)(2,1)} %collective-permute-done.14), channel_id=1, source_target_pairs={{0,1},{1,0},{2,3},{3,2},{4,5},{5,4},{6,7},{7,6},{8,9},{9,8},{10,11... | collective-permute-start | bytes 1572872 | tf_op jit(solution)/shard_map/ppermute | solution.py:50
  77.8 11.2 %collective-permute-start.19 = (bf16[128,2048]{1,0:T(8,128)(2,1)}, bf16[128,2048]{1,0:T(8,128)(2,1)S(1)}, u32[]{:S(2)}, u32[]{:S(2)}) collective-permute-start(bf16[128,2048]{1,0:T(8,128)(2,1)} %collective-permute-done.15), channel_id=1, source_target_pairs={{0,1},{1,0},{2,3},{3,2},{4,5},{5,4},{6,7},{7,6},{8,9},{9,8},{10,11... | collective-permute-start | bytes 1572872 | tf_op jit(solution)/shard_map/ppermute | solution.py:50
  79.9 23.7 %collective-permute-start.7 = (bf16[2,2,64,2048]{3,2,1,0:T(8,128)(2,1)S(1)}, bf16[2,2,64,2048]{3,2,1,0:T(8,128)(2,1)S(1)}, u32[]{:S(2)}, u32[]{:S(2)}) collective-permute-start(bf16[2,2,64,2048]{3,2,1,0:T(8,128)(2,1)S(1)} %bitcast.295), channel_id=1, source_target_pairs={{0,2},{1,5},{2,0},{3,7},{4,6},{5,1},{6,4},{7,3},{8,10},{9,13},{10,... | collective-permute-start | bytes 3145736 | tf_op jit(solution)/shard_map/ppermute | solution.py:50
  83.5 23.0 %collective-permute-start.8 = (bf16[2,2,64,2048]{3,2,1,0:T(8,128)(2,1)S(1)}, bf16[2,2,64,2048]{3,2,1,0:T(8,128)(2,1)}, u32[]{:S(2)}, u32[]{:S(2)}) collective-permute-start(bf16[2,2,64,2048]{3,2,1,0:T(8,128)(2,1)S(1)} %bitcast.296), channel_id=1, source_target_pairs={{0,4},{1,3},{2,6},{3,1},{4,0},{5,7},{6,2},{7,5},{8,12},{9,11},{10,... | collective-permute-start | bytes 3145736 | tf_op jit(solution)/shard_map/ppermute | solution.py:50
  86.8 34.9 %collective-permute-start.10 = (bf16[2,2,64,2048]{3,2,1,0:T(8,128)(2,1)S(1)}, bf16[2,2,64,2048]{3,2,1,0:T(8,128)(2,1)}, u32[]{:S(2)}, u32[]{:S(2)}) collective-permute-start(bf16[2,2,64,2048]{3,2,1,0:T(8,128)(2,1)S(1)} %bitcast.297), channel_id=1, source_target_pairs={{0,1},{1,0},{2,3},{3,2},{4,5},{5,4},{6,7},{7,6},{8,9},{9,8},{10,11... | collective-permute-start | bytes 3145736 | tf_op jit(solution)/shard_map/ppermute | solution.py:50
  103.6 15.7 %collective-permute-start.9 = (bf16[2,2,64,2048]{3,2,1,0:T(8,128)(2,1)S(1)}, bf16[2,2,64,2048]{3,2,1,0:T(8,128)(2,1)}, u32[]{:S(2)}, u32[]{:S(2)}) collective-permute-start(bf16[2,2,64,2048]{3,2,1,0:T(8,128)(2,1)S(1)} %collective-permute-done.7), channel_id=1, source_target_pairs={{0,4},{1,3},{2,6},{3,1},{4,0},{5,7},{6,2},{7,5},{8,12},{9,11},{10,... | collective-permute-start | bytes 3145736 | tf_op jit(solution)/shard_map/ppermute | solution.py:50
  106.5 17.6 %collective-permute-start.11 = (bf16[2,2,64,2048]{3,2,1,0:T(8,128)(2,1)S(1)}, bf16[2,2,64,2048]{3,2,1,0:T(8,128)(2,1)S(1)}, u32[]{:S(2)}, u32[]{:S(2)}) collective-permute-start(bf16[2,2,64,2048]{3,2,1,0:T(8,128)(2,1)S(1)} %collective-permute-done.7), channel_id=1, source_target_pairs={{0,1},{1,0},{2,3},{3,2},{4,5},{5,4},{6,7},{7,6},{8,9},{9,8},{10,11... | collective-permute-start | bytes 3145736 | tf_op jit(solution)/shard_map/ppermute | solution.py:50
  106.5 18.6 %collective-permute-start.12 = (bf16[2,2,64,2048]{3,2,1,0:T(8,128)(2,1)}, bf16[2,2,64,2048]{3,2,1,0:T(8,128)(2,1)S(1)}, u32[]{:S(2)}, u32[]{:S(2)}) collective-permute-start(bf16[2,2,64,2048]{3,2,1,0:T(8,128)(2,1)} %collective-permute-done.8), channel_id=1, source_target_pairs={{0,1},{1,0},{2,3},{3,2},{4,5},{5,4},{6,7},{7,6},{8,9},{9,8},{10,11... | collective-permute-start | bytes 3145736 | tf_op jit(solution)/shard_map/ppermute | solution.py:50
  126.2 151.7 %all-gather.10.cloned.1.call-start = ((), (), s32[]{:S(2)}) async-start(), calls=%async_computation.14 | async-start | bytes 2621440 | tf_op jit(solution)/shard_map/all_gather | solution.py:286
  147.5 13.6 %collective-permute-start.21 = (bf16[1024,256]{1,0:T(8,128)(2,1)S(1)}, bf16[1024,256]{1,0:T(8,128)(2,1)}, u32[]{:S(2)}, u32[]{:S(2)}) collective-permute-start(bf16[1024,256]{1,0:T(8,128)(2,1)S(1)} %copy.139), channel_id=1, source_target_pairs={{0,2},{1,5},{2,0},{3,7},{4,6},{5,1},{6,4},{7,3},{8,10},{9,13},{10,... | collective-permute-start | bytes 1572872 | tf_op jit(solution)/shard_map/ppermute | solution.py:50
  148.5 13.8 %collective-permute-start.22 = (bf16[1024,256]{1,0:T(8,128)(2,1)S(1)}, bf16[1024,256]{1,0:T(8,128)(2,1)}, u32[]{:S(2)}, u32[]{:S(2)}) collective-permute-start(bf16[1024,256]{1,0:T(8,128)(2,1)S(1)} %copy.139), channel_id=1, source_target_pairs={{0,4},{1,3},{2,6},{3,1},{4,0},{5,7},{6,2},{7,5},{8,12},{9,11},{10,... | collective-permute-start | bytes 1572872 | tf_op jit(solution)/shard_map/ppermute | solution.py:50
  175.3 9.9 %collective-permute-start.24 = (bf16[1024,256]{1,0:T(8,128)(2,1)S(1)}, bf16[1024,256]{1,0:T(8,128)(2,1)}, u32[]{:S(2)}, u32[]{:S(2)}) collective-permute-start(bf16[1024,256]{1,0:T(8,128)(2,1)S(1)} %copy.141), channel_id=1, source_target_pairs={{0,1},{1,0},{2,3},{3,2},{4,5},{5,4},{6,7},{7,6},{8,9},{9,8},{10,11... | collective-permute-start | bytes 1572872 | tf_op jit(solution)/shard_map/ppermute | solution.py:50
  175.6 10.8 %collective-permute-start.25 = (bf16[1024,256]{1,0:T(8,128)(2,1)}, bf16[1024,256]{1,0:T(8,128)(2,1)S(1)}, u32[]{:S(2)}, u32[]{:S(2)}) collective-permute-start(bf16[1024,256]{1,0:T(8,128)(2,1)} %collective-permute-done.21), channel_id=1, source_target_pairs={{0,1},{1,0},{2,3},{3,2},{4,5},{5,4},{6,7},{7,6},{8,9},{9,8},{10,11... | collective-permute-start | bytes 1572872 | tf_op jit(solution)/shard_map/ppermute | solution.py:50
  176.1 10.3 %collective-permute-start.26 = (bf16[1024,256]{1,0:T(8,128)(2,1)}, bf16[1024,256]{1,0:T(8,128)(2,1)S(1)}, u32[]{:S(2)}, u32[]{:S(2)}) collective-permute-start(bf16[1024,256]{1,0:T(8,128)(2,1)} %collective-permute-done.22), channel_id=1, source_target_pairs={{0,1},{1,0},{2,3},{3,2},{4,5},{5,4},{6,7},{7,6},{8,9},{9,8},{10,11... | collective-permute-start | bytes 1572872 | tf_op jit(solution)/shard_map/ppermute | solution.py:50
  186.6 49.5 %collective-permute-start.28 = (bf16[2,176,2048]{2,1,0:T(8,128)(2,1)S(1)}, bf16[2,176,2048]{2,1,0:T(8,128)(2,1)}, u32[]{:S(2)}, u32[]{:S(2)}) collective-permute-start(bf16[2,176,2048]{2,1,0:T(8,128)(2,1)S(1)} %bitcast.289), channel_id=1, source_target_pairs={{0,2},{1,5},{2,0},{3,7},{4,6},{5,1},{6,4},{7,3},{8,10},{9,13},{10,... | collective-permute-start | bytes 4325384 | tf_op jit(solution)/shard_map/ppermute | solution.py:50
  188.1 48.0 %collective-permute-start.29 = (bf16[2,176,2048]{2,1,0:T(8,128)(2,1)S(1)}, bf16[2,176,2048]{2,1,0:T(8,128)(2,1)}, u32[]{:S(2)}, u32[]{:S(2)}) collective-permute-start(bf16[2,176,2048]{2,1,0:T(8,128)(2,1)S(1)} %bitcast.290), channel_id=1, source_target_pairs={{0,4},{1,3},{2,6},{3,1},{4,0},{5,7},{6,2},{7,5},{8,12},{9,11},{10,... | collective-permute-start | bytes 4325384 | tf_op jit(solution)/shard_map/ppermute | solution.py:50
  189.6 46.4 %collective-permute-start.30 = (bf16[176,2048]{1,0:T(8,128)(2,1)S(1)}, bf16[176,2048]{1,0:T(8,128)(2,1)}, u32[]{:S(2)}, u32[]{:S(2)}) collective-permute-start(bf16[176,2048]{1,0:T(8,128)(2,1)S(1)} %copy-done.38), channel_id=1, source_target_pairs={{0,2},{1,5},{2,0},{3,7},{4,6},{5,1},{6,4},{7,3},{8,10},{9,13},{10,... | collective-permute-start | bytes 2162696 | tf_op jit(solution)/shard_map/ppermute | solution.py:50
  190.1 45.9 %collective-permute-start.31 = (bf16[176,2048]{1,0:T(8,128)(2,1)S(1)}, bf16[176,2048]{1,0:T(8,128)(2,1)S(1)}, u32[]{:S(2)}, u32[]{:S(2)}) collective-permute-start(bf16[176,2048]{1,0:T(8,128)(2,1)S(1)} %copy-done.38), channel_id=1, source_target_pairs={{0,4},{1,3},{2,6},{3,1},{4,0},{5,7},{6,2},{7,5},{8,12},{9,11},{10,... | collective-permute-start | bytes 2162696 | tf_op jit(solution)/shard_map/ppermute | solution.py:50
  210.7 168.7 %reduce-scatter.7.cloned.1.call-start = ((), (), s32[]{:S(2)}) async-start(), calls=%async_computation.15 | async-start | bytes 7208960 | tf_op jit(solution)/shard_map/reduce_scatter | solution.py:339
  236.9 40.9 %collective-permute-start.32 = (bf16[2,176,2048]{2,1,0:T(8,128)(2,1)}, bf16[2,176,2048]{2,1,0:T(8,128)(2,1)}, u32[]{:S(2)}, u32[]{:S(2)}) collective-permute-start(bf16[2,176,2048]{2,1,0:T(8,128)(2,1)} %collective-permute-done.28), channel_id=1, source_target_pairs={{0,4},{1,3},{2,6},{3,1},{4,0},{5,7},{6,2},{7,5},{8,12},{9,11},{10,... | collective-permute-start | bytes 4325384 | tf_op jit(solution)/shard_map/ppermute | solution.py:50
  238.8 39.0 %collective-permute-start.33 = (bf16[176,2048]{1,0:T(8,128)(2,1)}, bf16[176,2048]{1,0:T(8,128)(2,1)}, u32[]{:S(2)}, u32[]{:S(2)}) collective-permute-start(bf16[176,2048]{1,0:T(8,128)(2,1)} %collective-permute-done.30), channel_id=1, source_target_pairs={{0,4},{1,3},{2,6},{3,1},{4,0},{5,7},{6,2},{7,5},{8,12},{9,11},{10,... | collective-permute-start | bytes 2162696 | tf_op jit(solution)/shard_map/ppermute | solution.py:50
  277.9 148.6 %reduce-scatter.9.cloned.1.call-start = ((), (), s32[]{:S(2)}) async-start(), calls=%async_computation.16 | async-start | bytes 2621440 | tf_op jit(solution)/shard_map/reduce_scatter | solution.py:359
  278.6 13.9 %collective-permute-start.38 = (bf16[2,176,2048]{2,1,0:T(8,128)(2,1)S(1)}, bf16[2,176,2048]{2,1,0:T(8,128)(2,1)S(1)}, u32[]{:S(2)}, u32[]{:S(2)}) collective-permute-start(bf16[2,176,2048]{2,1,0:T(8,128)(2,1)S(1)} %bitcast.291), channel_id=1, source_target_pairs={{0,1},{1,0},{2,3},{3,2},{4,5},{5,4},{6,7},{7,6},{8,9},{9,8},{10,11... | collective-permute-start | bytes 4325384 | tf_op jit(solution)/shard_map/ppermute | solution.py:50
  278.8 13.9 %collective-permute-start.39 = (bf16[2,176,2048]{2,1,0:T(8,128)(2,1)}, bf16[2,176,2048]{2,1,0:T(8,128)(2,1)S(1)}, u32[]{:S(2)}, u32[]{:S(2)}) collective-permute-start(bf16[2,176,2048]{2,1,0:T(8,128)(2,1)} %collective-permute-done.28), channel_id=1, source_target_pairs={{0,1},{1,0},{2,3},{3,2},{4,5},{5,4},{6,7},{7,6},{8,9},{9,8},{10,11... | collective-permute-start | bytes 4325384 | tf_op jit(solution)/shard_map/ppermute | solution.py:50
  379.4 243.8 %reduce-scatter.11.cloned.1.call-start = ((), (), s32[]{:S(2)}) async-start(), calls=%async_computation.17 | async-start | bytes 14417920 | tf_op jit(solution)/shard_map/reduce_scatter | solution.py:362
  440.6 17.7 %collective-permute-start.42 = (bf16[4,128,2048]{2,1,0:T(8,128)(2,1)}, bf16[4,128,2048]{2,1,0:T(8,128)(2,1)S(1)}, u32[]{:S(2)}, u32[]{:S(2)}) collective-permute-start(bf16[4,128,2048]{2,1,0:T(8,128)(2,1)} %bitcast.56), channel_id=1, source_target_pairs={{0,1},{1,0},{2,3},{3,2},{4,5},{5,4},{6,7},{7,6},{8,9},{9,8},{10,11... | collective-permute-start | bytes 6291464 | tf_op jit(solution)/shard_map/ppermute | solution.py:50
  453.6 53.4 %collective-permute-start.52 = (bf16[4,128,2048]{2,1,0:T(8,128)(2,1)}, bf16[4,128,2048]{2,1,0:T(8,128)(2,1)}, u32[]{:S(2)}, u32[]{:S(2)}) collective-permute-start(bf16[4,128,2048]{2,1,0:T(8,128)(2,1)} %bitcast.63), channel_id=1, source_target_pairs={{0,1},{1,0},{2,3},{3,2},{4,5},{5,4},{6,7},{7,6},{8,9},{9,8},{10,11... | collective-permute-start | bytes 6291464 | tf_op jit(solution)/shard_map/ppermute | solution.py:50
  454.1 52.3 %all-to-all-start.5 = ((f32[8,1,128]{2,1,0:T(1,128)}), f32[8,1,128]{2,1,0:T(1,128)S(1)}, u32[]{:S(2)}, u32[]{:S(2)}) async-start(f32[8,1,128]{2,1,0:T(1,128)} %bitcast.91), calls=%async_computation.11 | async-start | bytes 8192 | tf_op jit(solution)/shard_map/all_to_all | solution.py:328
  457.8 219.9 %reduce-scatter.13.cloned.1.call-start = ((), (), s32[]{:S(2)}) async-start(), calls=%async_computation.18 | async-start | bytes 2621440 | tf_op jit(solution)/shard_map/reduce_scatter | solution.py:407
  463.6 48.6 %collective-permute-start.43 = (bf16[2,128,2048]{2,1,0:T(8,128)(2,1)}, bf16[2,128,2048]{2,1,0:T(8,128)(2,1)}, u32[]{:S(2)}, u32[]{:S(2)}) collective-permute-start(bf16[2,128,2048]{2,1,0:T(8,128)(2,1)} %slice.470), channel_id=1, source_target_pairs={{0,4},{1,3},{2,6},{3,1},{4,0},{5,7},{6,2},{7,5},{8,12},{9,11},{10,... | collective-permute-start | bytes 3145736 | tf_op jit(solution)/shard_map/ppermute | solution.py:50
  475.3 56.7 %collective-permute-start.61 = (bf16[4,176,2048]{2,1,0:T(8,128)(2,1)}, bf16[4,176,2048]{2,1,0:T(8,128)(2,1)}, u32[]{:S(2)}, u32[]{:S(2)}) collective-permute-start(bf16[4,176,2048]{2,1,0:T(8,128)(2,1)} %bitcast.86), channel_id=1, source_target_pairs={{0,1},{1,0},{2,3},{3,2},{4,5},{5,4},{6,7},{7,6},{8,9},{9,8},{10,11... | collective-permute-start | bytes 8650760 | tf_op jit(solution)/shard_map/ppermute | solution.py:50
  500.4 73.7 %collective-permute-start.58 = (bf16[4,2,176,2048]{3,2,1,0:T(8,128)(2,1)}, bf16[4,2,176,2048]{3,2,1,0:T(8,128)(2,1)}, u32[]{:S(2)}, u32[]{:S(2)}) collective-permute-start(bf16[4,2,176,2048]{3,2,1,0:T(8,128)(2,1)} %slice.461), channel_id=1, source_target_pairs={{0,1},{1,0},{2,3},{3,2},{4,5},{5,4},{6,7},{7,6},{8,9},{9,8},{10,11... | collective-permute-start | bytes 17301512 | tf_op jit(solution)/shard_map/ppermute | solution.py:50
  511.1 20.5 %collective-permute-start.53 = (bf16[2,128,2048]{2,1,0:T(8,128)(2,1)S(1)}, bf16[2,128,2048]{2,1,0:T(8,128)(2,1)S(1)}, u32[]{:S(2)}, u32[]{:S(2)}) collective-permute-start(bf16[2,128,2048]{2,1,0:T(8,128)(2,1)S(1)} %slice.469), channel_id=1, source_target_pairs={{0,4},{1,3},{2,6},{3,1},{4,0},{5,7},{6,2},{7,5},{8,12},{9,11},{10,... | collective-permute-start | bytes 3145736 | tf_op jit(solution)/shard_map/ppermute | solution.py:50
  515.7 27.5 %collective-permute-start.44 = (bf16[128,2048]{1,0:T(8,128)(2,1)}, bf16[128,2048]{1,0:T(8,128)(2,1)}, u32[]{:S(2)}, u32[]{:S(2)}) collective-permute-start(bf16[128,2048]{1,0:T(8,128)(2,1)} %fusion.57), channel_id=1, source_target_pairs={{0,2},{1,5},{2,0},{3,7},{4,6},{5,1},{6,4},{7,3},{8,10},{9,13},{10,... | collective-permute-start | bytes 1572872 | tf_op jit(solution)/shard_map/ppermute | solution.py:50
  539.7 30.6 %collective-permute-start.62 = (bf16[2,176,2048]{2,1,0:T(8,128)(2,1)}, bf16[2,176,2048]{2,1,0:T(8,128)(2,1)}, u32[]{:S(2)}, u32[]{:S(2)}) collective-permute-start(bf16[2,176,2048]{2,1,0:T(8,128)(2,1)} %slice.467), channel_id=1, source_target_pairs={{0,4},{1,3},{2,6},{3,1},{4,0},{5,7},{6,2},{7,5},{8,12},{9,11},{10,... | collective-permute-start | bytes 4325384 | tf_op jit(solution)/shard_map/ppermute | solution.py:50
  541.5 212.2 %collective-permute-start.54 = (bf16[128,2048]{1,0:T(8,128)(2,1)}, bf16[128,2048]{1,0:T(8,128)(2,1)}, u32[]{:S(2)}, u32[]{:S(2)}) collective-permute-start(bf16[128,2048]{1,0:T(8,128)(2,1)} %fusion.58), channel_id=1, source_target_pairs={{0,2},{1,5},{2,0},{3,7},{4,6},{5,1},{6,4},{7,3},{8,10},{9,13},{10,... | collective-permute-start | bytes 1572872 | tf_op jit(solution)/shard_map/ppermute | solution.py:50
  549.5 23.6 %collective-permute-start.45 = (bf16[128,2048]{1,0:T(8,128)(2,1)}, bf16[128,2048]{1,0:T(8,128)(2,1)}, u32[]{:S(2)}, u32[]{:S(2)}) collective-permute-start(bf16[128,2048]{1,0:T(8,128)(2,1)} %get-tuple-element.110), channel_id=1, source_target_pairs={{0,2},{1,5},{2,0},{3,7},{4,6},{5,1},{6,4},{7,3},{8,10},{9,13},{10,... | collective-permute-start | bytes 1572872 | tf_op jit(solution)/shard_map/ppermute | solution.py:50
  572.1 22.2 %collective-permute-start.46 = (bf16[128,2048]{1,0:T(8,128)(2,1)}, bf16[128,2048]{1,0:T(8,128)(2,1)}, u32[]{:S(2)}, u32[]{:S(2)}) collective-permute-start(bf16[128,2048]{1,0:T(8,128)(2,1)} %get-tuple-element.110), channel_id=1, source_target_pairs={{0,4},{1,3},{2,6},{3,1},{4,0},{5,7},{6,2},{7,5},{8,12},{9,11},{10,... | collective-permute-start | bytes 1572872 | tf_op jit(solution)/shard_map/ppermute | solution.py:50
  573.1 22.9 %collective-permute-start.47 = (bf16[128,2048]{1,0:T(8,128)(2,1)}, bf16[128,2048]{1,0:T(8,128)(2,1)}, u32[]{:S(2)}, u32[]{:S(2)}) collective-permute-start(bf16[128,2048]{1,0:T(8,128)(2,1)} %collective-permute-done.45), channel_id=1, source_target_pairs={{0,4},{1,3},{2,6},{3,1},{4,0},{5,7},{6,2},{7,5},{8,12},{9,11},{10,... | collective-permute-start | bytes 1572872 | tf_op jit(solution)/shard_map/ppermute | solution.py:50
  592.3 87.2 %collective-permute-start.59 = (bf16[2,2,176,2048]{3,2,1,0:T(8,128)(2,1)}, bf16[2,2,176,2048]{3,2,1,0:T(8,128)(2,1)}, u32[]{:S(2)}, u32[]{:S(2)}) collective-permute-start(bf16[2,2,176,2048]{3,2,1,0:T(8,128)(2,1)} %slice.463), channel_id=1, source_target_pairs={{0,4},{1,3},{2,6},{3,1},{4,0},{5,7},{6,2},{7,5},{8,12},{9,11},{10,... | collective-permute-start | bytes 8650760 | tf_op jit(solution)/shard_map/ppermute | solution.py:50
  623.3 116.0 %reduce-scatter.15.cloned.1.call-start = ((), (), s32[]{:S(2)}) async-start(), calls=%async_computation.19 | async-start | bytes 3932160 | tf_op jit(solution)/shard_map/reduce_scatter | solution.py:410
  668.4 22.0 %collective-permute-start.55 = (bf16[4,128,2048]{2,1,0:T(8,128)(2,1)}, bf16[4,128,2048]{2,1,0:T(8,128)(2,1)}, u32[]{:S(2)}, u32[]{:S(2)}) collective-permute-start(bf16[4,128,2048]{2,1,0:T(8,128)(2,1)} %bitcast.71), channel_id=1, source_target_pairs={{0,1},{1,0},{2,3},{3,2},{4,5},{5,4},{6,7},{7,6},{8,9},{9,8},{10,11... | collective-permute-start | bytes 6291464 | tf_op jit(solution)/shard_map/ppermute | solution.py:50
  677.8 11.4 %collective-permute-start.63 = (bf16[176,2048]{1,0:T(8,128)(2,1)S(1)}, bf16[176,2048]{1,0:T(8,128)(2,1)S(1)}, u32[]{:S(2)}, u32[]{:S(2)}) collective-permute-start(bf16[176,2048]{1,0:T(8,128)(2,1)S(1)} %fusion.56), channel_id=1, source_target_pairs={{0,2},{1,5},{2,0},{3,7},{4,6},{5,1},{6,4},{7,3},{8,10},{9,13},{10,... | collective-permute-start | bytes 2162696 | tf_op jit(solution)/shard_map/ppermute | solution.py:50
  684.4 25.9 %collective-permute-start.60 = (bf16[2,176,2048]{2,1,0:T(8,128)(2,1)S(1)}, bf16[2,176,2048]{2,1,0:T(8,128)(2,1)S(1)}, u32[]{:S(2)}, u32[]{:S(2)}) collective-permute-start(bf16[2,176,2048]{2,1,0:T(8,128)(2,1)S(1)} %fusion.25), channel_id=1, source_target_pairs={{0,2},{1,5},{2,0},{3,7},{4,6},{5,1},{6,4},{7,3},{8,10},{9,13},{10,... | collective-permute-start | bytes 4325384 | tf_op jit(solution)/shard_map/ppermute | solution.py:50
  696.3 19.1 %collective-permute-start.56 = (bf16[2,128,2048]{2,1,0:T(8,128)(2,1)}, bf16[2,128,2048]{2,1,0:T(8,128)(2,1)}, u32[]{:S(2)}, u32[]{:S(2)}) collective-permute-start(bf16[2,128,2048]{2,1,0:T(8,128)(2,1)} %slice.468), channel_id=1, source_target_pairs={{0,4},{1,3},{2,6},{3,1},{4,0},{5,7},{6,2},{7,5},{8,12},{9,11},{10,... | collective-permute-start | bytes 3145736 | tf_op jit(solution)/shard_map/ppermute | solution.py:50
  718.4 11.0 %collective-permute-start.57 = (bf16[128,2048]{1,0:T(8,128)(2,1)}, bf16[128,2048]{1,0:T(8,128)(2,1)}, u32[]{:S(2)}, u32[]{:S(2)}) collective-permute-start(bf16[128,2048]{1,0:T(8,128)(2,1)} %fusion.59), channel_id=1, source_target_pairs={{0,2},{1,5},{2,0},{3,7},{4,6},{5,1},{6,4},{7,3},{8,10},{9,13},{10,... | collective-permute-start | bytes 1572872 | tf_op jit(solution)/shard_map/ppermute | solution.py:50
  731.7 12.3 %all-to-all-start.2 = ((f32[32,3,128]{2,1,0:T(4,128)}), f32[32,3,128]{2,1,0:T(4,128)S(1)}, u32[]{:S(2)}, u32[]{:S(2)}) async-start(f32[32,3,128]{2,1,0:T(4,128)} %reshape.703), calls=%async_computation.6 | async-start | bytes 131072 | tf_op jit(solution)/shard_map/all_to_all | solution.py:441
  736.6 32.1 %reduce-scatter.17.cloned.1.call-start = ((), (), s32[]{:S(2)}) async-start(), calls=%async_computation.20 | async-start | bytes 1310720 | tf_op jit(solution)/shard_map/reduce_scatter | solution.py:412
  745.3 16.1 %all-to-all-start.4 = ((bf16[8,64,768]{2,1,0:T(8,128)(2,1)}), bf16[8,64,768]{2,1,0:T(8,128)(2,1)S(1)}, u32[]{:S(2)}, u32[]{:S(2)}) async-start(bf16[8,64,768]{2,1,0:T(8,128)(2,1)} %bitcast.298), calls=%async_computation.9 | async-start | bytes 1572864 | tf_op jit(solution)/shard_map/all_to_all | solution.py:414
  (116 other events, 1021.2 us)
Sparse Core Ops, SparseCore 0:
  9.7 30.6 all-gather.11
  42.5 68.4 all-gather.5
  126.3 47.1 all-gather.7
  210.8 44.6 all-gather.9
  278.0 101.3 reduce-scatter.6
  382.1 44.3 reduce-scatter.8
  429.0 194.2 reduce-scatter.10
  625.7 44.8 reduce-scatter.12
  677.8 61.4 reduce-scatter.14
  741.5 27.1 reduce-scatter.16

commit v3 on v2

v3 whole, which is shorter than its diff:
```python
import functools
import math

import jax
import jax.numpy as jnp
import numpy as np
from jax import lax
from jax.experimental import pallas as pl
from jax.experimental.pallas import tpu as pltpu
from jax.sharding import PartitionSpec as P

HEAD = 128
NORM_EPS = 1e-06
THETA = 1000000.0
F32 = jnp.float32
barrier = lax.optimization_barrier
BF16 = jnp.bfloat16


def dot(a, b, dims):
    return lax.dot_general(a, b, (dims, ((), ())), preferred_element_type=F32)


def mm(a, b):
    return dot(a, b, ((1,), (0,)))


def mm_nt(a, b):
    return dot(a, b, ((1,), (1,)))


def mm_tn(a, b):
    return dot(a, b, ((0,), (0,)))


def plane_order(size, me):
    if size == 8:
        even, odd = [0, 2, 4, 6, 1, 5, 3, 7], [0, 4, 2, 6, 1, 3, 5, 7]
        first = me % 2 == 0
        return [me ^ (a if a == b else jnp.where(first, a, b)) for a, b in zip(even, odd)]
    return [me ^ m for m in range(size)]


def first_hop(i):
    return i ^ 2 if i % 2 == 0 else i ^ 4


def second_hop(i):
    return i ^ 4 if i % 2 == 0 else i ^ 2


def send(block, size, target):
    return lax.ppermute(block, "expert", [(i, target(i)) for i in range(size)])


def core_swap(i):
    return i ^ 1


def gather_first(block, size):
    if size == 8:
        return [block, send(block, size, first_hop), send(block, size, second_hop)]
    return [block] + [send(block, size, lambda i, m=m: i ^ m) for m in range(1, size)]


def gather_second(parts, size):
    return parts + [send(parts[1], size, second_hop)] if size == 8 else parts


def gather_third(parts, size):
    return parts + [send(part, size, core_swap) for part in parts] if size == 8 else parts


def plane_gather(block, size):
    return gather_third(gather_second(gather_first(block, size), size), size)


def plane_place(parts, order, whole, place):
    for j, part in enumerate(parts):
        whole = place(whole, part, order[j])
    return whole


def plane_rows(parts, order):
    rows = parts[0].shape[0]
    whole = jnp.zeros((len(parts) * rows,) + parts[0].shape[1:], parts[0].dtype)
    return plane_place(
        parts,
        order,
        whole,
        lambda whole, part, source: lax.dynamic_update_slice_in_dim(whole, part, source * rows, 0),
    )


def sum_first(near, far, size):
    if size == 8:
        return near.astype(F32) + send(far.astype(BF16), size, core_swap).astype(F32)
    parts = jnp.concatenate([near.astype(BF16), far.astype(BF16)], axis=0)
    parts = parts.reshape((size, parts.shape[0] // size) + parts.shape[1:])
    total = parts[0].astype(F32)
    for m in range(1, size):
        total = total + send(parts[m], size, lambda i, m=m: i ^ m).astype(F32)
    return total


def sum_hop(near, size, hop):
    if size != 8:
        return near
    half = near.shape[0] // 2
    return near[:half] + send(near[half:].astype(BF16), size, hop).astype(F32)


def plane_sum(near, far, size):
    near = sum_hop(sum_first(near, far, size), size, second_hop)
    return sum_hop(near, size, first_hop)


def norm_scale(rows):
    return lax.rsqrt(jnp.mean(rows * rows, axis=-1, keepdims=True) + NORM_EPS)


def norm_back(rows, scale, gain, grad):
    unit = rows * scale
    weighted = grad * gain
    inner = jnp.mean(weighted * unit, axis=-1, keepdims=True)
    return scale * (weighted - unit * inner), jnp.sum(grad * unit, axis=0)


def swiglu_parts(gate, up):
    sig = jax.nn.sigmoid(gate)
    return sig, gate * sig * up


def swiglu_back(gate, up, grad):
    sig = jax.nn.sigmoid(gate)
    silu = gate * sig
    return grad * up * (sig + silu * (1.0 - sig)), grad * silu


def rotary_tables(row_count):
    half = HEAD // 2
    powers = -(np.arange(half, dtype=np.float32) * np.float32(2.0)) / np.float32(HEAD)
    freqs = np.power(np.float32(THETA), powers).astype(np.float32)
    angles = np.arange(row_count, dtype=np.float32)[:, None] * freqs[None, :]
    cos, sin = np.cos(angles), np.sin(angles)
    return np.concatenate([cos, cos], axis=1), np.concatenate([-sin, sin], axis=1)


def head_probs(query, key, scale):
    scores = mm_nt(query, key) * scale
    shape = scores.shape
    causal = lax.broadcasted_iota(jnp.int32, shape, 0) >= lax.broadcasted_iota(jnp.int32, shape, 1)
    scores = jnp.where(causal, scores, -1e30)
    raised = jnp.exp(scores - jnp.max(scores, axis=-1, keepdims=True))
    return raised / jnp.sum(raised, axis=-1, keepdims=True)


def attend_kernel(
    heads, seq, tokens, gain, weight, bias, cos, sin, normed_out, qkv_out, mixed_out, lin
):
    rows = tokens[...].astype(F32)
    normed_out[...] = (rows * norm_scale(rows) * gain[...]).astype(BF16)
    lin[...] = mm(normed_out[...], weight[...]) + bias[...]
    for s in range(tokens.shape[0] // seq):
        row = slice(s * seq, (s + 1) * seq)
        for h in range(heads):
            low = []
            for kind in range(3):
                at = (kind * heads + h) * HEAD
                part = lin[row, at : at + HEAD]
                if kind < 2:
                    part = part * cos[...] + pltpu.roll(part, HEAD // 2, 1) * sin[...]
                low.append(part.astype(BF16))
                qkv_out[row, at : at + HEAD] = low[-1]
            probs = head_probs(low[0], low[1], 1.0 / math.sqrt(HEAD))
            mixed_out[row, h * HEAD : (h + 1) * HEAD] = mm(probs.astype(BF16), low[2]).astype(BF16)


def attend(tokens, gain, weight, bias, seq):
    total, width = tokens.shape
    wide = weight.shape[1]
    heads = wide // (3 * HEAD)
    rows = 4 * seq
    cos, sin = rotary_tables(seq)

    def whole(shape):
        return pl.BlockSpec(shape, lambda i: (0, 0))

    def block(columns):
        return pl.BlockSpec((rows, columns), lambda i: (i, 0))

    return pl.pallas_call(
        functools.partial(attend_kernel, heads, seq),
        grid=(total // rows,),
        in_specs=[
            block(width),
            whole((1, width)),
            whole((width, wide)),
            whole((1, wide)),
            whole((seq, HEAD)),
            whole((seq, HEAD)),
        ],
        out_specs=[block(width), block(wide), block(heads * HEAD)],
        out_shape=[
            jax.ShapeDtypeStruct((total, width), BF16),
            jax.ShapeDtypeStruct((total, wide), BF16),
            jax.ShapeDtypeStruct((total, heads * HEAD), BF16),
        ],
        scratch_shapes=[pltpu.VMEM((rows, wide), F32)],
        compiler_params=pltpu.CompilerParams(vmem_limit_bytes=48 << 20),
        name="attend",
    )(tokens, gain[None], weight, bias[None], jnp.asarray(cos), jnp.asarray(sin))


def attend_back_kernel(heads, size, order, *refs):
    parts, refs = refs[:size], refs[size:]
    qkv, mixed, out_own, weight, cos, sin = refs[:6]
    normed_grad, qkv_grad, out_grad, bias_grad, branch, mixed_grad, near_mixed, near_grad = refs[6:]
    seq = parts[0].shape[0]
    scale = 1.0 / math.sqrt(HEAD)
    for j, part in enumerate(parts):
        branch[j * seq : (j + 1) * seq, :] = part[...]
    mixed_grad[...] = mm_nt(branch[...], out_own[...]).astype(BF16)

    def one(j, carry):
        near = pl.ds(pl.multiple_of(j * seq, seq), seq)
        far = pl.ds(pl.multiple_of(order[j] * seq, seq), seq)
        near_mixed[near, :] = mixed[far, :]
        for h in range(heads):
            at = [(kind * heads + h) * HEAD for kind in range(3)]
            query, key, value = [qkv[far, a : a + HEAD] for a in at]
            grad = mixed_grad[near, h * HEAD : (h + 1) * HEAD]
            probs = head_probs(query, key, scale)
            value_grad = mm_tn(probs.astype(BF16), grad)
            probs_grad = mm_nt(grad, value)
            score_grad = probs * (probs_grad - jnp.sum(probs_grad * probs, axis=-1, keepdims=True))
            score_grad = score_grad.astype(BF16)
            turned = [mm(score_grad, key) * scale, mm_tn(score_grad, query) * scale]
            turned = [g * cos[...] - pltpu.roll(g, HEAD // 2, 1) * sin[...] for g in turned]
            for a, g in zip(at, turned + [value_grad]):
                low = g.astype(BF16)
                near_grad[near, a : a + HEAD] = low
                qkv_grad[far, a : a + HEAD] = low
        return carry

    lax.fori_loop(0, size, one, 0)
    normed_grad[...] = mm_nt(near_grad[...], weight[...]).astype(BF16)
    bias_grad[...] = jnp.sum(near_grad[...].astype(F32), axis=0, keepdims=True)
    out_grad[...] = mm_tn(near_mixed[...], branch[...]).astype(BF16)


def attend_back(order, parts, qkv, mixed, out_own, weight):
    size = len(parts)
    seq, width = parts[0].shape
    wide = weight.shape[1]
    own = wide // 3
    cos, sin = rotary_tables(seq)

    def whole(shape):
        return pl.BlockSpec(shape, lambda i, order: (0, 0))

    inputs = list(parts) + [qkv, mixed, out_own, weight, jnp.asarray(cos), jnp.asarray(sin)]
    shapes = [
        jax.ShapeDtypeStruct((size * seq, width), BF16),
        jax.ShapeDtypeStruct((size * seq, wide), BF16),
        jax.ShapeDtypeStruct((own, width), BF16),
        jax.ShapeDtypeStruct((1, wide), F32),
    ]
    return pl.pallas_call(
        functools.partial(attend_back_kernel, own // HEAD, size),
        grid_spec=pltpu.PrefetchScalarGridSpec(
            num_scalar_prefetch=1,
            grid=(1,),
            in_specs=[whole(a.shape) for a in inputs],
            out_specs=[whole(a.shape) for a in shapes],
            scratch_shapes=[
                pltpu.VMEM((size * seq, width), BF16),
                pltpu.VMEM((size * seq, own), BF16),
                pltpu.VMEM((size * seq, own), BF16),
                pltpu.VMEM((size * seq, wide), BF16),
            ],
        ),
        out_shape=shapes,
        compiler_params=pltpu.CompilerParams(vmem_limit_bytes=60 << 20),
        name="attend_back",
    )(order, *inputs)


def shards(
    tokens,
    lengths,
    routes,
    gate_values,
    cotangent,
    norm1_gain,
    qkv_weight,
    qkv_bias,
    out_weight,
    norm2_gain,
    shared_in,
    shared_out,
    shared_gate,
    expert_in,
    expert_out,
):
    rows, width = tokens.shape
    top = routes.shape[1]
    group = lax.axis_size("expert")
    planes = lax.axis_size("dp")
    devices = group * planes
    both = ("dp", "expert")
    me = lax.axis_index("expert")
    plane = lax.axis_index("dp")
    heads = width // HEAD
    own_heads = heads // group
    shard = qkv_weight.shape[0]
    split = HEAD // shard
    lanes = group // split
    experts = group * expert_in.shape[0]
    valid_total = 23 * rows * devices // 32
    capacity = 5 * valid_total * top // (4 * experts * planes)
    slots = -(-capacity // 16) * 16
    order = plane_order(group, me)
    order_list = jnp.stack(order)
    group_rows = group * rows

    vectors = jnp.concatenate([norm1_gain, norm2_gain, shared_gate, qkv_bias]).astype(F32)
    vector_rows = -(-vectors.shape[0] // 128)
    vectors = jnp.pad(vectors, (0, vector_rows * 128 - vectors.shape[0])).reshape(vector_rows, 128)
    info = jnp.concatenate(
        [
            vectors,
            routes.T.astype(F32),
            gate_values.T,
            jnp.broadcast_to(lengths.astype(F32)[:, None], (1, rows)),
        ],
        axis=0,
    )
    lane, part = me // split, me % split
    out_parts = lax.all_gather(out_weight[None], "dp", axis=0, tiled=True)
    by_head = qkv_weight.reshape(shard, 3, split, own_heads, lanes, HEAD)
    by_head = by_head.transpose(4, 2, 0, 1, 3, 5).reshape(group, shard, 3 * own_heads * HEAD)
    by_head = lax.all_to_all(by_head, "expert", 0, 0, tiled=True)
    by_head, token_source, cot_source = barrier((by_head, tokens, cotangent))
    out_parts, info = barrier((out_parts, info))
    qkv_own = lax.all_gather(by_head, "dp", axis=0, tiled=True).reshape(width, 3 * own_heads * HEAD)

    told = lax.all_to_all(
        jnp.broadcast_to(info[None], (devices,) + info.shape), both, 0, 0, tiled=True
    )
    flat = told[:, :vector_rows].reshape(devices, vector_rows * 128)
    norm1_full = flat[:, :shard].reshape(width)
    norm2_full = flat[:, shard : 2 * shard].reshape(width)
    gate_full = flat[:, 2 * shard : 3 * shard].reshape(width)
    bias_full = flat[:, 3 * shard : 3 * shard + qkv_bias.shape[0]].reshape(
        3, split, own_heads, lanes, HEAD
    )
    rest = told[:, vector_rows:].reshape(planes, group, 2 * top + 1, rows)
    column = lax.dynamic_index_in_dim(rest, me, 1, keepdims=False)
    slot = jnp.arange(rows, dtype=F32)
    all_routes = rest[:, :, :top].astype(jnp.int32)
    all_gates = rest[:, :, top : 2 * top]
    all_valid = slot < rest[:, :, 2 * top]
    column_valid = (slot[None, :] < column[:, 2 * top]).astype(F32).reshape(planes * rows, 1)
    valid_float = (slot < lengths.astype(F32)[0]).astype(F32)[:, None]

    bias_own = lax.dynamic_index_in_dim(bias_full, part, 1, keepdims=False)
    bias_own = lax.dynamic_index_in_dim(bias_own, lane, 2, keepdims=False).reshape(-1)
    pairs = [[k * split + p for p in range(split)] for k in range(lanes)]
    out_seen = gather_second(
        gather_first(out_parts.reshape(split, own_heads, shard, width), group), group
    )
    cot_seen = gather_second(gather_first(cot_source, group), group)
    group_tokens = plane_rows(plane_gather(token_source, group), order)
    group_tokens, unit_in = barrier((group_tokens, shared_in.transpose(1, 2, 0)))
    unit_in = gather_first(unit_in, group)
    qkv_own, column_source = barrier((qkv_own, cotangent))
    column_cot = lax.all_gather(column_source, "dp", axis=0, tiled=True)

    own_width = own_heads * HEAD
    positions = jnp.arange(rows, dtype=jnp.int32)
    places = jnp.arange(group, dtype=jnp.int32)
    normed1, qkv, mixed = attend(group_tokens, norm1_full, qkv_own, bias_own, rows)
    mixed, unit_in, out_seen = barrier((mixed, unit_in, out_seen))
    mixed_parts = gather_first(mixed, group)
    out_whole = plane_place(
        gather_third(out_seen, group),
        order,
        jnp.zeros((lanes, split, own_heads, split, shard, width), BF16),
        lambda whole, block, source: lax.dynamic_update_slice(
            whole, block[None, :, :, None], (source // split, 0, 0, source % split, 0, 0)
        ),
    ).reshape(width, width)

    mixed_parts, column_cot, cot_seen = barrier((mixed_parts, column_cot, cot_seen))
    mixed_parts = gather_third(gather_second(mixed_parts, group), group)
    group_cot = plane_rows(gather_third(cot_seen, group), order)
    mixed_whole = plane_place(
        mixed_parts,
        order,
        jnp.zeros((group_rows, width), BF16),
        lambda whole, block, source: lax.dynamic_update_slice(whole, block, (0, source * own_width)),
    )
    mixed_whole, unit_out = barrier((mixed_whole, shared_out))
    unit_out = gather_first(unit_out, group)
    group_hidden = group_tokens.astype(F32) + mm(mixed_whole, out_whole)
    group_scale2 = norm_scale(group_hidden)
    group_normed = (group_hidden * group_scale2 * norm2_full).astype(BF16)
    hidden = lax.dynamic_slice_in_dim(group_hidden, me * rows, rows, 0)
    scale2 = lax.dynamic_slice_in_dim(group_scale2, me * rows, rows, 0)
    normed2 = lax.dynamic_slice_in_dim(group_normed, me * rows, rows, 0)
    column_normed = lax.all_gather(normed2, "dp", axis=0, tiled=True)

    named = all_routes == me
    taken = jnp.any(named, axis=2) & all_valid
    gate_here = jnp.sum(jnp.where(named, all_gates, 0.0), axis=2)
    before = (positions[:, None] < positions[None, :]).astype(BF16)
    inside = mm(taken.astype(BF16).reshape(devices, rows), before).reshape(planes, group, rows)
    counts = jnp.sum(taken.astype(F32), axis=2)
    ahead = places[None, :] < places[:, None]
    offsets = jnp.sum(jnp.where(ahead[None], counts[:, None, :], 0.0), axis=2)
    all_rank = (inside + offsets[:, :, None]).astype(jnp.int32)
    all_rank = jnp.where(taken & (all_rank < capacity), all_rank, -1)
    rank = lax.dynamic_index_in_dim(all_rank, plane, 0, keepdims=False)
    gate_own = lax.dynamic_index_in_dim(gate_here, plane, 0, keepdims=False)
    slot_ids = jnp.arange(slots, dtype=jnp.int32)[:, None]
    chosen = rank.reshape(1, group_rows) == slot_ids
    pick = chosen.astype(BF16)
    put = (jnp.take(rank, order_list, axis=0).reshape(1, group_rows) == slot_ids).astype(BF16)
    put_near, put_far = put[:, : group_rows // 2], put[:, group_rows // 2 :]
    row_gate = jnp.sum(
        jnp.where(chosen, gate_own.reshape(1, group_rows), 0.0), axis=1, keepdims=True
    )
    weight_in, weight_out = expert_in[0], expert_out[0]
    hidden_units = weight_out.shape[0]
    expert_rows = mm(pick, group_normed).astype(BF16)
    expert_rows, unit_in, unit_out = barrier((expert_rows, unit_in, unit_out))
    unit_in, unit_out = gather_second(unit_in, group), gather_second(unit_out, group)
    cot_rows = mm(pick, group_cot)
    val_grad = (cot_rows * row_gate).astype(BF16)
    expert_pre = mm(expert_rows, weight_in)
    e_gate, e_up = expert_pre[:, :hidden_units], expert_pre[:, hidden_units:]
    expert_act = swiglu_parts(e_gate, e_up)[1].astype(BF16)
    act_grad = mm_nt(val_grad, weight_out)
    part_units = hidden_units // planes
    gated_act = (expert_act.astype(F32) * row_gate).astype(BF16)
    gated_act = gated_act.reshape(slots, planes, part_units).transpose(1, 0, 2)
    gated_act = lax.all_to_all(gated_act, "dp", 0, 0, tiled=True)
    pre_grad = jnp.concatenate(swiglu_back(e_gate, e_up, act_grad), axis=1).astype(BF16)
    in_gate = mm_tn(expert_rows, pre_grad[:, :hidden_units]).astype(BF16)
    in_gate, pre_grad, unit_in, unit_out = barrier((in_gate, pre_grad, unit_in, unit_out))
    unit_in = jnp.concatenate(gather_third(unit_in, group), axis=1)
    unit_out = jnp.concatenate(gather_third(unit_out, group), axis=0)
    in_up = mm_tn(expert_rows, pre_grad[:, hidden_units:]).astype(BF16)
    row_grad = mm_nt(pre_grad, weight_in).astype(BF16)
    expert_val = mm(expert_act, weight_out)
    pair_dot = jnp.sum(cot_rows * expert_val, axis=1, keepdims=True)
    gated_val = (expert_val * row_gate).astype(BF16)
    grad_far = mm_tn(put_far, row_grad).astype(BF16)
    grad_near = mm_tn(put_near, row_grad).astype(BF16)
    routed_grad = plane_sum(grad_near, grad_far, group)
    units = shared_out.shape[0]
    in_gate_grad = lax.psum_scatter(in_gate, "dp", scatter_dimension=0, tiled=True)
    column_normed, in_up = barrier((column_normed, in_up))
    cot_parts, unit_out = barrier((column_cot, unit_out))
    cot_parts = gather_first(cot_parts, group)
    plane_units = group * units
    shared_weight = jax.nn.sigmoid(
        jnp.sum(column_normed.astype(F32) * gate_full, axis=1, keepdims=True)
    )
    unit_flat = unit_in.reshape(2 * plane_units, width)
    shared_pre = mm_nt(column_normed, unit_flat)
    s_gate, s_up = shared_pre[:, :plane_units], shared_pre[:, plane_units:]
    shared_act = swiglu_parts(s_gate, s_up)[1].astype(BF16)
    shared_val = mm(shared_act, unit_out)
    column_grad = column_cot.astype(F32) * column_valid
    shared_val_grad = (column_grad * shared_weight).astype(BF16)
    logit_grad = jnp.sum(column_grad * shared_val, axis=1, keepdims=True)
    logit_grad = logit_grad * shared_weight * (1.0 - shared_weight)
    gate_grad = jnp.sum(logit_grad * column_normed.astype(F32), axis=0)
    shared_act_grad = mm_nt(shared_val_grad, unit_out)
    shared_pre_grad = jnp.concatenate(swiglu_back(s_gate, s_up, shared_act_grad), axis=1)
    shared_pre_grad = shared_pre_grad.astype(BF16)
    shared_pre_grad, cot_parts = barrier((shared_pre_grad, cot_parts))
    cot_parts = gather_second(cot_parts, group)
    normed_term = mm(shared_pre_grad, unit_flat) + logit_grad * gate_full
    normed_term, in_gate_grad, cot_parts, routed_grad, gated_act = barrier(
        (normed_term.astype(BF16), in_gate_grad, cot_parts, routed_grad, gated_act)
    )
    shared_grad = lax.psum_scatter(normed_term, "dp", scatter_dimension=0, tiled=True)
    cot_parts = gather_third(cot_parts, group)
    half_units = plane_units // 2
    unit_grads = []
    for left, right in (
        (shared_act, shared_val_grad),
        (shared_pre_grad[:, :plane_units], column_normed),
        (shared_pre_grad[:, plane_units:], column_normed),
    ):
        far = mm_tn(left[:, half_units:], right).astype(BF16)
        unit_grads.append((mm_tn(left[:, :half_units], right).astype(BF16), far))
    shared_grad, in_up, unit_grads, gated_val, pair_dot = barrier(
        (shared_grad, in_up, unit_grads, gated_val, pair_dot)
    )
    shared_grad = shared_grad.astype(F32)
    in_up_grad = lax.psum_scatter(in_up, "dp", scatter_dimension=0, tiled=True)
    normed2_grad = shared_grad + routed_grad
    norm_term, norm2_part = norm_back(hidden, scale2, norm2_full, normed2_grad)
    hidden_grad = cotangent.astype(F32) * valid_float + norm_term
    branch_parts = gather_first(hidden_grad.astype(BF16), group)
    unit_grads = [sum_first(near, far, group) for near, far in unit_grads]
    branch_parts, unit_grads = barrier((gather_second(branch_parts, group), unit_grads))
    branch_parts = gather_third(branch_parts, group)
    unit_grads = [sum_hop(total, group, second_hop) for total in unit_grads]

    out_own = lax.dynamic_slice_in_dim(out_whole, me * own_width, own_width, 0)
    normed1_grad, qkv_grad, out_own_grad, bias_part = attend_back(
        order_list, branch_parts, qkv, mixed, out_own, qkv_own
    )
    out_own_grad = out_own_grad.reshape(own_heads, split, shard, width).transpose(1, 0, 2, 3)
    out_own_grad = lax.all_to_all(
        out_own_grad, "expert", 0, 0, axis_index_groups=pairs, tiled=True
    ).reshape(planes, shard, width)
    qkv_grad, unit_grads[0] = barrier((qkv_grad, unit_grads[0]))
    qkv_own_grad = mm_tn(normed1, qkv_grad).astype(BF16)

    flat_rows = group * shard * 3 * own_width // width
    shared_part = (shared_weight * shared_val).astype(BF16).reshape(planes, rows, width)
    joined = jnp.concatenate(
        [qkv_own_grad.reshape(planes, flat_rows, width), out_own_grad, shared_part], axis=1
    )
    (
        normed1_grad,
        bias_part,
        unit_grads,
        gated_val,
        pair_dot,
        gated_act,
    ) = barrier(
        (
            normed1_grad,
            bias_part.reshape(-1),
            unit_grads,
            gated_val,
            pair_dot,
            gated_act,
        )
    )
    joined = lax.psum_scatter(joined, "dp", scatter_dimension=0, tiled=True)[0]
    half_rows = group_rows // 2
    normed1_grad = plane_sum(normed1_grad[:half_rows], normed1_grad[half_rows:], group)
    expert_in_grad = jnp.concatenate([in_gate_grad, in_up_grad], axis=1)
    out_weight_grad = joined[flat_rows : flat_rows + shard]
    shared_sum = joined[flat_rows + shard :].astype(F32)
    qkv_own_grad = joined[:flat_rows]
    qkv_own_grad = lax.all_to_all(
        qkv_own_grad.reshape(group, shard, 3 * own_width), "expert", 0, 0, tiled=True
    )
    qkv_weight_grad = (
        qkv_own_grad.reshape(lanes, split, shard, 3, own_heads, HEAD)
        .transpose(2, 3, 1, 4, 0, 5)
        .reshape(shard, 3 * width)
        .astype(F32)
    )
    own_tokens = tokens.astype(F32)
    token_term, norm1_part = norm_back(own_tokens, norm_scale(own_tokens), norm1_full, normed1_grad)
    tokens_grad = hidden_grad + token_term

    value_far = mm_tn(put_far, gated_val).astype(BF16)
    value_near = mm_tn(put_near, gated_val).astype(BF16)
    routed_sum = plane_sum(value_near, value_far, group)
    pair_dots = jnp.sum(jnp.where(chosen, pair_dot, 0.0), axis=0).reshape(group, rows)
    pair_back = lax.all_to_all(pair_dots, "expert", 0, 0, tiled=True)
    gate_values_grad = jnp.sum(
        jnp.where(routes.T[None] == places[:, None, None], pair_back[:, None, :], 0.0), axis=0
    ).T

    unit_grads, gated_act = barrier((unit_grads, gated_act))
    all_pick = (all_rank.reshape(planes, 1, group_rows) == slot_ids[None]).astype(BF16)
    token_act = lax.dot_general(
        all_pick, gated_act, (((1,), (1,)), ((0,), (0,))), preferred_element_type=F32
    )
    token_act = token_act.astype(BF16).reshape(planes, group, rows, part_units)
    expert_out_grad = 0.0
    for source, cot_part in zip(order, cot_parts):
        act_part = lax.dynamic_index_in_dim(token_act, source, 1, keepdims=False)
        expert_out_grad = expert_out_grad + mm_tn(
            act_part.reshape(planes * rows, part_units), cot_part
        )

    unit_grads = [sum_hop(total, group, first_hop) for total in unit_grads]
    shared_out_grad, gate_part, up_part = unit_grads
    shared_in_grad = jnp.stack([gate_part, up_part]).transpose(2, 0, 1)

    here = (jnp.arange(split)[:, None] == part) & (jnp.arange(lanes)[None, :] == lane)
    bias_all = jnp.where(
        here[None, :, None, :, None], bias_part.reshape(3, 1, own_heads, 1, HEAD), 0.0
    ).reshape(devices, qkv_bias.shape[0])
    sums = jnp.concatenate(
        [
            norm1_part.reshape(devices, shard),
            norm2_part.reshape(devices, shard),
            gate_grad.reshape(devices, shard),
            bias_all,
        ],
        axis=1,
    )
    sums = jnp.pad(sums, ((0, 0), (0, vector_rows * 128 - sums.shape[1])))
    sums = lax.all_to_all(sums.reshape(devices, vector_rows, 128), both, 0, 0, tiled=True)
    sums, shared_out_grad, shared_in_grad, routed_sum = barrier(
        (sums, shared_out_grad, shared_in_grad, routed_sum)
    )
    sums = jnp.sum(sums, axis=0).reshape(-1)

    output = (valid_float * (hidden + shared_sum + routed_sum)).astype(BF16)
    return (
        output,
        tokens_grad,
        sums[:shard],
        qkv_weight_grad,
        sums[3 * shard : 3 * shard + qkv_bias.shape[0]],
        out_weight_grad.astype(F32),
        sums[shard : 2 * shard],
        shared_in_grad,
        shared_out_grad,
        sums[2 * shard : 3 * shard],
        expert_in_grad.astype(F32)[None],
        expert_out_grad.astype(F32)[None],
        gate_values_grad,
    )


def solution(mesh):
    both = ("dp", "expert")
    in_specs = (
        P(both, None),
        P(both),
        P(both, None),
        P(both, None),
        P(both, None),
        P(both),
        P(both, None),
        P(both),
        P(both, None),
        P(both),
        P(None, None, both),
        P(both, None),
        P(both),
        P("expert", None, None),
        P("expert", None, None),
    )
    out_specs = (
        P(both, None),
        P(both, None),
        P(both),
        P(both, None),
        P(both),
        P(both, None),
        P(both),
        P(None, None, both),
        P(both, None),
        P(both),
        P("expert", "dp", None),
        P("expert", "dp", None),
        P(both, None),
    )
    return jax.shard_map(shards, mesh=mesh, in_specs=in_specs, out_specs=out_specs, check_vma=False)
```

time: 787 us -> 675 us (0.86)
  waiting for transfers between devices: 256 us -> 172 us
  local copies, waits for them, and re-layouts: 182 us -> 127 us
  Pallas kernels: 0 us -> 34.3 us
  other arithmetic: 84.7 us -> 67.2 us
  starting transfers between devices: 73.1 us -> 83.7 us
    reduce_scatter x5 -> x3, waiting for transfers between devices: 60.8 us -> 0.01 us  [the longest x1 0.01 us: shards(): lax.psum_scatter(in_gate, 'dp', scatter_dimension=0, tiled=True)]
    reduce_scatter x1, waiting for transfers between devices: 47.1 us -> 10.8 us  [shards(): lax.psum_scatter(normed_term, 'dp', scatter_dimension=0, tiled=True)]
    pallas_call x0 -> x2, Pallas kernels: none -> 34.3 us  [the longest x1 22.2 us: attend_back(): pl.pallas_call(functools.partial(attend_back_kernel, own // HEAD, size),...]
    slice x19 -> x14, local copies, waits for them, and re-layouts: 36.8 us -> 16.1 us  [the longest x12 13.4 us: sum_hop(): return near[:half] + send(near[half:].astype(BF16), size, hop).astype(F32)]
    all_gather x1, waiting for transfers between devices: 0.01 us -> 19.1 us  [shards(): lax.all_gather(by_head, 'dp', axis=0, tiled=True)]
    another operation x10 -> x5, local copies, waits for them, and re-layouts: 16.5 us -> 4.41 us
    ppermute x64 -> x74, waiting for transfers between devices: 118 us -> 106 us  [send(): return lax.ppermute(block, 'expert', [(i, target(i)) for i in range(size)])]
    dot_general x23 -> x33, matrix products: 152 us -> 163 us  [dot(): return lax.dot_general(a, b, (dims, ((), ())), preferred_element_type=F32)]
  transfers between devices with their start and end apart: 80 -> 89, of which waited for: 26 -> 25; matrix products, arithmetic and copies ran while one was open for 51% -> 51% of each run, Pallas kernels for 0% -> 5%
where the time goes in v3:
time: 675 us; the launch traced here: 667 us
  waiting for transfers between devices  172 us (25%)
  matrix products  166 us (25%)
  local copies, waits for them, and re-layouts  127 us (19%)
  starting transfers between devices  83.7 us (12%)
  other arithmetic  67.2 us (10%)
  Pallas kernels  34.3 us (5%)
  between operations  17.4 us (3%)
    dot_general x33, matrix products, dot(): return lax.dot_general(a, b, (dims, ((), ())), preferred_element_type=F32)  163 us
    ppermute x74, waiting for transfers between devices, send(): return lax.ppermute(block, 'expert', [(i, target(i)) for i in range(size)])  106 us
    ppermute x74, starting transfers between devices, send(): return lax.ppermute(block, 'expert', [(i, target(i)) for i in range(size)])  53.2 us
    unnamed x191, local copies, waits for them, and re-layouts  46.1 us
    pallas_call x1, Pallas kernels, attend_back(): pl.pallas_call(functools.partial(attend_back_kernel, own // HEAD, size),...  22.2 us
    all_gather x1, waiting for transfers between devices, shards(): lax.all_gather(by_head, 'dp', axis=0, tiled=True)  19.1 us
    add x9, other arithmetic, sum_hop(): return near[:half] + send(near[half:].astype(BF16), size, hop).astype(F32)  18.7 us
    dynamic_update_slice x16, local copies, waits for them, and re-layouts, plane_rows(): lax.dynamic_update_slice_in_dim(whole, part, source * rows, 0)  15.5 us
  transfers between devices with their start and end apart: 89, of which 25 were waited for; matrix products, arithmetic and copies ran while one was open for 51% of the time, Pallas kernels for 5%

profile of v3, /device:TPU:0, one launch (start us, length us, event | category | flops | bytes accessed | tf_op | source)
XLA Modules:
  0.0 667.4 jit_solution(14626506907361358869)
XLA Ops:
  12.2 5.2 all-to-all-start
  19.0 11.0 %all-to-all-done = bf16[8,64,768]{2,1,0:T(8,128)(2,1)S(1)} async-done(((bf16[8,64,768]{2,1,0:T(8,128)(2,1)}), bf16[8,64,768]{2,1,0:T(8,128)(2,1)S(1)}, u32[]{:S(2)}, u32[]{:S(2)}) %all-to-all-start) | async-done | bytes 786464 | tf_op jit(solution)/shard_map/all_to_all | solution.py:343
  32.8 11.4 %collective-permute-done = bf16[128,2048]{1,0:T(8,128)(2,1)} collective-permute-done((bf16[128,2048]{1,0:T(8,128)(2,1)S(1)}, bf16[128,2048]{1,0:T(8,128)(2,1)}, u32[]{:S(2)}, u32[]{:S(2)}) %collective-permute-start) | collective-permute-done | bytes 524320 | tf_op jit(solution)/shard_map/ppermute | solution.py:53
  53.8 4.7 all-to-all-start.1
  68.4 6.9 %all-to-all-done.1 = f32[32,12,128]{2,1,0:T(8,128)S(1)} async-done(((f32[32,12,128]{2,1,0:T(8,128)}), f32[32,12,128]{2,1,0:T(8,128)S(1)}, u32[]{:S(2)}, u32[]{:S(2)}) %all-to-all-start.1) | async-done | bytes 196640 | tf_op jit(solution)/shard_map/all_to_all | solution.py:348
  81.6 7.8 %collective-permute-done.9 = bf16[2,2,64,2048]{3,2,1,0:T(8,128)(2,1)} collective-permute-done((bf16[2,2,64,2048]{3,2,1,0:T(8,128)(2,1)}, bf16[2,2,64,2048]{3,2,1,0:T(8,128)(2,1)}, u32[]{:S(2)}, u32[]{:S(2)}) %collective-permute-start.9) | collective-permute-done | bytes 1048608 | tf_op jit(solution)/shard_map/ppermute | solution.py:53
  91.8 19.1 %all-gather.6.cloned.1.call-done = bf16[32,64,768]{2,1,0:T(8,128)(2,1)} async-done(((bf16[8,64,768]{2,1,0:T(8,128)(2,1)}), bf16[32,64,768]{2,1,0:T(8,128)(2,1)}) %all-gather.6.cloned.1.call-update) | async-done | bytes 3145744 | tf_op jit(solution)/shard_map/all_gather | solution.py:346
  113.1 12.1 %attend.1 = (bf16[1024,2048]{1,0:T(8,128)(2,1)}, bf16[1024,768]{1,0:T(8,128)(2,1)S(1)}, bf16[1024,256]{1,0:T(8,128)(2,1)S(1)}) custom-call(bf16[1024,2048]{1,0:T(8,128)(2,1)} %constant_dynamic-update-slice_fusion.32.tokens, f32[1,2048]{1,0:T(1,128)S(1)} %broadcast_in_dim_reshape.4.gain, bf16[2048,768]{1,0:T(8,128)(2,1)S(1)} %bitcast.265, ...), custom_call_target="tpu_custom_call" | custom-call | tf_op jit(solution)/shard_map/attend/pallas_call | solution.py:192
  138.4 3.5 collective-permute-done.16
  141.9 10.1 %collective-permute-done.13 = bf16[1024,256]{1,0:T(8,128)(2,1)S(1)} collective-permute-done((bf16[1024,256]{1,0:T(8,128)(2,1)S(1)}, bf16[1024,256]{1,0:T(8,128)(2,1)S(1)}, u32[]{:S(2)}, u32[]{:S(2)}) %collective-permute-start.13) | collective-permute-done | bytes 524320 | tf_op jit(solution)/shard_map/ppermute | solution.py:53
  152.0 4.9 all-gather.8.cloned.1.call-done
  164.3 5.6 collective-permute-done.17
  171.9 4.1 fusion.18
  179.5 11.4 %multiply_reduce_fusion = (f32[1024]{0:T(1024)S(1)}, f32[1024,2048]{1,0:T(8,128)S(1)}) fusion(bf16[1024,2048]{1,0:T(8,128)(2,1)} %constant_dynamic-update-slice_fusion.32.tokens, bf16[1024,2048]{1,0:T(8,128)(2,1)S(1)} %constant_dynamic-update-slice_fusion.24, bf16[2048,2048]{1,0:T(8,128)(2,1)S(1)} %bitcast.271), kind=kOutput, calls=%fused_computation.6 | convolution fusion | flops 8598322176 | bytes 25169920 | tf_op jit(solution)/shard_map/dot_general | solution.py:21
  197.2 4.5 convolution_convert_fusion.13
  203.8 9.3 %fusion.2 = f32[464,2816]{1,0:T(8,128)S(1)} fusion(bf16[464,2048]{1,0:T(8,128)(2,1)S(1)} %convolution_convert_fusion.13, bf16[1,2048,2816]{2,1,0:T(8,128)(2,1)} %param.32), kind=kOutput, calls=%fused_computation.3 | convolution fusion | flops 5351931904 | bytes 18661376 | tf_op jit(solution)/shard_map/dot_general | solution.py:21
  213.2 6.0 multiply_convert_fusion.8
  222.0 4.3 all-to-all-start.2
  229.2 5.5 convolution_convert_fusion.1
  239.4 9.4 %fusion.13 = bf16[464,2048]{1,0:T(8,128)(2,1)} fusion(bf16[464,2816]{1,0:T(8,128)(2,1)S(1)} %pad_maximum_fusion.2, bf16[1,2048,2816]{2,1,0:T(8,128)(2,1)} %param.32), kind=kOutput, calls=%fused_computation.50 | convolution fusion | flops 5352882176 | bytes 16048128 | tf_op jit(solution)/shard_map/dot_general | solution.py:21
  259.7 5.3 convolution_convert_fusion
  287.6 2.8 constant_dynamic-update-slice_fusion.9
  293.2 11.4 %fusion.92 = f32[512,2816]{1,0:T(8,128)} fusion(bf16[512,2048]{1,0:T(8,128)(2,1)S(1)} %copy-done.11, bf16[2816,2048]{1,0:T(8,128)(2,1)} %bitcast.301), kind=kOutput, calls=%fused_computation.275 | convolution fusion | flops 5905580032 | bytes 19398656 | tf_op jit(solution)/shard_map/dot_general | solution.py:21
  304.6 7.7 %multiply_convert_fusion.7 = (bf16[512,1408]{1,0:T(8,128)(2,1)S(1)}, bf16[512,1408]{1,0:T(8,128)(2,1)S(1)}, bf16[512,1408]{1,0:T(8,128)(2,1)S(1)}) fusion(f32[512,2816]{1,0:T(8,128)} %fusion.92, bf16[1408,2048]{1,0:T(8,128)(2,1)S(1)} %bitcast.306, bf16[512,2048]{1,0:T(8,128)(2,1)} %all-gather.8.cloned.1.call-done, f32[512]{0:T(512)S(1)} %add_divide_fusion.2, ...), kind=kOutput, calls=%fused_computation.63 | convolution fusion | flops 2967076864 | bytes 17960960 | tf_op jit(solution)/shard_map/dot_general | solution.py:21
  312.4 3.5 convert_add_fusion.6
  317.8 8.8 %multiply_convert_fusion.1 = (bf16[512,2048]{1,0:T(8,128)(2,1)}, f32[512]{0:T(512)S(1)}) fusion(f32[512]{0:T(512)S(1)} %add_divide_fusion.2, f32[512]{0:T(512)S(1)} %fusion.83, bf16[512,2048]{1,0:T(8,128)(2,1)} %all-gather.8.cloned.1.call-done, bf16[512,1408]{1,0:T(8,128)(2,1)S(1)} %get-tuple-element.235, ...), kind=kOutput, calls=%fused_computation.26 | convolution fusion | flops 2959080960 | bytes 11409408 | tf_op jit(solution)/shard_map/dot_general | solution.py:21
  328.7 6.1 collective-permute-done.42
  336.2 6.4 collective-permute-done.46
  345.1 7.4 %add_convert_fusion = bf16[512,2048]{1,0:T(8,128)(2,1)} fusion(bf16[512,2816]{1,0:T(8,128)(2,1)S(1)} %pad_maximum_fusion.1, bf16[2816,2048]{1,0:T(8,128)(2,1)S(1)} %bitcast.304, f32[512]{0:T(512)S(1)} %subtract_multiply_fusion, f32[2048]{0:T(1024)S(1)} %mul.337), kind=kOutput, calls=%fused_computation.28 | convolution fusion | flops 5908725760 | bytes 16525312 | tf_op jit(solution)/shard_map/dot_general | solution.py:21
  352.5 6.7 %collective-permute-done.47 = bf16[128,2048]{1,0:T(8,128)(2,1)} collective-permute-done((bf16[128,2048]{1,0:T(8,128)(2,1)S(1)}, bf16[128,2048]{1,0:T(8,128)(2,1)}, u32[]{:S(2)}, u32[]{:S(2)}) %collective-permute-start.47) | collective-permute-done | bytes 524320 | tf_op jit(solution)/shard_map/ppermute | solution.py:53
  360.7 10.0 %collective-permute-done.44 = bf16[512,2048]{1,0:T(8,128)(2,1)} collective-permute-done((bf16[512,2048]{1,0:T(8,128)(2,1)}, bf16[512,2048]{1,0:T(8,128)(2,1)}, u32[]{:S(2)}, u32[]{:S(2)}) %collective-permute-start.44) | collective-permute-done | bytes 2097184 | tf_op jit(solution)/shard_map/ppermute | solution.py:53
  370.8 8.7 %multiply_reduce_fusion.2 = (f32[464]{0:T(512)S(1)}, bf16[464,2048]{1,0:T(8,128)(2,1)}) fusion(f32[464,2048]{1,0:T(8,128)} %fusion.18, f32[464]{0:T(512)S(1)} %select_reduce_fusion.1, bf16[464,1408]{1,0:T(8,128)(2,1)} %get-tuple-element.224, bf16[1,1408,2048]{2,1,0:T(8,128)(2,1)} %param.33), kind=kOutput, calls=%fused_computation.33 | convolution fusion | flops 2679766528 | bytes 12779136 | tf_op jit(solution)/shard_map/dot_general | solution.py:21
  379.5 5.2 convolution_convert_fusion.7
  384.7 5.2 convolution_convert_fusion.8
  389.9 3.5 convolution_convert_fusion.3
  393.3 3.3 convolution_convert_fusion.4
  396.6 3.5 convolution_convert_fusion.5
  400.1 3.5 convolution_convert_fusion.6
  403.6 10.8 %reduce-scatter.7.cloned.1.call-done = bf16[128,2048]{1,0:T(8,128)(2,1)} async-done(((bf16[512,2048]{1,0:T(8,128)(2,1)}), bf16[128,2048]{1,0:T(8,128)(2,1)}) %reduce-scatter.7.cloned.1.call-update) | async-done | bytes 524304 | tf_op jit(solution)/shard_map/reduce_scatter | solution.py:490
  417.6 3.1 fusion.87
  423.7 11.3 %collective-permute-done.48.refs_1_ = bf16[128,2048]{1,0:T(8,128)(2,1)S(1)} collective-permute-done((bf16[128,2048]{1,0:T(8,128)(2,1)}, bf16[128,2048]{1,0:T(8,128)(2,1)S(1)}, u32[]{:S(2)}, u32[]{:S(2)}) %collective-permute-start.48) | collective-permute-done | bytes 524320 | tf_op jit(solution)/shard_map/ppermute | solution.py:53
  438.2 3.7 convert_add_fusion.2
  442.0 3.7 convert_add_fusion.1
  452.0 3.2 slice.399
  455.2 3.1 slice.398
  460.5 22.2 %attend_back.1 = (bf16[1024,2048]{1,0:T(8,128)(2,1)}, bf16[1024,768]{1,0:T(8,128)(2,1)}, bf16[256,2048]{1,0:T(8,128)(2,1)}, f32[1,768]{1,0:T(1,128)}) custom-call(s32[8]{0:T(128)} %copy-done.56, bf16[128,2048]{1,0:T(8,128)(2,1)} %get-tuple-element.178.refs_0_, bf16[128,2048]{1,0:T(8,128)(2,1)} %copy-done.39, bf16[128,2048]{1,0:T(8,128)(2,1)} %copy-done.40, ...), custom_call_target="tpu_custom_call" | custom-call | tf_op jit(solution)/shard_map/attend_back/pallas_call | solution.py:269
  485.0 4.7 all-to-all-start.3
  490.4 4.6 convert_add_fusion.9
  495.0 4.9 convolution_convert_fusion.2
  499.9 5.5 reshape.716
  505.4 6.6 pad_maximum_fusion
  516.1 5.5 convert_add_fusion.8
  522.5 3.3 all-to-all-start.6
  528.7 3.3 fusion.16
  532.7 7.2 %constant_dynamic-slice_fusion = (bf16[4,1,128,352]{2,1,3,0:T(2,128)(2,1)S(1)}, bf16[4,1,128,352]{2,1,3,0:T(2,128)(2,1)S(1)}, bf16[4,1,128,352]{2,1,3,0:T(2,128)...) fusion(bf16[4,8,128,352]{2,1,3,0:T(8,128)(2,1)S(1)} %bitcast.26, ...), kind=kLoop, calls=%fused_computation.206 | loop fusion | bytes 5767200 | tf_op jit(solution)/shard_map/jit(dynamic_index_in_dim)/dynamic_slice | solution.py:585
  572.0 4.5 add_bitcast_fusion
  587.0 3.0 convert_add_fusion.4
  592.9 5.5 collective-permute-done.62
  599.3 15.9 %collective-permute-done.68 = bf16[256,2048]{1,0:T(8,128)(2,1)S(1)} collective-permute-done((bf16[256,2048]{1,0:T(8,128)(2,1)S(1)}, bf16[256,2048]{1,0:T(8,128)(2,1)S(1)}, u32[]{:S(2)}, u32[]{:S(2)}) %collective-permute-start.68) | collective-permute-done | bytes 1048608 | tf_op jit(solution)/shard_map/ppermute | solution.py:53
  619.5 4.3 all-to-all-start.4
  628.6 3.6 all-to-all-done.4
  633.5 4.3 maximum_convert_fusion
  640.7 3.5 all-to-all-start.5
  648.4 8.4 %all-to-all-done.5 = bf16[8,64,768]{2,1,0:T(8,128)(2,1)S(1)} async-done(((bf16[8,64,768]{2,1,0:T(8,128)(2,1)}), bf16[8,64,768]{2,1,0:T(8,128)(2,1)S(1)}, u32[]{:S(2)}, u32[]{:S(2)}) %all-to-all-start.5) | async-done | bytes 786464 | tf_op jit(solution)/shard_map/all_to_all | solution.py:555
  (508 shorter events, 224.8 us)
Async XLA Ops:
  7.2 45.9 %all-gather.12.cloned.1.call-start = ((), (), s32[]{:S(2)}) async-start(), calls=%async_computation.18 | async-start | bytes 1310720 | tf_op jit(solution)/shard_map/all_gather | solution.py:340
  12.2 17.8 %all-to-all-start = ((bf16[8,64,768]{2,1,0:T(8,128)(2,1)}), bf16[8,64,768]{2,1,0:T(8,128)(2,1)S(1)}, u32[]{:S(2)}, u32[]{:S(2)}) async-start(bf16[8,64,768]{2,1,0:T(8,128)(2,1)} %reshape.707), calls=%async_computation | async-start | bytes 1572864 | tf_op jit(solution)/shard_map/all_to_all | solution.py:343
  17.4 93.6 %all-gather.6.cloned.1.call-start = ((), (), s32[]{:S(2)}) async-start(), calls=%async_computation.11 | async-start | bytes 3932160 | tf_op jit(solution)/shard_map/all_gather | solution.py:346
  30.9 17.8 %collective-permute-start.1 = (bf16[128,2048]{1,0:T(8,128)(2,1)S(1)}, bf16[128,2048]{1,0:T(8,128)(2,1)}, u32[]{:S(2)}, u32[]{:S(2)}) collective-permute-start(bf16[128,2048]{1,0:T(8,128)(2,1)S(1)} %copy-done.12), channel_id=1, source_target_pairs={{0,4},{1,3},{2,6},{3,1},{4,0},{5,7},{6,2},{7,5},{8,12},{9,11},{10,... | collective-permute-start | bytes 1572872 | tf_op jit(solution)/shard_map/ppermute | solution.py:53
  31.6 29.6 %collective-permute-start.3 = (bf16[128,2048]{1,0:T(8,128)(2,1)S(1)}, bf16[128,2048]{1,0:T(8,128)(2,1)}, u32[]{:S(2)}, u32[]{:S(2)}) collective-permute-start(bf16[128,2048]{1,0:T(8,128)(2,1)S(1)} %copy-done.12), channel_id=1, source_target_pairs={{0,1},{1,0},{2,3},{3,2},{4,5},{5,4},{6,7},{7,6},{8,9},{9,8},{10,11... | collective-permute-start | bytes 1572872 | tf_op jit(solution)/shard_map/ppermute | solution.py:53
  31.6 93.7 %collective-permute-start.14 = (bf16[128,2048]{1,0:T(8,128)(2,1)}, bf16[128,2048]{1,0:T(8,128)(2,1)}, u32[]{:S(2)}, u32[]{:S(2)}) collective-permute-start(bf16[128,2048]{1,0:T(8,128)(2,1)} %param.23), channel_id=1, source_target_pairs={{0,2},{1,5},{2,0},{3,7},{4,6},{5,1},{6,4},{7,3},{8,10},{9,13},{10,... | collective-permute-start | bytes 1572872 | tf_op jit(solution)/shard_map/ppermute | solution.py:53
  44.2 14.3 %collective-permute-start.2 = (bf16[128,2048]{1,0:T(8,128)(2,1)}, bf16[128,2048]{1,0:T(8,128)(2,1)S(1)}, u32[]{:S(2)}, u32[]{:S(2)}) collective-permute-start(bf16[128,2048]{1,0:T(8,128)(2,1)} %collective-permute-done), channel_id=1, source_target_pairs={{0,4},{1,3},{2,6},{3,1},{4,0},{5,7},{6,2},{7,5},{8,12},{9,11},{10,... | collective-permute-start | bytes 1572872 | tf_op jit(solution)/shard_map/ppermute | solution.py:53
  48.7 15.8 %collective-permute-start.4 = (bf16[128,2048]{1,0:T(8,128)(2,1)}, bf16[128,2048]{1,0:T(8,128)(2,1)}, u32[]{:S(2)}, u32[]{:S(2)}) collective-permute-start(bf16[128,2048]{1,0:T(8,128)(2,1)} %collective-permute-done), channel_id=1, source_target_pairs={{0,1},{1,0},{2,3},{3,2},{4,5},{5,4},{6,7},{7,6},{8,9},{9,8},{10,11... | collective-permute-start | bytes 1572872 | tf_op jit(solution)/shard_map/ppermute | solution.py:53
  48.7 17.8 %collective-permute-start.5 = (bf16[128,2048]{1,0:T(8,128)(2,1)}, bf16[128,2048]{1,0:T(8,128)(2,1)}, u32[]{:S(2)}, u32[]{:S(2)}) collective-permute-start(bf16[128,2048]{1,0:T(8,128)(2,1)} %collective-permute-done.1), channel_id=1, source_target_pairs={{0,1},{1,0},{2,3},{3,2},{4,5},{5,4},{6,7},{7,6},{8,9},{9,8},{10,11... | collective-permute-start | bytes 1572872 | tf_op jit(solution)/shard_map/ppermute | solution.py:53
  53.8 21.5 %all-to-all-start.1 = ((f32[32,12,128]{2,1,0:T(8,128)}), f32[32,12,128]{2,1,0:T(8,128)S(1)}, u32[]{:S(2)}, u32[]{:S(2)}) async-start(f32[32,12,128]{2,1,0:T(8,128)} %broadcast_in_dim.175), calls=%async_computation.1 | async-start | bytes 524288 | tf_op jit(solution)/shard_map/all_to_all | solution.py:348
  58.5 98.4 %all-gather.8.cloned.1.call-start = ((), (), s32[]{:S(2)}) async-start(), calls=%async_computation.12 | async-start | bytes 2621440 | tf_op jit(solution)/shard_map/all_gather | solution.py:378
  58.5 68.3 %collective-permute-start.10 = (bf16[2,2,64,2048]{3,2,1,0:T(8,128)(2,1)}, bf16[2,2,64,2048]{3,2,1,0:T(8,128)(2,1)S(1)}, u32[]{:S(2)}, u32[]{:S(2)}) collective-permute-start(bf16[2,2,64,2048]{3,2,1,0:T(8,128)(2,1)} %bitcast.291), channel_id=1, source_target_pairs={{0,4},{1,3},{2,6},{3,1},{4,0},{5,7},{6,2},{7,5},{8,12},{9,11},{10,... | collective-permute-start | bytes 3145736 | tf_op jit(solution)/shard_map/ppermute | solution.py:53
  61.2 28.2 %collective-permute-start.9 = (bf16[2,2,64,2048]{3,2,1,0:T(8,128)(2,1)}, bf16[2,2,64,2048]{3,2,1,0:T(8,128)(2,1)}, u32[]{:S(2)}, u32[]{:S(2)}) collective-permute-start(bf16[2,2,64,2048]{3,2,1,0:T(8,128)(2,1)} %bitcast.292), channel_id=1, source_target_pairs={{0,2},{1,5},{2,0},{3,7},{4,6},{5,1},{6,4},{7,3},{8,10},{9,13},{10,... | collective-permute-start | bytes 3145736 | tf_op jit(solution)/shard_map/ppermute | solution.py:53
  78.0 51.5 %collective-permute-start.8 = (bf16[2,176,2048]{2,1,0:T(8,128)(2,1)S(1)}, bf16[2,176,2048]{2,1,0:T(8,128)(2,1)}, u32[]{:S(2)}, u32[]{:S(2)}) collective-permute-start(bf16[2,176,2048]{2,1,0:T(8,128)(2,1)S(1)} %bitcast.285), channel_id=1, source_target_pairs={{0,4},{1,3},{2,6},{3,1},{4,0},{5,7},{6,2},{7,5},{8,12},{9,11},{10,... | collective-permute-start | bytes 4325384 | tf_op jit(solution)/shard_map/ppermute | solution.py:53
  79.4 50.2 %collective-permute-start.7 = (bf16[2,176,2048]{2,1,0:T(8,128)(2,1)S(1)}, bf16[2,176,2048]{2,1,0:T(8,128)(2,1)}, u32[]{:S(2)}, u32[]{:S(2)}) collective-permute-start(bf16[2,176,2048]{2,1,0:T(8,128)(2,1)S(1)} %bitcast.286), channel_id=1, source_target_pairs={{0,2},{1,5},{2,0},{3,7},{4,6},{5,1},{6,4},{7,3},{8,10},{9,13},{10,... | collective-permute-start | bytes 4325384 | tf_op jit(solution)/shard_map/ppermute | solution.py:53
  89.4 40.1 %collective-permute-start.11 = (bf16[2,2,64,2048]{3,2,1,0:T(8,128)(2,1)}, bf16[2,2,64,2048]{3,2,1,0:T(8,128)(2,1)}, u32[]{:S(2)}, u32[]{:S(2)}) collective-permute-start(bf16[2,2,64,2048]{3,2,1,0:T(8,128)(2,1)} %collective-permute-done.9), channel_id=1, source_target_pairs={{0,4},{1,3},{2,6},{3,1},{4,0},{5,7},{6,2},{7,5},{8,12},{9,11},{10,... | collective-permute-start | bytes 3145736 | tf_op jit(solution)/shard_map/ppermute | solution.py:53
  110.9 169.5 %all-gather.10.cloned.1.call-start = ((), (), s32[]{:S(2)}) async-start(), calls=%async_computation.13 | async-start | bytes 2621440 | tf_op jit(solution)/shard_map/all_gather | solution.py:412
  126.8 15.0 %collective-permute-start.16 = (bf16[128,2048]{1,0:T(8,128)(2,1)}, bf16[128,2048]{1,0:T(8,128)(2,1)S(1)}, u32[]{:S(2)}, u32[]{:S(2)}) collective-permute-start(bf16[128,2048]{1,0:T(8,128)(2,1)} %collective-permute-done.14), channel_id=1, source_target_pairs={{0,4},{1,3},{2,6},{3,1},{4,0},{5,7},{6,2},{7,5},{8,12},{9,11},{10,... | collective-permute-start | bytes 1572872 | tf_op jit(solution)/shard_map/ppermute | solution.py:53
  135.1 16.8 %collective-permute-start.13 = (bf16[1024,256]{1,0:T(8,128)(2,1)S(1)}, bf16[1024,256]{1,0:T(8,128)(2,1)S(1)}, u32[]{:S(2)}, u32[]{:S(2)}) collective-permute-start(bf16[1024,256]{1,0:T(8,128)(2,1)S(1)} %get-tuple-element.126.refs_9_), channel_id=1, source_target_pairs={{0,4},{1,3},{2,6},{3,1},{4,0},{5,7},{6,2},{7,5},{8,12},{9,11},{10,... | collective-permute-start | bytes 1572872 | tf_op jit(solution)/shard_map/ppermute | solution.py:53
  136.7 15.3 %collective-permute-start.12 = (bf16[1024,256]{1,0:T(8,128)(2,1)S(1)}, bf16[1024,256]{1,0:T(8,128)(2,1)S(1)}, u32[]{:S(2)}, u32[]{:S(2)}) collective-permute-start(bf16[1024,256]{1,0:T(8,128)(2,1)S(1)} %get-tuple-element.126.refs_9_), channel_id=1, source_target_pairs={{0,2},{1,5},{2,0},{3,7},{4,6},{5,1},{6,4},{7,3},{8,10},{9,13},{10,... | collective-permute-start | bytes 1572872 | tf_op jit(solution)/shard_map/ppermute | solution.py:53
  176.1 25.7 %collective-permute-start.27 = (bf16[176,2048]{1,0:T(8,128)(2,1)S(1)}, bf16[176,2048]{1,0:T(8,128)(2,1)S(1)}, u32[]{:S(2)}, u32[]{:S(2)}) collective-permute-start(bf16[176,2048]{1,0:T(8,128)(2,1)S(1)} %copy-done.32), channel_id=1, source_target_pairs={{0,4},{1,3},{2,6},{3,1},{4,0},{5,7},{6,2},{7,5},{8,12},{9,11},{10,... | collective-permute-start | bytes 2162696 | tf_op jit(solution)/shard_map/ppermute | solution.py:53
  178.0 23.7 %collective-permute-start.26 = (bf16[176,2048]{1,0:T(8,128)(2,1)S(1)}, bf16[176,2048]{1,0:T(8,128)(2,1)}, u32[]{:S(2)}, u32[]{:S(2)}) collective-permute-start(bf16[176,2048]{1,0:T(8,128)(2,1)S(1)} %copy-done.32), channel_id=1, source_target_pairs={{0,2},{1,5},{2,0},{3,7},{4,6},{5,1},{6,4},{7,3},{8,10},{9,13},{10,... | collective-permute-start | bytes 2162696 | tf_op jit(solution)/shard_map/ppermute | solution.py:53
  201.8 32.9 %collective-permute-start.33 = (bf16[176,2048]{1,0:T(8,128)(2,1)}, bf16[176,2048]{1,0:T(8,128)(2,1)}, u32[]{:S(2)}, u32[]{:S(2)}) collective-permute-start(bf16[176,2048]{1,0:T(8,128)(2,1)} %collective-permute-done.26), channel_id=1, source_target_pairs={{0,4},{1,3},{2,6},{3,1},{4,0},{5,7},{6,2},{7,5},{8,12},{9,11},{10,... | collective-permute-start | bytes 2162696 | tf_op jit(solution)/shard_map/ppermute | solution.py:53
  202.1 32.6 %collective-permute-start.32 = (bf16[2,176,2048]{2,1,0:T(8,128)(2,1)}, bf16[2,176,2048]{2,1,0:T(8,128)(2,1)}, u32[]{:S(2)}, u32[]{:S(2)}) collective-permute-start(bf16[2,176,2048]{2,1,0:T(8,128)(2,1)} %collective-permute-done.7), channel_id=1, source_target_pairs={{0,4},{1,3},{2,6},{3,1},{4,0},{5,7},{6,2},{7,5},{8,12},{9,11},{10,... | collective-permute-start | bytes 4325384 | tf_op jit(solution)/shard_map/ppermute | solution.py:53
  222.0 138.7 %all-to-all-start.2 = ((bf16[4,464,352]{2,1,0:T(8,128)(2,1)}), bf16[4,464,352]{2,1,0:T(8,128)(2,1)}, u32[]{:S(2)}, u32[]{:S(2)}) async-start(bf16[4,464,352]{2,1,0:T(8,128)(2,1)} %bitcast.258), calls=%async_computation.3 | async-start | bytes 2850816 | tf_op jit(solution)/shard_map/all_to_all | solution.py:448
  226.4 144.4 %reduce-scatter.5.cloned.1.call-start = ((), (), s32[]{:S(2)}) async-start(), calls=%async_computation.14 | async-start | bytes 7208960 | tf_op jit(solution)/shard_map/reduce_scatter | solution.py:463
  234.7 36.4 %collective-permute-start.34 = (bf16[176,2048]{1,0:T(8,128)(2,1)S(1)}, bf16[176,2048]{1,0:T(8,128)(2,1)}, u32[]{:S(2)}, u32[]{:S(2)}) collective-permute-start(bf16[176,2048]{1,0:T(8,128)(2,1)S(1)} %copy-done.32), channel_id=1, source_target_pairs={{0,1},{1,0},{2,3},{3,2},{4,5},{5,4},{6,7},{7,6},{8,9},{9,8},{10,11... | collective-permute-start | bytes 2162696 | tf_op jit(solution)/shard_map/ppermute | solution.py:53
  234.7 38.9 %collective-permute-start.35 = (bf16[176,2048]{1,0:T(8,128)(2,1)}, bf16[176,2048]{1,0:T(8,128)(2,1)}, u32[]{:S(2)}, u32[]{:S(2)}) collective-permute-start(bf16[176,2048]{1,0:T(8,128)(2,1)} %collective-permute-done.26), channel_id=1, source_target_pairs={{0,1},{1,0},{2,3},{3,2},{4,5},{5,4},{6,7},{7,6},{8,9},{9,8},{10,11... | collective-permute-start | bytes 2162696 | tf_op jit(solution)/shard_map/ppermute | solution.py:53
  235.2 40.6 %collective-permute-start.36 = (bf16[176,2048]{1,0:T(8,128)(2,1)}, bf16[176,2048]{1,0:T(8,128)(2,1)}, u32[]{:S(2)}, u32[]{:S(2)}) collective-permute-start(bf16[176,2048]{1,0:T(8,128)(2,1)} %copy-done.33), channel_id=1, source_target_pairs={{0,1},{1,0},{2,3},{3,2},{4,5},{5,4},{6,7},{7,6},{8,9},{9,8},{10,11... | collective-permute-start | bytes 2162696 | tf_op jit(solution)/shard_map/ppermute | solution.py:53
  235.3 43.0 %collective-permute-start.37 = (bf16[176,2048]{1,0:T(8,128)(2,1)}, bf16[176,2048]{1,0:T(8,128)(2,1)}, u32[]{:S(2)}, u32[]{:S(2)}) collective-permute-start(bf16[176,2048]{1,0:T(8,128)(2,1)} %collective-permute-done.33), channel_id=1, source_target_pairs={{0,1},{1,0},{2,3},{3,2},{4,5},{5,4},{6,7},{7,6},{8,9},{9,8},{10,11... | collective-permute-start | bytes 2162696 | tf_op jit(solution)/shard_map/ppermute | solution.py:53
  235.7 46.8 %collective-permute-start.38 = (bf16[2,176,2048]{2,1,0:T(8,128)(2,1)}, bf16[2,176,2048]{2,1,0:T(8,128)(2,1)}, u32[]{:S(2)}, u32[]{:S(2)}) collective-permute-start(bf16[2,176,2048]{2,1,0:T(8,128)(2,1)} %bitcast.283), channel_id=1, source_target_pairs={{0,1},{1,0},{2,3},{3,2},{4,5},{5,4},{6,7},{7,6},{8,9},{9,8},{10,11... | collective-permute-start | bytes 4325384 | tf_op jit(solution)/shard_map/ppermute | solution.py:53
  248.8 165.5 %reduce-scatter.7.cloned.1.call-start = ((), (), s32[]{:S(2)}) async-start(), calls=%async_computation.15 | async-start | bytes 2621440 | tf_op jit(solution)/shard_map/reduce_scatter | solution.py:490
  271.1 14.7 %collective-permute-start.39 = (bf16[2,176,2048]{2,1,0:T(8,128)(2,1)}, bf16[2,176,2048]{2,1,0:T(8,128)(2,1)S(1)}, u32[]{:S(2)}, u32[]{:S(2)}) collective-permute-start(bf16[2,176,2048]{2,1,0:T(8,128)(2,1)} %collective-permute-done.7), channel_id=1, source_target_pairs={{0,1},{1,0},{2,3},{3,2},{4,5},{5,4},{6,7},{7,6},{8,9},{9,8},{10,11... | collective-permute-start | bytes 4325384 | tf_op jit(solution)/shard_map/ppermute | solution.py:53
  275.8 14.6 %collective-permute-start.41 = (bf16[2,176,2048]{2,1,0:T(8,128)(2,1)}, bf16[2,176,2048]{2,1,0:T(8,128)(2,1)}, u32[]{:S(2)}, u32[]{:S(2)}) collective-permute-start(bf16[2,176,2048]{2,1,0:T(8,128)(2,1)} %collective-permute-done.32), channel_id=1, source_target_pairs={{0,1},{1,0},{2,3},{3,2},{4,5},{5,4},{6,7},{7,6},{8,9},{9,8},{10,11... | collective-permute-start | bytes 4325384 | tf_op jit(solution)/shard_map/ppermute | solution.py:53
  278.3 34.1 %collective-permute-start.45 = (bf16[512,2048]{1,0:T(8,128)(2,1)}, bf16[512,2048]{1,0:T(8,128)(2,1)}, u32[]{:S(2)}, u32[]{:S(2)}) collective-permute-start(bf16[512,2048]{1,0:T(8,128)(2,1)} %convolution_convert_fusion.11), channel_id=1, source_target_pairs={{0,1},{1,0},{2,3},{3,2},{4,5},{5,4},{6,7},{7,6},{8,9},{9,8},{10,11... | collective-permute-start | bytes 6291464 | tf_op jit(solution)/shard_map/ppermute | solution.py:53
  282.5 46.2 %collective-permute-start.43 = (bf16[512,2048]{1,0:T(8,128)(2,1)}, bf16[512,2048]{1,0:T(8,128)(2,1)}, u32[]{:S(2)}, u32[]{:S(2)}) collective-permute-start(bf16[512,2048]{1,0:T(8,128)(2,1)} %all-gather.8.cloned.1.call-done), channel_id=1, source_target_pairs={{0,4},{1,3},{2,6},{3,1},{4,0},{5,7},{6,2},{7,5},{8,12},{9,11},{10,... | collective-permute-start | bytes 6291464 | tf_op jit(solution)/shard_map/ppermute | solution.py:53
  285.9 48.9 %collective-permute-start.42 = (bf16[512,2048]{1,0:T(8,128)(2,1)}, bf16[512,2048]{1,0:T(8,128)(2,1)}, u32[]{:S(2)}, u32[]{:S(2)}) collective-permute-start(bf16[512,2048]{1,0:T(8,128)(2,1)} %all-gather.8.cloned.1.call-done), channel_id=1, source_target_pairs={{0,2},{1,5},{2,0},{3,7},{4,6},{5,1},{6,4},{7,3},{8,10},{9,13},{10,... | collective-permute-start | bytes 6291464 | tf_op jit(solution)/shard_map/ppermute | solution.py:53
  316.0 26.5 %collective-permute-start.46 = (bf16[256,2048]{1,0:T(8,128)(2,1)S(1)}, bf16[256,2048]{1,0:T(8,128)(2,1)S(1)}, u32[]{:S(2)}, u32[]{:S(2)}) collective-permute-start(bf16[256,2048]{1,0:T(8,128)(2,1)S(1)} %slice.403), channel_id=1, source_target_pairs={{0,4},{1,3},{2,6},{3,1},{4,0},{5,7},{6,2},{7,5},{8,12},{9,11},{10,... | collective-permute-start | bytes 3145736 | tf_op jit(solution)/shard_map/ppermute | solution.py:53
  334.8 36.0 %collective-permute-start.44 = (bf16[512,2048]{1,0:T(8,128)(2,1)}, bf16[512,2048]{1,0:T(8,128)(2,1)}, u32[]{:S(2)}, u32[]{:S(2)}) collective-permute-start(bf16[512,2048]{1,0:T(8,128)(2,1)} %collective-permute-done.42), channel_id=1, source_target_pairs={{0,4},{1,3},{2,6},{3,1},{4,0},{5,7},{6,2},{7,5},{8,12},{9,11},{10,... | collective-permute-start | bytes 6291464 | tf_op jit(solution)/shard_map/ppermute | solution.py:53
  344.2 15.0 %collective-permute-start.47 = (bf16[128,2048]{1,0:T(8,128)(2,1)S(1)}, bf16[128,2048]{1,0:T(8,128)(2,1)}, u32[]{:S(2)}, u32[]{:S(2)}) collective-permute-start(bf16[128,2048]{1,0:T(8,128)(2,1)S(1)} %slice.409), channel_id=1, source_target_pairs={{0,2},{1,5},{2,0},{3,7},{4,6},{5,1},{6,4},{7,3},{8,10},{9,13},{10,... | collective-permute-start | bytes 1572872 | tf_op jit(solution)/shard_map/ppermute | solution.py:53
  370.8 262.7 %reduce-scatter.11.cloned.1.call-start = ((), (), s32[]{:S(2)}) async-start(), calls=%async_computation.17 | async-start | bytes 7208960 | tf_op jit(solution)/shard_map/reduce_scatter | solution.py:505
  414.4 22.5 %collective-permute-start.51 = (bf16[704,2048]{1,0:T(8,128)(2,1)}, bf16[704,2048]{1,0:T(8,128)(2,1)S(1)}, u32[]{:S(2)}, u32[]{:S(2)}) collective-permute-start(bf16[704,2048]{1,0:T(8,128)(2,1)} %convolution_convert_fusion.7), channel_id=1, source_target_pairs={{0,1},{1,0},{2,3},{3,2},{4,5},{5,4},{6,7},{7,6},{8,9},{9,8},{10,11... | collective-permute-start | bytes 8650760 | tf_op jit(solution)/shard_map/ppermute | solution.py:53
  414.5 23.7 %collective-permute-start.52 = (bf16[704,2048]{1,0:T(8,128)(2,1)}, bf16[704,2048]{1,0:T(8,128)(2,1)S(1)}, u32[]{:S(2)}, u32[]{:S(2)}) collective-permute-start(bf16[704,2048]{1,0:T(8,128)(2,1)} %convolution_convert_fusion.5), channel_id=1, source_target_pairs={{0,1},{1,0},{2,3},{3,2},{4,5},{5,4},{6,7},{7,6},{8,9},{9,8},{10,11... | collective-permute-start | bytes 8650760 | tf_op jit(solution)/shard_map/ppermute | solution.py:53
  415.8 26.1 %collective-permute-start.53 = (bf16[704,2048]{1,0:T(8,128)(2,1)}, bf16[704,2048]{1,0:T(8,128)(2,1)S(1)}, u32[]{:S(2)}, u32[]{:S(2)}) collective-permute-start(bf16[704,2048]{1,0:T(8,128)(2,1)} %convolution_convert_fusion.3), channel_id=1, source_target_pairs={{0,1},{1,0},{2,3},{3,2},{4,5},{5,4},{6,7},{7,6},{8,9},{9,8},{10,11... | collective-permute-start | bytes 8650760 | tf_op jit(solution)/shard_map/ppermute | solution.py:53
  420.7 14.3 %collective-permute-start.48 = (bf16[128,2048]{1,0:T(8,128)(2,1)}, bf16[128,2048]{1,0:T(8,128)(2,1)S(1)}, u32[]{:S(2)}, u32[]{:S(2)}) collective-permute-start(bf16[128,2048]{1,0:T(8,128)(2,1)} %get-tuple-element.178.refs_0_), channel_id=1, source_target_pairs={{0,2},{1,5},{2,0},{3,7},{4,6},{5,1},{6,4},{7,3},{8,10},{9,13},{10,... | collective-permute-start | bytes 1572872 | tf_op jit(solution)/shard_map/ppermute | solution.py:53
  422.2 23.5 %collective-permute-start.49 = (bf16[128,2048]{1,0:T(8,128)(2,1)}, bf16[128,2048]{1,0:T(8,128)(2,1)S(1)}, u32[]{:S(2)}, u32[]{:S(2)}) collective-permute-start(bf16[128,2048]{1,0:T(8,128)(2,1)} %get-tuple-element.178.refs_0_), channel_id=1, source_target_pairs={{0,4},{1,3},{2,6},{3,1},{4,0},{5,7},{6,2},{7,5},{8,12},{9,11},{10,... | collective-permute-start | bytes 1572872 | tf_op jit(solution)/shard_map/ppermute | solution.py:53
  447.1 42.7 %collective-permute-start.58 = (bf16[352,2048]{1,0:T(8,128)(2,1)}, bf16[352,2048]{1,0:T(8,128)(2,1)}, u32[]{:S(2)}, u32[]{:S(2)}) collective-permute-start(bf16[352,2048]{1,0:T(8,128)(2,1)} %slice.400), channel_id=1, source_target_pairs={{0,4},{1,3},{2,6},{3,1},{4,0},{5,7},{6,2},{7,5},{8,12},{9,11},{10,... | collective-permute-start | bytes 4325384 | tf_op jit(solution)/shard_map/ppermute | solution.py:53
  458.3 100.7 %collective-permute-start.70 = (bf16[512,2048]{1,0:T(8,128)(2,1)}, bf16[512,2048]{1,0:T(8,128)(2,1)}, u32[]{:S(2)}, u32[]{:S(2)}) collective-permute-start(bf16[512,2048]{1,0:T(8,128)(2,1)} %all-gather.8.cloned.1.call-done), channel_id=1, source_target_pairs={{0,1},{1,0},{2,3},{3,2},{4,5},{5,4},{6,7},{7,6},{8,9},{9,8},{10,11... | collective-permute-start | bytes 6291464 | tf_op jit(solution)/shard_map/ppermute | solution.py:53
  458.4 103.7 %collective-permute-start.71 = (bf16[512,2048]{1,0:T(8,128)(2,1)}, bf16[512,2048]{1,0:T(8,128)(2,1)}, u32[]{:S(2)}, u32[]{:S(2)}) collective-permute-start(bf16[512,2048]{1,0:T(8,128)(2,1)} %collective-permute-done.42), channel_id=1, source_target_pairs={{0,1},{1,0},{2,3},{3,2},{4,5},{5,4},{6,7},{7,6},{8,9},{9,8},{10,11... | collective-permute-start | bytes 6291464 | tf_op jit(solution)/shard_map/ppermute | solution.py:53
  458.9 107.3 %collective-permute-start.72 = (bf16[512,2048]{1,0:T(8,128)(2,1)}, bf16[512,2048]{1,0:T(8,128)(2,1)}, u32[]{:S(2)}, u32[]{:S(2)}) collective-permute-start(bf16[512,2048]{1,0:T(8,128)(2,1)} %collective-permute-done.43), channel_id=1, source_target_pairs={{0,1},{1,0},{2,3},{3,2},{4,5},{5,4},{6,7},{7,6},{8,9},{9,8},{10,11... | collective-permute-start | bytes 6291464 | tf_op jit(solution)/shard_map/ppermute | solution.py:53
  458.9 53.1 %collective-permute-start.60 = (bf16[352,2048]{1,0:T(8,128)(2,1)}, bf16[352,2048]{1,0:T(8,128)(2,1)}, u32[]{:S(2)}, u32[]{:S(2)}) collective-permute-start(bf16[352,2048]{1,0:T(8,128)(2,1)} %slice.398), channel_id=1, source_target_pairs={{0,4},{1,3},{2,6},{3,1},{4,0},{5,7},{6,2},{7,5},{8,12},{9,11},{10,... | collective-permute-start | bytes 4325384 | tf_op jit(solution)/shard_map/ppermute | solution.py:53
  485.0 20.4 %all-to-all-start.3 = ((bf16[2,2,64,2048]{3,2,1,0:T(8,128)(2,1)}), bf16[2,2,64,2048]{3,2,1,0:T(8,128)(2,1)}, u32[]{:S(2)}, u32[]{:S(2)}) async-start(bf16[2,2,64,2048]{3,2,1,0:T(8,128)(2,1)} %bitcast.259), calls=%async_computation.5 | async-start | bytes 2097152 | tf_op jit(solution)/shard_map/all_to_all | solution.py:520
  489.7 148.1 %reduce-scatter.9.cloned.1.call-start = ((), (), s32[]{:S(2)}) async-start(), calls=%async_computation.16 | async-start | bytes 7864320 | tf_op jit(solution)/shard_map/reduce_scatter | solution.py:548
  489.8 26.3 %collective-permute-start.59 = (bf16[352,2048]{1,0:T(8,128)(2,1)}, bf16[352,2048]{1,0:T(8,128)(2,1)}, u32[]{:S(2)}, u32[]{:S(2)}) collective-permute-start(bf16[352,2048]{1,0:T(8,128)(2,1)} %slice.399), channel_id=1, source_target_pairs={{0,4},{1,3},{2,6},{3,1},{4,0},{5,7},{6,2},{7,5},{8,12},{9,11},{10,... | collective-permute-start | bytes 4325384 | tf_op jit(solution)/shard_map/ppermute | solution.py:53
  512.0 59.4 %collective-permute-start.73 = (bf16[512,2048]{1,0:T(8,128)(2,1)}, bf16[512,2048]{1,0:T(8,128)(2,1)}, u32[]{:S(2)}, u32[]{:S(2)}) collective-permute-start(bf16[512,2048]{1,0:T(8,128)(2,1)} %collective-permute-done.44), channel_id=1, source_target_pairs={{0,1},{1,0},{2,3},{3,2},{4,5},{5,4},{6,7},{7,6},{8,9},{9,8},{10,11... | collective-permute-start | bytes 6291464 | tf_op jit(solution)/shard_map/ppermute | solution.py:53
  522.5 54.4 %all-to-all-start.6 = ((f32[8,1,128]{2,1,0:T(1,128)}), f32[8,1,128]{2,1,0:T(1,128)S(1)}, u32[]{:S(2)}, u32[]{:S(2)}) async-start(f32[8,1,128]{2,1,0:T(1,128)} %bitcast.73), calls=%async_computation.10 | async-start | bytes 8192 | tf_op jit(solution)/shard_map/all_to_all | solution.py:572
  526.8 50.7 %collective-permute-start.66 = (bf16[176,2048]{1,0:T(8,128)(2,1)}, bf16[176,2048]{1,0:T(8,128)(2,1)}, u32[]{:S(2)}, u32[]{:S(2)}) collective-permute-start(bf16[176,2048]{1,0:T(8,128)(2,1)} %slice.404), channel_id=1, source_target_pairs={{0,2},{1,5},{2,0},{3,7},{4,6},{5,1},{6,4},{7,3},{8,10},{9,13},{10,... | collective-permute-start | bytes 2162696 | tf_op jit(solution)/shard_map/ppermute | solution.py:53
  559.0 20.5 %collective-permute-start.65 = (bf16[176,2048]{1,0:T(8,128)(2,1)}, bf16[176,2048]{1,0:T(8,128)(2,1)}, u32[]{:S(2)}, u32[]{:S(2)}) collective-permute-start(bf16[176,2048]{1,0:T(8,128)(2,1)} %slice.405), channel_id=1, source_target_pairs={{0,2},{1,5},{2,0},{3,7},{4,6},{5,1},{6,4},{7,3},{8,10},{9,13},{10,... | collective-permute-start | bytes 2162696 | tf_op jit(solution)/shard_map/ppermute | solution.py:53
  562.1 28.4 %collective-permute-start.64 = (bf16[176,2048]{1,0:T(8,128)(2,1)}, bf16[176,2048]{1,0:T(8,128)(2,1)}, u32[]{:S(2)}, u32[]{:S(2)}) collective-permute-start(bf16[176,2048]{1,0:T(8,128)(2,1)} %slice.406), channel_id=1, source_target_pairs={{0,2},{1,5},{2,0},{3,7},{4,6},{5,1},{6,4},{7,3},{8,10},{9,13},{10,... | collective-permute-start | bytes 2162696 | tf_op jit(solution)/shard_map/ppermute | solution.py:53
  566.2 20.7 %collective-permute-start.67 = (bf16[512,2048]{1,0:T(8,128)(2,1)}, bf16[512,2048]{1,0:T(8,128)(2,1)}, u32[]{:S(2)}, u32[]{:S(2)}) collective-permute-start(bf16[512,2048]{1,0:T(8,128)(2,1)} %convolution_convert_fusion.9), channel_id=1, source_target_pairs={{0,1},{1,0},{2,3},{3,2},{4,5},{5,4},{6,7},{7,6},{8,9},{9,8},{10,11... | collective-permute-start | bytes 6291464 | tf_op jit(solution)/shard_map/ppermute | solution.py:53
  583.5 14.9 %collective-permute-start.62 = (bf16[256,2048]{1,0:T(8,128)(2,1)S(1)}, bf16[256,2048]{1,0:T(8,128)(2,1)S(1)}, u32[]{:S(2)}, u32[]{:S(2)}) collective-permute-start(bf16[256,2048]{1,0:T(8,128)(2,1)S(1)} %slice.402), channel_id=1, source_target_pairs={{0,4},{1,3},{2,6},{3,1},{4,0},{5,7},{6,2},{7,5},{8,12},{9,11},{10,... | collective-permute-start | bytes 3145736 | tf_op jit(solution)/shard_map/ppermute | solution.py:53
  590.1 25.1 %collective-permute-start.68 = (bf16[256,2048]{1,0:T(8,128)(2,1)S(1)}, bf16[256,2048]{1,0:T(8,128)(2,1)S(1)}, u32[]{:S(2)}, u32[]{:S(2)}) collective-permute-start(bf16[256,2048]{1,0:T(8,128)(2,1)S(1)} %slice.401), channel_id=1, source_target_pairs={{0,4},{1,3},{2,6},{3,1},{4,0},{5,7},{6,2},{7,5},{8,12},{9,11},{10,... | collective-permute-start | bytes 3145736 | tf_op jit(solution)/shard_map/ppermute | solution.py:53
  598.8 19.4 %collective-permute-start.63 = (bf16[128,2048]{1,0:T(8,128)(2,1)S(1)}, bf16[128,2048]{1,0:T(8,128)(2,1)S(1)}, u32[]{:S(2)}, u32[]{:S(2)}) collective-permute-start(bf16[128,2048]{1,0:T(8,128)(2,1)S(1)} %slice.408), channel_id=1, source_target_pairs={{0,2},{1,5},{2,0},{3,7},{4,6},{5,1},{6,4},{7,3},{8,10},{9,13},{10,... | collective-permute-start | bytes 1572872 | tf_op jit(solution)/shard_map/ppermute | solution.py:53
  640.7 16.1 %all-to-all-start.5 = ((bf16[8,64,768]{2,1,0:T(8,128)(2,1)}), bf16[8,64,768]{2,1,0:T(8,128)(2,1)S(1)}, u32[]{:S(2)}, u32[]{:S(2)}) async-start(bf16[8,64,768]{2,1,0:T(8,128)(2,1)} %reshape.726), calls=%async_computation.8 | async-start | bytes 1572864 | tf_op jit(solution)/shard_map/all_to_all | solution.py:555
  (108 other events, 1306.3 us)
Sparse Core Ops, SparseCore 0:
  9.6 30.6 all-gather.11
  42.4 68.4 all-gather.5
  112.5 44.3 all-gather.7
  197.3 56.1 all-gather.9
  255.7 108.4 reduce-scatter.4
  370.9 43.4 reduce-scatter.6
  416.8 101.6 reduce-scatter.10
  520.9 112.3 reduce-scatter.8

commit v4 on v3

--- a/solution.py
+++ b/solution.py
@@ -484,11 +484,10 @@
     shared_pre_grad, cot_parts = barrier((shared_pre_grad, cot_parts))
     cot_parts = gather_second(cot_parts, group)
     normed_term = mm(shared_pre_grad, unit_flat) + logit_grad * gate_full
-    normed_term, in_gate_grad, cot_parts, routed_grad, gated_act = barrier(
-        (normed_term.astype(BF16), in_gate_grad, cot_parts, routed_grad, gated_act)
+    normed_term, in_gate_grad, routed_grad, gated_act = barrier(
+        (normed_term.astype(BF16), in_gate_grad, routed_grad, gated_act)
     )
     shared_grad = lax.psum_scatter(normed_term, "dp", scatter_dimension=0, tiled=True)
-    cot_parts = gather_third(cot_parts, group)
     half_units = plane_units // 2
     unit_grads = []
     for left, right in (
@@ -498,9 +497,10 @@
     ):
         far = mm_tn(left[:, half_units:], right).astype(BF16)
         unit_grads.append((mm_tn(left[:, :half_units], right).astype(BF16), far))
-    shared_grad, in_up, unit_grads, gated_val, pair_dot = barrier(
-        (shared_grad, in_up, unit_grads, gated_val, pair_dot)
-    )
+    shared_grad, in_up, unit_grads, gated_val, pair_dot, cot_parts = barrier(
+        (shared_grad, in_up, unit_grads, gated_val, pair_dot, cot_parts)
+    )
+    cot_parts = gather_third(cot_parts, group)
     shared_grad = shared_grad.astype(F32)
     in_up_grad = lax.psum_scatter(in_up, "dp", scatter_dimension=0, tiled=True)
     normed2_grad = shared_grad + routed_grad
@@ -548,7 +548,7 @@
     joined = lax.psum_scatter(joined, "dp", scatter_dimension=0, tiled=True)[0]
     half_rows = group_rows // 2
     normed1_grad = plane_sum(normed1_grad[:half_rows], normed1_grad[half_rows:], group)
-    expert_in_grad = jnp.concatenate([in_gate_grad, in_up_grad], axis=1)
+    expert_in_grad = jnp.concatenate([in_gate_grad, in_up_grad], axis=1).astype(F32)
     out_weight_grad = joined[flat_rows : flat_rows + shard]
     shared_sum = joined[flat_rows + shard :].astype(F32)
     qkv_own_grad = joined[:flat_rows]
@@ -574,7 +574,7 @@
         jnp.where(routes.T[None] == places[:, None, None], pair_back[:, None, :], 0.0), axis=0
     ).T
 
-    unit_grads, gated_act = barrier((unit_grads, gated_act))
+    unit_grads, gated_act, expert_in_grad = barrier((unit_grads, gated_act, expert_in_grad))
     all_pick = (all_rank.reshape(planes, 1, group_rows) == slot_ids[None]).astype(BF16)
     token_act = lax.dot_general(
         all_pick, gated_act, (((1,), (1,)), ((0,), (0,))), preferred_element_type=F32
@@ -623,7 +623,7 @@
         shared_in_grad,
         shared_out_grad,
         sums[2 * shard : 3 * shard],
-        expert_in_grad.astype(F32)[None],
+        expert_in_grad[None],
         expert_out_grad.astype(F32)[None],
         gate_values_grad,
     )

time: 675 us -> 669 us (level)
  waiting for transfers between devices: 172 us -> 164 us
    ppermute x74, waiting for transfers between devices: 106 us -> 82.7 us  [send(): return lax.ppermute(block, 'expert', [(i, target(i)) for i in range(size)])]
    unnamed x191 -> x215, local copies, waits for them, and re-layouts: 46.1 us -> 58.6 us
    all_to_all x1, waiting for transfers between devices: 0.15 us -> 10.9 us  [shards(): pair_back = lax.all_to_all(pair_dots, 'expert', 0, 0, tiled=True)]
    reduce_scatter x1, waiting for transfers between devices: 0.01 us -> 9.27 us  [shards(): lax.psum_scatter(in_gate, 'dp', scatter_dimension=0, tiled=True)]
  transfers between devices with their start and end apart: 89 -> 89, of which waited for: 25 -> 27; matrix products, arithmetic and copies ran while one was open for 51% -> 50% of each run, Pallas kernels for 5% -> 5%
where the time goes in v4:
time: 669 us; the launch traced here: 662 us
  matrix products  169 us (25%)
  waiting for transfers between devices  164 us (25%)
  local copies, waits for them, and re-layouts  132 us (20%)
  starting transfers between devices  83.8 us (13%)
  other arithmetic  61.7 us (9%)
  Pallas kernels  34.4 us (5%)
  between operations  17.5 us (3%)
    dot_general x33, matrix products, dot(): return lax.dot_general(a, b, (dims, ((), ())), preferred_element_type=F32)  166 us
    ppermute x74, waiting for transfers between devices, send(): return lax.ppermute(block, 'expert', [(i, target(i)) for i in range(size)])  82.7 us
    unnamed x215, local copies, waits for them, and re-layouts  58.6 us
    ppermute x74, starting transfers between devices, send(): return lax.ppermute(block, 'expert', [(i, target(i)) for i in range(size)])  54.4 us
    pallas_call x1, Pallas kernels, attend_back(): pl.pallas_call(functools.partial(attend_back_kernel, own // HEAD, size),...  22.2 us
    add x9, other arithmetic, sum_hop(): return near[:half] + send(near[half:].astype(BF16), size, hop).astype(F32)  21.6 us
    all_gather x1, waiting for transfers between devices, shards(): lax.all_gather(by_head, 'dp', axis=0, tiled=True)  19.1 us
    dynamic_update_slice x16, local copies, waits for them, and re-layouts, plane_rows(): lax.dynamic_update_slice_in_dim(whole, part, source * rows, 0)  15.5 us
  transfers between devices with their start and end apart: 89, of which 27 were waited for; matrix products, arithmetic and copies ran while one was open for 50% of the time, Pallas kernels for 5%

profile of v4, /device:TPU:0, one launch (start us, length us, event | category | flops | bytes accessed | tf_op | source)
XLA Modules:
  0.0 662.0 jit_solution(9522178907432393604)
XLA Ops:
  12.2 5.2 all-to-all-start
  19.0 11.0 %all-to-all-done = bf16[8,64,768]{2,1,0:T(8,128)(2,1)S(1)} async-done(((bf16[8,64,768]{2,1,0:T(8,128)(2,1)}), bf16[8,64,768]{2,1,0:T(8,128)(2,1)S(1)}, u32[]{:S(2)}, u32[]{:S(2)}) %all-to-all-start) | async-done | bytes 786464 | tf_op jit(solution)/shard_map/all_to_all | solution.py:343
  32.8 11.4 %collective-permute-done = bf16[128,2048]{1,0:T(8,128)(2,1)} collective-permute-done((bf16[128,2048]{1,0:T(8,128)(2,1)S(1)}, bf16[128,2048]{1,0:T(8,128)(2,1)}, u32[]{:S(2)}, u32[]{:S(2)}) %collective-permute-start) | collective-permute-done | bytes 524320 | tf_op jit(solution)/shard_map/ppermute | solution.py:53
  53.8 4.7 all-to-all-start.1
  68.4 6.9 %all-to-all-done.1 = f32[32,12,128]{2,1,0:T(8,128)S(1)} async-done(((f32[32,12,128]{2,1,0:T(8,128)}), f32[32,12,128]{2,1,0:T(8,128)S(1)}, u32[]{:S(2)}, u32[]{:S(2)}) %all-to-all-start.1) | async-done | bytes 196640 | tf_op jit(solution)/shard_map/all_to_all | solution.py:348
  81.6 7.8 %collective-permute-done.9 = bf16[2,2,64,2048]{3,2,1,0:T(8,128)(2,1)} collective-permute-done((bf16[2,2,64,2048]{3,2,1,0:T(8,128)(2,1)}, bf16[2,2,64,2048]{3,2,1,0:T(8,128)(2,1)}, u32[]{:S(2)}, u32[]{:S(2)}) %collective-permute-start.9) | collective-permute-done | bytes 1048608 | tf_op jit(solution)/shard_map/ppermute | solution.py:53
  91.8 19.1 %all-gather.6.cloned.1.call-done = bf16[32,64,768]{2,1,0:T(8,128)(2,1)} async-done(((bf16[8,64,768]{2,1,0:T(8,128)(2,1)}), bf16[32,64,768]{2,1,0:T(8,128)(2,1)}) %all-gather.6.cloned.1.call-update) | async-done | bytes 3145744 | tf_op jit(solution)/shard_map/all_gather | solution.py:346
  113.1 12.2 %attend.1 = (bf16[1024,2048]{1,0:T(8,128)(2,1)}, bf16[1024,768]{1,0:T(8,128)(2,1)S(1)}, bf16[1024,256]{1,0:T(8,128)(2,1)S(1)}) custom-call(bf16[1024,2048]{1,0:T(8,128)(2,1)} %constant_dynamic-update-slice_fusion.32.tokens, f32[1,2048]{1,0:T(1,128)S(1)} %broadcast_in_dim_reshape.4.gain, bf16[2048,768]{1,0:T(8,128)(2,1)S(1)} %bitcast.264, ...), custom_call_target="tpu_custom_call" | custom-call | tf_op jit(solution)/shard_map/attend/pallas_call | solution.py:192
  138.4 3.5 collective-permute-done.16
  141.9 10.1 %collective-permute-done.13 = bf16[1024,256]{1,0:T(8,128)(2,1)S(1)} collective-permute-done((bf16[1024,256]{1,0:T(8,128)(2,1)S(1)}, bf16[1024,256]{1,0:T(8,128)(2,1)S(1)}, u32[]{:S(2)}, u32[]{:S(2)}) %collective-permute-start.13) | collective-permute-done | bytes 524320 | tf_op jit(solution)/shard_map/ppermute | solution.py:53
  152.0 4.9 all-gather.8.cloned.1.call-done
  164.3 5.6 collective-permute-done.17
  171.9 4.0 fusion.18
  179.5 11.4 %multiply_reduce_fusion = (f32[1024]{0:T(1024)S(1)}, f32[1024,2048]{1,0:T(8,128)S(1)}) fusion(bf16[1024,2048]{1,0:T(8,128)(2,1)} %constant_dynamic-update-slice_fusion.32.tokens, bf16[1024,2048]{1,0:T(8,128)(2,1)S(1)} %constant_dynamic-update-slice_fusion.24, bf16[2048,2048]{1,0:T(8,128)(2,1)S(1)} %bitcast.272), kind=kOutput, calls=%fused_computation.6 | convolution fusion | flops 8598322176 | bytes 25169920 | tf_op jit(solution)/shard_map/dot_general | solution.py:21
  197.2 4.5 convolution_convert_fusion.13
  203.8 9.3 %fusion.2 = f32[464,2816]{1,0:T(8,128)S(1)} fusion(bf16[464,2048]{1,0:T(8,128)(2,1)S(1)} %convolution_convert_fusion.13, bf16[1,2048,2816]{2,1,0:T(8,128)(2,1)} %param.32), kind=kOutput, calls=%fused_computation.3 | convolution fusion | flops 5351931904 | bytes 18661376 | tf_op jit(solution)/shard_map/dot_general | solution.py:21
  213.2 6.0 multiply_convert_fusion.8
  222.0 4.3 all-to-all-start.2
  229.1 5.5 convolution_convert_fusion.1
  239.4 9.4 %fusion.13 = bf16[464,2048]{1,0:T(8,128)(2,1)} fusion(bf16[464,2816]{1,0:T(8,128)(2,1)S(1)} %pad_maximum_fusion.2, bf16[1,2048,2816]{2,1,0:T(8,128)(2,1)} %param.32), kind=kOutput, calls=%fused_computation.50 | convolution fusion | flops 5352882176 | bytes 16048128 | tf_op jit(solution)/shard_map/dot_general | solution.py:21
  251.5 2.8 constant_dynamic-update-slice_fusion.13
  259.6 5.3 convolution_convert_fusion
  287.4 2.8 constant_dynamic-update-slice_fusion.9
  290.2 2.8 constant_dynamic-update-slice_fusion.8
  293.0 11.4 %fusion.92 = f32[512,2816]{1,0:T(8,128)} fusion(bf16[512,2048]{1,0:T(8,128)(2,1)S(1)} %copy-done.14, bf16[2816,2048]{1,0:T(8,128)(2,1)} %bitcast.301), kind=kOutput, calls=%fused_computation.275 | convolution fusion | flops 5905580032 | bytes 19398656 | tf_op jit(solution)/shard_map/dot_general | solution.py:21
  304.3 7.7 %multiply_convert_fusion.7 = (bf16[512,1408]{1,0:T(8,128)(2,1)S(1)}, bf16[512,1408]{1,0:T(8,128)(2,1)S(1)}, bf16[512,1408]{1,0:T(8,128)(2,1)S(1)}) fusion(f32[512,2816]{1,0:T(8,128)} %fusion.92, bf16[1408,2048]{1,0:T(8,128)(2,1)S(1)} %bitcast.306, bf16[512,2048]{1,0:T(8,128)(2,1)} %all-gather.8.cloned.1.call-done, f32[512]{0:T(512)S(1)} %add_divide_fusion.2, ...), kind=kOutput, calls=%fused_computation.63 | convolution fusion | flops 2967076864 | bytes 17960960 | tf_op jit(solution)/shard_map/dot_general | solution.py:21
  312.1 3.5 convert_add_fusion.6
  317.6 8.9 %multiply_convert_fusion.1 = (bf16[512,2048]{1,0:T(8,128)(2,1)}, f32[512]{0:T(512)S(1)}) fusion(f32[512]{0:T(512)S(1)} %add_divide_fusion.2, f32[512]{0:T(512)S(1)} %fusion.83, bf16[512,2048]{1,0:T(8,128)(2,1)} %all-gather.8.cloned.1.call-done, bf16[512,1408]{1,0:T(8,128)(2,1)S(1)} %get-tuple-element.237, ...), kind=kOutput, calls=%fused_computation.26 | convolution fusion | flops 2959080960 | bytes 11409408 | tf_op jit(solution)/shard_map/dot_general | solution.py:21
  328.6 6.0 collective-permute-done.42
  334.6 7.8 %collective-permute-done.45 = bf16[256,2048]{1,0:T(8,128)(2,1)S(1)} collective-permute-done((bf16[256,2048]{1,0:T(8,128)(2,1)S(1)}, bf16[256,2048]{1,0:T(8,128)(2,1)S(1)}, u32[]{:S(2)}, u32[]{:S(2)}) %collective-permute-start.45) | collective-permute-done | bytes 1048608 | tf_op jit(solution)/shard_map/ppermute | solution.py:53
  344.9 7.5 %add_convert_fusion = bf16[512,2048]{1,0:T(8,128)(2,1)} fusion(bf16[512,2816]{1,0:T(8,128)(2,1)S(1)} %pad_maximum_fusion.1, bf16[2816,2048]{1,0:T(8,128)(2,1)S(1)} %bitcast.304, f32[512]{0:T(512)S(1)} %subtract_multiply_fusion, f32[2048]{0:T(1024)S(1)} %mul.337), kind=kOutput, calls=%fused_computation.28 | convolution fusion | flops 5908725760 | bytes 16525312 | tf_op jit(solution)/shard_map/dot_general | solution.py:21
  354.9 9.3 %reduce-scatter.5.cloned.1.call-done = bf16[512,1408]{1,0:T(8,128)(2,1)} async-done(((bf16[2048,1408]{1,0:T(8,128)(2,1)}), bf16[512,1408]{1,0:T(8,128)(2,1)}) %reduce-scatter.5.cloned.1.call-update) | async-done | bytes 1441808 | tf_op jit(solution)/shard_map/reduce_scatter | solution.py:463
  364.2 9.3 %multiply_reduce_fusion.2 = (f32[464]{0:T(512)}, bf16[464,2048]{1,0:T(8,128)(2,1)}) fusion(f32[464,2048]{1,0:T(8,128)} %fusion.18, f32[464]{0:T(512)S(1)} %select_reduce_fusion.1, bf16[464,1408]{1,0:T(8,128)(2,1)} %get-tuple-element.226, bf16[1,1408,2048]{2,1,0:T(8,128)(2,1)} %param.33), kind=kOutput, calls=%fused_computation.33 | convolution fusion | flops 2679766528 | bytes 12779136 | tf_op jit(solution)/shard_map/dot_general | solution.py:21
  374.9 5.2 convolution_convert_fusion.7
  380.2 5.2 convolution_convert_fusion.8
  385.4 3.5 convolution_convert_fusion.3
  388.8 3.3 convolution_convert_fusion.4
  392.1 3.5 convolution_convert_fusion.5
  395.6 3.5 convolution_convert_fusion.6
  399.9 9.8 %reduce-scatter.7.cloned.1.call-done = bf16[128,2048]{1,0:T(8,128)(2,1)} async-done(((bf16[512,2048]{1,0:T(8,128)(2,1)}), bf16[128,2048]{1,0:T(8,128)(2,1)}) %reduce-scatter.7.cloned.1.call-update) | async-done | bytes 524304 | tf_op jit(solution)/shard_map/reduce_scatter | solution.py:490
  412.8 2.9 fusion.87
  418.6 11.3 %collective-permute-done.48.refs_1_ = bf16[128,2048]{1,0:T(8,128)(2,1)S(1)} collective-permute-done((bf16[128,2048]{1,0:T(8,128)(2,1)S(1)}, bf16[128,2048]{1,0:T(8,128)(2,1)S(1)}, u32[]{:S(2)}, u32[]{:S(2)}) %collective-permute-start.48) | collective-permute-done | bytes 524320 | tf_op jit(solution)/shard_map/ppermute | solution.py:53
  451.7 22.2 %attend_back.1 = (bf16[1024,2048]{1,0:T(8,128)(2,1)}, bf16[1024,768]{1,0:T(8,128)(2,1)}, bf16[256,2048]{1,0:T(8,128)(2,1)}, f32[1,768]{1,0:T(1,128)}) custom-call(s32[8]{0:T(128)} %copy-done.67, bf16[128,2048]{1,0:T(8,128)(2,1)} %copy-done.33, bf16[128,2048]{1,0:T(8,128)(2,1)} %copy-done.45, bf16[128,2048]{1,0:T(8,128)(2,1)} %copy-done.46, ...), custom_call_target="tpu_custom_call" | custom-call | tf_op jit(solution)/shard_map/attend_back/pallas_call | solution.py:269
  476.2 4.6 all-to-all-start.3
  481.1 4.0 convert_add_fusion.9
  485.1 4.3 convert_add_fusion.7
  491.0 3.4 convert_add_fusion.8
  497.4 4.9 convolution_convert_fusion.2
  502.3 5.5 reshape.687
  507.9 4.3 convolution_convert_fusion.9
  512.2 6.6 pad_maximum_fusion
  520.1 3.0 convert_add_fusion.5
  528.9 3.5 convert_add_fusion.4
  538.0 3.3 all-to-all-start.6
  541.5 10.9 %all-to-all-done.6 = f32[8,1,128]{2,1,0:T(1,128)S(1)} async-done(((f32[8,1,128]{2,1,0:T(1,128)}), f32[8,1,128]{2,1,0:T(1,128)S(1)}, u32[]{:S(2)}, u32[]{:S(2)}) %all-to-all-start.6) | async-done | bytes 4128 | tf_op jit(solution)/shard_map/all_to_all | solution.py:572
  562.1 3.9 collective-permute-done.63
  568.7 3.0 all-to-all-start.4
  571.7 3.9 collective-permute-done.69
  579.5 4.9 maximum_convert_fusion
  586.1 3.2 fusion.16
  590.1 6.2 constant_dynamic-slice_fusion
  620.9 4.6 add_bitcast_fusion
  635.2 3.5 all-to-all-start.5
  642.9 8.4 %all-to-all-done.5 = bf16[8,64,768]{2,1,0:T(8,128)(2,1)S(1)} async-done(((bf16[8,64,768]{2,1,0:T(8,128)(2,1)}), bf16[8,64,768]{2,1,0:T(8,128)(2,1)S(1)}, u32[]{:S(2)}, u32[]{:S(2)}) %all-to-all-start.5) | async-done | bytes 786464 | tf_op jit(solution)/shard_map/all_to_all | solution.py:555
  (533 shorter events, 232.5 us)
Async XLA Ops:
  7.2 45.9 %all-gather.12.cloned.1.call-start = ((), (), s32[]{:S(2)}) async-start(), calls=%async_computation.18 | async-start | bytes 1310720 | tf_op jit(solution)/shard_map/all_gather | solution.py:340
  12.2 17.8 %all-to-all-start = ((bf16[8,64,768]{2,1,0:T(8,128)(2,1)}), bf16[8,64,768]{2,1,0:T(8,128)(2,1)S(1)}, u32[]{:S(2)}, u32[]{:S(2)}) async-start(bf16[8,64,768]{2,1,0:T(8,128)(2,1)} %reshape.678), calls=%async_computation | async-start | bytes 1572864 | tf_op jit(solution)/shard_map/all_to_all | solution.py:343
  17.3 93.6 %all-gather.6.cloned.1.call-start = ((), (), s32[]{:S(2)}) async-start(), calls=%async_computation.11 | async-start | bytes 3932160 | tf_op jit(solution)/shard_map/all_gather | solution.py:346
  30.0 14.2 %collective-permute-start = (bf16[128,2048]{1,0:T(8,128)(2,1)S(1)}, bf16[128,2048]{1,0:T(8,128)(2,1)}, u32[]{:S(2)}, u32[]{:S(2)}) collective-permute-start(bf16[128,2048]{1,0:T(8,128)(2,1)S(1)} %copy-done.16), channel_id=1, source_target_pairs={{0,2},{1,5},{2,0},{3,7},{4,6},{5,1},{6,4},{7,3},{8,10},{9,13},{10,... | collective-permute-start | bytes 1572872 | tf_op jit(solution)/shard_map/ppermute | solution.py:53
  30.9 17.8 %collective-permute-start.1 = (bf16[128,2048]{1,0:T(8,128)(2,1)S(1)}, bf16[128,2048]{1,0:T(8,128)(2,1)}, u32[]{:S(2)}, u32[]{:S(2)}) collective-permute-start(bf16[128,2048]{1,0:T(8,128)(2,1)S(1)} %copy-done.16), channel_id=1, source_target_pairs={{0,4},{1,3},{2,6},{3,1},{4,0},{5,7},{6,2},{7,5},{8,12},{9,11},{10,... | collective-permute-start | bytes 1572872 | tf_op jit(solution)/shard_map/ppermute | solution.py:53
  31.6 29.6 %collective-permute-start.3 = (bf16[128,2048]{1,0:T(8,128)(2,1)S(1)}, bf16[128,2048]{1,0:T(8,128)(2,1)}, u32[]{:S(2)}, u32[]{:S(2)}) collective-permute-start(bf16[128,2048]{1,0:T(8,128)(2,1)S(1)} %copy-done.16), channel_id=1, source_target_pairs={{0,1},{1,0},{2,3},{3,2},{4,5},{5,4},{6,7},{7,6},{8,9},{9,8},{10,11... | collective-permute-start | bytes 1572872 | tf_op jit(solution)/shard_map/ppermute | solution.py:53
  31.6 93.7 %collective-permute-start.14 = (bf16[128,2048]{1,0:T(8,128)(2,1)}, bf16[128,2048]{1,0:T(8,128)(2,1)}, u32[]{:S(2)}, u32[]{:S(2)}) collective-permute-start(bf16[128,2048]{1,0:T(8,128)(2,1)} %param.23), channel_id=1, source_target_pairs={{0,2},{1,5},{2,0},{3,7},{4,6},{5,1},{6,4},{7,3},{8,10},{9,13},{10,... | collective-permute-start | bytes 1572872 | tf_op jit(solution)/shard_map/ppermute | solution.py:53
  44.2 14.3 %collective-permute-start.2 = (bf16[128,2048]{1,0:T(8,128)(2,1)}, bf16[128,2048]{1,0:T(8,128)(2,1)S(1)}, u32[]{:S(2)}, u32[]{:S(2)}) collective-permute-start(bf16[128,2048]{1,0:T(8,128)(2,1)} %collective-permute-done), channel_id=1, source_target_pairs={{0,4},{1,3},{2,6},{3,1},{4,0},{5,7},{6,2},{7,5},{8,12},{9,11},{10,... | collective-permute-start | bytes 1572872 | tf_op jit(solution)/shard_map/ppermute | solution.py:53
  48.7 15.8 %collective-permute-start.4 = (bf16[128,2048]{1,0:T(8,128)(2,1)}, bf16[128,2048]{1,0:T(8,128)(2,1)}, u32[]{:S(2)}, u32[]{:S(2)}) collective-permute-start(bf16[128,2048]{1,0:T(8,128)(2,1)} %collective-permute-done), channel_id=1, source_target_pairs={{0,1},{1,0},{2,3},{3,2},{4,5},{5,4},{6,7},{7,6},{8,9},{9,8},{10,11... | collective-permute-start | bytes 1572872 | tf_op jit(solution)/shard_map/ppermute | solution.py:53
  48.7 17.8 %collective-permute-start.5 = (bf16[128,2048]{1,0:T(8,128)(2,1)}, bf16[128,2048]{1,0:T(8,128)(2,1)}, u32[]{:S(2)}, u32[]{:S(2)}) collective-permute-start(bf16[128,2048]{1,0:T(8,128)(2,1)} %collective-permute-done.1), channel_id=1, source_target_pairs={{0,1},{1,0},{2,3},{3,2},{4,5},{5,4},{6,7},{7,6},{8,9},{9,8},{10,11... | collective-permute-start | bytes 1572872 | tf_op jit(solution)/shard_map/ppermute | solution.py:53
  53.8 21.5 %all-to-all-start.1 = ((f32[32,12,128]{2,1,0:T(8,128)}), f32[32,12,128]{2,1,0:T(8,128)S(1)}, u32[]{:S(2)}, u32[]{:S(2)}) async-start(f32[32,12,128]{2,1,0:T(8,128)} %broadcast_in_dim.177), calls=%async_computation.1 | async-start | bytes 524288 | tf_op jit(solution)/shard_map/all_to_all | solution.py:348
  58.5 98.4 %all-gather.8.cloned.1.call-start = ((), (), s32[]{:S(2)}) async-start(), calls=%async_computation.12 | async-start | bytes 2621440 | tf_op jit(solution)/shard_map/all_gather | solution.py:378
  58.5 68.3 %collective-permute-start.10 = (bf16[2,2,64,2048]{3,2,1,0:T(8,128)(2,1)}, bf16[2,2,64,2048]{3,2,1,0:T(8,128)(2,1)S(1)}, u32[]{:S(2)}, u32[]{:S(2)}) collective-permute-start(bf16[2,2,64,2048]{3,2,1,0:T(8,128)(2,1)} %bitcast.291), channel_id=1, source_target_pairs={{0,4},{1,3},{2,6},{3,1},{4,0},{5,7},{6,2},{7,5},{8,12},{9,11},{10,... | collective-permute-start | bytes 3145736 | tf_op jit(solution)/shard_map/ppermute | solution.py:53
  61.2 28.2 %collective-permute-start.9 = (bf16[2,2,64,2048]{3,2,1,0:T(8,128)(2,1)}, bf16[2,2,64,2048]{3,2,1,0:T(8,128)(2,1)}, u32[]{:S(2)}, u32[]{:S(2)}) collective-permute-start(bf16[2,2,64,2048]{3,2,1,0:T(8,128)(2,1)} %bitcast.292), channel_id=1, source_target_pairs={{0,2},{1,5},{2,0},{3,7},{4,6},{5,1},{6,4},{7,3},{8,10},{9,13},{10,... | collective-permute-start | bytes 3145736 | tf_op jit(solution)/shard_map/ppermute | solution.py:53
  78.0 51.5 %collective-permute-start.8 = (bf16[2,176,2048]{2,1,0:T(8,128)(2,1)S(1)}, bf16[2,176,2048]{2,1,0:T(8,128)(2,1)}, u32[]{:S(2)}, u32[]{:S(2)}) collective-permute-start(bf16[2,176,2048]{2,1,0:T(8,128)(2,1)S(1)} %bitcast.287), channel_id=1, source_target_pairs={{0,4},{1,3},{2,6},{3,1},{4,0},{5,7},{6,2},{7,5},{8,12},{9,11},{10,... | collective-permute-start | bytes 4325384 | tf_op jit(solution)/shard_map/ppermute | solution.py:53
  79.4 50.2 %collective-permute-start.7 = (bf16[2,176,2048]{2,1,0:T(8,128)(2,1)S(1)}, bf16[2,176,2048]{2,1,0:T(8,128)(2,1)}, u32[]{:S(2)}, u32[]{:S(2)}) collective-permute-start(bf16[2,176,2048]{2,1,0:T(8,128)(2,1)S(1)} %bitcast.288), channel_id=1, source_target_pairs={{0,2},{1,5},{2,0},{3,7},{4,6},{5,1},{6,4},{7,3},{8,10},{9,13},{10,... | collective-permute-start | bytes 4325384 | tf_op jit(solution)/shard_map/ppermute | solution.py:53
  89.4 40.1 %collective-permute-start.11 = (bf16[2,2,64,2048]{3,2,1,0:T(8,128)(2,1)}, bf16[2,2,64,2048]{3,2,1,0:T(8,128)(2,1)}, u32[]{:S(2)}, u32[]{:S(2)}) collective-permute-start(bf16[2,2,64,2048]{3,2,1,0:T(8,128)(2,1)} %collective-permute-done.9), channel_id=1, source_target_pairs={{0,4},{1,3},{2,6},{3,1},{4,0},{5,7},{6,2},{7,5},{8,12},{9,11},{10,... | collective-permute-start | bytes 3145736 | tf_op jit(solution)/shard_map/ppermute | solution.py:53
  110.9 169.3 %all-gather.10.cloned.1.call-start = ((), (), s32[]{:S(2)}) async-start(), calls=%async_computation.13 | async-start | bytes 2621440 | tf_op jit(solution)/shard_map/all_gather | solution.py:412
  126.9 15.0 %collective-permute-start.16 = (bf16[128,2048]{1,0:T(8,128)(2,1)}, bf16[128,2048]{1,0:T(8,128)(2,1)S(1)}, u32[]{:S(2)}, u32[]{:S(2)}) collective-permute-start(bf16[128,2048]{1,0:T(8,128)(2,1)} %collective-permute-done.14), channel_id=1, source_target_pairs={{0,4},{1,3},{2,6},{3,1},{4,0},{5,7},{6,2},{7,5},{8,12},{9,11},{10,... | collective-permute-start | bytes 1572872 | tf_op jit(solution)/shard_map/ppermute | solution.py:53
  135.1 16.8 %collective-permute-start.13 = (bf16[1024,256]{1,0:T(8,128)(2,1)S(1)}, bf16[1024,256]{1,0:T(8,128)(2,1)S(1)}, u32[]{:S(2)}, u32[]{:S(2)}) collective-permute-start(bf16[1024,256]{1,0:T(8,128)(2,1)S(1)} %get-tuple-element.127.refs_9_), channel_id=1, source_target_pairs={{0,4},{1,3},{2,6},{3,1},{4,0},{5,7},{6,2},{7,5},{8,12},{9,11},{10,... | collective-permute-start | bytes 1572872 | tf_op jit(solution)/shard_map/ppermute | solution.py:53
  136.7 15.3 %collective-permute-start.12 = (bf16[1024,256]{1,0:T(8,128)(2,1)S(1)}, bf16[1024,256]{1,0:T(8,128)(2,1)S(1)}, u32[]{:S(2)}, u32[]{:S(2)}) collective-permute-start(bf16[1024,256]{1,0:T(8,128)(2,1)S(1)} %get-tuple-element.127.refs_9_), channel_id=1, source_target_pairs={{0,2},{1,5},{2,0},{3,7},{4,6},{5,1},{6,4},{7,3},{8,10},{9,13},{10,... | collective-permute-start | bytes 1572872 | tf_op jit(solution)/shard_map/ppermute | solution.py:53
  176.0 25.7 %collective-permute-start.27 = (bf16[176,2048]{1,0:T(8,128)(2,1)S(1)}, bf16[176,2048]{1,0:T(8,128)(2,1)S(1)}, u32[]{:S(2)}, u32[]{:S(2)}) collective-permute-start(bf16[176,2048]{1,0:T(8,128)(2,1)S(1)} %copy-done.38), channel_id=1, source_target_pairs={{0,4},{1,3},{2,6},{3,1},{4,0},{5,7},{6,2},{7,5},{8,12},{9,11},{10,... | collective-permute-start | bytes 2162696 | tf_op jit(solution)/shard_map/ppermute | solution.py:53
  178.0 23.7 %collective-permute-start.26 = (bf16[176,2048]{1,0:T(8,128)(2,1)S(1)}, bf16[176,2048]{1,0:T(8,128)(2,1)}, u32[]{:S(2)}, u32[]{:S(2)}) collective-permute-start(bf16[176,2048]{1,0:T(8,128)(2,1)S(1)} %copy-done.38), channel_id=1, source_target_pairs={{0,2},{1,5},{2,0},{3,7},{4,6},{5,1},{6,4},{7,3},{8,10},{9,13},{10,... | collective-permute-start | bytes 2162696 | tf_op jit(solution)/shard_map/ppermute | solution.py:53
  201.7 32.9 %collective-permute-start.33 = (bf16[176,2048]{1,0:T(8,128)(2,1)}, bf16[176,2048]{1,0:T(8,128)(2,1)}, u32[]{:S(2)}, u32[]{:S(2)}) collective-permute-start(bf16[176,2048]{1,0:T(8,128)(2,1)} %collective-permute-done.26), channel_id=1, source_target_pairs={{0,4},{1,3},{2,6},{3,1},{4,0},{5,7},{6,2},{7,5},{8,12},{9,11},{10,... | collective-permute-start | bytes 2162696 | tf_op jit(solution)/shard_map/ppermute | solution.py:53
  202.1 32.5 %collective-permute-start.32 = (bf16[2,176,2048]{2,1,0:T(8,128)(2,1)}, bf16[2,176,2048]{2,1,0:T(8,128)(2,1)}, u32[]{:S(2)}, u32[]{:S(2)}) collective-permute-start(bf16[2,176,2048]{2,1,0:T(8,128)(2,1)} %collective-permute-done.7), channel_id=1, source_target_pairs={{0,4},{1,3},{2,6},{3,1},{4,0},{5,7},{6,2},{7,5},{8,12},{9,11},{10,... | collective-permute-start | bytes 4325384 | tf_op jit(solution)/shard_map/ppermute | solution.py:53
  222.0 132.9 %all-to-all-start.2 = ((bf16[4,464,352]{2,1,0:T(8,128)(2,1)}), bf16[4,464,352]{2,1,0:T(8,128)(2,1)}, u32[]{:S(2)}, u32[]{:S(2)}) async-start(bf16[4,464,352]{2,1,0:T(8,128)(2,1)} %bitcast.257), calls=%async_computation.3 | async-start | bytes 2850816 | tf_op jit(solution)/shard_map/all_to_all | solution.py:448
  226.3 137.8 %reduce-scatter.5.cloned.1.call-start = ((), (), s32[]{:S(2)}) async-start(), calls=%async_computation.14 | async-start | bytes 7208960 | tf_op jit(solution)/shard_map/reduce_scatter | solution.py:463
  234.7 36.4 %collective-permute-start.34 = (bf16[176,2048]{1,0:T(8,128)(2,1)S(1)}, bf16[176,2048]{1,0:T(8,128)(2,1)}, u32[]{:S(2)}, u32[]{:S(2)}) collective-permute-start(bf16[176,2048]{1,0:T(8,128)(2,1)S(1)} %copy-done.38), channel_id=1, source_target_pairs={{0,1},{1,0},{2,3},{3,2},{4,5},{5,4},{6,7},{7,6},{8,9},{9,8},{10,11... | collective-permute-start | bytes 2162696 | tf_op jit(solution)/shard_map/ppermute | solution.py:53
  234.7 38.9 %collective-permute-start.35 = (bf16[176,2048]{1,0:T(8,128)(2,1)}, bf16[176,2048]{1,0:T(8,128)(2,1)}, u32[]{:S(2)}, u32[]{:S(2)}) collective-permute-start(bf16[176,2048]{1,0:T(8,128)(2,1)} %collective-permute-done.26), channel_id=1, source_target_pairs={{0,1},{1,0},{2,3},{3,2},{4,5},{5,4},{6,7},{7,6},{8,9},{9,8},{10,11... | collective-permute-start | bytes 2162696 | tf_op jit(solution)/shard_map/ppermute | solution.py:53
  235.2 40.5 %collective-permute-start.36 = (bf16[176,2048]{1,0:T(8,128)(2,1)}, bf16[176,2048]{1,0:T(8,128)(2,1)}, u32[]{:S(2)}, u32[]{:S(2)}) collective-permute-start(bf16[176,2048]{1,0:T(8,128)(2,1)} %copy-done.39), channel_id=1, source_target_pairs={{0,1},{1,0},{2,3},{3,2},{4,5},{5,4},{6,7},{7,6},{8,9},{9,8},{10,11... | collective-permute-start | bytes 2162696 | tf_op jit(solution)/shard_map/ppermute | solution.py:53
  235.2 42.9 %collective-permute-start.37 = (bf16[176,2048]{1,0:T(8,128)(2,1)}, bf16[176,2048]{1,0:T(8,128)(2,1)}, u32[]{:S(2)}, u32[]{:S(2)}) collective-permute-start(bf16[176,2048]{1,0:T(8,128)(2,1)} %collective-permute-done.33), channel_id=1, source_target_pairs={{0,1},{1,0},{2,3},{3,2},{4,5},{5,4},{6,7},{7,6},{8,9},{9,8},{10,11... | collective-permute-start | bytes 2162696 | tf_op jit(solution)/shard_map/ppermute | solution.py:53
  235.7 46.7 %collective-permute-start.38 = (bf16[2,176,2048]{2,1,0:T(8,128)(2,1)}, bf16[2,176,2048]{2,1,0:T(8,128)(2,1)}, u32[]{:S(2)}, u32[]{:S(2)}) collective-permute-start(bf16[2,176,2048]{2,1,0:T(8,128)(2,1)} %bitcast.285), channel_id=1, source_target_pairs={{0,1},{1,0},{2,3},{3,2},{4,5},{5,4},{6,7},{7,6},{8,9},{9,8},{10,11... | collective-permute-start | bytes 4325384 | tf_op jit(solution)/shard_map/ppermute | solution.py:53
  248.8 160.9 %reduce-scatter.7.cloned.1.call-start = ((), (), s32[]{:S(2)}) async-start(), calls=%async_computation.15 | async-start | bytes 2621440 | tf_op jit(solution)/shard_map/reduce_scatter | solution.py:490
  271.0 14.7 %collective-permute-start.39 = (bf16[2,176,2048]{2,1,0:T(8,128)(2,1)}, bf16[2,176,2048]{2,1,0:T(8,128)(2,1)S(1)}, u32[]{:S(2)}, u32[]{:S(2)}) collective-permute-start(bf16[2,176,2048]{2,1,0:T(8,128)(2,1)} %collective-permute-done.7), channel_id=1, source_target_pairs={{0,1},{1,0},{2,3},{3,2},{4,5},{5,4},{6,7},{7,6},{8,9},{9,8},{10,11... | collective-permute-start | bytes 4325384 | tf_op jit(solution)/shard_map/ppermute | solution.py:53
  275.6 14.5 %collective-permute-start.41 = (bf16[2,176,2048]{2,1,0:T(8,128)(2,1)}, bf16[2,176,2048]{2,1,0:T(8,128)(2,1)}, u32[]{:S(2)}, u32[]{:S(2)}) collective-permute-start(bf16[2,176,2048]{2,1,0:T(8,128)(2,1)} %collective-permute-done.32), channel_id=1, source_target_pairs={{0,1},{1,0},{2,3},{3,2},{4,5},{5,4},{6,7},{7,6},{8,9},{9,8},{10,11... | collective-permute-start | bytes 4325384 | tf_op jit(solution)/shard_map/ppermute | solution.py:53
  278.1 33.9 %collective-permute-start.44 = (bf16[512,2048]{1,0:T(8,128)(2,1)}, bf16[512,2048]{1,0:T(8,128)(2,1)}, u32[]{:S(2)}, u32[]{:S(2)}) collective-permute-start(bf16[512,2048]{1,0:T(8,128)(2,1)} %convolution_convert_fusion.11), channel_id=1, source_target_pairs={{0,1},{1,0},{2,3},{3,2},{4,5},{5,4},{6,7},{7,6},{8,9},{9,8},{10,11... | collective-permute-start | bytes 6291464 | tf_op jit(solution)/shard_map/ppermute | solution.py:53
  282.4 46.2 %collective-permute-start.43 = (bf16[512,2048]{1,0:T(8,128)(2,1)}, bf16[512,2048]{1,0:T(8,128)(2,1)}, u32[]{:S(2)}, u32[]{:S(2)}) collective-permute-start(bf16[512,2048]{1,0:T(8,128)(2,1)} %all-gather.8.cloned.1.call-done), channel_id=1, source_target_pairs={{0,4},{1,3},{2,6},{3,1},{4,0},{5,7},{6,2},{7,5},{8,12},{9,11},{10,... | collective-permute-start | bytes 6291464 | tf_op jit(solution)/shard_map/ppermute | solution.py:53
  285.7 48.9 %collective-permute-start.42 = (bf16[512,2048]{1,0:T(8,128)(2,1)}, bf16[512,2048]{1,0:T(8,128)(2,1)}, u32[]{:S(2)}, u32[]{:S(2)}) collective-permute-start(bf16[512,2048]{1,0:T(8,128)(2,1)} %all-gather.8.cloned.1.call-done), channel_id=1, source_target_pairs={{0,2},{1,5},{2,0},{3,7},{4,6},{5,1},{6,4},{7,3},{8,10},{9,13},{10,... | collective-permute-start | bytes 6291464 | tf_op jit(solution)/shard_map/ppermute | solution.py:53
  315.7 26.6 %collective-permute-start.45 = (bf16[256,2048]{1,0:T(8,128)(2,1)S(1)}, bf16[256,2048]{1,0:T(8,128)(2,1)S(1)}, u32[]{:S(2)}, u32[]{:S(2)}) collective-permute-start(bf16[256,2048]{1,0:T(8,128)(2,1)S(1)} %slice.403), channel_id=1, source_target_pairs={{0,4},{1,3},{2,6},{3,1},{4,0},{5,7},{6,2},{7,5},{8,12},{9,11},{10,... | collective-permute-start | bytes 3145736 | tf_op jit(solution)/shard_map/ppermute | solution.py:53
  364.2 215.3 %reduce-scatter.11.cloned.1.call-start = ((), (), s32[]{:S(2)}) async-start(), calls=%async_computation.17 | async-start | bytes 7208960 | tf_op jit(solution)/shard_map/reduce_scatter | solution.py:505
  373.5 26.4 %collective-permute-start.47 = (bf16[512,2048]{1,0:T(8,128)(2,1)}, bf16[512,2048]{1,0:T(8,128)(2,1)}, u32[]{:S(2)}, u32[]{:S(2)}) collective-permute-start(bf16[512,2048]{1,0:T(8,128)(2,1)} %collective-permute-done.42), channel_id=1, source_target_pairs={{0,4},{1,3},{2,6},{3,1},{4,0},{5,7},{6,2},{7,5},{8,12},{9,11},{10,... | collective-permute-start | bytes 6291464 | tf_op jit(solution)/shard_map/ppermute | solution.py:53
  409.7 22.0 %collective-permute-start.51 = (bf16[704,2048]{1,0:T(8,128)(2,1)}, bf16[704,2048]{1,0:T(8,128)(2,1)S(1)}, u32[]{:S(2)}, u32[]{:S(2)}) collective-permute-start(bf16[704,2048]{1,0:T(8,128)(2,1)} %convolution_convert_fusion.7), channel_id=1, source_target_pairs={{0,1},{1,0},{2,3},{3,2},{4,5},{5,4},{6,7},{7,6},{8,9},{9,8},{10,11... | collective-permute-start | bytes 8650760 | tf_op jit(solution)/shard_map/ppermute | solution.py:53
  409.8 23.1 %collective-permute-start.52 = (bf16[704,2048]{1,0:T(8,128)(2,1)}, bf16[704,2048]{1,0:T(8,128)(2,1)S(1)}, u32[]{:S(2)}, u32[]{:S(2)}) collective-permute-start(bf16[704,2048]{1,0:T(8,128)(2,1)} %convolution_convert_fusion.5), channel_id=1, source_target_pairs={{0,1},{1,0},{2,3},{3,2},{4,5},{5,4},{6,7},{7,6},{8,9},{9,8},{10,11... | collective-permute-start | bytes 8650760 | tf_op jit(solution)/shard_map/ppermute | solution.py:53
  411.1 23.1 %collective-permute-start.53 = (bf16[704,2048]{1,0:T(8,128)(2,1)}, bf16[704,2048]{1,0:T(8,128)(2,1)S(1)}, u32[]{:S(2)}, u32[]{:S(2)}) collective-permute-start(bf16[704,2048]{1,0:T(8,128)(2,1)} %convolution_convert_fusion.3), channel_id=1, source_target_pairs={{0,1},{1,0},{2,3},{3,2},{4,5},{5,4},{6,7},{7,6},{8,9},{9,8},{10,11... | collective-permute-start | bytes 8650760 | tf_op jit(solution)/shard_map/ppermute | solution.py:53
  417.1 20.9 %collective-permute-start.49 = (bf16[128,2048]{1,0:T(8,128)(2,1)S(1)}, bf16[128,2048]{1,0:T(8,128)(2,1)S(1)}, u32[]{:S(2)}, u32[]{:S(2)}) collective-permute-start(bf16[128,2048]{1,0:T(8,128)(2,1)S(1)} %get-tuple-element.179.refs_0_), channel_id=1, source_target_pairs={{0,4},{1,3},{2,6},{3,1},{4,0},{5,7},{6,2},{7,5},{8,12},{9,11},{10,... | collective-permute-start | bytes 1572872 | tf_op jit(solution)/shard_map/ppermute | solution.py:53
  440.8 40.3 %collective-permute-start.58 = (bf16[352,2048]{1,0:T(8,128)(2,1)}, bf16[352,2048]{1,0:T(8,128)(2,1)S(1)}, u32[]{:S(2)}, u32[]{:S(2)}) collective-permute-start(bf16[352,2048]{1,0:T(8,128)(2,1)} %slice.400), channel_id=1, source_target_pairs={{0,4},{1,3},{2,6},{3,1},{4,0},{5,7},{6,2},{7,5},{8,12},{9,11},{10,... | collective-permute-start | bytes 4325384 | tf_op jit(solution)/shard_map/ppermute | solution.py:53
  443.5 41.6 %collective-permute-start.60 = (bf16[352,2048]{1,0:T(8,128)(2,1)}, bf16[352,2048]{1,0:T(8,128)(2,1)}, u32[]{:S(2)}, u32[]{:S(2)}) collective-permute-start(bf16[352,2048]{1,0:T(8,128)(2,1)} %slice.398), channel_id=1, source_target_pairs={{0,4},{1,3},{2,6},{3,1},{4,0},{5,7},{6,2},{7,5},{8,12},{9,11},{10,... | collective-permute-start | bytes 4325384 | tf_op jit(solution)/shard_map/ppermute | solution.py:53
  447.0 44.0 %collective-permute-start.59 = (bf16[352,2048]{1,0:T(8,128)(2,1)}, bf16[352,2048]{1,0:T(8,128)(2,1)}, u32[]{:S(2)}, u32[]{:S(2)}) collective-permute-start(bf16[352,2048]{1,0:T(8,128)(2,1)} %slice.399), channel_id=1, source_target_pairs={{0,4},{1,3},{2,6},{3,1},{4,0},{5,7},{6,2},{7,5},{8,12},{9,11},{10,... | collective-permute-start | bytes 4325384 | tf_op jit(solution)/shard_map/ppermute | solution.py:53
  476.2 36.0 %all-to-all-start.3 = ((bf16[2,2,64,2048]{3,2,1,0:T(8,128)(2,1)}), bf16[2,2,64,2048]{3,2,1,0:T(8,128)(2,1)}, u32[]{:S(2)}, u32[]{:S(2)}) async-start(bf16[2,2,64,2048]{3,2,1,0:T(8,128)(2,1)} %bitcast.258), calls=%async_computation.5 | async-start | bytes 2097152 | tf_op jit(solution)/shard_map/all_to_all | solution.py:520
  480.8 151.3 %reduce-scatter.9.cloned.1.call-start = ((), (), s32[]{:S(2)}) async-start(), calls=%async_computation.16 | async-start | bytes 7864320 | tf_op jit(solution)/shard_map/reduce_scatter | solution.py:548
  496.1 24.1 %collective-permute-start.61 = (bf16[512,2048]{1,0:T(8,128)(2,1)}, bf16[512,2048]{1,0:T(8,128)(2,1)}, u32[]{:S(2)}, u32[]{:S(2)}) collective-permute-start(bf16[512,2048]{1,0:T(8,128)(2,1)} %slice.228), channel_id=1, source_target_pairs={{0,1},{1,0},{2,3},{3,2},{4,5},{5,4},{6,7},{7,6},{8,9},{9,8},{10,11... | collective-permute-start | bytes 6291464 | tf_op jit(solution)/shard_map/ppermute | solution.py:53
  512.2 16.8 %collective-permute-start.67 = (bf16[512,2048]{1,0:T(8,128)(2,1)}, bf16[512,2048]{1,0:T(8,128)(2,1)}, u32[]{:S(2)}, u32[]{:S(2)}) collective-permute-start(bf16[512,2048]{1,0:T(8,128)(2,1)} %convolution_convert_fusion.9), channel_id=1, source_target_pairs={{0,1},{1,0},{2,3},{3,2},{4,5},{5,4},{6,7},{7,6},{8,9},{9,8},{10,11... | collective-permute-start | bytes 6291464 | tf_op jit(solution)/shard_map/ppermute | solution.py:53
  525.8 27.1 %collective-permute-start.62 = (bf16[256,2048]{1,0:T(8,128)(2,1)S(1)}, bf16[256,2048]{1,0:T(8,128)(2,1)S(1)}, u32[]{:S(2)}, u32[]{:S(2)}) collective-permute-start(bf16[256,2048]{1,0:T(8,128)(2,1)S(1)} %slice.402), channel_id=1, source_target_pairs={{0,4},{1,3},{2,6},{3,1},{4,0},{5,7},{6,2},{7,5},{8,12},{9,11},{10,... | collective-permute-start | bytes 3145736 | tf_op jit(solution)/shard_map/ppermute | solution.py:53
  527.9 80.6 %collective-permute-start.70 = (bf16[512,2048]{1,0:T(8,128)(2,1)}, bf16[512,2048]{1,0:T(8,128)(2,1)}, u32[]{:S(2)}, u32[]{:S(2)}) collective-permute-start(bf16[512,2048]{1,0:T(8,128)(2,1)} %all-gather.8.cloned.1.call-done), channel_id=1, source_target_pairs={{0,1},{1,0},{2,3},{3,2},{4,5},{5,4},{6,7},{7,6},{8,9},{9,8},{10,11... | collective-permute-start | bytes 6291464 | tf_op jit(solution)/shard_map/ppermute | solution.py:53
  528.4 83.3 %collective-permute-start.71 = (bf16[512,2048]{1,0:T(8,128)(2,1)}, bf16[512,2048]{1,0:T(8,128)(2,1)}, u32[]{:S(2)}, u32[]{:S(2)}) collective-permute-start(bf16[512,2048]{1,0:T(8,128)(2,1)} %collective-permute-done.42), channel_id=1, source_target_pairs={{0,1},{1,0},{2,3},{3,2},{4,5},{5,4},{6,7},{7,6},{8,9},{9,8},{10,11... | collective-permute-start | bytes 6291464 | tf_op jit(solution)/shard_map/ppermute | solution.py:53
  528.4 87.3 %collective-permute-start.72 = (bf16[512,2048]{1,0:T(8,128)(2,1)}, bf16[512,2048]{1,0:T(8,128)(2,1)}, u32[]{:S(2)}, u32[]{:S(2)}) collective-permute-start(bf16[512,2048]{1,0:T(8,128)(2,1)} %collective-permute-done.43), channel_id=1, source_target_pairs={{0,1},{1,0},{2,3},{3,2},{4,5},{5,4},{6,7},{7,6},{8,9},{9,8},{10,11... | collective-permute-start | bytes 6291464 | tf_op jit(solution)/shard_map/ppermute | solution.py:53
  535.6 21.2 %collective-permute-start.68 = (bf16[256,2048]{1,0:T(8,128)(2,1)}, bf16[256,2048]{1,0:T(8,128)(2,1)}, u32[]{:S(2)}, u32[]{:S(2)}) collective-permute-start(bf16[256,2048]{1,0:T(8,128)(2,1)} %slice.401), channel_id=1, source_target_pairs={{0,4},{1,3},{2,6},{3,1},{4,0},{5,7},{6,2},{7,5},{8,12},{9,11},{10,... | collective-permute-start | bytes 3145736 | tf_op jit(solution)/shard_map/ppermute | solution.py:53
  538.0 14.4 %all-to-all-start.6 = ((f32[8,1,128]{2,1,0:T(1,128)}), f32[8,1,128]{2,1,0:T(1,128)S(1)}, u32[]{:S(2)}, u32[]{:S(2)}) async-start(f32[8,1,128]{2,1,0:T(1,128)} %bitcast.72), calls=%async_computation.10 | async-start | bytes 8192 | tf_op jit(solution)/shard_map/all_to_all | solution.py:572
  553.9 67.0 %collective-permute-start.73 = (bf16[512,2048]{1,0:T(8,128)(2,1)}, bf16[512,2048]{1,0:T(8,128)(2,1)}, u32[]{:S(2)}, u32[]{:S(2)}) collective-permute-start(bf16[512,2048]{1,0:T(8,128)(2,1)} %collective-permute-done.47), channel_id=1, source_target_pairs={{0,1},{1,0},{2,3},{3,2},{4,5},{5,4},{6,7},{7,6},{8,9},{9,8},{10,11... | collective-permute-start | bytes 6291464 | tf_op jit(solution)/shard_map/ppermute | solution.py:53
  568.7 62.1 %all-to-all-start.4 = ((f32[32,3,128]{2,1,0:T(4,128)}), f32[32,3,128]{2,1,0:T(4,128)S(1)}, u32[]{:S(2)}, u32[]{:S(2)}) async-start(f32[32,3,128]{2,1,0:T(4,128)} %reshape.695), calls=%async_computation.7 | async-start | bytes 131072 | tf_op jit(solution)/shard_map/all_to_all | solution.py:608
  584.4 41.1 %collective-permute-start.66 = (bf16[176,2048]{1,0:T(8,128)(2,1)S(1)}, bf16[176,2048]{1,0:T(8,128)(2,1)S(1)}, u32[]{:S(2)}, u32[]{:S(2)}) collective-permute-start(bf16[176,2048]{1,0:T(8,128)(2,1)S(1)} %slice.404), channel_id=1, source_target_pairs={{0,2},{1,5},{2,0},{3,7},{4,6},{5,1},{6,4},{7,3},{8,10},{9,13},{10,... | collective-permute-start | bytes 2162696 | tf_op jit(solution)/shard_map/ppermute | solution.py:53
  608.6 17.1 %collective-permute-start.65 = (bf16[176,2048]{1,0:T(8,128)(2,1)S(1)}, bf16[176,2048]{1,0:T(8,128)(2,1)S(1)}, u32[]{:S(2)}, u32[]{:S(2)}) collective-permute-start(bf16[176,2048]{1,0:T(8,128)(2,1)S(1)} %slice.405), channel_id=1, source_target_pairs={{0,2},{1,5},{2,0},{3,7},{4,6},{5,1},{6,4},{7,3},{8,10},{9,13},{10,... | collective-permute-start | bytes 2162696 | tf_op jit(solution)/shard_map/ppermute | solution.py:53
  611.6 16.0 %collective-permute-start.64 = (bf16[176,2048]{1,0:T(8,128)(2,1)S(1)}, bf16[176,2048]{1,0:T(8,128)(2,1)S(1)}, u32[]{:S(2)}, u32[]{:S(2)}) collective-permute-start(bf16[176,2048]{1,0:T(8,128)(2,1)S(1)} %slice.406), channel_id=1, source_target_pairs={{0,2},{1,5},{2,0},{3,7},{4,6},{5,1},{6,4},{7,3},{8,10},{9,13},{10,... | collective-permute-start | bytes 2162696 | tf_op jit(solution)/shard_map/ppermute | solution.py:53
  635.2 16.1 %all-to-all-start.5 = ((bf16[8,64,768]{2,1,0:T(8,128)(2,1)}), bf16[8,64,768]{2,1,0:T(8,128)(2,1)S(1)}, u32[]{:S(2)}, u32[]{:S(2)}) async-start(bf16[8,64,768]{2,1,0:T(8,128)(2,1)} %reshape.697), calls=%async_computation.9 | async-start | bytes 1572864 | tf_op jit(solution)/shard_map/all_to_all | solution.py:555
  (120 other events, 1382.2 us)
Sparse Core Ops, SparseCore 0:
  9.6 30.6 all-gather.11
  42.4 68.4 all-gather.5
  112.5 44.3 all-gather.7
  197.3 56.2 all-gather.9
  255.7 108.4 reduce-scatter.4
  366.3 43.3 reduce-scatter.6
  412.1 101.5 reduce-scatter.10
  518.9 111.1 reduce-scatter.8

commit v5 on v4

--- a/solution.py
+++ b/solution.py
@@ -529,6 +529,7 @@
         [qkv_own_grad.reshape(planes, flat_rows, width), out_own_grad, shared_part], axis=1
     )
     (
+        joined,
         normed1_grad,
         bias_part,
         unit_grads,
@@ -537,6 +538,7 @@
         gated_act,
     ) = barrier(
         (
+            joined,
             normed1_grad,
             bias_part.reshape(-1),
             unit_grads,

time: 669 us -> 666 us (level)
    unnamed x215 -> x211, local copies, waits for them, and re-layouts: 58.6 us -> 58.5 us
where the time goes in v5:
time: 666 us; the launch traced here: 659 us
  matrix products  167 us (25%)
  waiting for transfers between devices  164 us (25%)
  local copies, waits for them, and re-layouts  129 us (19%)
  starting transfers between devices  83.9 us (13%)
  other arithmetic  63 us (9%)
  Pallas kernels  34.3 us (5%)
  between operations  17.5 us (3%)
    dot_general x33, matrix products, dot(): return lax.dot_general(a, b, (dims, ((), ())), preferred_element_type=F32)  163 us
    ppermute x74, waiting for transfers between devices, send(): return lax.ppermute(block, 'expert', [(i, target(i)) for i in range(size)])  80.8 us
    unnamed x211, local copies, waits for them, and re-layouts  58.5 us
    ppermute x74, starting transfers between devices, send(): return lax.ppermute(block, 'expert', [(i, target(i)) for i in range(size)])  54.6 us
    add x9, other arithmetic, sum_hop(): return near[:half] + send(near[half:].astype(BF16), size, hop).astype(F32)  22.7 us
    pallas_call x1, Pallas kernels, attend_back(): pl.pallas_call(functools.partial(attend_back_kernel, own // HEAD, size),...  22.2 us
    all_gather x1, waiting for transfers between devices, shards(): lax.all_gather(by_head, 'dp', axis=0, tiled=True)  19.1 us
    dynamic_update_slice x16, local copies, waits for them, and re-layouts, plane_rows(): lax.dynamic_update_slice_in_dim(whole, part, source * rows, 0)  15.5 us
  transfers between devices with their start and end apart: 89, of which 27 were waited for; matrix products, arithmetic and copies ran while one was open for 50% of the time, Pallas kernels for 5%

profile of v5, /device:TPU:0, one launch (start us, length us, event | category | flops | bytes accessed | tf_op | source)
XLA Modules:
  0.0 658.5 jit_solution(14126336756656445128)
XLA Ops:
  12.2 5.2 all-to-all-start
  19.0 11.0 %all-to-all-done = bf16[8,64,768]{2,1,0:T(8,128)(2,1)S(1)} async-done(((bf16[8,64,768]{2,1,0:T(8,128)(2,1)}), bf16[8,64,768]{2,1,0:T(8,128)(2,1)S(1)}, u32[]{:S(2)}, u32[]{:S(2)}) %all-to-all-start) | async-done | bytes 786464 | tf_op jit(solution)/shard_map/all_to_all | solution.py:343
  32.8 11.4 %collective-permute-done = bf16[128,2048]{1,0:T(8,128)(2,1)} collective-permute-done((bf16[128,2048]{1,0:T(8,128)(2,1)S(1)}, bf16[128,2048]{1,0:T(8,128)(2,1)}, u32[]{:S(2)}, u32[]{:S(2)}) %collective-permute-start) | collective-permute-done | bytes 524320 | tf_op jit(solution)/shard_map/ppermute | solution.py:53
  53.8 4.7 all-to-all-start.1
  68.4 6.9 %all-to-all-done.1 = f32[32,12,128]{2,1,0:T(8,128)S(1)} async-done(((f32[32,12,128]{2,1,0:T(8,128)}), f32[32,12,128]{2,1,0:T(8,128)S(1)}, u32[]{:S(2)}, u32[]{:S(2)}) %all-to-all-start.1) | async-done | bytes 196640 | tf_op jit(solution)/shard_map/all_to_all | solution.py:348
  81.6 7.8 %collective-permute-done.9 = bf16[2,2,64,2048]{3,2,1,0:T(8,128)(2,1)} collective-permute-done((bf16[2,2,64,2048]{3,2,1,0:T(8,128)(2,1)}, bf16[2,2,64,2048]{3,2,1,0:T(8,128)(2,1)}, u32[]{:S(2)}, u32[]{:S(2)}) %collective-permute-start.9) | collective-permute-done | bytes 1048608 | tf_op jit(solution)/shard_map/ppermute | solution.py:53
  91.8 19.1 %all-gather.6.cloned.1.call-done = bf16[32,64,768]{2,1,0:T(8,128)(2,1)} async-done(((bf16[8,64,768]{2,1,0:T(8,128)(2,1)}), bf16[32,64,768]{2,1,0:T(8,128)(2,1)}) %all-gather.6.cloned.1.call-update) | async-done | bytes 3145744 | tf_op jit(solution)/shard_map/all_gather | solution.py:346
  113.1 12.2 %attend.1 = (bf16[1024,2048]{1,0:T(8,128)(2,1)}, bf16[1024,768]{1,0:T(8,128)(2,1)S(1)}, bf16[1024,256]{1,0:T(8,128)(2,1)S(1)}) custom-call(bf16[1024,2048]{1,0:T(8,128)(2,1)} %constant_dynamic-update-slice_fusion.32.tokens, f32[1,2048]{1,0:T(1,128)S(1)} %broadcast_in_dim_reshape.4.gain, bf16[2048,768]{1,0:T(8,128)(2,1)S(1)} %bitcast.264, ...), custom_call_target="tpu_custom_call" | custom-call | tf_op jit(solution)/shard_map/attend/pallas_call | solution.py:192
  138.4 3.5 collective-permute-done.16
  141.9 10.1 %collective-permute-done.13 = bf16[1024,256]{1,0:T(8,128)(2,1)S(1)} collective-permute-done((bf16[1024,256]{1,0:T(8,128)(2,1)S(1)}, bf16[1024,256]{1,0:T(8,128)(2,1)S(1)}, u32[]{:S(2)}, u32[]{:S(2)}) %collective-permute-start.13) | collective-permute-done | bytes 524320 | tf_op jit(solution)/shard_map/ppermute | solution.py:53
  152.0 4.9 all-gather.8.cloned.1.call-done
  164.3 5.6 collective-permute-done.17
  171.9 4.0 fusion.18
  179.5 11.4 %multiply_reduce_fusion = (f32[1024]{0:T(1024)S(1)}, f32[1024,2048]{1,0:T(8,128)S(1)}) fusion(bf16[1024,2048]{1,0:T(8,128)(2,1)} %constant_dynamic-update-slice_fusion.32.tokens, bf16[1024,2048]{1,0:T(8,128)(2,1)S(1)} %constant_dynamic-update-slice_fusion.24, bf16[2048,2048]{1,0:T(8,128)(2,1)S(1)} %bitcast.270), kind=kOutput, calls=%fused_computation.6 | convolution fusion | flops 8598322176 | bytes 25169920 | tf_op jit(solution)/shard_map/dot_general | solution.py:21
  197.2 4.5 convolution_convert_fusion.13
  203.8 9.3 %fusion.2 = f32[464,2816]{1,0:T(8,128)S(1)} fusion(bf16[464,2048]{1,0:T(8,128)(2,1)S(1)} %convolution_convert_fusion.13, bf16[1,2048,2816]{2,1,0:T(8,128)(2,1)} %param.32), kind=kOutput, calls=%fused_computation.3 | convolution fusion | flops 5351931904 | bytes 18661376 | tf_op jit(solution)/shard_map/dot_general | solution.py:21
  213.2 6.0 multiply_convert_fusion.8
  221.9 4.3 all-to-all-start.2
  229.1 5.5 convolution_convert_fusion.1
  239.3 9.4 %fusion.13 = bf16[464,2048]{1,0:T(8,128)(2,1)} fusion(bf16[464,2816]{1,0:T(8,128)(2,1)S(1)} %pad_maximum_fusion.2, bf16[1,2048,2816]{2,1,0:T(8,128)(2,1)} %param.32), kind=kOutput, calls=%fused_computation.50 | convolution fusion | flops 5352882176 | bytes 16048128 | tf_op jit(solution)/shard_map/dot_general | solution.py:21
  248.8 2.7 constant_dynamic-update-slice_fusion.14
  251.5 2.8 constant_dynamic-update-slice_fusion.13
  259.5 5.3 convolution_convert_fusion
  287.3 2.8 constant_dynamic-update-slice_fusion.9
  290.1 2.8 constant_dynamic-update-slice_fusion.8
  292.9 11.3 %fusion.92 = f32[512,2816]{1,0:T(8,128)} fusion(bf16[512,2048]{1,0:T(8,128)(2,1)S(1)} %copy-done.14, bf16[2816,2048]{1,0:T(8,128)(2,1)} %bitcast.299), kind=kOutput, calls=%fused_computation.275 | convolution fusion | flops 5905580032 | bytes 19398656 | tf_op jit(solution)/shard_map/dot_general | solution.py:21
  304.3 7.7 %multiply_convert_fusion.7 = (bf16[512,1408]{1,0:T(8,128)(2,1)S(1)}, bf16[512,1408]{1,0:T(8,128)(2,1)S(1)}, bf16[512,1408]{1,0:T(8,128)(2,1)S(1)}) fusion(f32[512,2816]{1,0:T(8,128)} %fusion.92, bf16[1408,2048]{1,0:T(8,128)(2,1)S(1)} %bitcast.304, bf16[512,2048]{1,0:T(8,128)(2,1)} %all-gather.8.cloned.1.call-done, f32[512]{0:T(512)S(1)} %add_divide_fusion.2, ...), kind=kOutput, calls=%fused_computation.63 | convolution fusion | flops 2967076864 | bytes 17960960 | tf_op jit(solution)/shard_map/dot_general | solution.py:21
  312.0 3.5 convert_add_fusion.6
  317.5 8.9 %multiply_reduce_fusion.1 = (f32[512]{0:T(512)S(1)}, bf16[512,2048]{1,0:T(8,128)(2,1)}) fusion(bf16[512,2048]{1,0:T(8,128)(2,1)} %all-gather.8.cloned.1.call-done, f32[512]{0:T(512)S(1)} %fusion.83, f32[512]{0:T(512)S(1)} %add_divide_fusion.2, bf16[512,1408]{1,0:T(8,128)(2,1)S(1)} %get-tuple-element.239, ...), kind=kOutput, calls=%fused_computation.29 | convolution fusion | flops 2959080960 | bytes 11409408 | tf_op jit(solution)/shard_map/dot_general | solution.py:21
  328.5 6.0 collective-permute-done.42
  334.5 7.8 %collective-permute-done.45 = bf16[256,2048]{1,0:T(8,128)(2,1)S(1)} collective-permute-done((bf16[256,2048]{1,0:T(8,128)(2,1)S(1)}, bf16[256,2048]{1,0:T(8,128)(2,1)S(1)}, u32[]{:S(2)}, u32[]{:S(2)}) %collective-permute-start.45) | collective-permute-done | bytes 1048608 | tf_op jit(solution)/shard_map/ppermute | solution.py:53
  344.9 7.4 %add_convert_fusion = bf16[512,2048]{1,0:T(8,128)(2,1)} fusion(bf16[512,2816]{1,0:T(8,128)(2,1)S(1)} %pad_maximum_fusion.1, bf16[2816,2048]{1,0:T(8,128)(2,1)S(1)} %bitcast.302, f32[512]{0:T(512)S(1)} %subtract_multiply_fusion, f32[2048]{0:T(1024)S(1)} %mul.337), kind=kOutput, calls=%fused_computation.28 | convolution fusion | flops 5908725760 | bytes 16525312 | tf_op jit(solution)/shard_map/dot_general | solution.py:21
  354.8 9.4 %reduce-scatter.5.cloned.1.call-done = bf16[512,1408]{1,0:T(8,128)(2,1)} async-done(((bf16[2048,1408]{1,0:T(8,128)(2,1)}), bf16[512,1408]{1,0:T(8,128)(2,1)}) %reduce-scatter.5.cloned.1.call-update) | async-done | bytes 1441808 | tf_op jit(solution)/shard_map/reduce_scatter | solution.py:463
  364.3 8.6 %multiply_reduce_fusion.2 = (f32[464]{0:T(512)S(1)}, bf16[464,2048]{1,0:T(8,128)(2,1)}) fusion(f32[464,2048]{1,0:T(8,128)} %fusion.18, f32[464]{0:T(512)S(1)} %select_reduce_fusion.1, bf16[464,1408]{1,0:T(8,128)(2,1)} %get-tuple-element.228, bf16[1,1408,2048]{2,1,0:T(8,128)(2,1)} %param.33), kind=kOutput, calls=%fused_computation.33 | convolution fusion | flops 2679766528 | bytes 12779136 | tf_op jit(solution)/shard_map/dot_general | solution.py:21
  374.4 5.2 convolution_convert_fusion.7
  379.6 5.1 convolution_convert_fusion.8
  384.8 3.5 convolution_convert_fusion.3
  388.2 3.3 convolution_convert_fusion.4
  391.5 3.5 convolution_convert_fusion.5
  395.0 3.5 convolution_convert_fusion.6
  399.3 10.4 %reduce-scatter.7.cloned.1.call-done = bf16[128,2048]{1,0:T(8,128)(2,1)} async-done(((bf16[512,2048]{1,0:T(8,128)(2,1)}), bf16[128,2048]{1,0:T(8,128)(2,1)}) %reduce-scatter.7.cloned.1.call-update) | async-done | bytes 524304 | tf_op jit(solution)/shard_map/reduce_scatter | solution.py:490
  412.8 2.9 fusion.87
  418.6 11.2 %collective-permute-done.48.refs_1_ = bf16[128,2048]{1,0:T(8,128)(2,1)S(1)} collective-permute-done((bf16[128,2048]{1,0:T(8,128)(2,1)S(1)}, bf16[128,2048]{1,0:T(8,128)(2,1)S(1)}, u32[]{:S(2)}, u32[]{:S(2)}) %collective-permute-start.48) | collective-permute-done | bytes 524320 | tf_op jit(solution)/shard_map/ppermute | solution.py:53
  450.7 22.2 %attend_back.1 = (bf16[1024,2048]{1,0:T(8,128)(2,1)}, bf16[1024,768]{1,0:T(8,128)(2,1)}, bf16[256,2048]{1,0:T(8,128)(2,1)}, f32[1,768]{1,0:T(1,128)}) custom-call(s32[8]{0:T(128)} %copy-done.67, bf16[128,2048]{1,0:T(8,128)(2,1)} %copy-done.33, bf16[128,2048]{1,0:T(8,128)(2,1)} %copy-done.45, bf16[128,2048]{1,0:T(8,128)(2,1)} %copy-done.46, ...), custom_call_target="tpu_custom_call" | custom-call | tf_op jit(solution)/shard_map/attend_back/pallas_call | solution.py:269
  475.2 4.4 all-to-all-start.3
  480.0 4.1 convert_add_fusion.9
  484.1 4.9 convolution_convert_fusion.2
  489.0 5.5 reshape.687
  494.5 6.7 %pad_maximum_fusion = bf16[4,384,2048]{2,1,0:T(8,128)(2,1)} fusion(bf16[4,128,2048]{2,1,0:T(8,128)(2,1)} %bitcast.275, bf16[4,64,2048]{2,1,0:T(8,128)(2,1)} %bitcast.60, bf16[4,192,2048]{2,1,0:T(8,128)(2,1)S(1)} %reshape.687), kind=kLoop, calls=%fused_computation.12 | loop fusion | flops 18874368 | bytes 12582912 | tf_op jit(solution)/shard_map/concatenate | solution.py:528
  501.2 4.3 convert_add_fusion.7
  505.6 4.5 convert_add_fusion.8
  515.8 3.0 convert_add_fusion.5
  523.9 3.6 convert_add_fusion.4
  532.6 3.3 all-to-all-start.6
  536.1 11.2 %all-to-all-done.6 = f32[8,1,128]{2,1,0:T(1,128)S(1)} async-done(((f32[8,1,128]{2,1,0:T(1,128)}), f32[8,1,128]{2,1,0:T(1,128)S(1)}, u32[]{:S(2)}, u32[]{:S(2)}) %all-to-all-start.6) | async-done | bytes 4128 | tf_op jit(solution)/shard_map/all_to_all | solution.py:574
  557.0 3.9 collective-permute-done.63
  563.7 3.0 all-to-all-start.4
  566.7 3.8 collective-permute-done.69
  574.3 5.0 maximum_convert_fusion
  581.0 3.2 fusion.16
  585.0 6.2 constant_dynamic-slice_fusion
  615.9 4.5 add_bitcast_fusion
  631.6 3.7 all-to-all-start.5
  639.3 8.5 %all-to-all-done.5 = bf16[8,64,768]{2,1,0:T(8,128)(2,1)S(1)} async-done(((bf16[8,64,768]{2,1,0:T(8,128)(2,1)}), bf16[8,64,768]{2,1,0:T(8,128)(2,1)S(1)}, u32[]{:S(2)}, u32[]{:S(2)}) %all-to-all-start.5) | async-done | bytes 786464 | tf_op jit(solution)/shard_map/all_to_all | solution.py:557
  (528 shorter events, 229.3 us)
Async XLA Ops:
  7.2 45.9 %all-gather.12.cloned.1.call-start = ((), (), s32[]{:S(2)}) async-start(), calls=%async_computation.18 | async-start | bytes 1310720 | tf_op jit(solution)/shard_map/all_gather | solution.py:340
  12.2 17.8 %all-to-all-start = ((bf16[8,64,768]{2,1,0:T(8,128)(2,1)}), bf16[8,64,768]{2,1,0:T(8,128)(2,1)S(1)}, u32[]{:S(2)}, u32[]{:S(2)}) async-start(bf16[8,64,768]{2,1,0:T(8,128)(2,1)} %reshape.678), calls=%async_computation | async-start | bytes 1572864 | tf_op jit(solution)/shard_map/all_to_all | solution.py:343
  17.4 93.6 %all-gather.6.cloned.1.call-start = ((), (), s32[]{:S(2)}) async-start(), calls=%async_computation.11 | async-start | bytes 3932160 | tf_op jit(solution)/shard_map/all_gather | solution.py:346
  30.0 14.2 %collective-permute-start = (bf16[128,2048]{1,0:T(8,128)(2,1)S(1)}, bf16[128,2048]{1,0:T(8,128)(2,1)}, u32[]{:S(2)}, u32[]{:S(2)}) collective-permute-start(bf16[128,2048]{1,0:T(8,128)(2,1)S(1)} %copy-done.16), channel_id=1, source_target_pairs={{0,2},{1,5},{2,0},{3,7},{4,6},{5,1},{6,4},{7,3},{8,10},{9,13},{10,... | collective-permute-start | bytes 1572872 | tf_op jit(solution)/shard_map/ppermute | solution.py:53
  30.9 17.8 %collective-permute-start.1 = (bf16[128,2048]{1,0:T(8,128)(2,1)S(1)}, bf16[128,2048]{1,0:T(8,128)(2,1)}, u32[]{:S(2)}, u32[]{:S(2)}) collective-permute-start(bf16[128,2048]{1,0:T(8,128)(2,1)S(1)} %copy-done.16), channel_id=1, source_target_pairs={{0,4},{1,3},{2,6},{3,1},{4,0},{5,7},{6,2},{7,5},{8,12},{9,11},{10,... | collective-permute-start | bytes 1572872 | tf_op jit(solution)/shard_map/ppermute | solution.py:53
  31.6 29.6 %collective-permute-start.3 = (bf16[128,2048]{1,0:T(8,128)(2,1)S(1)}, bf16[128,2048]{1,0:T(8,128)(2,1)}, u32[]{:S(2)}, u32[]{:S(2)}) collective-permute-start(bf16[128,2048]{1,0:T(8,128)(2,1)S(1)} %copy-done.16), channel_id=1, source_target_pairs={{0,1},{1,0},{2,3},{3,2},{4,5},{5,4},{6,7},{7,6},{8,9},{9,8},{10,11... | collective-permute-start | bytes 1572872 | tf_op jit(solution)/shard_map/ppermute | solution.py:53
  31.6 93.7 %collective-permute-start.14 = (bf16[128,2048]{1,0:T(8,128)(2,1)}, bf16[128,2048]{1,0:T(8,128)(2,1)}, u32[]{:S(2)}, u32[]{:S(2)}) collective-permute-start(bf16[128,2048]{1,0:T(8,128)(2,1)} %param.23), channel_id=1, source_target_pairs={{0,2},{1,5},{2,0},{3,7},{4,6},{5,1},{6,4},{7,3},{8,10},{9,13},{10,... | collective-permute-start | bytes 1572872 | tf_op jit(solution)/shard_map/ppermute | solution.py:53
  44.2 14.3 %collective-permute-start.2 = (bf16[128,2048]{1,0:T(8,128)(2,1)}, bf16[128,2048]{1,0:T(8,128)(2,1)S(1)}, u32[]{:S(2)}, u32[]{:S(2)}) collective-permute-start(bf16[128,2048]{1,0:T(8,128)(2,1)} %collective-permute-done), channel_id=1, source_target_pairs={{0,4},{1,3},{2,6},{3,1},{4,0},{5,7},{6,2},{7,5},{8,12},{9,11},{10,... | collective-permute-start | bytes 1572872 | tf_op jit(solution)/shard_map/ppermute | solution.py:53
  48.7 15.8 %collective-permute-start.4 = (bf16[128,2048]{1,0:T(8,128)(2,1)}, bf16[128,2048]{1,0:T(8,128)(2,1)}, u32[]{:S(2)}, u32[]{:S(2)}) collective-permute-start(bf16[128,2048]{1,0:T(8,128)(2,1)} %collective-permute-done), channel_id=1, source_target_pairs={{0,1},{1,0},{2,3},{3,2},{4,5},{5,4},{6,7},{7,6},{8,9},{9,8},{10,11... | collective-permute-start | bytes 1572872 | tf_op jit(solution)/shard_map/ppermute | solution.py:53
  48.7 17.8 %collective-permute-start.5 = (bf16[128,2048]{1,0:T(8,128)(2,1)}, bf16[128,2048]{1,0:T(8,128)(2,1)}, u32[]{:S(2)}, u32[]{:S(2)}) collective-permute-start(bf16[128,2048]{1,0:T(8,128)(2,1)} %collective-permute-done.1), channel_id=1, source_target_pairs={{0,1},{1,0},{2,3},{3,2},{4,5},{5,4},{6,7},{7,6},{8,9},{9,8},{10,11... | collective-permute-start | bytes 1572872 | tf_op jit(solution)/shard_map/ppermute | solution.py:53
  53.8 21.5 %all-to-all-start.1 = ((f32[32,12,128]{2,1,0:T(8,128)}), f32[32,12,128]{2,1,0:T(8,128)S(1)}, u32[]{:S(2)}, u32[]{:S(2)}) async-start(f32[32,12,128]{2,1,0:T(8,128)} %broadcast_in_dim.177), calls=%async_computation.1 | async-start | bytes 524288 | tf_op jit(solution)/shard_map/all_to_all | solution.py:348
  58.5 98.4 %all-gather.8.cloned.1.call-start = ((), (), s32[]{:S(2)}) async-start(), calls=%async_computation.12 | async-start | bytes 2621440 | tf_op jit(solution)/shard_map/all_gather | solution.py:378
  58.5 68.3 %collective-permute-start.10 = (bf16[2,2,64,2048]{3,2,1,0:T(8,128)(2,1)}, bf16[2,2,64,2048]{3,2,1,0:T(8,128)(2,1)S(1)}, u32[]{:S(2)}, u32[]{:S(2)}) collective-permute-start(bf16[2,2,64,2048]{3,2,1,0:T(8,128)(2,1)} %bitcast.289), channel_id=1, source_target_pairs={{0,4},{1,3},{2,6},{3,1},{4,0},{5,7},{6,2},{7,5},{8,12},{9,11},{10,... | collective-permute-start | bytes 3145736 | tf_op jit(solution)/shard_map/ppermute | solution.py:53
  61.2 28.2 %collective-permute-start.9 = (bf16[2,2,64,2048]{3,2,1,0:T(8,128)(2,1)}, bf16[2,2,64,2048]{3,2,1,0:T(8,128)(2,1)}, u32[]{:S(2)}, u32[]{:S(2)}) collective-permute-start(bf16[2,2,64,2048]{3,2,1,0:T(8,128)(2,1)} %bitcast.290), channel_id=1, source_target_pairs={{0,2},{1,5},{2,0},{3,7},{4,6},{5,1},{6,4},{7,3},{8,10},{9,13},{10,... | collective-permute-start | bytes 3145736 | tf_op jit(solution)/shard_map/ppermute | solution.py:53
  78.0 51.5 %collective-permute-start.8 = (bf16[2,176,2048]{2,1,0:T(8,128)(2,1)S(1)}, bf16[2,176,2048]{2,1,0:T(8,128)(2,1)}, u32[]{:S(2)}, u32[]{:S(2)}) collective-permute-start(bf16[2,176,2048]{2,1,0:T(8,128)(2,1)S(1)} %bitcast.285), channel_id=1, source_target_pairs={{0,4},{1,3},{2,6},{3,1},{4,0},{5,7},{6,2},{7,5},{8,12},{9,11},{10,... | collective-permute-start | bytes 4325384 | tf_op jit(solution)/shard_map/ppermute | solution.py:53
  79.4 50.2 %collective-permute-start.7 = (bf16[2,176,2048]{2,1,0:T(8,128)(2,1)S(1)}, bf16[2,176,2048]{2,1,0:T(8,128)(2,1)}, u32[]{:S(2)}, u32[]{:S(2)}) collective-permute-start(bf16[2,176,2048]{2,1,0:T(8,128)(2,1)S(1)} %bitcast.286), channel_id=1, source_target_pairs={{0,2},{1,5},{2,0},{3,7},{4,6},{5,1},{6,4},{7,3},{8,10},{9,13},{10,... | collective-permute-start | bytes 4325384 | tf_op jit(solution)/shard_map/ppermute | solution.py:53
  89.4 40.1 %collective-permute-start.11 = (bf16[2,2,64,2048]{3,2,1,0:T(8,128)(2,1)}, bf16[2,2,64,2048]{3,2,1,0:T(8,128)(2,1)}, u32[]{:S(2)}, u32[]{:S(2)}) collective-permute-start(bf16[2,2,64,2048]{3,2,1,0:T(8,128)(2,1)} %collective-permute-done.9), channel_id=1, source_target_pairs={{0,4},{1,3},{2,6},{3,1},{4,0},{5,7},{6,2},{7,5},{8,12},{9,11},{10,... | collective-permute-start | bytes 3145736 | tf_op jit(solution)/shard_map/ppermute | solution.py:53
  110.9 169.3 %all-gather.10.cloned.1.call-start = ((), (), s32[]{:S(2)}) async-start(), calls=%async_computation.13 | async-start | bytes 2621440 | tf_op jit(solution)/shard_map/all_gather | solution.py:412
  126.8 15.0 %collective-permute-start.16 = (bf16[128,2048]{1,0:T(8,128)(2,1)}, bf16[128,2048]{1,0:T(8,128)(2,1)S(1)}, u32[]{:S(2)}, u32[]{:S(2)}) collective-permute-start(bf16[128,2048]{1,0:T(8,128)(2,1)} %collective-permute-done.14), channel_id=1, source_target_pairs={{0,4},{1,3},{2,6},{3,1},{4,0},{5,7},{6,2},{7,5},{8,12},{9,11},{10,... | collective-permute-start | bytes 1572872 | tf_op jit(solution)/shard_map/ppermute | solution.py:53
  135.1 16.8 %collective-permute-start.13 = (bf16[1024,256]{1,0:T(8,128)(2,1)S(1)}, bf16[1024,256]{1,0:T(8,128)(2,1)S(1)}, u32[]{:S(2)}, u32[]{:S(2)}) collective-permute-start(bf16[1024,256]{1,0:T(8,128)(2,1)S(1)} %get-tuple-element.128.refs_9_), channel_id=1, source_target_pairs={{0,4},{1,3},{2,6},{3,1},{4,0},{5,7},{6,2},{7,5},{8,12},{9,11},{10,... | collective-permute-start | bytes 1572872 | tf_op jit(solution)/shard_map/ppermute | solution.py:53
  136.7 15.3 %collective-permute-start.12 = (bf16[1024,256]{1,0:T(8,128)(2,1)S(1)}, bf16[1024,256]{1,0:T(8,128)(2,1)S(1)}, u32[]{:S(2)}, u32[]{:S(2)}) collective-permute-start(bf16[1024,256]{1,0:T(8,128)(2,1)S(1)} %get-tuple-element.128.refs_9_), channel_id=1, source_target_pairs={{0,2},{1,5},{2,0},{3,7},{4,6},{5,1},{6,4},{7,3},{8,10},{9,13},{10,... | collective-permute-start | bytes 1572872 | tf_op jit(solution)/shard_map/ppermute | solution.py:53
  176.0 25.6 %collective-permute-start.27 = (bf16[176,2048]{1,0:T(8,128)(2,1)S(1)}, bf16[176,2048]{1,0:T(8,128)(2,1)S(1)}, u32[]{:S(2)}, u32[]{:S(2)}) collective-permute-start(bf16[176,2048]{1,0:T(8,128)(2,1)S(1)} %copy-done.38), channel_id=1, source_target_pairs={{0,4},{1,3},{2,6},{3,1},{4,0},{5,7},{6,2},{7,5},{8,12},{9,11},{10,... | collective-permute-start | bytes 2162696 | tf_op jit(solution)/shard_map/ppermute | solution.py:53
  178.0 23.7 %collective-permute-start.26 = (bf16[176,2048]{1,0:T(8,128)(2,1)S(1)}, bf16[176,2048]{1,0:T(8,128)(2,1)}, u32[]{:S(2)}, u32[]{:S(2)}) collective-permute-start(bf16[176,2048]{1,0:T(8,128)(2,1)S(1)} %copy-done.38), channel_id=1, source_target_pairs={{0,2},{1,5},{2,0},{3,7},{4,6},{5,1},{6,4},{7,3},{8,10},{9,13},{10,... | collective-permute-start | bytes 2162696 | tf_op jit(solution)/shard_map/ppermute | solution.py:53
  201.7 32.9 %collective-permute-start.33 = (bf16[176,2048]{1,0:T(8,128)(2,1)}, bf16[176,2048]{1,0:T(8,128)(2,1)}, u32[]{:S(2)}, u32[]{:S(2)}) collective-permute-start(bf16[176,2048]{1,0:T(8,128)(2,1)} %collective-permute-done.26), channel_id=1, source_target_pairs={{0,4},{1,3},{2,6},{3,1},{4,0},{5,7},{6,2},{7,5},{8,12},{9,11},{10,... | collective-permute-start | bytes 2162696 | tf_op jit(solution)/shard_map/ppermute | solution.py:53
  202.1 32.5 %collective-permute-start.32 = (bf16[2,176,2048]{2,1,0:T(8,128)(2,1)}, bf16[2,176,2048]{2,1,0:T(8,128)(2,1)}, u32[]{:S(2)}, u32[]{:S(2)}) collective-permute-start(bf16[2,176,2048]{2,1,0:T(8,128)(2,1)} %collective-permute-done.7), channel_id=1, source_target_pairs={{0,4},{1,3},{2,6},{3,1},{4,0},{5,7},{6,2},{7,5},{8,12},{9,11},{10,... | collective-permute-start | bytes 4325384 | tf_op jit(solution)/shard_map/ppermute | solution.py:53
  221.9 132.9 %all-to-all-start.2 = ((bf16[4,464,352]{2,1,0:T(8,128)(2,1)}), bf16[4,464,352]{2,1,0:T(8,128)(2,1)}, u32[]{:S(2)}, u32[]{:S(2)}) async-start(bf16[4,464,352]{2,1,0:T(8,128)(2,1)} %bitcast.257), calls=%async_computation.3 | async-start | bytes 2850816 | tf_op jit(solution)/shard_map/all_to_all | solution.py:448
  226.3 137.9 %reduce-scatter.5.cloned.1.call-start = ((), (), s32[]{:S(2)}) async-start(), calls=%async_computation.14 | async-start | bytes 7208960 | tf_op jit(solution)/shard_map/reduce_scatter | solution.py:463
  234.6 36.4 %collective-permute-start.34 = (bf16[176,2048]{1,0:T(8,128)(2,1)S(1)}, bf16[176,2048]{1,0:T(8,128)(2,1)}, u32[]{:S(2)}, u32[]{:S(2)}) collective-permute-start(bf16[176,2048]{1,0:T(8,128)(2,1)S(1)} %copy-done.38), channel_id=1, source_target_pairs={{0,1},{1,0},{2,3},{3,2},{4,5},{5,4},{6,7},{7,6},{8,9},{9,8},{10,11... | collective-permute-start | bytes 2162696 | tf_op jit(solution)/shard_map/ppermute | solution.py:53
  234.6 38.8 %collective-permute-start.35 = (bf16[176,2048]{1,0:T(8,128)(2,1)}, bf16[176,2048]{1,0:T(8,128)(2,1)}, u32[]{:S(2)}, u32[]{:S(2)}) collective-permute-start(bf16[176,2048]{1,0:T(8,128)(2,1)} %collective-permute-done.26), channel_id=1, source_target_pairs={{0,1},{1,0},{2,3},{3,2},{4,5},{5,4},{6,7},{7,6},{8,9},{9,8},{10,11... | collective-permute-start | bytes 2162696 | tf_op jit(solution)/shard_map/ppermute | solution.py:53
  235.1 40.5 %collective-permute-start.36 = (bf16[176,2048]{1,0:T(8,128)(2,1)}, bf16[176,2048]{1,0:T(8,128)(2,1)}, u32[]{:S(2)}, u32[]{:S(2)}) collective-permute-start(bf16[176,2048]{1,0:T(8,128)(2,1)} %copy-done.39), channel_id=1, source_target_pairs={{0,1},{1,0},{2,3},{3,2},{4,5},{5,4},{6,7},{7,6},{8,9},{9,8},{10,11... | collective-permute-start | bytes 2162696 | tf_op jit(solution)/shard_map/ppermute | solution.py:53
  235.2 42.9 %collective-permute-start.37 = (bf16[176,2048]{1,0:T(8,128)(2,1)}, bf16[176,2048]{1,0:T(8,128)(2,1)}, u32[]{:S(2)}, u32[]{:S(2)}) collective-permute-start(bf16[176,2048]{1,0:T(8,128)(2,1)} %collective-permute-done.33), channel_id=1, source_target_pairs={{0,1},{1,0},{2,3},{3,2},{4,5},{5,4},{6,7},{7,6},{8,9},{9,8},{10,11... | collective-permute-start | bytes 2162696 | tf_op jit(solution)/shard_map/ppermute | solution.py:53
  235.6 46.7 %collective-permute-start.38 = (bf16[2,176,2048]{2,1,0:T(8,128)(2,1)}, bf16[2,176,2048]{2,1,0:T(8,128)(2,1)}, u32[]{:S(2)}, u32[]{:S(2)}) collective-permute-start(bf16[2,176,2048]{2,1,0:T(8,128)(2,1)} %bitcast.283), channel_id=1, source_target_pairs={{0,1},{1,0},{2,3},{3,2},{4,5},{5,4},{6,7},{7,6},{8,9},{9,8},{10,11... | collective-permute-start | bytes 4325384 | tf_op jit(solution)/shard_map/ppermute | solution.py:53
  248.7 161.0 %reduce-scatter.7.cloned.1.call-start = ((), (), s32[]{:S(2)}) async-start(), calls=%async_computation.15 | async-start | bytes 2621440 | tf_op jit(solution)/shard_map/reduce_scatter | solution.py:490
  270.9 14.7 %collective-permute-start.39 = (bf16[2,176,2048]{2,1,0:T(8,128)(2,1)}, bf16[2,176,2048]{2,1,0:T(8,128)(2,1)S(1)}, u32[]{:S(2)}, u32[]{:S(2)}) collective-permute-start(bf16[2,176,2048]{2,1,0:T(8,128)(2,1)} %collective-permute-done.7), channel_id=1, source_target_pairs={{0,1},{1,0},{2,3},{3,2},{4,5},{5,4},{6,7},{7,6},{8,9},{9,8},{10,11... | collective-permute-start | bytes 4325384 | tf_op jit(solution)/shard_map/ppermute | solution.py:53
  273.4 13.9 %collective-permute-start.40 = (bf16[2,176,2048]{2,1,0:T(8,128)(2,1)}, bf16[2,176,2048]{2,1,0:T(8,128)(2,1)}, u32[]{:S(2)}, u32[]{:S(2)}) collective-permute-start(bf16[2,176,2048]{2,1,0:T(8,128)(2,1)} %collective-permute-done.8), channel_id=1, source_target_pairs={{0,1},{1,0},{2,3},{3,2},{4,5},{5,4},{6,7},{7,6},{8,9},{9,8},{10,11... | collective-permute-start | bytes 4325384 | tf_op jit(solution)/shard_map/ppermute | solution.py:53
  275.6 14.6 %collective-permute-start.41 = (bf16[2,176,2048]{2,1,0:T(8,128)(2,1)}, bf16[2,176,2048]{2,1,0:T(8,128)(2,1)}, u32[]{:S(2)}, u32[]{:S(2)}) collective-permute-start(bf16[2,176,2048]{2,1,0:T(8,128)(2,1)} %collective-permute-done.32), channel_id=1, source_target_pairs={{0,1},{1,0},{2,3},{3,2},{4,5},{5,4},{6,7},{7,6},{8,9},{9,8},{10,11... | collective-permute-start | bytes 4325384 | tf_op jit(solution)/shard_map/ppermute | solution.py:53
  278.1 33.9 %collective-permute-start.44 = (bf16[512,2048]{1,0:T(8,128)(2,1)}, bf16[512,2048]{1,0:T(8,128)(2,1)}, u32[]{:S(2)}, u32[]{:S(2)}) collective-permute-start(bf16[512,2048]{1,0:T(8,128)(2,1)} %convolution_convert_fusion.11), channel_id=1, source_target_pairs={{0,1},{1,0},{2,3},{3,2},{4,5},{5,4},{6,7},{7,6},{8,9},{9,8},{10,11... | collective-permute-start | bytes 6291464 | tf_op jit(solution)/shard_map/ppermute | solution.py:53
  282.3 46.2 %collective-permute-start.43 = (bf16[512,2048]{1,0:T(8,128)(2,1)}, bf16[512,2048]{1,0:T(8,128)(2,1)}, u32[]{:S(2)}, u32[]{:S(2)}) collective-permute-start(bf16[512,2048]{1,0:T(8,128)(2,1)} %all-gather.8.cloned.1.call-done), channel_id=1, source_target_pairs={{0,4},{1,3},{2,6},{3,1},{4,0},{5,7},{6,2},{7,5},{8,12},{9,11},{10,... | collective-permute-start | bytes 6291464 | tf_op jit(solution)/shard_map/ppermute | solution.py:53
  285.6 48.9 %collective-permute-start.42 = (bf16[512,2048]{1,0:T(8,128)(2,1)}, bf16[512,2048]{1,0:T(8,128)(2,1)}, u32[]{:S(2)}, u32[]{:S(2)}) collective-permute-start(bf16[512,2048]{1,0:T(8,128)(2,1)} %all-gather.8.cloned.1.call-done), channel_id=1, source_target_pairs={{0,2},{1,5},{2,0},{3,7},{4,6},{5,1},{6,4},{7,3},{8,10},{9,13},{10,... | collective-permute-start | bytes 6291464 | tf_op jit(solution)/shard_map/ppermute | solution.py:53
  315.7 26.6 %collective-permute-start.45 = (bf16[256,2048]{1,0:T(8,128)(2,1)S(1)}, bf16[256,2048]{1,0:T(8,128)(2,1)S(1)}, u32[]{:S(2)}, u32[]{:S(2)}) collective-permute-start(bf16[256,2048]{1,0:T(8,128)(2,1)S(1)} %slice.403), channel_id=1, source_target_pairs={{0,4},{1,3},{2,6},{3,1},{4,0},{5,7},{6,2},{7,5},{8,12},{9,11},{10,... | collective-permute-start | bytes 3145736 | tf_op jit(solution)/shard_map/ppermute | solution.py:53
  364.2 210.1 %reduce-scatter.11.cloned.1.call-start = ((), (), s32[]{:S(2)}) async-start(), calls=%async_computation.17 | async-start | bytes 7208960 | tf_op jit(solution)/shard_map/reduce_scatter | solution.py:505
  372.9 26.4 %collective-permute-start.47 = (bf16[512,2048]{1,0:T(8,128)(2,1)}, bf16[512,2048]{1,0:T(8,128)(2,1)}, u32[]{:S(2)}, u32[]{:S(2)}) collective-permute-start(bf16[512,2048]{1,0:T(8,128)(2,1)} %collective-permute-done.42), channel_id=1, source_target_pairs={{0,4},{1,3},{2,6},{3,1},{4,0},{5,7},{6,2},{7,5},{8,12},{9,11},{10,... | collective-permute-start | bytes 6291464 | tf_op jit(solution)/shard_map/ppermute | solution.py:53
  409.7 22.0 %collective-permute-start.51 = (bf16[704,2048]{1,0:T(8,128)(2,1)}, bf16[704,2048]{1,0:T(8,128)(2,1)S(1)}, u32[]{:S(2)}, u32[]{:S(2)}) collective-permute-start(bf16[704,2048]{1,0:T(8,128)(2,1)} %convolution_convert_fusion.7), channel_id=1, source_target_pairs={{0,1},{1,0},{2,3},{3,2},{4,5},{5,4},{6,7},{7,6},{8,9},{9,8},{10,11... | collective-permute-start | bytes 8650760 | tf_op jit(solution)/shard_map/ppermute | solution.py:53
  409.8 23.1 %collective-permute-start.52 = (bf16[704,2048]{1,0:T(8,128)(2,1)}, bf16[704,2048]{1,0:T(8,128)(2,1)S(1)}, u32[]{:S(2)}, u32[]{:S(2)}) collective-permute-start(bf16[704,2048]{1,0:T(8,128)(2,1)} %convolution_convert_fusion.5), channel_id=1, source_target_pairs={{0,1},{1,0},{2,3},{3,2},{4,5},{5,4},{6,7},{7,6},{8,9},{9,8},{10,11... | collective-permute-start | bytes 8650760 | tf_op jit(solution)/shard_map/ppermute | solution.py:53
  411.0 23.1 %collective-permute-start.53 = (bf16[704,2048]{1,0:T(8,128)(2,1)}, bf16[704,2048]{1,0:T(8,128)(2,1)S(1)}, u32[]{:S(2)}, u32[]{:S(2)}) collective-permute-start(bf16[704,2048]{1,0:T(8,128)(2,1)} %convolution_convert_fusion.3), channel_id=1, source_target_pairs={{0,1},{1,0},{2,3},{3,2},{4,5},{5,4},{6,7},{7,6},{8,9},{9,8},{10,11... | collective-permute-start | bytes 8650760 | tf_op jit(solution)/shard_map/ppermute | solution.py:53
  415.7 14.2 %collective-permute-start.48 = (bf16[128,2048]{1,0:T(8,128)(2,1)S(1)}, bf16[128,2048]{1,0:T(8,128)(2,1)S(1)}, u32[]{:S(2)}, u32[]{:S(2)}) collective-permute-start(bf16[128,2048]{1,0:T(8,128)(2,1)S(1)} %get-tuple-element.180.refs_0_), channel_id=1, source_target_pairs={{0,2},{1,5},{2,0},{3,7},{4,6},{5,1},{6,4},{7,3},{8,10},{9,13},{10,... | collective-permute-start | bytes 1572872 | tf_op jit(solution)/shard_map/ppermute | solution.py:53
  417.2 20.9 %collective-permute-start.49 = (bf16[128,2048]{1,0:T(8,128)(2,1)S(1)}, bf16[128,2048]{1,0:T(8,128)(2,1)S(1)}, u32[]{:S(2)}, u32[]{:S(2)}) collective-permute-start(bf16[128,2048]{1,0:T(8,128)(2,1)S(1)} %get-tuple-element.180.refs_0_), channel_id=1, source_target_pairs={{0,4},{1,3},{2,6},{3,1},{4,0},{5,7},{6,2},{7,5},{8,12},{9,11},{10,... | collective-permute-start | bytes 1572872 | tf_op jit(solution)/shard_map/ppermute | solution.py:53
  439.3 40.7 %collective-permute-start.58 = (bf16[352,2048]{1,0:T(8,128)(2,1)S(1)}, bf16[352,2048]{1,0:T(8,128)(2,1)S(1)}, u32[]{:S(2)}, u32[]{:S(2)}) collective-permute-start(bf16[352,2048]{1,0:T(8,128)(2,1)S(1)} %slice.400), channel_id=1, source_target_pairs={{0,4},{1,3},{2,6},{3,1},{4,0},{5,7},{6,2},{7,5},{8,12},{9,11},{10,... | collective-permute-start | bytes 4325384 | tf_op jit(solution)/shard_map/ppermute | solution.py:53
  447.1 54.1 %collective-permute-start.60 = (bf16[352,2048]{1,0:T(8,128)(2,1)}, bf16[352,2048]{1,0:T(8,128)(2,1)}, u32[]{:S(2)}, u32[]{:S(2)}) collective-permute-start(bf16[352,2048]{1,0:T(8,128)(2,1)} %slice.398), channel_id=1, source_target_pairs={{0,4},{1,3},{2,6},{3,1},{4,0},{5,7},{6,2},{7,5},{8,12},{9,11},{10,... | collective-permute-start | bytes 4325384 | tf_op jit(solution)/shard_map/ppermute | solution.py:53
  447.3 58.2 %collective-permute-start.59 = (bf16[352,2048]{1,0:T(8,128)(2,1)}, bf16[352,2048]{1,0:T(8,128)(2,1)}, u32[]{:S(2)}, u32[]{:S(2)}) collective-permute-start(bf16[352,2048]{1,0:T(8,128)(2,1)} %slice.399), channel_id=1, source_target_pairs={{0,4},{1,3},{2,6},{3,1},{4,0},{5,7},{6,2},{7,5},{8,12},{9,11},{10,... | collective-permute-start | bytes 4325384 | tf_op jit(solution)/shard_map/ppermute | solution.py:53
  475.2 19.3 %all-to-all-start.3 = ((bf16[2,2,64,2048]{3,2,1,0:T(8,128)(2,1)}), bf16[2,2,64,2048]{3,2,1,0:T(8,128)(2,1)}, u32[]{:S(2)}, u32[]{:S(2)}) async-start(bf16[2,2,64,2048]{3,2,1,0:T(8,128)(2,1)} %bitcast.258), calls=%async_computation.5 | async-start | bytes 2097152 | tf_op jit(solution)/shard_map/all_to_all | solution.py:520
  479.7 148.8 %reduce-scatter.9.cloned.1.call-start = ((), (), s32[]{:S(2)}) async-start(), calls=%async_computation.16 | async-start | bytes 7864320 | tf_op jit(solution)/shard_map/reduce_scatter | solution.py:550
  521.0 26.8 %collective-permute-start.62 = (bf16[256,2048]{1,0:T(8,128)(2,1)S(1)}, bf16[256,2048]{1,0:T(8,128)(2,1)S(1)}, u32[]{:S(2)}, u32[]{:S(2)}) collective-permute-start(bf16[256,2048]{1,0:T(8,128)(2,1)S(1)} %slice.402), channel_id=1, source_target_pairs={{0,4},{1,3},{2,6},{3,1},{4,0},{5,7},{6,2},{7,5},{8,12},{9,11},{10,... | collective-permute-start | bytes 3145736 | tf_op jit(solution)/shard_map/ppermute | solution.py:53
  523.1 80.4 %collective-permute-start.70 = (bf16[512,2048]{1,0:T(8,128)(2,1)}, bf16[512,2048]{1,0:T(8,128)(2,1)}, u32[]{:S(2)}, u32[]{:S(2)}) collective-permute-start(bf16[512,2048]{1,0:T(8,128)(2,1)} %all-gather.8.cloned.1.call-done), channel_id=1, source_target_pairs={{0,1},{1,0},{2,3},{3,2},{4,5},{5,4},{6,7},{7,6},{8,9},{9,8},{10,11... | collective-permute-start | bytes 6291464 | tf_op jit(solution)/shard_map/ppermute | solution.py:53
  523.4 83.2 %collective-permute-start.71 = (bf16[512,2048]{1,0:T(8,128)(2,1)}, bf16[512,2048]{1,0:T(8,128)(2,1)}, u32[]{:S(2)}, u32[]{:S(2)}) collective-permute-start(bf16[512,2048]{1,0:T(8,128)(2,1)} %collective-permute-done.42), channel_id=1, source_target_pairs={{0,1},{1,0},{2,3},{3,2},{4,5},{5,4},{6,7},{7,6},{8,9},{9,8},{10,11... | collective-permute-start | bytes 6291464 | tf_op jit(solution)/shard_map/ppermute | solution.py:53
  523.6 87.1 %collective-permute-start.72 = (bf16[512,2048]{1,0:T(8,128)(2,1)}, bf16[512,2048]{1,0:T(8,128)(2,1)}, u32[]{:S(2)}, u32[]{:S(2)}) collective-permute-start(bf16[512,2048]{1,0:T(8,128)(2,1)} %collective-permute-done.43), channel_id=1, source_target_pairs={{0,1},{1,0},{2,3},{3,2},{4,5},{5,4},{6,7},{7,6},{8,9},{9,8},{10,11... | collective-permute-start | bytes 6291464 | tf_op jit(solution)/shard_map/ppermute | solution.py:53
  530.6 21.1 %collective-permute-start.68 = (bf16[256,2048]{1,0:T(8,128)(2,1)}, bf16[256,2048]{1,0:T(8,128)(2,1)}, u32[]{:S(2)}, u32[]{:S(2)}) collective-permute-start(bf16[256,2048]{1,0:T(8,128)(2,1)} %slice.401), channel_id=1, source_target_pairs={{0,4},{1,3},{2,6},{3,1},{4,0},{5,7},{6,2},{7,5},{8,12},{9,11},{10,... | collective-permute-start | bytes 3145736 | tf_op jit(solution)/shard_map/ppermute | solution.py:53
  532.6 14.7 %all-to-all-start.6 = ((f32[8,1,128]{2,1,0:T(1,128)}), f32[8,1,128]{2,1,0:T(1,128)S(1)}, u32[]{:S(2)}, u32[]{:S(2)}) async-start(f32[8,1,128]{2,1,0:T(1,128)} %bitcast.72), calls=%async_computation.10 | async-start | bytes 8192 | tf_op jit(solution)/shard_map/all_to_all | solution.py:574
  548.8 67.1 %collective-permute-start.73 = (bf16[512,2048]{1,0:T(8,128)(2,1)}, bf16[512,2048]{1,0:T(8,128)(2,1)}, u32[]{:S(2)}, u32[]{:S(2)}) collective-permute-start(bf16[512,2048]{1,0:T(8,128)(2,1)} %collective-permute-done.47), channel_id=1, source_target_pairs={{0,1},{1,0},{2,3},{3,2},{4,5},{5,4},{6,7},{7,6},{8,9},{9,8},{10,11... | collective-permute-start | bytes 6291464 | tf_op jit(solution)/shard_map/ppermute | solution.py:53
  563.7 62.1 %all-to-all-start.4 = ((f32[32,3,128]{2,1,0:T(4,128)}), f32[32,3,128]{2,1,0:T(4,128)S(1)}, u32[]{:S(2)}, u32[]{:S(2)}) async-start(f32[32,3,128]{2,1,0:T(4,128)} %reshape.695), calls=%async_computation.7 | async-start | bytes 131072 | tf_op jit(solution)/shard_map/all_to_all | solution.py:610
  579.4 41.0 %collective-permute-start.66 = (bf16[176,2048]{1,0:T(8,128)(2,1)S(1)}, bf16[176,2048]{1,0:T(8,128)(2,1)S(1)}, u32[]{:S(2)}, u32[]{:S(2)}) collective-permute-start(bf16[176,2048]{1,0:T(8,128)(2,1)S(1)} %slice.404), channel_id=1, source_target_pairs={{0,2},{1,5},{2,0},{3,7},{4,6},{5,1},{6,4},{7,3},{8,10},{9,13},{10,... | collective-permute-start | bytes 2162696 | tf_op jit(solution)/shard_map/ppermute | solution.py:53
  603.5 17.2 %collective-permute-start.65 = (bf16[176,2048]{1,0:T(8,128)(2,1)S(1)}, bf16[176,2048]{1,0:T(8,128)(2,1)S(1)}, u32[]{:S(2)}, u32[]{:S(2)}) collective-permute-start(bf16[176,2048]{1,0:T(8,128)(2,1)S(1)} %slice.405), channel_id=1, source_target_pairs={{0,2},{1,5},{2,0},{3,7},{4,6},{5,1},{6,4},{7,3},{8,10},{9,13},{10,... | collective-permute-start | bytes 2162696 | tf_op jit(solution)/shard_map/ppermute | solution.py:53
  606.6 16.0 %collective-permute-start.64 = (bf16[176,2048]{1,0:T(8,128)(2,1)S(1)}, bf16[176,2048]{1,0:T(8,128)(2,1)S(1)}, u32[]{:S(2)}, u32[]{:S(2)}) collective-permute-start(bf16[176,2048]{1,0:T(8,128)(2,1)S(1)} %slice.406), channel_id=1, source_target_pairs={{0,2},{1,5},{2,0},{3,7},{4,6},{5,1},{6,4},{7,3},{8,10},{9,13},{10,... | collective-permute-start | bytes 2162696 | tf_op jit(solution)/shard_map/ppermute | solution.py:53
  631.6 16.3 %all-to-all-start.5 = ((bf16[8,64,768]{2,1,0:T(8,128)(2,1)}), bf16[8,64,768]{2,1,0:T(8,128)(2,1)S(1)}, u32[]{:S(2)}, u32[]{:S(2)}) async-start(bf16[8,64,768]{2,1,0:T(8,128)(2,1)} %reshape.697), calls=%async_computation.9 | async-start | bytes 1572864 | tf_op jit(solution)/shard_map/all_to_all | solution.py:557
  (118 other events, 1325.1 us)
Sparse Core Ops, SparseCore 0:
  9.6 30.6 all-gather.11
  42.4 68.4 all-gather.5
  112.5 44.3 all-gather.7
  197.3 56.1 all-gather.9
  255.7 108.4 reduce-scatter.4
  366.3 43.3 reduce-scatter.6
  412.1 101.5 reduce-scatter.10
  516.1 112.2 reduce-scatter.8

commit v6 on v5

--- a/solution.py
+++ b/solution.py
@@ -520,7 +520,6 @@
     out_own_grad = lax.all_to_all(
         out_own_grad, "expert", 0, 0, axis_index_groups=pairs, tiled=True
     ).reshape(planes, shard, width)
-    qkv_grad, unit_grads[0] = barrier((qkv_grad, unit_grads[0]))
     qkv_own_grad = mm_tn(normed1, qkv_grad).astype(BF16)
 
     flat_rows = group * shard * 3 * own_width // width

time: 666 us -> 666 us (level)
    unnamed x211 -> x213, local copies, waits for them, and re-layouts: 58.5 us -> 58.2 us
  transfers between devices with their start and end apart: 89 -> 88, of which waited for: 27 -> 27; matrix products, arithmetic and copies ran while one was open for 50% -> 50% of each run, Pallas kernels for 5% -> 5%
where the time goes in v6:
time: 666 us; the launch traced here: 659 us
  matrix products  168 us (25%)
  waiting for transfers between devices  165 us (25%)
  local copies, waits for them, and re-layouts  128 us (19%)
  starting transfers between devices  78.6 us (12%)
  other arithmetic  62.7 us (9%)
  Pallas kernels  34.6 us (5%)
  between operations  17.4 us (3%)
    dot_general x33, matrix products, dot(): return lax.dot_general(a, b, (dims, ((), ())), preferred_element_type=F32)  165 us
    ppermute x74, waiting for transfers between devices, send(): return lax.ppermute(block, 'expert', [(i, target(i)) for i in range(size)])  80.9 us
    unnamed x213, local copies, waits for them, and re-layouts  58.2 us
    ppermute x74, starting transfers between devices, send(): return lax.ppermute(block, 'expert', [(i, target(i)) for i in range(size)])  53.8 us
    pallas_call x1, Pallas kernels, attend_back(): pl.pallas_call(functools.partial(attend_back_kernel, own // HEAD, size),...  22.4 us
    add x9, other arithmetic, sum_hop(): return near[:half] + send(near[half:].astype(BF16), size, hop).astype(F32)  22.1 us
    all_gather x1, waiting for transfers between devices, shards(): lax.all_gather(by_head, 'dp', axis=0, tiled=True)  19.1 us
    dynamic_update_slice x16, local copies, waits for them, and re-layouts, plane_rows(): lax.dynamic_update_slice_in_dim(whole, part, source * rows, 0)  15.5 us
  transfers between devices with their start and end apart: 88, of which 27 were waited for; matrix products, arithmetic and copies ran while one was open for 50% of the time, Pallas kernels for 5%

profile of v6, /device:TPU:0, one launch (start us, length us, event | category | flops | bytes accessed | tf_op | source)
XLA Modules:
  0.0 658.5 jit_solution(6362611024007664170)
XLA Ops:
  12.2 5.2 all-to-all-start
  19.0 11.0 %all-to-all-done = bf16[8,64,768]{2,1,0:T(8,128)(2,1)S(1)} async-done(((bf16[8,64,768]{2,1,0:T(8,128)(2,1)}), bf16[8,64,768]{2,1,0:T(8,128)(2,1)S(1)}, u32[]{:S(2)}, u32[]{:S(2)}) %all-to-all-start) | async-done | bytes 786464 | tf_op jit(solution)/shard_map/all_to_all | solution.py:343
  32.8 11.4 %collective-permute-done = bf16[128,2048]{1,0:T(8,128)(2,1)} collective-permute-done((bf16[128,2048]{1,0:T(8,128)(2,1)S(1)}, bf16[128,2048]{1,0:T(8,128)(2,1)}, u32[]{:S(2)}, u32[]{:S(2)}) %collective-permute-start) | collective-permute-done | bytes 524320 | tf_op jit(solution)/shard_map/ppermute | solution.py:53
  53.8 4.7 all-to-all-start.1
  68.4 6.9 %all-to-all-done.1 = f32[32,12,128]{2,1,0:T(8,128)S(1)} async-done(((f32[32,12,128]{2,1,0:T(8,128)}), f32[32,12,128]{2,1,0:T(8,128)S(1)}, u32[]{:S(2)}, u32[]{:S(2)}) %all-to-all-start.1) | async-done | bytes 196640 | tf_op jit(solution)/shard_map/all_to_all | solution.py:348
  81.6 7.8 %collective-permute-done.9 = bf16[2,2,64,2048]{3,2,1,0:T(8,128)(2,1)} collective-permute-done((bf16[2,2,64,2048]{3,2,1,0:T(8,128)(2,1)}, bf16[2,2,64,2048]{3,2,1,0:T(8,128)(2,1)}, u32[]{:S(2)}, u32[]{:S(2)}) %collective-permute-start.9) | collective-permute-done | bytes 1048608 | tf_op jit(solution)/shard_map/ppermute | solution.py:53
  91.8 19.1 %all-gather.6.cloned.1.call-done = bf16[32,64,768]{2,1,0:T(8,128)(2,1)} async-done(((bf16[8,64,768]{2,1,0:T(8,128)(2,1)}), bf16[32,64,768]{2,1,0:T(8,128)(2,1)}) %all-gather.6.cloned.1.call-update) | async-done | bytes 3145744 | tf_op jit(solution)/shard_map/all_gather | solution.py:346
  113.1 12.2 %attend.1 = (bf16[1024,2048]{1,0:T(8,128)(2,1)}, bf16[1024,768]{1,0:T(8,128)(2,1)S(1)}, bf16[1024,256]{1,0:T(8,128)(2,1)S(1)}) custom-call(bf16[1024,2048]{1,0:T(8,128)(2,1)} %constant_dynamic-update-slice_fusion.32.tokens, f32[1,2048]{1,0:T(1,128)S(1)} %broadcast_in_dim_reshape.4.gain, bf16[2048,768]{1,0:T(8,128)(2,1)S(1)} %bitcast.264, ...), custom_call_target="tpu_custom_call" | custom-call | tf_op jit(solution)/shard_map/attend/pallas_call | solution.py:192
  138.4 3.5 collective-permute-done.16
  141.9 10.1 %collective-permute-done.13 = bf16[1024,256]{1,0:T(8,128)(2,1)S(1)} collective-permute-done((bf16[1024,256]{1,0:T(8,128)(2,1)S(1)}, bf16[1024,256]{1,0:T(8,128)(2,1)S(1)}, u32[]{:S(2)}, u32[]{:S(2)}) %collective-permute-start.13) | collective-permute-done | bytes 524320 | tf_op jit(solution)/shard_map/ppermute | solution.py:53
  152.0 4.9 all-gather.8.cloned.1.call-done
  164.3 5.6 collective-permute-done.17
  171.9 4.0 fusion.18
  179.5 11.4 %multiply_reduce_fusion = (f32[1024]{0:T(1024)S(1)}, f32[1024,2048]{1,0:T(8,128)S(1)}) fusion(bf16[1024,2048]{1,0:T(8,128)(2,1)} %constant_dynamic-update-slice_fusion.32.tokens, bf16[1024,2048]{1,0:T(8,128)(2,1)S(1)} %constant_dynamic-update-slice_fusion.24, bf16[2048,2048]{1,0:T(8,128)(2,1)S(1)} %bitcast.272), kind=kOutput, calls=%fused_computation.6 | convolution fusion | flops 8598322176 | bytes 25169920 | tf_op jit(solution)/shard_map/dot_general | solution.py:21
  197.2 4.5 convolution_convert_fusion.13
  203.8 9.3 %fusion.2 = f32[464,2816]{1,0:T(8,128)S(1)} fusion(bf16[464,2048]{1,0:T(8,128)(2,1)S(1)} %convolution_convert_fusion.13, bf16[1,2048,2816]{2,1,0:T(8,128)(2,1)} %param.32), kind=kOutput, calls=%fused_computation.3 | convolution fusion | flops 5351931904 | bytes 18661376 | tf_op jit(solution)/shard_map/dot_general | solution.py:21
  213.2 6.0 multiply_convert_fusion.8
  221.9 4.3 all-to-all-start.2
  229.1 5.5 convolution_convert_fusion.1
  239.4 9.4 %fusion.13 = bf16[464,2048]{1,0:T(8,128)(2,1)} fusion(bf16[464,2816]{1,0:T(8,128)(2,1)S(1)} %pad_maximum_fusion.2, bf16[1,2048,2816]{2,1,0:T(8,128)(2,1)} %param.32), kind=kOutput, calls=%fused_computation.50 | convolution fusion | flops 5352882176 | bytes 16048128 | tf_op jit(solution)/shard_map/dot_general | solution.py:21
  248.8 2.7 constant_dynamic-update-slice_fusion.14
  251.5 2.8 constant_dynamic-update-slice_fusion.13
  259.6 5.3 convolution_convert_fusion
  287.4 2.8 constant_dynamic-update-slice_fusion.9
  290.2 2.8 constant_dynamic-update-slice_fusion.8
  293.0 11.4 %fusion.92 = f32[512,2816]{1,0:T(8,128)} fusion(bf16[512,2048]{1,0:T(8,128)(2,1)S(1)} %copy-done.15, bf16[2816,2048]{1,0:T(8,128)(2,1)} %bitcast.303), kind=kOutput, calls=%fused_computation.275 | convolution fusion | flops 5905580032 | bytes 19398656 | tf_op jit(solution)/shard_map/dot_general | solution.py:21
  304.4 7.7 %multiply_convert_fusion.7 = (bf16[512,1408]{1,0:T(8,128)(2,1)S(1)}, bf16[512,1408]{1,0:T(8,128)(2,1)S(1)}, bf16[512,1408]{1,0:T(8,128)(2,1)S(1)}) fusion(f32[512,2816]{1,0:T(8,128)} %fusion.92, bf16[1408,2048]{1,0:T(8,128)(2,1)S(1)} %bitcast.308, bf16[512,2048]{1,0:T(8,128)(2,1)} %all-gather.8.cloned.1.call-done, f32[512]{0:T(512)S(1)} %add_divide_fusion.2, ...), kind=kOutput, calls=%fused_computation.63 | convolution fusion | flops 2967076864 | bytes 17960960 | tf_op jit(solution)/shard_map/dot_general | solution.py:21
  312.1 3.5 convert_add_fusion.6
  317.6 8.9 %multiply_reduce_fusion.1 = (f32[512]{0:T(512)S(1)}, bf16[512,2048]{1,0:T(8,128)(2,1)}) fusion(bf16[512,2048]{1,0:T(8,128)(2,1)} %all-gather.8.cloned.1.call-done, f32[512]{0:T(512)S(1)} %fusion.83, f32[512]{0:T(512)S(1)} %add_divide_fusion.2, bf16[512,1408]{1,0:T(8,128)(2,1)S(1)} %get-tuple-element.235, ...), kind=kOutput, calls=%fused_computation.29 | convolution fusion | flops 2959080960 | bytes 11409408 | tf_op jit(solution)/shard_map/dot_general | solution.py:21
  328.6 6.0 collective-permute-done.42
  334.6 7.8 %collective-permute-done.45 = bf16[256,2048]{1,0:T(8,128)(2,1)S(1)} collective-permute-done((bf16[256,2048]{1,0:T(8,128)(2,1)S(1)}, bf16[256,2048]{1,0:T(8,128)(2,1)S(1)}, u32[]{:S(2)}, u32[]{:S(2)}) %collective-permute-start.45) | collective-permute-done | bytes 1048608 | tf_op jit(solution)/shard_map/ppermute | solution.py:53
  344.9 7.4 %add_convert_fusion = bf16[512,2048]{1,0:T(8,128)(2,1)} fusion(bf16[512,2816]{1,0:T(8,128)(2,1)S(1)} %pad_maximum_fusion.1, bf16[2816,2048]{1,0:T(8,128)(2,1)S(1)} %bitcast.306, f32[512]{0:T(512)S(1)} %subtract_multiply_fusion, f32[2048]{0:T(1024)S(1)} %mul.337), kind=kOutput, calls=%fused_computation.28 | convolution fusion | flops 5908725760 | bytes 16525312 | tf_op jit(solution)/shard_map/dot_general | solution.py:21
  354.9 9.3 %reduce-scatter.5.cloned.1.call-done = bf16[512,1408]{1,0:T(8,128)(2,1)} async-done(((bf16[2048,1408]{1,0:T(8,128)(2,1)}), bf16[512,1408]{1,0:T(8,128)(2,1)}) %reduce-scatter.5.cloned.1.call-update) | async-done | bytes 1441808 | tf_op jit(solution)/shard_map/reduce_scatter | solution.py:463
  364.3 8.7 %multiply_reduce_fusion.2 = (f32[464]{0:T(512)S(1)}, bf16[464,2048]{1,0:T(8,128)(2,1)}) fusion(f32[464,2048]{1,0:T(8,128)} %fusion.18, f32[464]{0:T(512)S(1)} %select_reduce_fusion.1, bf16[464,1408]{1,0:T(8,128)(2,1)} %get-tuple-element.224, bf16[1,1408,2048]{2,1,0:T(8,128)(2,1)} %param.33), kind=kOutput, calls=%fused_computation.33 | convolution fusion | flops 2679766528 | bytes 12779136 | tf_op jit(solution)/shard_map/dot_general | solution.py:21
  374.4 5.2 convolution_convert_fusion.7
  379.7 5.2 convolution_convert_fusion.8
  384.8 3.5 convolution_convert_fusion.3
  388.3 3.3 convolution_convert_fusion.4
  391.6 3.5 convolution_convert_fusion.5
  395.0 3.5 convolution_convert_fusion.6
  399.3 10.4 %reduce-scatter.7.cloned.1.call-done = bf16[128,2048]{1,0:T(8,128)(2,1)} async-done(((bf16[512,2048]{1,0:T(8,128)(2,1)}), bf16[128,2048]{1,0:T(8,128)(2,1)}) %reduce-scatter.7.cloned.1.call-update) | async-done | bytes 524304 | tf_op jit(solution)/shard_map/reduce_scatter | solution.py:490
  412.8 2.9 fusion.87
  418.7 11.2 %collective-permute-done.48.refs_1_ = bf16[128,2048]{1,0:T(8,128)(2,1)S(1)} collective-permute-done((bf16[128,2048]{1,0:T(8,128)(2,1)S(1)}, bf16[128,2048]{1,0:T(8,128)(2,1)S(1)}, u32[]{:S(2)}, u32[]{:S(2)}) %collective-permute-start.48) | collective-permute-done | bytes 524320 | tf_op jit(solution)/shard_map/ppermute | solution.py:53
  451.2 22.4 %attend_back.1 = (bf16[1024,2048]{1,0:T(8,128)(2,1)}, bf16[1024,768]{1,0:T(8,128)(2,1)}, bf16[256,2048]{1,0:T(8,128)(2,1)}, f32[1,768]{1,0:T(1,128)}) custom-call(s32[8]{0:T(128)} %copy-done.68, bf16[128,2048]{1,0:T(8,128)(2,1)} %copy-done.34, bf16[128,2048]{1,0:T(8,128)(2,1)} %copy-done.46, bf16[128,2048]{1,0:T(8,128)(2,1)} %copy-done.47, ...), custom_call_target="tpu_custom_call" | custom-call | tf_op jit(solution)/shard_map/attend_back/pallas_call | solution.py:269
  473.6 6.2 convolution_convert_fusion.2
  479.8 4.5 reshape.687
  485.7 4.8 all_to_all.39
  490.6 7.0 %pad_maximum_fusion = bf16[4,384,2048]{2,1,0:T(8,128)(2,1)} fusion(bf16[4,128,2048]{2,1,0:T(8,128)(2,1)} %bitcast.279, bf16[4,64,2048]{2,1,0:T(8,128)(2,1)S(1)} %bitcast.275, bf16[4,192,2048]{2,1,0:T(8,128)(2,1)S(1)} %copy-done.10), kind=kLoop, calls=%fused_computation.12 | loop fusion | flops 18874368 | bytes 12582912 | tf_op jit(solution)/shard_map/concatenate | solution.py:527
  497.6 4.5 convert_add_fusion.7
  502.1 4.3 convert_add_fusion.8
  506.5 3.5 convert_add_fusion.9
  515.7 3.0 convert_add_fusion.5
  523.6 3.7 convert_add_fusion.4
  532.5 3.3 all-to-all-start.6
  536.0 11.2 %all-to-all-done.6 = f32[8,1,128]{2,1,0:T(1,128)S(1)} async-done(((f32[8,1,128]{2,1,0:T(1,128)}), f32[8,1,128]{2,1,0:T(1,128)S(1)}, u32[]{:S(2)}, u32[]{:S(2)}) %all-to-all-start.6) | async-done | bytes 4128 | tf_op jit(solution)/shard_map/all_to_all | solution.py:573
  556.9 3.9 collective-permute-done.63
  563.5 3.0 all-to-all-start.4
  566.6 3.8 collective-permute-done.69
  574.2 5.0 maximum_convert_fusion
  580.8 3.2 fusion.16
  584.8 6.2 constant_dynamic-slice_fusion
  615.7 4.5 add_bitcast_fusion
  631.6 3.7 all-to-all-start.5
  639.3 8.5 %all-to-all-done.5 = bf16[8,64,768]{2,1,0:T(8,128)(2,1)S(1)} async-done(((bf16[8,64,768]{2,1,0:T(8,128)(2,1)}), bf16[8,64,768]{2,1,0:T(8,128)(2,1)S(1)}, u32[]{:S(2)}, u32[]{:S(2)}) %all-to-all-start.5) | async-done | bytes 786464 | tf_op jit(solution)/shard_map/all_to_all | solution.py:556
  (530 shorter events, 228.4 us)
Async XLA Ops:
  7.2 45.9 %all-gather.12.cloned.1.call-start = ((), (), s32[]{:S(2)}) async-start(), calls=%async_computation.18 | async-start | bytes 1310720 | tf_op jit(solution)/shard_map/all_gather | solution.py:340
  12.2 17.8 %all-to-all-start = ((bf16[8,64,768]{2,1,0:T(8,128)(2,1)}), bf16[8,64,768]{2,1,0:T(8,128)(2,1)S(1)}, u32[]{:S(2)}, u32[]{:S(2)}) async-start(bf16[8,64,768]{2,1,0:T(8,128)(2,1)} %reshape.678), calls=%async_computation | async-start | bytes 1572864 | tf_op jit(solution)/shard_map/all_to_all | solution.py:343
  17.4 93.6 %all-gather.6.cloned.1.call-start = ((), (), s32[]{:S(2)}) async-start(), calls=%async_computation.11 | async-start | bytes 3932160 | tf_op jit(solution)/shard_map/all_gather | solution.py:346
  30.0 14.2 %collective-permute-start = (bf16[128,2048]{1,0:T(8,128)(2,1)S(1)}, bf16[128,2048]{1,0:T(8,128)(2,1)}, u32[]{:S(2)}, u32[]{:S(2)}) collective-permute-start(bf16[128,2048]{1,0:T(8,128)(2,1)S(1)} %copy-done.17), channel_id=1, source_target_pairs={{0,2},{1,5},{2,0},{3,7},{4,6},{5,1},{6,4},{7,3},{8,10},{9,13},{10,... | collective-permute-start | bytes 1572872 | tf_op jit(solution)/shard_map/ppermute | solution.py:53
  30.9 17.8 %collective-permute-start.1 = (bf16[128,2048]{1,0:T(8,128)(2,1)S(1)}, bf16[128,2048]{1,0:T(8,128)(2,1)}, u32[]{:S(2)}, u32[]{:S(2)}) collective-permute-start(bf16[128,2048]{1,0:T(8,128)(2,1)S(1)} %copy-done.17), channel_id=1, source_target_pairs={{0,4},{1,3},{2,6},{3,1},{4,0},{5,7},{6,2},{7,5},{8,12},{9,11},{10,... | collective-permute-start | bytes 1572872 | tf_op jit(solution)/shard_map/ppermute | solution.py:53
  31.6 29.6 %collective-permute-start.3 = (bf16[128,2048]{1,0:T(8,128)(2,1)S(1)}, bf16[128,2048]{1,0:T(8,128)(2,1)}, u32[]{:S(2)}, u32[]{:S(2)}) collective-permute-start(bf16[128,2048]{1,0:T(8,128)(2,1)S(1)} %copy-done.17), channel_id=1, source_target_pairs={{0,1},{1,0},{2,3},{3,2},{4,5},{5,4},{6,7},{7,6},{8,9},{9,8},{10,11... | collective-permute-start | bytes 1572872 | tf_op jit(solution)/shard_map/ppermute | solution.py:53
  31.6 93.7 %collective-permute-start.14 = (bf16[128,2048]{1,0:T(8,128)(2,1)}, bf16[128,2048]{1,0:T(8,128)(2,1)}, u32[]{:S(2)}, u32[]{:S(2)}) collective-permute-start(bf16[128,2048]{1,0:T(8,128)(2,1)} %param.23), channel_id=1, source_target_pairs={{0,2},{1,5},{2,0},{3,7},{4,6},{5,1},{6,4},{7,3},{8,10},{9,13},{10,... | collective-permute-start | bytes 1572872 | tf_op jit(solution)/shard_map/ppermute | solution.py:53
  44.2 14.3 %collective-permute-start.2 = (bf16[128,2048]{1,0:T(8,128)(2,1)}, bf16[128,2048]{1,0:T(8,128)(2,1)S(1)}, u32[]{:S(2)}, u32[]{:S(2)}) collective-permute-start(bf16[128,2048]{1,0:T(8,128)(2,1)} %collective-permute-done), channel_id=1, source_target_pairs={{0,4},{1,3},{2,6},{3,1},{4,0},{5,7},{6,2},{7,5},{8,12},{9,11},{10,... | collective-permute-start | bytes 1572872 | tf_op jit(solution)/shard_map/ppermute | solution.py:53
  48.7 15.8 %collective-permute-start.4 = (bf16[128,2048]{1,0:T(8,128)(2,1)}, bf16[128,2048]{1,0:T(8,128)(2,1)}, u32[]{:S(2)}, u32[]{:S(2)}) collective-permute-start(bf16[128,2048]{1,0:T(8,128)(2,1)} %collective-permute-done), channel_id=1, source_target_pairs={{0,1},{1,0},{2,3},{3,2},{4,5},{5,4},{6,7},{7,6},{8,9},{9,8},{10,11... | collective-permute-start | bytes 1572872 | tf_op jit(solution)/shard_map/ppermute | solution.py:53
  48.7 17.8 %collective-permute-start.5 = (bf16[128,2048]{1,0:T(8,128)(2,1)}, bf16[128,2048]{1,0:T(8,128)(2,1)}, u32[]{:S(2)}, u32[]{:S(2)}) collective-permute-start(bf16[128,2048]{1,0:T(8,128)(2,1)} %collective-permute-done.1), channel_id=1, source_target_pairs={{0,1},{1,0},{2,3},{3,2},{4,5},{5,4},{6,7},{7,6},{8,9},{9,8},{10,11... | collective-permute-start | bytes 1572872 | tf_op jit(solution)/shard_map/ppermute | solution.py:53
  53.8 21.5 %all-to-all-start.1 = ((f32[32,12,128]{2,1,0:T(8,128)}), f32[32,12,128]{2,1,0:T(8,128)S(1)}, u32[]{:S(2)}, u32[]{:S(2)}) async-start(f32[32,12,128]{2,1,0:T(8,128)} %broadcast_in_dim.177), calls=%async_computation.1 | async-start | bytes 524288 | tf_op jit(solution)/shard_map/all_to_all | solution.py:348
  58.5 98.4 %all-gather.8.cloned.1.call-start = ((), (), s32[]{:S(2)}) async-start(), calls=%async_computation.12 | async-start | bytes 2621440 | tf_op jit(solution)/shard_map/all_gather | solution.py:378
  58.5 68.3 %collective-permute-start.10 = (bf16[2,2,64,2048]{3,2,1,0:T(8,128)(2,1)}, bf16[2,2,64,2048]{3,2,1,0:T(8,128)(2,1)S(1)}, u32[]{:S(2)}, u32[]{:S(2)}) collective-permute-start(bf16[2,2,64,2048]{3,2,1,0:T(8,128)(2,1)} %bitcast.293), channel_id=1, source_target_pairs={{0,4},{1,3},{2,6},{3,1},{4,0},{5,7},{6,2},{7,5},{8,12},{9,11},{10,... | collective-permute-start | bytes 3145736 | tf_op jit(solution)/shard_map/ppermute | solution.py:53
  61.2 28.2 %collective-permute-start.9 = (bf16[2,2,64,2048]{3,2,1,0:T(8,128)(2,1)}, bf16[2,2,64,2048]{3,2,1,0:T(8,128)(2,1)}, u32[]{:S(2)}, u32[]{:S(2)}) collective-permute-start(bf16[2,2,64,2048]{3,2,1,0:T(8,128)(2,1)} %bitcast.294), channel_id=1, source_target_pairs={{0,2},{1,5},{2,0},{3,7},{4,6},{5,1},{6,4},{7,3},{8,10},{9,13},{10,... | collective-permute-start | bytes 3145736 | tf_op jit(solution)/shard_map/ppermute | solution.py:53
  78.0 51.5 %collective-permute-start.8 = (bf16[2,176,2048]{2,1,0:T(8,128)(2,1)S(1)}, bf16[2,176,2048]{2,1,0:T(8,128)(2,1)}, u32[]{:S(2)}, u32[]{:S(2)}) collective-permute-start(bf16[2,176,2048]{2,1,0:T(8,128)(2,1)S(1)} %bitcast.289), channel_id=1, source_target_pairs={{0,4},{1,3},{2,6},{3,1},{4,0},{5,7},{6,2},{7,5},{8,12},{9,11},{10,... | collective-permute-start | bytes 4325384 | tf_op jit(solution)/shard_map/ppermute | solution.py:53
  79.4 50.2 %collective-permute-start.7 = (bf16[2,176,2048]{2,1,0:T(8,128)(2,1)S(1)}, bf16[2,176,2048]{2,1,0:T(8,128)(2,1)}, u32[]{:S(2)}, u32[]{:S(2)}) collective-permute-start(bf16[2,176,2048]{2,1,0:T(8,128)(2,1)S(1)} %bitcast.290), channel_id=1, source_target_pairs={{0,2},{1,5},{2,0},{3,7},{4,6},{5,1},{6,4},{7,3},{8,10},{9,13},{10,... | collective-permute-start | bytes 4325384 | tf_op jit(solution)/shard_map/ppermute | solution.py:53
  89.4 40.1 %collective-permute-start.11 = (bf16[2,2,64,2048]{3,2,1,0:T(8,128)(2,1)}, bf16[2,2,64,2048]{3,2,1,0:T(8,128)(2,1)}, u32[]{:S(2)}, u32[]{:S(2)}) collective-permute-start(bf16[2,2,64,2048]{3,2,1,0:T(8,128)(2,1)} %collective-permute-done.9), channel_id=1, source_target_pairs={{0,4},{1,3},{2,6},{3,1},{4,0},{5,7},{6,2},{7,5},{8,12},{9,11},{10,... | collective-permute-start | bytes 3145736 | tf_op jit(solution)/shard_map/ppermute | solution.py:53
  110.9 169.3 %all-gather.10.cloned.1.call-start = ((), (), s32[]{:S(2)}) async-start(), calls=%async_computation.13 | async-start | bytes 2621440 | tf_op jit(solution)/shard_map/all_gather | solution.py:412
  125.3 13.1 %collective-permute-start.15 = (bf16[128,2048]{1,0:T(8,128)(2,1)}, bf16[128,2048]{1,0:T(8,128)(2,1)S(1)}, u32[]{:S(2)}, u32[]{:S(2)}) collective-permute-start(bf16[128,2048]{1,0:T(8,128)(2,1)} %param.23), channel_id=1, source_target_pairs={{0,4},{1,3},{2,6},{3,1},{4,0},{5,7},{6,2},{7,5},{8,12},{9,11},{10,... | collective-permute-start | bytes 1572872 | tf_op jit(solution)/shard_map/ppermute | solution.py:53
  126.8 15.0 %collective-permute-start.16 = (bf16[128,2048]{1,0:T(8,128)(2,1)}, bf16[128,2048]{1,0:T(8,128)(2,1)S(1)}, u32[]{:S(2)}, u32[]{:S(2)}) collective-permute-start(bf16[128,2048]{1,0:T(8,128)(2,1)} %collective-permute-done.14), channel_id=1, source_target_pairs={{0,4},{1,3},{2,6},{3,1},{4,0},{5,7},{6,2},{7,5},{8,12},{9,11},{10,... | collective-permute-start | bytes 1572872 | tf_op jit(solution)/shard_map/ppermute | solution.py:53
  135.1 16.8 %collective-permute-start.13 = (bf16[1024,256]{1,0:T(8,128)(2,1)S(1)}, bf16[1024,256]{1,0:T(8,128)(2,1)S(1)}, u32[]{:S(2)}, u32[]{:S(2)}) collective-permute-start(bf16[1024,256]{1,0:T(8,128)(2,1)S(1)} %get-tuple-element.126.refs_9_), channel_id=1, source_target_pairs={{0,4},{1,3},{2,6},{3,1},{4,0},{5,7},{6,2},{7,5},{8,12},{9,11},{10,... | collective-permute-start | bytes 1572872 | tf_op jit(solution)/shard_map/ppermute | solution.py:53
  136.7 15.3 %collective-permute-start.12 = (bf16[1024,256]{1,0:T(8,128)(2,1)S(1)}, bf16[1024,256]{1,0:T(8,128)(2,1)S(1)}, u32[]{:S(2)}, u32[]{:S(2)}) collective-permute-start(bf16[1024,256]{1,0:T(8,128)(2,1)S(1)} %get-tuple-element.126.refs_9_), channel_id=1, source_target_pairs={{0,2},{1,5},{2,0},{3,7},{4,6},{5,1},{6,4},{7,3},{8,10},{9,13},{10,... | collective-permute-start | bytes 1572872 | tf_op jit(solution)/shard_map/ppermute | solution.py:53
  176.0 25.7 %collective-permute-start.27 = (bf16[176,2048]{1,0:T(8,128)(2,1)S(1)}, bf16[176,2048]{1,0:T(8,128)(2,1)S(1)}, u32[]{:S(2)}, u32[]{:S(2)}) collective-permute-start(bf16[176,2048]{1,0:T(8,128)(2,1)S(1)} %copy-done.39), channel_id=1, source_target_pairs={{0,4},{1,3},{2,6},{3,1},{4,0},{5,7},{6,2},{7,5},{8,12},{9,11},{10,... | collective-permute-start | bytes 2162696 | tf_op jit(solution)/shard_map/ppermute | solution.py:53
  178.0 23.7 %collective-permute-start.26 = (bf16[176,2048]{1,0:T(8,128)(2,1)S(1)}, bf16[176,2048]{1,0:T(8,128)(2,1)}, u32[]{:S(2)}, u32[]{:S(2)}) collective-permute-start(bf16[176,2048]{1,0:T(8,128)(2,1)S(1)} %copy-done.39), channel_id=1, source_target_pairs={{0,2},{1,5},{2,0},{3,7},{4,6},{5,1},{6,4},{7,3},{8,10},{9,13},{10,... | collective-permute-start | bytes 2162696 | tf_op jit(solution)/shard_map/ppermute | solution.py:53
  201.7 32.9 %collective-permute-start.33 = (bf16[176,2048]{1,0:T(8,128)(2,1)}, bf16[176,2048]{1,0:T(8,128)(2,1)}, u32[]{:S(2)}, u32[]{:S(2)}) collective-permute-start(bf16[176,2048]{1,0:T(8,128)(2,1)} %collective-permute-done.26), channel_id=1, source_target_pairs={{0,4},{1,3},{2,6},{3,1},{4,0},{5,7},{6,2},{7,5},{8,12},{9,11},{10,... | collective-permute-start | bytes 2162696 | tf_op jit(solution)/shard_map/ppermute | solution.py:53
  202.1 32.5 %collective-permute-start.32 = (bf16[2,176,2048]{2,1,0:T(8,128)(2,1)}, bf16[2,176,2048]{2,1,0:T(8,128)(2,1)}, u32[]{:S(2)}, u32[]{:S(2)}) collective-permute-start(bf16[2,176,2048]{2,1,0:T(8,128)(2,1)} %collective-permute-done.7), channel_id=1, source_target_pairs={{0,4},{1,3},{2,6},{3,1},{4,0},{5,7},{6,2},{7,5},{8,12},{9,11},{10,... | collective-permute-start | bytes 4325384 | tf_op jit(solution)/shard_map/ppermute | solution.py:53
  221.9 132.9 %all-to-all-start.2 = ((bf16[4,464,352]{2,1,0:T(8,128)(2,1)}), bf16[4,464,352]{2,1,0:T(8,128)(2,1)}, u32[]{:S(2)}, u32[]{:S(2)}) async-start(bf16[4,464,352]{2,1,0:T(8,128)(2,1)} %bitcast.257), calls=%async_computation.3 | async-start | bytes 2850816 | tf_op jit(solution)/shard_map/all_to_all | solution.py:448
  226.3 137.9 %reduce-scatter.5.cloned.1.call-start = ((), (), s32[]{:S(2)}) async-start(), calls=%async_computation.14 | async-start | bytes 7208960 | tf_op jit(solution)/shard_map/reduce_scatter | solution.py:463
  234.6 36.4 %collective-permute-start.34 = (bf16[176,2048]{1,0:T(8,128)(2,1)S(1)}, bf16[176,2048]{1,0:T(8,128)(2,1)}, u32[]{:S(2)}, u32[]{:S(2)}) collective-permute-start(bf16[176,2048]{1,0:T(8,128)(2,1)S(1)} %copy-done.39), channel_id=1, source_target_pairs={{0,1},{1,0},{2,3},{3,2},{4,5},{5,4},{6,7},{7,6},{8,9},{9,8},{10,11... | collective-permute-start | bytes 2162696 | tf_op jit(solution)/shard_map/ppermute | solution.py:53
  234.6 38.8 %collective-permute-start.35 = (bf16[176,2048]{1,0:T(8,128)(2,1)}, bf16[176,2048]{1,0:T(8,128)(2,1)}, u32[]{:S(2)}, u32[]{:S(2)}) collective-permute-start(bf16[176,2048]{1,0:T(8,128)(2,1)} %collective-permute-done.26), channel_id=1, source_target_pairs={{0,1},{1,0},{2,3},{3,2},{4,5},{5,4},{6,7},{7,6},{8,9},{9,8},{10,11... | collective-permute-start | bytes 2162696 | tf_op jit(solution)/shard_map/ppermute | solution.py:53
  235.1 40.5 %collective-permute-start.36 = (bf16[176,2048]{1,0:T(8,128)(2,1)}, bf16[176,2048]{1,0:T(8,128)(2,1)}, u32[]{:S(2)}, u32[]{:S(2)}) collective-permute-start(bf16[176,2048]{1,0:T(8,128)(2,1)} %copy-done.40), channel_id=1, source_target_pairs={{0,1},{1,0},{2,3},{3,2},{4,5},{5,4},{6,7},{7,6},{8,9},{9,8},{10,11... | collective-permute-start | bytes 2162696 | tf_op jit(solution)/shard_map/ppermute | solution.py:53
  235.2 42.9 %collective-permute-start.37 = (bf16[176,2048]{1,0:T(8,128)(2,1)}, bf16[176,2048]{1,0:T(8,128)(2,1)}, u32[]{:S(2)}, u32[]{:S(2)}) collective-permute-start(bf16[176,2048]{1,0:T(8,128)(2,1)} %collective-permute-done.33), channel_id=1, source_target_pairs={{0,1},{1,0},{2,3},{3,2},{4,5},{5,4},{6,7},{7,6},{8,9},{9,8},{10,11... | collective-permute-start | bytes 2162696 | tf_op jit(solution)/shard_map/ppermute | solution.py:53
  235.6 46.7 %collective-permute-start.38 = (bf16[2,176,2048]{2,1,0:T(8,128)(2,1)}, bf16[2,176,2048]{2,1,0:T(8,128)(2,1)}, u32[]{:S(2)}, u32[]{:S(2)}) collective-permute-start(bf16[2,176,2048]{2,1,0:T(8,128)(2,1)} %bitcast.287), channel_id=1, source_target_pairs={{0,1},{1,0},{2,3},{3,2},{4,5},{5,4},{6,7},{7,6},{8,9},{9,8},{10,11... | collective-permute-start | bytes 4325384 | tf_op jit(solution)/shard_map/ppermute | solution.py:53
  248.7 160.9 %reduce-scatter.7.cloned.1.call-start = ((), (), s32[]{:S(2)}) async-start(), calls=%async_computation.15 | async-start | bytes 2621440 | tf_op jit(solution)/shard_map/reduce_scatter | solution.py:490
  271.0 14.7 %collective-permute-start.39 = (bf16[2,176,2048]{2,1,0:T(8,128)(2,1)}, bf16[2,176,2048]{2,1,0:T(8,128)(2,1)S(1)}, u32[]{:S(2)}, u32[]{:S(2)}) collective-permute-start(bf16[2,176,2048]{2,1,0:T(8,128)(2,1)} %collective-permute-done.7), channel_id=1, source_target_pairs={{0,1},{1,0},{2,3},{3,2},{4,5},{5,4},{6,7},{7,6},{8,9},{9,8},{10,11... | collective-permute-start | bytes 4325384 | tf_op jit(solution)/shard_map/ppermute | solution.py:53
  273.5 13.9 %collective-permute-start.40 = (bf16[2,176,2048]{2,1,0:T(8,128)(2,1)}, bf16[2,176,2048]{2,1,0:T(8,128)(2,1)}, u32[]{:S(2)}, u32[]{:S(2)}) collective-permute-start(bf16[2,176,2048]{2,1,0:T(8,128)(2,1)} %collective-permute-done.8), channel_id=1, source_target_pairs={{0,1},{1,0},{2,3},{3,2},{4,5},{5,4},{6,7},{7,6},{8,9},{9,8},{10,11... | collective-permute-start | bytes 4325384 | tf_op jit(solution)/shard_map/ppermute | solution.py:53
  275.6 14.6 %collective-permute-start.41 = (bf16[2,176,2048]{2,1,0:T(8,128)(2,1)}, bf16[2,176,2048]{2,1,0:T(8,128)(2,1)}, u32[]{:S(2)}, u32[]{:S(2)}) collective-permute-start(bf16[2,176,2048]{2,1,0:T(8,128)(2,1)} %collective-permute-done.32), channel_id=1, source_target_pairs={{0,1},{1,0},{2,3},{3,2},{4,5},{5,4},{6,7},{7,6},{8,9},{9,8},{10,11... | collective-permute-start | bytes 4325384 | tf_op jit(solution)/shard_map/ppermute | solution.py:53
  278.1 34.0 %collective-permute-start.44 = (bf16[512,2048]{1,0:T(8,128)(2,1)}, bf16[512,2048]{1,0:T(8,128)(2,1)}, u32[]{:S(2)}, u32[]{:S(2)}) collective-permute-start(bf16[512,2048]{1,0:T(8,128)(2,1)} %convolution_convert_fusion.11), channel_id=1, source_target_pairs={{0,1},{1,0},{2,3},{3,2},{4,5},{5,4},{6,7},{7,6},{8,9},{9,8},{10,11... | collective-permute-start | bytes 6291464 | tf_op jit(solution)/shard_map/ppermute | solution.py:53
  282.3 46.2 %collective-permute-start.43 = (bf16[512,2048]{1,0:T(8,128)(2,1)}, bf16[512,2048]{1,0:T(8,128)(2,1)}, u32[]{:S(2)}, u32[]{:S(2)}) collective-permute-start(bf16[512,2048]{1,0:T(8,128)(2,1)} %all-gather.8.cloned.1.call-done), channel_id=1, source_target_pairs={{0,4},{1,3},{2,6},{3,1},{4,0},{5,7},{6,2},{7,5},{8,12},{9,11},{10,... | collective-permute-start | bytes 6291464 | tf_op jit(solution)/shard_map/ppermute | solution.py:53
  285.7 48.9 %collective-permute-start.42 = (bf16[512,2048]{1,0:T(8,128)(2,1)}, bf16[512,2048]{1,0:T(8,128)(2,1)}, u32[]{:S(2)}, u32[]{:S(2)}) collective-permute-start(bf16[512,2048]{1,0:T(8,128)(2,1)} %all-gather.8.cloned.1.call-done), channel_id=1, source_target_pairs={{0,2},{1,5},{2,0},{3,7},{4,6},{5,1},{6,4},{7,3},{8,10},{9,13},{10,... | collective-permute-start | bytes 6291464 | tf_op jit(solution)/shard_map/ppermute | solution.py:53
  315.8 26.6 %collective-permute-start.45 = (bf16[256,2048]{1,0:T(8,128)(2,1)S(1)}, bf16[256,2048]{1,0:T(8,128)(2,1)S(1)}, u32[]{:S(2)}, u32[]{:S(2)}) collective-permute-start(bf16[256,2048]{1,0:T(8,128)(2,1)S(1)} %slice.403), channel_id=1, source_target_pairs={{0,4},{1,3},{2,6},{3,1},{4,0},{5,7},{6,2},{7,5},{8,12},{9,11},{10,... | collective-permute-start | bytes 3145736 | tf_op jit(solution)/shard_map/ppermute | solution.py:53
  364.2 210.0 %reduce-scatter.11.cloned.1.call-start = ((), (), s32[]{:S(2)}) async-start(), calls=%async_computation.17 | async-start | bytes 7208960 | tf_op jit(solution)/shard_map/reduce_scatter | solution.py:505
  372.9 26.4 %collective-permute-start.47 = (bf16[512,2048]{1,0:T(8,128)(2,1)}, bf16[512,2048]{1,0:T(8,128)(2,1)}, u32[]{:S(2)}, u32[]{:S(2)}) collective-permute-start(bf16[512,2048]{1,0:T(8,128)(2,1)} %collective-permute-done.42), channel_id=1, source_target_pairs={{0,4},{1,3},{2,6},{3,1},{4,0},{5,7},{6,2},{7,5},{8,12},{9,11},{10,... | collective-permute-start | bytes 6291464 | tf_op jit(solution)/shard_map/ppermute | solution.py:53
  409.7 218.7 %reduce-scatter.9.cloned.1.call-start = ((), (), s32[]{:S(2)}) async-start(), calls=%async_computation.16 | async-start | bytes 7864320 | tf_op jit(solution)/shard_map/reduce_scatter | solution.py:549
  409.7 22.0 %collective-permute-start.51 = (bf16[704,2048]{1,0:T(8,128)(2,1)}, bf16[704,2048]{1,0:T(8,128)(2,1)S(1)}, u32[]{:S(2)}, u32[]{:S(2)}) collective-permute-start(bf16[704,2048]{1,0:T(8,128)(2,1)} %convolution_convert_fusion.7), channel_id=1, source_target_pairs={{0,1},{1,0},{2,3},{3,2},{4,5},{5,4},{6,7},{7,6},{8,9},{9,8},{10,11... | collective-permute-start | bytes 8650760 | tf_op jit(solution)/shard_map/ppermute | solution.py:53
  409.8 23.1 %collective-permute-start.52 = (bf16[704,2048]{1,0:T(8,128)(2,1)}, bf16[704,2048]{1,0:T(8,128)(2,1)S(1)}, u32[]{:S(2)}, u32[]{:S(2)}) collective-permute-start(bf16[704,2048]{1,0:T(8,128)(2,1)} %convolution_convert_fusion.5), channel_id=1, source_target_pairs={{0,1},{1,0},{2,3},{3,2},{4,5},{5,4},{6,7},{7,6},{8,9},{9,8},{10,11... | collective-permute-start | bytes 8650760 | tf_op jit(solution)/shard_map/ppermute | solution.py:53
  411.1 23.1 %collective-permute-start.53 = (bf16[704,2048]{1,0:T(8,128)(2,1)}, bf16[704,2048]{1,0:T(8,128)(2,1)S(1)}, u32[]{:S(2)}, u32[]{:S(2)}) collective-permute-start(bf16[704,2048]{1,0:T(8,128)(2,1)} %convolution_convert_fusion.3), channel_id=1, source_target_pairs={{0,1},{1,0},{2,3},{3,2},{4,5},{5,4},{6,7},{7,6},{8,9},{9,8},{10,11... | collective-permute-start | bytes 8650760 | tf_op jit(solution)/shard_map/ppermute | solution.py:53
  415.7 14.2 %collective-permute-start.48 = (bf16[128,2048]{1,0:T(8,128)(2,1)S(1)}, bf16[128,2048]{1,0:T(8,128)(2,1)S(1)}, u32[]{:S(2)}, u32[]{:S(2)}) collective-permute-start(bf16[128,2048]{1,0:T(8,128)(2,1)S(1)} %get-tuple-element.178.refs_0_), channel_id=1, source_target_pairs={{0,2},{1,5},{2,0},{3,7},{4,6},{5,1},{6,4},{7,3},{8,10},{9,13},{10,... | collective-permute-start | bytes 1572872 | tf_op jit(solution)/shard_map/ppermute | solution.py:53
  417.2 20.9 %collective-permute-start.49 = (bf16[128,2048]{1,0:T(8,128)(2,1)S(1)}, bf16[128,2048]{1,0:T(8,128)(2,1)S(1)}, u32[]{:S(2)}, u32[]{:S(2)}) collective-permute-start(bf16[128,2048]{1,0:T(8,128)(2,1)S(1)} %get-tuple-element.178.refs_0_), channel_id=1, source_target_pairs={{0,4},{1,3},{2,6},{3,1},{4,0},{5,7},{6,2},{7,5},{8,12},{9,11},{10,... | collective-permute-start | bytes 1572872 | tf_op jit(solution)/shard_map/ppermute | solution.py:53
  441.4 56.1 %collective-permute-start.60 = (bf16[352,2048]{1,0:T(8,128)(2,1)}, bf16[352,2048]{1,0:T(8,128)(2,1)}, u32[]{:S(2)}, u32[]{:S(2)}) collective-permute-start(bf16[352,2048]{1,0:T(8,128)(2,1)} %slice.398), channel_id=1, source_target_pairs={{0,4},{1,3},{2,6},{3,1},{4,0},{5,7},{6,2},{7,5},{8,12},{9,11},{10,... | collective-permute-start | bytes 4325384 | tf_op jit(solution)/shard_map/ppermute | solution.py:53
  448.2 53.9 %collective-permute-start.59 = (bf16[352,2048]{1,0:T(8,128)(2,1)}, bf16[352,2048]{1,0:T(8,128)(2,1)}, u32[]{:S(2)}, u32[]{:S(2)}) collective-permute-start(bf16[352,2048]{1,0:T(8,128)(2,1)} %slice.399), channel_id=1, source_target_pairs={{0,4},{1,3},{2,6},{3,1},{4,0},{5,7},{6,2},{7,5},{8,12},{9,11},{10,... | collective-permute-start | bytes 4325384 | tf_op jit(solution)/shard_map/ppermute | solution.py:53
  448.4 58.1 %collective-permute-start.58 = (bf16[352,2048]{1,0:T(8,128)(2,1)}, bf16[352,2048]{1,0:T(8,128)(2,1)}, u32[]{:S(2)}, u32[]{:S(2)}) collective-permute-start(bf16[352,2048]{1,0:T(8,128)(2,1)} %slice.400), channel_id=1, source_target_pairs={{0,4},{1,3},{2,6},{3,1},{4,0},{5,7},{6,2},{7,5},{8,12},{9,11},{10,... | collective-permute-start | bytes 4325384 | tf_op jit(solution)/shard_map/ppermute | solution.py:53
  520.9 26.8 %collective-permute-start.62 = (bf16[256,2048]{1,0:T(8,128)(2,1)S(1)}, bf16[256,2048]{1,0:T(8,128)(2,1)S(1)}, u32[]{:S(2)}, u32[]{:S(2)}) collective-permute-start(bf16[256,2048]{1,0:T(8,128)(2,1)S(1)} %slice.402), channel_id=1, source_target_pairs={{0,4},{1,3},{2,6},{3,1},{4,0},{5,7},{6,2},{7,5},{8,12},{9,11},{10,... | collective-permute-start | bytes 3145736 | tf_op jit(solution)/shard_map/ppermute | solution.py:53
  523.0 80.3 %collective-permute-start.70 = (bf16[512,2048]{1,0:T(8,128)(2,1)}, bf16[512,2048]{1,0:T(8,128)(2,1)}, u32[]{:S(2)}, u32[]{:S(2)}) collective-permute-start(bf16[512,2048]{1,0:T(8,128)(2,1)} %all-gather.8.cloned.1.call-done), channel_id=1, source_target_pairs={{0,1},{1,0},{2,3},{3,2},{4,5},{5,4},{6,7},{7,6},{8,9},{9,8},{10,11... | collective-permute-start | bytes 6291464 | tf_op jit(solution)/shard_map/ppermute | solution.py:53
  523.0 83.4 %collective-permute-start.71 = (bf16[512,2048]{1,0:T(8,128)(2,1)}, bf16[512,2048]{1,0:T(8,128)(2,1)}, u32[]{:S(2)}, u32[]{:S(2)}) collective-permute-start(bf16[512,2048]{1,0:T(8,128)(2,1)} %collective-permute-done.42), channel_id=1, source_target_pairs={{0,1},{1,0},{2,3},{3,2},{4,5},{5,4},{6,7},{7,6},{8,9},{9,8},{10,11... | collective-permute-start | bytes 6291464 | tf_op jit(solution)/shard_map/ppermute | solution.py:53
  523.5 87.0 %collective-permute-start.72 = (bf16[512,2048]{1,0:T(8,128)(2,1)}, bf16[512,2048]{1,0:T(8,128)(2,1)}, u32[]{:S(2)}, u32[]{:S(2)}) collective-permute-start(bf16[512,2048]{1,0:T(8,128)(2,1)} %collective-permute-done.43), channel_id=1, source_target_pairs={{0,1},{1,0},{2,3},{3,2},{4,5},{5,4},{6,7},{7,6},{8,9},{9,8},{10,11... | collective-permute-start | bytes 6291464 | tf_op jit(solution)/shard_map/ppermute | solution.py:53
  530.4 21.2 %collective-permute-start.68 = (bf16[256,2048]{1,0:T(8,128)(2,1)}, bf16[256,2048]{1,0:T(8,128)(2,1)}, u32[]{:S(2)}, u32[]{:S(2)}) collective-permute-start(bf16[256,2048]{1,0:T(8,128)(2,1)} %slice.401), channel_id=1, source_target_pairs={{0,4},{1,3},{2,6},{3,1},{4,0},{5,7},{6,2},{7,5},{8,12},{9,11},{10,... | collective-permute-start | bytes 3145736 | tf_op jit(solution)/shard_map/ppermute | solution.py:53
  532.5 14.6 %all-to-all-start.6 = ((f32[8,1,128]{2,1,0:T(1,128)}), f32[8,1,128]{2,1,0:T(1,128)S(1)}, u32[]{:S(2)}, u32[]{:S(2)}) async-start(f32[8,1,128]{2,1,0:T(1,128)} %bitcast.72), calls=%async_computation.10 | async-start | bytes 8192 | tf_op jit(solution)/shard_map/all_to_all | solution.py:573
  548.7 67.0 %collective-permute-start.73 = (bf16[512,2048]{1,0:T(8,128)(2,1)}, bf16[512,2048]{1,0:T(8,128)(2,1)}, u32[]{:S(2)}, u32[]{:S(2)}) collective-permute-start(bf16[512,2048]{1,0:T(8,128)(2,1)} %collective-permute-done.47), channel_id=1, source_target_pairs={{0,1},{1,0},{2,3},{3,2},{4,5},{5,4},{6,7},{7,6},{8,9},{9,8},{10,11... | collective-permute-start | bytes 6291464 | tf_op jit(solution)/shard_map/ppermute | solution.py:53
  563.5 62.1 %all-to-all-start.4 = ((f32[32,3,128]{2,1,0:T(4,128)}), f32[32,3,128]{2,1,0:T(4,128)S(1)}, u32[]{:S(2)}, u32[]{:S(2)}) async-start(f32[32,3,128]{2,1,0:T(4,128)} %reshape.695), calls=%async_computation.7 | async-start | bytes 131072 | tf_op jit(solution)/shard_map/all_to_all | solution.py:609
  579.3 40.9 %collective-permute-start.66 = (bf16[176,2048]{1,0:T(8,128)(2,1)S(1)}, bf16[176,2048]{1,0:T(8,128)(2,1)S(1)}, u32[]{:S(2)}, u32[]{:S(2)}) collective-permute-start(bf16[176,2048]{1,0:T(8,128)(2,1)S(1)} %slice.404), channel_id=1, source_target_pairs={{0,2},{1,5},{2,0},{3,7},{4,6},{5,1},{6,4},{7,3},{8,10},{9,13},{10,... | collective-permute-start | bytes 2162696 | tf_op jit(solution)/shard_map/ppermute | solution.py:53
  603.3 17.1 %collective-permute-start.65 = (bf16[176,2048]{1,0:T(8,128)(2,1)S(1)}, bf16[176,2048]{1,0:T(8,128)(2,1)S(1)}, u32[]{:S(2)}, u32[]{:S(2)}) collective-permute-start(bf16[176,2048]{1,0:T(8,128)(2,1)S(1)} %slice.405), channel_id=1, source_target_pairs={{0,2},{1,5},{2,0},{3,7},{4,6},{5,1},{6,4},{7,3},{8,10},{9,13},{10,... | collective-permute-start | bytes 2162696 | tf_op jit(solution)/shard_map/ppermute | solution.py:53
  606.5 15.9 %collective-permute-start.64 = (bf16[176,2048]{1,0:T(8,128)(2,1)S(1)}, bf16[176,2048]{1,0:T(8,128)(2,1)S(1)}, u32[]{:S(2)}, u32[]{:S(2)}) collective-permute-start(bf16[176,2048]{1,0:T(8,128)(2,1)S(1)} %slice.406), channel_id=1, source_target_pairs={{0,2},{1,5},{2,0},{3,7},{4,6},{5,1},{6,4},{7,3},{8,10},{9,13},{10,... | collective-permute-start | bytes 2162696 | tf_op jit(solution)/shard_map/ppermute | solution.py:53
  631.6 16.3 %all-to-all-start.5 = ((bf16[8,64,768]{2,1,0:T(8,128)(2,1)}), bf16[8,64,768]{2,1,0:T(8,128)(2,1)S(1)}, u32[]{:S(2)}, u32[]{:S(2)}) async-start(bf16[8,64,768]{2,1,0:T(8,128)(2,1)} %reshape.697), calls=%async_computation.9 | async-start | bytes 1572864 | tf_op jit(solution)/shard_map/all_to_all | solution.py:556
  (118 other events, 1356.5 us)
Sparse Core Ops, SparseCore 0:
  9.6 30.6 all-gather.11
  42.4 68.4 all-gather.5
  112.5 44.3 all-gather.7
  197.3 56.1 all-gather.9
  255.6 108.4 reduce-scatter.4
  366.3 43.2 reduce-scatter.6
  412.1 101.5 reduce-scatter.10
  516.1 112.2 reduce-scatter.8
